TPU v7x, 32 devices: a whole 2x2x4 slice. The times are simulated.
32 devices in a mesh: dp: 16 (over z, y, x), tensor: 2 (over core).
Axes of the slice: x: 2, y: 2, z: 4, core: 2. Of those that a mesh axis runs over, the one named last changes fastest.
Arguments:
- tokens: bfloat16 [16384, 768], P('dp'), may hold values from -6 to 6
- w_qkv: bfloat16 [3, 768, 768], P(None, None, 'tensor'), may hold values from -0.21875 to 0.21875
- bias_qv: float32 [2, 768], P(None, 'tensor'), may hold values from -3 to 3
- w_out: bfloat16 [768, 768], P('tensor'), may hold values from -0.875 to 0.875
- bias_out: float32 [768], replicated, may hold values from -2 to 2
- gain_attn: float32 [768], replicated, may hold values from 0.5 to 1.5
- shift_attn: float32 [768], replicated, may hold values from -2 to 2
- w_up: bfloat16 [768, 3072], P(None, 'tensor'), may hold values from -0.21875 to 0.21875
- bias_up: float32 [3072], P('tensor'), may hold values from -3 to 3
- w_down: bfloat16 [3072, 768], P('tensor'), may hold values from -0.21875 to 0.21875
- bias_down: float32 [768], replicated, may hold values from -2 to 2
- gain_ffn: float32 [768], replicated, may hold values from 0.5 to 1.5
- shift_ffn: float32 [768], replicated, may hold values from -2 to 2
- out_grad: bfloat16 [16384, 768], P('dp'), may hold values from -6 to 6
- bucket_len: int32 [16], P('dp'), may hold values from 128 to 512, as said below
- seq_lengths: int32 [16, 8], P('dp'), may hold values from 32 to 512, as said below
- keep_mask: int32 [16, 8], P('dp'), may hold values 0 or 1
Outputs:
- mixed: bfloat16 [16384, 768], P('dp')
- input_grad: float32 [16384, 768], P('dp')
- grad_w_qkv: float32 [3, 768, 768], P(None, None, 'tensor')
- grad_bias_qv: float32 [2, 768], P(None, 'tensor')
- grad_w_out: float32 [768, 768], P('tensor')
- grad_bias_out: float32 [768], replicated
- grad_gain_attn: float32 [768], replicated
- grad_shift_attn: float32 [768], replicated
- grad_w_up: float32 [768, 3072], P(None, 'tensor')
- grad_bias_up: float32 [3072], P('tensor')
- grad_w_down: float32 [3072, 768], P('tensor')
- grad_bias_down: float32 [768], replicated
- grad_gain_ffn: float32 [768], replicated
- grad_shift_ffn: float32 [768], replicated
Inputs may be any that keep to these rules, and one draw needn't show every extreme that they name: `bucket_len`: group 0 has 512, group 1 has 128, every other group one of the two. seq_lengths[g, j] lies between bucket_len[g] // 4 and bucket_len[g]; slot 0 of every group equals bucket_len[g]; slots j >= 1024 // bucket_len[g] are not used. `keep_mask`: slots j >= 1024 // bucket_len[g] are not used.
All inputs are finite; a program needn't handle non-finite values. No bound on the sum of `keep_mask` on one device may be relied on, other than what follows from the above.
Results may differ from a plain program's by a relative error of at most 0.014.
The roundings to bfloat16 on the way count: a program that leaves them out, or rounds other values in their place, can miss the bound.
Values may be sent and summed in bfloat16 or wider, within the bound.
No kernel may reach another device: no remote copies, remote signals or barrier semaphores. Data moves between devices by JAX's collectives and lax.ppermute only.
A program may use at most 128 MiB of HBM per device.

v0:
```python
import jax
import jax.numpy as jnp
from jax import lax
from jax.sharding import PartitionSpec as P

HD = 64
BUCKET_LONG = 512


def layer_norm(residual, scale_vec, shift_vec):
    centre = residual - jnp.mean(residual, axis=-1, keepdims=True)
    spread = jnp.mean(centre * centre, axis=-1, keepdims=True)
    return centre * lax.rsqrt(spread + 1e-05) * scale_vec + shift_vec


def gelu_exact(pre_act):
    return jax.nn.gelu(pre_act, approximate=False)


def masked_scores(queries, key_rows, seq_ids, pos_ids, seq_lens):
    heads_q = queries.reshape(BUCKET_LONG, -1, HD)
    heads_k = key_rows.reshape(BUCKET_LONG, -1, HD)
    scores = (
        jnp.einsum("qhe,khe->hqk", heads_q, heads_k, preferred_element_type=jnp.float32) * 0.125
    )
    allowed = (seq_ids[:, None] == seq_ids[None, :]) & (pos_ids[None, :] < seq_lens[None, :])
    return jnp.where(allowed[None], scores, -1e30)


def attend_forward(pieces):
    queries, key_rows, values, seq_ids, pos_ids, seq_lens = pieces
    scores = masked_scores(queries, key_rows, seq_ids, pos_ids, seq_lens)
    top_score = jnp.max(scores, axis=-1, keepdims=True)
    expo = jnp.exp(scores - top_score)
    row_total = jnp.sum(expo, axis=-1, keepdims=True)
    weights = expo / row_total
    log_total = (top_score + jnp.log(row_total))[..., 0]
    heads_v = values.reshape(BUCKET_LONG, -1, HD)
    mixed_rows = jnp.einsum(
        "hqk,khe->qhe", weights.astype(jnp.bfloat16), heads_v, preferred_element_type=jnp.float32
    )
    return (mixed_rows.reshape(BUCKET_LONG, values.shape[1]).astype(jnp.bfloat16), log_total)


def attend_backward(pieces):
    queries, key_rows, values, grad_rows, log_total, seq_ids, pos_ids, seq_lens = pieces
    local_width = queries.shape[1]
    scores = masked_scores(queries, key_rows, seq_ids, pos_ids, seq_lens)
    weights = jnp.exp(scores - log_total[..., None])
    heads_q = queries.reshape(BUCKET_LONG, -1, HD)
    heads_k = key_rows.reshape(BUCKET_LONG, -1, HD)
    heads_v = values.reshape(BUCKET_LONG, -1, HD)
    heads_g = grad_rows.reshape(BUCKET_LONG, -1, HD)
    grad_weights = jnp.einsum("qhe,khe->hqk", heads_g, heads_v, preferred_element_type=jnp.float32)
    grad_values = jnp.einsum(
        "hqk,qhe->khe", weights.astype(jnp.bfloat16), heads_g, preferred_element_type=jnp.float32
    )
    inner = jnp.sum(weights * grad_weights, axis=-1, keepdims=True)
    grad_scores = (weights * (grad_weights - inner)).astype(jnp.bfloat16)
    grad_queries = (
        jnp.einsum("hqk,khe->qhe", grad_scores, heads_k, preferred_element_type=jnp.float32) * 0.125
    )
    grad_keys = (
        jnp.einsum("hqk,qhe->khe", grad_scores, heads_q, preferred_element_type=jnp.float32) * 0.125
    )
    return (
        grad_queries.reshape(BUCKET_LONG, local_width).astype(jnp.bfloat16),
        grad_keys.reshape(BUCKET_LONG, local_width).astype(jnp.bfloat16),
        grad_values.reshape(BUCKET_LONG, local_width).astype(jnp.bfloat16),
    )


def per_device(
    tokens,
    w_qkv,
    bias_qv,
    w_out,
    bias_out,
    gain_attn,
    shift_attn,
    w_up,
    bias_up,
    w_down,
    bias_down,
    gain_ffn,
    shift_ffn,
    out_grad,
    bucket_len,
    seq_lengths,
    keep_mask,
):
    row_count = tokens.shape[0]
    block_count = row_count // BUCKET_LONG
    seq_span = bucket_len[0]
    places = jnp.arange(row_count, dtype=jnp.int32)
    seq_ids = places // seq_span
    pos_ids = places - seq_ids * seq_span
    slot_hit = (
        seq_ids[:, None] == jnp.arange(seq_lengths.shape[1], dtype=jnp.int32)[None, :]
    ).astype(jnp.int32)
    row_len = jnp.sum(slot_hit * seq_lengths[0][None, :], axis=-1)
    keep_col = (jnp.sum(slot_hit * keep_mask[0][None, :], axis=-1) > 0)[:, None]

    def blocked(array_in):
        return array_in.reshape((block_count, BUCKET_LONG) + array_in.shape[1:])

    inputs_f = tokens.astype(jnp.float32)
    projected = jnp.einsum("rd,kde->kre", tokens, w_qkv, preferred_element_type=jnp.float32)
    queries = (projected[0] + bias_qv[0]).astype(jnp.bfloat16)
    key_rows = projected[1].astype(jnp.bfloat16)
    values = (projected[2] + bias_qv[1]).astype(jnp.bfloat16)
    attended, log_total = lax.map(
        attend_forward,
        (
            blocked(queries),
            blocked(key_rows),
            blocked(values),
            blocked(seq_ids),
            blocked(pos_ids),
            blocked(row_len),
        ),
    )
    attended = attended.reshape(row_count, -1)
    attn_part = jnp.dot(attended, w_out, preferred_element_type=jnp.float32)
    grad_in = out_grad.astype(jnp.float32)
    kept_grad = jnp.where(keep_col, grad_in, 0.0)
    skip_grad = grad_in - kept_grad
    attn_sum = lax.psum(attn_part, "tensor") + bias_out
    normed, norm_pull = jax.vjp(layer_norm, inputs_f + attn_sum, gain_attn, shift_attn)
    normed_low = normed.astype(jnp.bfloat16)
    pre_act = jnp.dot(normed_low, w_up, preferred_element_type=jnp.float32) + bias_up
    activated, gelu_pull = jax.vjp(gelu_exact, pre_act)
    act_low = activated.astype(jnp.bfloat16)
    ffn_part = jnp.dot(act_low, w_down, preferred_element_type=jnp.float32)
    ffn_sum = lax.psum(ffn_part, "tensor") + bias_down
    final, final_pull = jax.vjp(layer_norm, normed + ffn_sum, gain_ffn, shift_ffn)
    mixed = jnp.where(keep_col, final, inputs_f).astype(jnp.bfloat16)
    grad_r2, grad_gain_ffn, grad_shift_ffn = final_pull(kept_grad)
    grad_ffn = grad_r2.astype(jnp.bfloat16)
    grad_bias_down = jnp.sum(grad_ffn.astype(jnp.float32), axis=0)
    grad_w_down = jnp.einsum("rf,rd->fd", act_low, grad_ffn, preferred_element_type=jnp.float32)
    grad_act = jnp.einsum("rd,fd->rf", grad_ffn, w_down, preferred_element_type=jnp.float32)
    (grad_pre,) = gelu_pull(grad_act)
    grad_pre_low = grad_pre.astype(jnp.bfloat16)
    grad_bias_up = jnp.sum(grad_pre_low.astype(jnp.float32), axis=0)
    grad_w_up = jnp.einsum(
        "rd,rf->df", normed_low, grad_pre_low, preferred_element_type=jnp.float32
    )
    ffn_parts = (grad_w_down, grad_bias_down, grad_w_up, grad_bias_up)
    hidden_part = jnp.einsum("rf,df->rd", grad_pre_low, w_up, preferred_element_type=jnp.float32)
    grad_normed = grad_r2 + lax.psum(hidden_part, "tensor")
    grad_r1, grad_gain_attn, grad_shift_attn = norm_pull(grad_normed)
    grad_attn = grad_r1.astype(jnp.bfloat16)
    grad_bias_out = jnp.sum(grad_attn.astype(jnp.float32), axis=0)
    grad_w_out = jnp.einsum("rl,rd->ld", attended, grad_attn, preferred_element_type=jnp.float32)
    grad_heads = jnp.einsum(
        "rd,ld->rl", grad_attn, w_out, preferred_element_type=jnp.float32
    ).astype(jnp.bfloat16)
    grad_q, grad_k, grad_v = lax.map(
        attend_backward,
        (
            blocked(queries),
            blocked(key_rows),
            blocked(values),
            blocked(grad_heads),
            log_total,
            blocked(seq_ids),
            blocked(pos_ids),
            blocked(row_len),
        ),
    )
    grad_stack = jnp.stack(
        [
            grad_q.reshape(row_count, -1),
            grad_k.reshape(row_count, -1),
            grad_v.reshape(row_count, -1),
        ]
    )
    grad_w_qkv = jnp.einsum("rd,kre->kde", tokens, grad_stack, preferred_element_type=jnp.float32)
    grad_sums = jnp.sum(grad_stack.astype(jnp.float32), axis=1)
    grad_bias_qv = jnp.stack([grad_sums[0], grad_sums[2]])
    input_part = jnp.einsum("kre,kde->rd", grad_stack, w_qkv, preferred_element_type=jnp.float32)
    norm_local = (grad_gain_attn, grad_shift_attn, grad_gain_ffn, grad_shift_ffn)
    norm_terms = tuple((jnp.zeros_like(member) for member in norm_local))
    base_grad = skip_grad + grad_r1
    summed_in = (
        lax.psum(input_part.astype(jnp.bfloat16), "tensor").astype(jnp.float32),
        lax.psum(norm_terms[0].astype(jnp.bfloat16), "tensor").astype(jnp.float32),
        lax.psum(norm_terms[1].astype(jnp.bfloat16), "tensor").astype(jnp.float32),
        lax.psum(norm_terms[2].astype(jnp.bfloat16), "tensor").astype(jnp.float32),
        lax.psum(norm_terms[3].astype(jnp.bfloat16), "tensor").astype(jnp.float32),
    )
    input_grad = base_grad + summed_in[0]
    summed = lax.psum(
        (
            grad_w_qkv,
            grad_bias_qv,
            grad_w_out,
            grad_bias_out,
            norm_local[0],
            norm_local[1],
            norm_local[2],
            norm_local[3],
            ffn_parts[0],
            ffn_parts[1],
            ffn_parts[2],
            ffn_parts[3],
        ),
        "dp",
    )
    attn_parts = summed[:8]
    ffn_parts = summed[8:]
    return (
        mixed,
        input_grad,
        attn_parts[0],
        attn_parts[1],
        attn_parts[2],
        attn_parts[3],
        attn_parts[4],
        attn_parts[5],
        ffn_parts[2],
        ffn_parts[3],
        ffn_parts[0],
        ffn_parts[1],
        attn_parts[6],
        attn_parts[7],
    )


def solution(mesh):
    in_specs = (
        P("dp", None),
        P(None, None, "tensor"),
        P(None, "tensor"),
        P("tensor", None),
        P(),
        P(),
        P(),
        P(None, "tensor"),
        P("tensor"),
        P("tensor", None),
        P(),
        P(),
        P(),
        P("dp", None),
        P("dp"),
        P("dp", None),
        P("dp", None),
    )
    out_specs = (
        P("dp", None),
        P("dp", None),
        P(None, None, "tensor"),
        P(None, "tensor"),
        P("tensor", None),
        P(),
        P(),
        P(),
        P(None, "tensor"),
        P("tensor"),
        P("tensor", None),
        P(),
        P(),
        P(),
    )
    return jax.shard_map(
        per_device, mesh=mesh, in_specs=in_specs, out_specs=out_specs, check_vma=False
    )
```

profile of v0, /device:TPU:0, one launch (start us, length us, event | category | flops | bytes accessed | tf_op | source)
XLA Modules:
  0.0 700.6 jit_solution(5666783777506900615)
XLA Ops:
  7.2 4.2 convolution_bitcast_fusion
  15.7 3.6 squeeze.30
  22.1 3.4 squeeze.29
  25.5 3.6 fusion.33
  30.0 20.4 %while.26 = (s32[]{:T(128)}, bf16[2,512,384]{2,1,0:T(8,128)(2,1)}, f32[2,6,512]{2,1,0:T(8,128)}, bf16[2,512,384]{1,2,0:T(8,128)(2,1)}, s32[2,512]{1,0:T(2,128)S(...) while((s32[]{:T(128)}, bf16[2,512,384]{2,1,0:T(8,128)(2,1)}, ...), condition=%wide.region_5.6_spmd, body=%wide.region_2.5_spmd.sunk | while | flops 422245888 | bytes 25541764 | solution.py:112
  50.5 3.9 fusion.50
  54.5 26.0 %all-reduce.8.cloned.1.call-done = f32[1024,768]{1,0:T(8,128)} async-done(((f32[1024,768]{1,0:T(8,128)}), f32[1024,768]{1,0:T(8,128)}) %all-reduce.8.cloned.1.call-update) | async-done | bytes 3145744 | tf_op jit(solution)/shard_map/psum | solution.py:128
  80.5 2.8 fusion.46
  84.2 17.9 %multiply_convert_fusion.1 = (bf16[1024,1536]{1,0:T(8,128)(2,1)S(1)}, f32[1024,1536]{1,0:T(8,128)}, f32[1024,1536]{1,0:T(8,128)}) fusion(f32[1536]{0:T(1024)S(1)} %copy-done.51, bf16[768,1536]{1,0:T(8,128)(2,1)S(1)} %copy-done, f32[1024,768]{1,0:T(8,128)S(1)} %get-tuple-element.316, f32[768]{0:T(1024)S(1)} %copy-done.44, f32[768]{0:T(1024)S(1)} %copy-done.25, ...), kind=kOutput, calls=%fused_computation.49 | convolution fusion | flops 2523660288 | bytes 21254144 | tf_op jit(solution)/shard_map/dot_general | solution.py:131
  103.8 4.3 fusion.51
  108.7 23.9 %all-reduce.10.cloned.1.call-done = f32[1024,768]{1,0:T(8,128)} async-done(((f32[1024,768]{1,0:T(8,128)}), f32[1024,768]{1,0:T(8,128)}) %all-reduce.10.cloned.1.call-update) | async-done | bytes 3145744 | tf_op jit(solution)/shard_map/psum | solution.py:135
  132.6 4.0 fusion.44
  140.3 3.1 fusion.43
  146.2 5.1 convert_reduce_fusion
  153.0 4.3 fusion.52
  157.4 24.5 %all-reduce.12.cloned.1.call-done = f32[1024,768]{1,0:T(8,128)} async-done(((f32[1024,768]{1,0:T(8,128)}), f32[1024,768]{1,0:T(8,128)}) %all-reduce.12.cloned.1.call-update) | async-done | bytes 3145744 | tf_op jit(solution)/shard_map/psum | solution.py:151
  181.9 5.4 multiply_reduce_fusion.1
  187.3 2.9 fusion.42
  196.4 49.0 %while.27 = (s32[]{:T(128)}, bf16[2,512,384]{2,1,0:T(8,128)(2,1)}, bf16[2,512,384]{2,1,0:T(8,128)(2,1)}, bf16[2,512,384]{2,1,0:T(8,128)(2,1)}, bf16[2,512,384]{1...) while((s32[]{:T(128)}, bf16[2,512,384]{2,1,0:T(8,128)(2,1)}, ...), condition=%wide.region_19.20_spmd, body=%wide.region_17.19_spmd.sunk | while | flops 1031730688 | bytes 111246560 | solution.py:159
  204.6 7.5 %multiply_reduce_fusion.6 = (f32[6,512]{1,0:T(8,128)S(1)}, f32[6,512,512]{1,2,0:T(8,128)}) fusion(f32[6,512,512]{1,2,0:T(8,128)} %copy-done.2, f32[6,512]{1,0:T(8,128)S(1)} %dynamic-slice_bitcast_fusion.2, pred[512,512]{0,1:T(8,128)(4,1)S(1)} %compare_and_fusion.5, bf16[512,6,64]{0,2,1:T(8,128)(2,1)S(1)} %bitcast.144, ...), kind=kOutput, calls=%fused_computation.20.clone.1 | convolution fusion | flops 209187840 | bytes 13656064 | tf_op jit(solution)/shard_map/while/body/eval_jaxpr/qhe,khe->hqk/dot_general | solution.py:54
  212.1 4.7 multiply_convert_fusion.3
  229.0 7.5 %multiply_reduce_fusion.6 = (f32[6,512]{1,0:T(8,128)S(1)}, f32[6,512,512]{1,2,0:T(8,128)}) fusion(f32[6,512,512]{1,2,0:T(8,128)} %copy-done.2, f32[6,512]{1,0:T(8,128)S(1)} %dynamic-slice_bitcast_fusion.2, pred[512,512]{0,1:T(8,128)(4,1)S(1)} %compare_and_fusion.5, bf16[512,6,64]{0,2,1:T(8,128)(2,1)S(1)} %bitcast.144, ...), kind=kOutput, calls=%fused_computation.20.clone.1 | convolution fusion | flops 209187840 | bytes 13656064 | tf_op jit(solution)/shard_map/while/body/eval_jaxpr/qhe,khe->hqk/dot_general | solution.py:54
  236.5 4.7 multiply_convert_fusion.3
  245.4 5.8 bitcast_convert_fusion
  251.3 6.9 fusion.54
  258.2 4.6 fusion.38
  264.9 3.9 convolution_bitcast_fusion.1
  271.8 81.3 %all-reduce = (f32[2,384]{1,0:T(2,128)}, f32[768]{0:T(1024)}, f32[768]{0:T(1024)}, f32[768]{0:T(1024)}, f32[1536]{0:T(1024)}, /*index=5*/f32[768]{0:T(1024)}, f32[768]{0:T(1024)}, f32[768]{0:T(1024)}) all-reduce(f32[2,384]{1,0:T(2,128)S(1)} %pad_maximum_fusion.1, ...), channel_id=1, replica_groups=mesh['dp'=16,'tensor'=2] {'dp'}, use_global_device_ids=true, to_apply=%region_23.24 | all-reduce | flops 6912 | bytes 55296 | tf_op jit(solution)/shard_map/psum | solution.py:194
  353.1 4.1 fusion.28
  357.2 322.7 %all-reduce.16.cloned.1.call-done = (f32[3,768,384]{1,2,0:T(8,128)}, f32[384,768]{1,0:T(8,128)}, f32[768,1536]{1,0:T(8,128)}, f32[1536,768]{1,0:T(8,128)}) async-done(((f32[3,768,384]{1,2,0:T(8,128)}, f32[384,768]{1,0:T(8,128)}, f32[768,1536]{1,0:T(8,128)}, f32[1536,768]{1,0:T(8,128)}), (f32[3,768,384]{1,2,0:T(8,128)}, f32[384,768]{1,0:T(8,128)}, f32[768,1536]{1,0:T(8,128)}, ...) | async-done | bytes 14155792 | tf_op jit(solution)/shard_map/psum | solution.py:194
  679.9 5.2 copy.77
  686.2 5.5 copy.147
  (233 shorter events, 77.7 us)
Async XLA Ops:
  7.2 76.7 %copy-start = (bf16[768,1536]{1,0:T(8,128)(2,1)S(1)}, bf16[768,1536]{1,0:T(8,128)(2,1)}, u32[]{:S(2)}) copy-start(bf16[768,1536]{1,0:T(8,128)(2,1)} %param.28) | copy-start | bytes 7077892
  7.2 73.3 %all-reduce.8.cloned.1.call-start = ((), (), s32[]{:S(2)}) async-start(), calls=%async_computation | async-start | bytes 6291456 | tf_op jit(solution)/shard_map/psum | solution.py:128
  50.5 30.0 %copy-start.42 = (f32[768]{0:T(1024)S(1)}, f32[768]{0:T(1024)}, u32[]{:S(2)}) copy-start(f32[768]{0:T(1024)} %param.25) | copy-start | bytes 9220
  54.4 78.2 %all-reduce.10.cloned.1.call-start = ((), (), s32[]{:S(2)}) async-start(), calls=%async_computation.1 | async-start | bytes 6291456 | tf_op jit(solution)/shard_map/psum | solution.py:135
  83.3 18.8 %copy-start.4 = (f32[1024,768]{1,0:T(8,128)}, f32[1024,768]{1,0:T(8,128)S(1)}, u32[]{:S(2)}) copy-start(f32[1024,768]{1,0:T(8,128)S(1)} %get-tuple-element.316) | copy-start | bytes 9437188
  84.2 103.1 %copy-start.23 = (f32[1024]{0:T(1024)}, f32[1024]{0:T(1024)S(1)}, u32[]{:S(2)}) copy-start(f32[1024]{0:T(1024)S(1)} %fusion.36) | copy-start | bytes 12292
  84.2 19.6 %copy-start.49 = (bf16[1536,768]{1,0:T(8,128)(2,1)S(1)}, bf16[1536,768]{1,0:T(8,128)(2,1)}, u32[]{:S(2)}) copy-start(bf16[1536,768]{1,0:T(8,128)(2,1)} %param.30) | copy-start | bytes 7077892
  108.0 24.6 %copy-start.43 = (f32[768]{0:T(1024)S(1)}, f32[768]{0:T(1024)}, u32[]{:S(2)}) copy-start(f32[768]{0:T(1024)} %param.31) | copy-start | bytes 9220
  108.1 73.8 %all-reduce.12.cloned.1.call-start = ((), (), s32[]{:S(2)}) async-start(), calls=%async_computation.2 | async-start | bytes 6291456 | tf_op jit(solution)/shard_map/psum | solution.py:151
  108.7 31.6 %copy-start.37 = (pred[1024]{0:T(1024)(128)(4,1)}, pred[1024]{0:T(1024)(128)(4,1)S(1)}, u32[]{:S(2)}) copy-start(pred[1024]{0:T(1024)(128)(4,1)S(1)} %broadcast_compare_fusion) | copy-start | bytes 3076
  132.6 13.4 %slice-start.4 = ((s8[6291456]{0:T(1024)(128)(4,1)}), s8[4194304]{0:T(1024)(128)(4,1)S(1)}, s32[]{:S(2)}) async-start(s8[6291456]{0:T(1024)(128)(4,1)} %bitcast.170), calls=%async_computation.9 | async-start | bytes 8388608
  138.0 8.0 %slice-start.5 = ((s8[6291456]{0:T(1024)(128)(4,1)}), s8[2097152]{0:T(1024)(128)(4,1)S(1)}, s32[]{:S(2)}) async-start(s8[6291456]{0:T(1024)(128)(4,1)} %bitcast.170), calls=%async_computation.10 | async-start | bytes 4194304
  140.3 5.7 slice-start.2
  140.3 5.7 slice-start.3
  146.0 5.3 copy-start.19
  157.3 195.8 %all-reduce.14.cloned.1.call-start = ((), (), s32[]{:S(2)}) async-start(), calls=%async_computation.3 | async-start | bytes 3145728 | tf_op jit(solution)/shard_map/psum | solution.py:187
  204.6 7.5 %copy-start.3 = (f32[6,512,512]{1,2,0:T(8,128)S(1)}, f32[6,512,512]{1,2,0:T(8,128)}, u32[]{:S(2)}) copy-start(f32[6,512,512]{1,2,0:T(8,128)} %copy-done.2) | copy-start | bytes 18874372 | tf_op jit(solution)/shard_map/while
  229.0 7.5 %copy-start.3 = (f32[6,512,512]{1,2,0:T(8,128)S(1)}, f32[6,512,512]{1,2,0:T(8,128)}, u32[]{:S(2)}) copy-start(f32[6,512,512]{1,2,0:T(8,128)} %copy-done.2) | copy-start | bytes 18874372 | tf_op jit(solution)/shard_map/while
  245.3 5.9 copy-start.20
  251.2 7.0 %copy-start.24 = (f32[1024]{0:T(1024)S(1)}, f32[1024]{0:T(1024)}, u32[]{:S(2)}) copy-start(f32[1024]{0:T(1024)} %copy-done.23) | copy-start | bytes 12292
  251.2 7.0 %copy-start.26 = (f32[768]{0:T(1024)S(1)}, f32[768]{0:T(1024)}, u32[]{:S(2)}) copy-start(f32[768]{0:T(1024)} %param.26) | copy-start | bytes 9220
  251.2 7.0 copy-start.45
  251.2 428.7 %all-reduce.16.cloned.1.call-start = ((), (), s32[]{:S(2)}) async-start(), calls=%async_computation.4 | async-start | bytes 28311552 | tf_op jit(solution)/shard_map/psum | solution.py:194
  251.2 6.9 copy-start.5
  251.3 6.9 copy-start.54
  258.2 6.5 copy-start.18
  268.9 84.2 %copy-start.28 = (f32[1024]{0:T(1024)S(1)}, f32[1024]{0:T(1024)}, u32[]{:S(2)}) copy-start(f32[1024]{0:T(1024)} %copy-done.27) | copy-start | bytes 12292
  268.9 84.2 %copy-start.38 = (pred[1024]{0:T(1024)(128)(4,1)S(1)}, pred[1024]{0:T(1024)(128)(4,1)}, u32[]{:S(2)}) copy-start(pred[1024]{0:T(1024)(128)(4,1)} %copy-done.37) | copy-start | bytes 3076
  270.1 83.1 %copy-start.9 = (bf16[1024,768]{1,0:T(8,128)(2,1)S(1)}, bf16[1024,768]{1,0:T(8,128)(2,1)}, u32[]{:S(2)}) copy-start(bf16[1024,768]{1,0:T(8,128)(2,1)} %param.34) | copy-start | bytes 4718596
  685.1 6.5 slice-start
  686.2 5.5 slice-start.1
  686.2 7.7 %copy-start.1 = (bf16[768,1536]{1,0:T(8,128)(2,1)S(1)}, bf16[768,1536]{1,0:T(8,128)(2,1)}, u32[]{:S(2)}) copy-start(bf16[768,1536]{1,0:T(8,128)(2,1)} %param.28) | copy-start | bytes 7077892
  (36 other events, 94.0 us)
Sparse Core Ops, SparseCore 0:
  54.6 25.8 all-reduce.7
  108.2 24.3 all-reduce.9
  157.5 24.3 all-reduce.11
  251.3 21.5 all-reduce.13
  280.3 399.5 all-reduce.15
where the time goes:
time: 705 us; the launch traced here: 701 us
  waiting for transfers between devices  397 us (56%)
  matrix products  96.2 us (14%)
  blocking collectives  81.3 us (12%)
  local copies, waits for them, and re-layouts  62.2 us (9%)
  other arithmetic  47.9 us (7%)
  between operations  15.2 us (2%)
    psum x1, waiting for transfers between devices, per_device(): lax.psum((grad_w_qkv, grad_bias_qv, grad_w_out, grad_bias_out, norm_local...  323 us
    psum x1, blocking collectives, per_device(): lax.psum((grad_w_qkv, grad_bias_qv, grad_w_out, grad_bias_out, norm_local...  81.3 us
    psum x1, waiting for transfers between devices, per_device(): attn_sum = lax.psum(attn_part, 'tensor') + bias_out  26 us
    psum x1, waiting for transfers between devices, per_device(): grad_normed = grad_r2 + lax.psum(hidden_part, 'tensor')  24.5 us
    psum x1, waiting for transfers between devices, per_device(): ffn_sum = lax.psum(ffn_part, 'tensor') + bias_down  23.9 us
    unnamed x122, local copies, waits for them, and re-layouts  23 us
    dot_general x1, matrix products, per_device(): jnp.dot(normed_low, w_up, preferred_element_type=jnp.float32) + bias_up  17.9 us
    dot_general x2, matrix products, attend_backward(): jnp.einsum('qhe,khe->hqk', heads_g, heads_v, preferred_element_type=jnp.f...  15 us
  transfers between devices with their start and end apart: 5, of which 4 were waited for; matrix products, arithmetic and copies ran while one was open for 3% of the time, Pallas kernels for 0%

commit v1 on v0

v1 whole, which is shorter than its diff:
```python
import functools

import jax
import jax.numpy as jnp
from jax import lax
from jax.experimental import pallas as pl
from jax.experimental.pallas import tpu as pltpu
from jax.sharding import PartitionSpec as P

HD = 64
BUCKET_LONG = 512
LANES = 128
EPS = 1e-05
F32 = jnp.float32
BF16 = jnp.bfloat16
NEG = -1e30
MIB = 1 << 20

STEP_BITS = (
    ((0, 1, 2, 3), (1, 0, 2, 3)),
    ((2, 0, 1, 3), (0, 1, 2, 3)),
    ((1, 0, 2, 3), (2, 1, 0, 3)),
)


def dot_nn(left, right):
    return lax.dot_general(left, right, (((1,), (0,)), ((), ())), preferred_element_type=F32)


def dot_nt(left, right):
    return lax.dot_general(left, right, (((1,), (1,)), ((), ())), preferred_element_type=F32)


def dot_tn(left, right):
    return lax.dot_general(left, right, (((0,), (0,)), ((), ())), preferred_element_type=F32)


def whole(shape):
    rank = len(shape)
    return pl.BlockSpec(shape, lambda *_: (0,) * rank)


def shaped(shape, dtype):
    return jax.ShapeDtypeStruct(shape, dtype)


def call(body, out_shape, grid, scalars, in_specs, out_specs, scratch, vmem, flops, moved, trans=0):
    return pl.pallas_call(
        body,
        out_shape=out_shape,
        grid_spec=pltpu.PrefetchScalarGridSpec(
            num_scalar_prefetch=scalars,
            grid=grid,
            in_specs=in_specs,
            out_specs=out_specs,
            scratch_shapes=scratch,
        ),
        compiler_params=pltpu.CompilerParams(
            dimension_semantics=("arbitrary",) * len(grid), vmem_limit_bytes=vmem * MIB
        ),
        cost_estimate=pl.CostEstimate(flops=flops, bytes_accessed=moved, transcendentals=trans),
    )


def bucket_shift(bucket_ref):
    return jnp.where(bucket_ref[0] >= BUCKET_LONG, 9, 7)


def mask_columns(ids_ref, bucket_ref, lens_ref, rows):
    shift = bucket_shift(bucket_ref)
    first = ids_ref[0] * lax.shift_right_logical(BUCKET_LONG, shift)
    place = lax.broadcasted_iota(jnp.int32, (rows, LANES), 0)
    lane = lax.broadcasted_iota(jnp.int32, (rows, LANES), 1) & (HD - 1)
    seq = lax.shift_right_logical(place, jnp.full((rows, LANES), shift, jnp.int32))
    pos = place - lax.shift_left(seq, jnp.full((rows, LANES), shift, jnp.int32))
    length = jnp.full((rows, LANES), lens_ref[0, first], jnp.int32)
    for slot in range(1, 4):
        length = jnp.where(seq == slot, lens_ref[0, first + slot], length)
    hit = seq == lane
    query_cols = jnp.where(hit, 1.0, 0.0)
    key_cols = jnp.where(hit & (pos < length), 0.0, NEG)
    key_cols = jnp.where(lane < 4, key_cols, jnp.where(lane < 7, 1.0, 0.0))
    return query_cols.astype(BF16), key_cols.astype(BF16)


def low_half(rows):
    return lax.broadcasted_iota(jnp.int32, (rows, LANES), 1) < HD


def attn_fwd_body(last, ids, bucket, lens, x_ref, w_ref, b_ref, *rest):
    if last:
        (other_o, wo_own, wo_other, bias_out, gain, shift_vec) = rest[:6]
        qa_ref, k_ref, v_ref, o_ref, n_ref, rstd_ref, hb_ref = rest[6:13]
        q_s, am_s, bm_s = rest[13:]
    else:
        qa_ref, k_ref, v_ref, o_ref = rest[:4]
        q_s, am_s, bm_s = rest[4:]
    rows = x_ref.shape[0]
    pairs = w_ref.shape[2] // LANES
    am, bm = mask_columns(ids, bucket, lens, rows)
    am_s[...] = am
    bm_s[...] = bm
    x = x_ref[...]
    q = ((dot_nn(x, w_ref[0]) + b_ref[0:1, :]).astype(BF16).astype(F32) * 0.125).astype(BF16)
    k = dot_nn(x, w_ref[1]).astype(BF16)
    v = (dot_nn(x, w_ref[2]) + b_ref[1:2, :]).astype(BF16)
    for p in range(pairs):
        cols = slice(p * LANES, (p + 1) * LANES)
        q_s[p] = q[:, cols]
        k_ref[p] = k[:, cols]
        v_ref[p] = v[:, cols]
    tile = rows // 2

    def step(i, carry):
        p = i // 2
        r0 = pl.multiple_of((i % 2) * tile, tile)
        qp = q_s[p, pl.ds(r0, tile), :]
        amb = am_s[pl.ds(r0, tile), :]
        kp = k_ref[p]
        vp = v_ref[p]
        bmb = bm_s[...]
        low_t, low_r = low_half(tile), low_half(rows)
        sums, tops = [], []
        for par in range(2):
            own_t = low_t if par == 0 else jnp.logical_not(low_t)
            own_r = low_r if par == 0 else jnp.logical_not(low_r)
            scores = dot_nt(jnp.where(own_t, qp, amb), jnp.where(own_r, kp, bmb))
            top = jnp.max(scores, axis=1, keepdims=True)
            expo = jnp.exp(scores - top).astype(BF16)
            sums.append(dot_nn(expo, jnp.where(own_r, vp, jnp.ones_like(vp))))
            tops.append(top)
        lane = lax.broadcasted_iota(jnp.int32, (tile, LANES), 1) & (HD - 1)
        for par in range(2):
            own_t = low_t if par == 0 else jnp.logical_not(low_t)
            neg_log = -(tops[par] + jnp.log(jnp.where(own_t, 1.0, sums[par])))
            hi = neg_log.astype(BF16)
            mid = (neg_log - hi.astype(F32)).astype(BF16)
            lo = (neg_log - hi.astype(F32) - mid.astype(F32)).astype(BF16)
            cols = jnp.where(lane == 4, hi, jnp.where(lane == 5, mid, jnp.where(lane == 6, lo, amb)))
            qa_ref[2 * p + par, pl.ds(r0, tile), :] = jnp.where(own_t, qp, cols)
        total = pltpu.roll(jnp.where(low_t, sums[1], sums[0]), HD, 1)
        o_ref[p, pl.ds(r0, tile), :] = (jnp.where(low_t, sums[0], sums[1]) / total).astype(BF16)
        return carry

    lax.fori_loop(0, 2 * pairs, step, 0)
    if last:
        block = rows // 4

        def norm(i, carry):
            r = pl.ds(pl.multiple_of(i * block, block), block)
            acc = x_ref[r, :].astype(F32) + bias_out[...]
            for p in range(pairs):
                cols = slice(p * LANES, (p + 1) * LANES)
                acc += dot_nn(o_ref[p, r, :], wo_own[cols, :])
                acc += dot_nn(other_o[p, r, :], wo_other[cols, :])
            centre = acc - jnp.mean(acc, axis=1, keepdims=True)
            rstd = lax.rsqrt(jnp.mean(centre * centre, axis=1, keepdims=True) + EPS)
            normed = centre * rstd
            n_ref[r, :] = normed
            rstd_ref[r, :] = jnp.broadcast_to(rstd, (block, LANES))
            hb_ref[r, :] = (normed * gain[...] + shift_vec[...]).astype(BF16)
            return carry

        lax.fori_loop(0, 4, norm, 0)


def attn_fwd(last, scal, tokens, w, b, rows, extra=()):
    width = tokens.shape[1]
    local = w.shape[2]
    pairs = local // LANES
    trio = (pairs, rows, LANES)
    outs = [shaped((2 * pairs, rows, LANES), BF16)] + [shaped(trio, BF16)] * 3
    if last:
        outs += [shaped((rows, width), F32), shaped((rows, LANES), F32), shaped((rows, width), BF16)]
    flops = 2 * rows * local * (3 * width + 4 * rows + (2 * width if last else 0))
    moved = 2 * (rows * width + 3 * width * local + 5 * rows * local) + (rows * width * 6 if last else 0)
    return call(
        functools.partial(attn_fwd_body, last),
        outs,
        (1,),
        3,
        [
            pl.BlockSpec((rows, width), lambda i, ids, *_: (ids[0], 0)),
            whole(w.shape),
            whole(b.shape),
        ]
        + [whole(e.shape) for e in extra],
        [whole(o.shape) for o in outs],
        [pltpu.VMEM(trio, BF16), pltpu.VMEM((rows, LANES), BF16), pltpu.VMEM((rows, LANES), BF16)],
        30,
        flops,
        moved,
        2 * pairs * rows * rows,
    )(*scal, tokens, w, b, *extra)


def keep_of(ids, bucket, keep, block):
    shift = bucket_shift(bucket)
    first = ids[0] * lax.shift_right_logical(BUCKET_LONG, shift)
    return keep[0, first + lax.shift_right_logical(block * LANES, shift)] > 0


def fold_rows(array_in):
    rows, cols = array_in.shape
    return jnp.sum(array_in.reshape(rows // 8, 8, cols), axis=0)


def ffn_fwd_body(
    ids, bucket, keep, hb_ref, n_ref, up_own, up_other, bu_own, bu_other, down_own, down_other,
    gain_a, shift_a, bias_down, gain_f, shift_f, x_ref, g_ref,
    gb_own, gb_other, gp_own, gp_other, mixed_ref, dr2_ref, df_ref, vec_ref, acc, fold_s,
):
    i = pl.program_id(0)
    rows, width = hb_ref.shape

    @pl.when(i == 0)
    def _():
        acc[...] = n_ref[...] * gain_a[...] + shift_a[...] + bias_down[...]

    half = rows // 2
    for r in range(2):
        rs = slice(r * half, (r + 1) * half)
        hb = hb_ref[rs, :]
        total = None
        for up, bu, down, gb, gp in (
            (up_own, bu_own, down_own, gb_own, gp_own),
            (up_other, bu_other, down_other, gb_other, gp_other),
        ):
            u = dot_nn(hb, up[...]) + bu[...]
            cdf = 0.5 * (1.0 + lax.erf(u * 0.7071067811865476))
            pdf = jnp.exp(-0.5 * u * u) * 0.3989422804014327
            gp[rs, :] = cdf + u * pdf
            act = (u * cdf).astype(BF16)
            gb[rs, :] = act
            part = dot_nn(act, down[...])
            total = part if total is None else total + part
        acc[rs, :] += total

    @pl.when(i == pl.num_programs(0) - 1)
    def _():
        fold_s[...] = jnp.zeros_like(fold_s)

        def norm(blk, carry):
            r = pl.ds(pl.multiple_of(blk * LANES, LANES), LANES)
            kept = keep_of(ids, bucket, keep, blk)
            res = acc[r, :]
            centre = res - jnp.mean(res, axis=1, keepdims=True)
            rstd = lax.rsqrt(jnp.mean(centre * centre, axis=1, keepdims=True) + EPS)
            normed = centre * rstd
            final = normed * gain_f[...] + shift_f[...]
            mixed_ref[r, :] = jnp.where(kept, final, x_ref[r, :].astype(F32)).astype(BF16)
            grad = jnp.where(kept, g_ref[r, :].astype(F32), 0.0)
            fold_s[0] += fold_rows(grad * normed)
            fold_s[1] += fold_rows(grad)
            scaled = grad * gain_f[...]
            mean_a = jnp.mean(scaled, axis=1, keepdims=True)
            mean_b = jnp.mean(scaled * normed, axis=1, keepdims=True)
            dr2 = (scaled - mean_a - normed * mean_b) * rstd
            dr2_ref[r, :] = dr2
            df = dr2.astype(BF16)
            df_ref[r, :] = df
            fold_s[2] += fold_rows(df.astype(F32))
            return carry

        lax.fori_loop(0, rows // LANES, norm, 0)
        vec_ref[...] = jnp.sum(fold_s[...], axis=1)


def ffn_fwd(scal, hb, n1, up_own, up_other, bu_own, bu_other, down_own, down_other, vecs, tokens, out_grad):
    rows, width = hb.shape
    hidden = up_own.shape[1]
    chunk = 256
    ids_rows = pl.BlockSpec((rows, width), lambda i, ids, *_: (ids[0], 0))
    up_spec = pl.BlockSpec((width, chunk), lambda i, *_: (0, i))
    bu_spec = pl.BlockSpec((1, chunk), lambda i, *_: (0, i))
    down_spec = pl.BlockSpec((chunk, width), lambda i, *_: (i, 0))
    act_spec = pl.BlockSpec((rows, chunk), lambda i, *_: (0, i))
    outs = [
        shaped((rows, hidden), BF16), shaped((rows, hidden), BF16),
        shaped((rows, hidden), F32), shaped((rows, hidden), F32),
        shaped((rows, width), BF16), shaped((rows, width), F32), shaped((rows, width), BF16),
        shaped((3, width), F32),
    ]
    return call(
        ffn_fwd_body,
        outs,
        (hidden // chunk,),
        3,
        [whole(hb.shape), whole(n1.shape), up_spec, up_spec, bu_spec, bu_spec, down_spec, down_spec]
        + [whole(vec.shape) for vec in vecs]
        + [ids_rows, ids_rows],
        [act_spec] * 4 + [whole(o.shape) for o in outs[4:]],
        [pltpu.VMEM((rows, width), F32), pltpu.VMEM((3, 8, width), F32)],
        30,
        8 * rows * width * hidden,
        12 * rows * hidden + 8 * width * hidden + 20 * rows * width,
        4 * rows * hidden,
    )(*scal, hb, n1, up_own, up_other, bu_own, bu_other, down_own, down_other, *vecs, tokens, out_grad)


def down_grad_body(pos, gb_own, gb_other, df_ref, out_own, out_other):
    i = pl.program_id(0)
    count, size, _ = out_own.shape
    per = gb_own.shape[1] // size
    df = df_ref[...]
    for table, gb, out in ((1, gb_other, out_other), (0, gb_own, out_own)):
        value = dot_tn(gb[...], df).astype(BF16)
        for c in range(per):
            out[pos[table, i * per + c]] = value[c * size : (c + 1) * size, :]


def down_grad(pos, gb_own, gb_other, df, count):
    rows, width = df.shape
    hidden = gb_own.shape[1]
    size = hidden // count
    chunk = size * (4 if count % 4 == 0 else 1)
    gb_spec = pl.BlockSpec((rows, chunk), lambda i, *_: (0, i))
    outs = [shaped((count, size, width), BF16)] * 2
    return call(
        down_grad_body,
        outs,
        (hidden // chunk,),
        1,
        [gb_spec, gb_spec, whole(df.shape)],
        [whole(o.shape) for o in outs],
        [],
        24,
        4 * rows * width * hidden,
        4 * rows * hidden + 4 * width * hidden + 2 * rows * width,
    )(pos, gb_own, gb_other, df)


def ffn_bwd_body(
    pos, df_ref, dr2_ref, hb_ref, gp_own, gp_other, down_own, down_other, up_own, up_other,
    n_ref, rstd_ref, gain_a, o_own, o_other,
    out_own, out_other, bu_own, bu_other, dr1_ref, da_ref, vec_ref, acc, fold_s,
):
    i = pl.program_id(0)
    rows, width = df_ref.shape
    count = out_own.shape[0]
    up_rows = width // count
    chunk = up_own.shape[1]
    per_line = width // chunk
    line = pl.multiple_of((i // per_line) * up_rows, up_rows)
    col = pl.multiple_of((i % per_line) * chunk, chunk)

    @pl.when(i == 0)
    def _():
        acc[...] = dr2_ref[...]

    df = df_ref[...]
    hb = hb_ref[...]
    total = None
    for table, gp, down, up, bu, out in (
        (1, gp_other, down_other, up_other, bu_other, out_other),
        (0, gp_own, down_own, up_own, bu_own, out_own),
    ):
        du = (dot_nt(df, down[...]) * gp[...]).astype(BF16)
        bu[...] = jnp.sum(fold_rows(du.astype(F32)), axis=0, keepdims=True)
        value = dot_tn(hb, du).astype(BF16)
        for a in range(count):
            out[pos[table, a], pl.ds(line, up_rows), pl.ds(col, chunk)] = value[a * up_rows : (a + 1) * up_rows, :]
        part = dot_nt(du, up[...])
        total = part if total is None else total + part
    acc[...] += total

    @pl.when(i == pl.num_programs(0) - 1)
    def _():
        fold_s[...] = jnp.zeros_like(fold_s)

        def norm(blk, carry):
            r = pl.ds(pl.multiple_of(blk * LANES, LANES), LANES)
            grad = acc[r, :]
            normed = n_ref[r, :]
            fold_s[0] += fold_rows(grad * normed)
            fold_s[1] += fold_rows(grad)
            scaled = grad * gain_a[...]
            mean_a = jnp.mean(scaled, axis=1, keepdims=True)
            mean_b = jnp.mean(scaled * normed, axis=1, keepdims=True)
            dr1 = (scaled - mean_a - normed * mean_b) * rstd_ref[r, 0:1]
            dr1_ref[r, :] = dr1
            da = dr1.astype(BF16)
            da_ref[r, :] = da
            fold_s[2] += fold_rows(da.astype(F32))
            return carry

        lax.fori_loop(0, rows // LANES, norm, 0)
        vec_ref[...] = jnp.sum(fold_s[...], axis=1)
        da = da_ref[...]
        pairs = o_own.shape[0]
        size = pairs * LANES // count
        first = out_own.shape[1] - size
        for table, o_ref, out in ((1, o_other, out_other), (0, o_own, out_own)):
            value = jnp.concatenate([dot_tn(o_ref[p], da) for p in range(pairs)], axis=0)
            for a in range(count):
                out[pos[table, a], first : first + size, :] = value[a * size : (a + 1) * size, :].astype(BF16)


def ffn_bwd(pos, df, dr2, hb, gp_own, gp_other, down_own, down_other, up_own, up_other, n1, rstd, gain_a, o_own, o_other, count):
    rows, width = df.shape
    hidden = up_own.shape[1]
    local = o_own.shape[0] * LANES
    chunk = 256
    block = (width * hidden + local * width) // (count * width)
    up_spec = pl.BlockSpec((width, chunk), lambda i, *_: (0, i))
    down_spec = pl.BlockSpec((chunk, width), lambda i, *_: (i, 0))
    act_spec = pl.BlockSpec((rows, chunk), lambda i, *_: (0, i))
    bu_spec = pl.BlockSpec((1, chunk), lambda i, *_: (0, i))
    outs = [
        shaped((count, block, width), BF16), shaped((count, block, width), BF16),
        shaped((1, hidden), F32), shaped((1, hidden), F32),
        shaped((rows, width), F32), shaped((rows, width), BF16), shaped((3, width), F32),
    ]
    return call(
        ffn_bwd_body,
        outs,
        (hidden // chunk,),
        1,
        [whole(df.shape), whole(dr2.shape), whole(hb.shape), act_spec, act_spec, down_spec, down_spec, up_spec, up_spec]
        + [whole(n1.shape), whole(rstd.shape), whole(gain_a.shape), whole(o_own.shape), whole(o_other.shape)],
        [whole(o.shape) for o in outs[:2]] + [bu_spec] * 2 + [whole(o.shape) for o in outs[4:]],
        [pltpu.VMEM((rows, width), F32), pltpu.VMEM((3, 8, width), F32)],
        40,
        12 * rows * width * hidden + 4 * rows * local * width,
        8 * rows * hidden + 12 * width * hidden + 20 * rows * width,
    )(pos, df, dr2, hb, gp_own, gp_other, down_own, down_other, up_own, up_other, n1, rstd, gain_a, o_own, o_other)


def attn_bwd_body(table, ids, bucket, lens, keep, pos, qa_ref, k_ref, v_ref, da_ref, wo_ref, w_ref, x_ref, *rest):
    if table == 1:
        dr1_ref, g_ref, dw_ref, db_ref, ig_ref, do_s, dq_s, dk_s, dv_s, bm_s = rest
    else:
        ig_in, dw_ref, db_ref, ig_ref, do_s, dq_s, dk_s, dv_s, bm_s = rest
    rows, width = da_ref.shape
    pairs = k_ref.shape[0]
    local = pairs * LANES
    _, bm = mask_columns(ids, bucket, lens, rows)
    bm_s[...] = bm
    do = dot_nt(da_ref[...], wo_ref[...]).astype(BF16)
    for p in range(pairs):
        do_s[p] = do[:, p * LANES : (p + 1) * LANES]
    tile = rows // 2

    def step(p, carry):
        kp = k_ref[p]
        vp = v_ref[p]
        bmb = bm_s[...]
        low_t, low_r = low_half(tile), low_half(rows)
        zero_t, zero_r = jnp.zeros((tile, LANES), BF16), jnp.zeros((rows, LANES), BF16)
        dk_sum = dv_sum = None
        for rb in range(2):
            r = pl.ds(rb * tile, tile)
            dop = do_s[p, r, :]
            dq = None
            for par in range(2):
                own_t = low_t if par == 0 else jnp.logical_not(low_t)
                own_r = low_r if par == 0 else jnp.logical_not(low_r)
                qa = qa_ref[2 * p + par, r, :]
                doa = jnp.where(own_t, dop, zero_t)
                prob = jnp.exp(dot_nt(jnp.where(own_r, kp, bmb), qa))
                dprob = dot_nt(vp, doa)
                inner = jnp.sum(prob * dprob, axis=0, keepdims=True)
                dscore = (prob * (dprob - inner)).astype(BF16)
                dv = dot_nn(prob.astype(BF16), doa)
                dk = dot_nn(dscore, jnp.where(own_t, qa, zero_t))
                dqp = dot_tn(dscore, jnp.where(own_r, kp, zero_r))
                dv_sum = dv if dv_sum is None else dv_sum + dv
                dk_sum = dk if dk_sum is None else dk_sum + dk
                dq = dqp if dq is None else dq + dqp
            dq_s[p, r, :] = (dq * 0.125).astype(BF16)
        dk_s[p] = dk_sum.astype(BF16)
        dv_s[p] = dv_sum.astype(BF16)
        return carry

    lax.fori_loop(0, pairs, step, 0)
    x = x_ref[...]
    count, block, _ = dw_ref.shape
    size = width // count
    grads = []
    for j, ref in enumerate((dq_s, dk_s, dv_s)):
        grad = jnp.concatenate([ref[p] for p in range(pairs)], axis=1)
        grads.append(grad)
        if j != 1:
            db_ref[j // 2 : j // 2 + 1, :] = jnp.sum(fold_rows(grad.astype(F32)), axis=0, keepdims=True)
        value = dot_tn(x, grad).astype(BF16)
        for a in range(count):
            dw_ref[pos[table, a], j * size : (j + 1) * size, :] = value[a * size : (a + 1) * size, :]
    back = dot_nt(grads[0], w_ref[0]) + dot_nt(grads[1], w_ref[1]) + dot_nt(grads[2], w_ref[2])
    if table == 1:
        for blk in range(rows // LANES):
            r = slice(blk * LANES, (blk + 1) * LANES)
            kept = keep_of(ids, bucket, keep, blk)
            ig_ref[r, :] = back[r, :] + (dr1_ref[r, :] + jnp.where(kept, 0.0, g_ref[r, :].astype(F32)))
    else:
        ig_ref[...] = back + ig_in[...]


def attn_bwd(table, scal, pos, qa, k, v, da, wo, w, tokens, extra, count):
    rows, width = da.shape
    pairs = k.shape[0]
    local = pairs * LANES
    ids_rows = pl.BlockSpec((rows, width), lambda i, ids, *_: (ids[0], 0))
    outs = [
        shaped((count, 3 * width // count, local), BF16),
        shaped((2, local), F32),
        shaped((rows, width), F32),
    ]
    trio = pltpu.VMEM((pairs, rows, LANES), BF16)
    extra_specs = [whole(extra[0].shape)] + ([ids_rows] if table == 1 else [])
    return call(
        functools.partial(attn_bwd_body, table),
        outs,
        (1,),
        5,
        [whole(qa.shape), whole(k.shape), whole(v.shape), whole(da.shape), whole(wo.shape), whole(w.shape), ids_rows]
        + extra_specs,
        [whole(o.shape) for o in outs],
        [trio] * 4 + [pltpu.VMEM((rows, LANES), BF16)],
        40,
        2 * rows * local * (7 * width + 10 * rows),
        2 * (rows * local * 4 + width * local * 7 + rows * width * 2) + 8 * rows * width,
        2 * pairs * rows * rows,
    )(*scal, pos, qa, k, v, da, wo, w, tokens, *extra)


def place_body(splits, pos, low_ref, high_ref, *out_refs):
    low = pos[pl.program_id(0)] < pos.shape[0] // 2
    for ref, chosen in ((low_ref, low), (high_ref, jnp.logical_not(low))):

        @pl.when(chosen)
        def _(ref=ref):
            for out, pieces in zip(out_refs, splits, strict=True):
                for index, start, size, c0, c1 in pieces:
                    out[index + (slice(None), slice(c0, c1))] = ref[0, start : start + size, :].astype(F32)


def place(pos, low, high, outs, out_specs, splits):
    half, block, width = low.shape
    count = 2 * half
    return call(
        functools.partial(place_body, splits),
        outs,
        (count,),
        1,
        [
            pl.BlockSpec((1, block, width), lambda a, pos: (jnp.minimum(pos[a], half - 1), 0, 0)),
            pl.BlockSpec((1, block, width), lambda a, pos: (jnp.maximum(pos[a] - half, 0), 0, 0)),
        ],
        out_specs,
        [],
        16,
        0,
        6 * count * block * width,
    )(pos, low, high)


def swap_cores(array_in, cores):
    return lax.ppermute(array_in, "tensor", [(c, cores - 1 - c) for c in range(cores)])


def sum_over_groups(mesh, batch, own, other):
    groups, cores = mesh.shape["dp"], mesh.shape["tensor"]
    steps = own.shape[0].bit_length() - 1

    def exchange(array_in, step):
        pairs = []
        for i in range(groups):
            for c in range(cores):
                j = i ^ (1 << STEP_BITS[batch][c % 2][step])
                pairs.append((i * cores + c, j * cores + c))
        return lax.ppermute(array_in, ("dp", "tensor"), pairs)

    def added(left, right):
        return (left.astype(F32) + right.astype(F32)).astype(BF16)

    current = added(own, swap_cores(other, cores))
    for step in range(steps):
        half = current.shape[0] // 2
        current = added(current[:half], exchange(current[half:], step))
    outer = groups >> steps
    if outer > 1:
        inner = 1 << steps
        members = [[o * inner + i for o in range(outer)] for i in range(inner)]
        current = lax.psum(current, "dp", axis_index_groups=members)
    for step in range(steps - 1, 0, -1):
        current = jnp.concatenate([current, exchange(current, step)], axis=0)
    return current, exchange(current, 0)


def block_places(mesh, count):
    steps = count.bit_length() - 1
    core = lax.axis_index("tensor")
    rel = (lax.axis_index("dp") & (count - 1)) ^ jnp.arange(count, dtype=jnp.int32)
    tables = []
    for bits in STEP_BITS:
        both = []
        for order in bits:
            place_of = jnp.zeros_like(rel)
            for step in range(steps):
                place_of |= ((rel >> order[step]) & 1) << (steps - 1 - step)
            both.append(place_of)
        even = (core % 2) == 0
        tables.append(jnp.stack([jnp.where(even, both[0], both[1]), jnp.where(even, both[1], both[0])]))
    return jnp.stack(tables)


def per_device(
    mesh,
    tokens,
    w_qkv,
    bias_qv,
    w_out,
    bias_out,
    gain_attn,
    shift_attn,
    w_up,
    bias_up,
    w_down,
    bias_down,
    gain_ffn,
    shift_ffn,
    out_grad,
    bucket_len,
    seq_lengths,
    keep_mask,
):
    cores = mesh.shape["tensor"]
    count = min(16, mesh.shape["dp"])
    width = tokens.shape[1]
    rows = tokens.shape[0] // cores
    hidden = w_up.shape[1]
    local = w_qkv.shape[2]
    core = lax.axis_index("tensor").astype(jnp.int32)
    ids = core[None]
    places = block_places(mesh, count)
    own_row = lambda vec: vec.reshape(1, -1)

    w_qkv_o = swap_cores(w_qkv, cores)
    bias_qv_o = swap_cores(bias_qv, cores)
    w_out_o = swap_cores(w_out, cores)
    bias_up_o = swap_cores(bias_up, cores)
    w_up_o = swap_cores(w_up, cores)
    w_down_o = swap_cores(w_down, cores)

    attn_scal = (ids, bucket_len, seq_lengths)
    qa, k, v, o = attn_fwd(False, attn_scal, tokens, w_qkv, bias_qv, rows)
    qa_o, k_o, v_o, o_o, n1, rstd, hb = attn_fwd(
        True,
        attn_scal,
        tokens,
        w_qkv_o,
        bias_qv_o,
        rows,
        (o, w_out_o, w_out, own_row(bias_out), own_row(gain_attn), own_row(shift_attn)),
    )
    keep_scal = (ids, bucket_len, keep_mask)
    vecs = tuple(own_row(vec) for vec in (gain_attn, shift_attn, bias_down, gain_ffn, shift_ffn))
    gb, gb_o, gp, gp_o, mixed, dr2, df, vec_f = ffn_fwd(
        keep_scal, hb, n1, w_up, w_up_o, own_row(bias_up), own_row(bias_up_o), w_down, w_down_o, vecs, tokens, out_grad
    )
    down_own, down_other = down_grad(places[0], gb, gb_o, df, count)
    down_low, down_high = sum_over_groups(mesh, 0, down_own, down_other)
    up_own, up_other, bu, bu_o, dr1, da, vec_a = ffn_bwd(
        places[1], df, dr2, hb, gp, gp_o, w_down, w_down_o, w_up, w_up_o, n1, rstd, own_row(gain_attn), o, o_o, count
    )
    up_low, up_high = sum_over_groups(mesh, 1, up_own, up_other)
    bwd_scal = (ids, bucket_len, seq_lengths, keep_mask)
    qkv_other, db_o, ig_part = attn_bwd(
        1, bwd_scal, places[2], qa_o, k_o, v_o, da, w_out_o, w_qkv_o, tokens, (dr1, out_grad), count
    )
    qkv_own, db, ig = attn_bwd(0, bwd_scal, places[2], qa, k, v, da, w_out, w_qkv, tokens, (ig_part,), count)
    qkv_low, qkv_high = sum_over_groups(mesh, 2, qkv_own, qkv_other)

    def both_cores(first, second):
        return jnp.where(core == 0, jnp.concatenate([first, second], -1), jnp.concatenate([second, first], -1))

    small = jnp.concatenate(
        [both_cores(db, db_o).reshape(-1), both_cores(bu, bu_o).reshape(-1), vec_a.reshape(-1), vec_f.reshape(-1)]
    ).reshape(-1, width)
    small = lax.psum(small, ("dp", "tensor"))
    pair_rows = 2 * local * cores // width
    up_lines = hidden * cores // width
    grad_bias_qv = lax.dynamic_slice(small[:pair_rows].reshape(2, -1), (0, core * local), (2, local))
    grad_bias_up = lax.dynamic_slice(small[pair_rows : pair_rows + up_lines].reshape(-1), (core * hidden,), (hidden,))
    norms = small[pair_rows + up_lines :]

    def rows_of_both(part):
        other = swap_cores(part, cores)
        return jnp.where(core == 0, jnp.concatenate([part, other]), jnp.concatenate([other, part]))

    size = hidden // count
    grad_w_down = place(
        places[0, 0],
        down_low,
        down_high,
        [shaped((hidden, width), F32)],
        [pl.BlockSpec((size, width), lambda a, _: (a, 0))],
        [[((), 0, size, 0, width)]],
    )[0]
    size, out_size = width // count, local // count
    lines = hidden // width
    grad_w_up, grad_w_out = place(
        places[1, 0],
        up_low,
        up_high,
        [shaped((width, hidden), F32), shaped((local, width), F32)],
        [pl.BlockSpec((size, hidden), lambda a, _: (a, 0)), pl.BlockSpec((out_size, width), lambda a, _: (a, 0))],
        [
            [((), n * size, size, n * width, (n + 1) * width) for n in range(lines)],
            [((), lines * size, out_size, 0, width)],
        ],
    )
    grad_w_qkv = place(
        places[2, 0],
        qkv_low,
        qkv_high,
        [shaped((3, width, local), F32)],
        [pl.BlockSpec((3, size, local), lambda a, _: (0, a, 0))],
        [[((n,), n * size, size, 0, local) for n in range(3)]],
    )[0]
    return (
        rows_of_both(mixed),
        rows_of_both(ig),
        grad_w_qkv,
        grad_bias_qv,
        grad_w_out,
        norms[2],
        norms[0],
        norms[1],
        grad_w_up,
        grad_bias_up,
        grad_w_down,
        norms[5],
        norms[3],
        norms[4],
    )


def solution(mesh):
    in_specs = (
        P("dp", None),
        P(None, None, "tensor"),
        P(None, "tensor"),
        P("tensor", None),
        P(),
        P(),
        P(),
        P(None, "tensor"),
        P("tensor"),
        P("tensor", None),
        P(),
        P(),
        P(),
        P("dp", None),
        P("dp"),
        P("dp", None),
        P("dp", None),
    )
    out_specs = (
        P("dp", None),
        P("dp", None),
        P(None, None, "tensor"),
        P(None, "tensor"),
        P("tensor", None),
        P(),
        P(),
        P(),
        P(None, "tensor"),
        P("tensor"),
        P("tensor", None),
        P(),
        P(),
        P(),
    )
    return jax.shard_map(
        functools.partial(per_device, mesh),
        mesh=mesh,
        in_specs=in_specs,
        out_specs=out_specs,
        check_vma=False,
    )
```

time: 705 us -> 330 us (0.47)
  waiting for transfers between devices: 397 us -> 60.6 us
  Pallas kernels: 0 us -> 111 us
  matrix products: 96.2 us -> 0 us
  starting transfers between devices: 0.2 us -> 46.4 us
  local copies, waits for them, and re-layouts: 62.2 us -> 30.4 us
  blocking collectives: 81.3 us -> 51.5 us
  other arithmetic: 47.9 us -> 25.9 us
  between operations: 15.2 us -> 2.19 us
    psum x5 -> x0, waiting for transfers between devices: 397 us -> none  [the longest x1 323 us: per_device(): lax.psum((grad_w_qkv, grad_bias_qv, grad_w_out, grad_bias_out, norm_local...]
    pallas_call x0 -> x10, Pallas kernels: none -> 111 us  [the longest x3 31 us: place(): call(functools.partial(place_body, splits), outs, (count,), 1, [pl.BlockS...]
    dot_general x26 -> x0, matrix products: 96.2 us -> none  [the longest x1 17.9 us: per_device(): jnp.dot(normed_low, w_up, preferred_element_type=jnp.float32) + bias_up]
    ppermute x0 -> x35, waiting for transfers between devices: none -> 60.6 us  [the longest x24 59.7 us: exchange(): return lax.ppermute(array_in, ('dp', 'tensor'), pairs)]
    ppermute x0 -> x35, starting transfers between devices: none -> 46.4 us  [the longest x24 43.8 us: exchange(): return lax.ppermute(array_in, ('dp', 'tensor'), pairs)]
    psum x1, blocking collectives: 81.3 us -> 51.5 us  [per_device(): small = lax.psum(small, ('dp', 'tensor'))]
    reduce_sum x14 -> x0, other arithmetic: 28.1 us -> none  [the longest x4 12.7 us: layer_norm(): centre = residual - jnp.mean(residual, axis=-1, keepdims=True)]
    dynamic_update_slice x14 -> x0, local copies, waits for them, and re-layouts: 8.82 us -> none  [per_device(): lax.map(attend_forward, (blocked(queries), blocked(key_rows), blocked(val...]
  transfers between devices with their start and end apart: 5 -> 35, of which waited for: 4 -> 13; matrix products, arithmetic and copies ran while one was open for 3% -> 12% of each run, Pallas kernels for 0% -> 20%
where the time goes in v1:
time: 330 us; the launch traced here: 329 us
  Pallas kernels  111 us (34%)
  waiting for transfers between devices  60.6 us (18%)
  blocking collectives  51.5 us (16%)
  starting transfers between devices  46.4 us (14%)
  local copies, waits for them, and re-layouts  30.4 us (9%)
  other arithmetic  25.9 us (8%)
    ppermute x24, waiting for transfers between devices, exchange(): return lax.ppermute(array_in, ('dp', 'tensor'), pairs)  59.7 us
    psum x1, blocking collectives, per_device(): small = lax.psum(small, ('dp', 'tensor'))  51.5 us
    ppermute x24, starting transfers between devices, exchange(): return lax.ppermute(array_in, ('dp', 'tensor'), pairs)  43.8 us
    pallas_call x3, Pallas kernels, place(): call(functools.partial(place_body, splits), outs, (count,), 1, [pl.BlockS...  31 us
    pallas_call x2, Pallas kernels, attn_bwd(): call(functools.partial(attn_bwd_body, table), outs, (1,), 5, [whole(qa.sh...  23.1 us
    pallas_call x1, Pallas kernels, ffn_bwd(): call(ffn_bwd_body, outs, (hidden // chunk,), 1, [whole(df.shape), whole(d...  19.6 us
    pallas_call x2, Pallas kernels, attn_fwd(): call(functools.partial(attn_fwd_body, last), outs, (1,), 3, [pl.BlockSpec...  19 us
    unnamed x116, local copies, waits for them, and re-layouts  17.4 us
  transfers between devices with their start and end apart: 35, of which 13 were waited for; matrix products, arithmetic and copies ran while one was open for 12% of the time, Pallas kernels for 20%

profile of v1, /device:TPU:0, one launch (start us, length us, event | category | flops | bytes accessed | tf_op | source)
XLA Modules:
  0.0 328.6 jit_solution(14027281737598842703)
XLA Ops:
  7.1 7.3 %shard_map.272 = (bf16[6,512,128]{2,1,0:T(8,128)(2,1)S(1)}, bf16[3,512,128]{2,1,0:T(8,128)(2,1)S(1)}, bf16[3,512,128]{2,1,0:T(8,128)(2,1)S(1)}, bf16[3,512,128]{2,1,0:T(8,128)(2,1)S(1)}) custom-call(s32[1]{0:T(128)} %bitcast.ids, s32[1]{0:T(128)S(6)} %copy.31.bucket, s32[1,8]{1,0:T(1,128)S(1)} %copy-done.11, bf16[1024,768]{1,0:T(8,128)(2,1)S(1)} %copy-done.6, ...), custom_call_target="tpu_custom_call" | custom-call | flops 1711276032 | bytes 4521984 | tf_op jit(solution)/shard_map/pallas_call | solution.py:177
  17.3 11.8 %shard_map.273 = (bf16[6,512,128]{2,1,0:T(8,128)(2,1)S(1)}, bf16[3,512,128]{2,1,0:T(8,128)(2,1)S(1)}, bf16[3,512,128]{2,1,0:T(8,128)(2,1)S(1)}, bf16[3,512,128]{...) custom-call(s32[1]{0:T(128)} %bitcast.ids, ...), custom_call_target="tpu_custom_call" | custom-call | flops 2315255808 | bytes 6881280 | tf_op jit(solution)/shard_map/pallas_call | solution.py:177
  29.3 14.5 %shard_map.274 = (bf16[512,1536]{1,0:T(8,128)(2,1)S(1)}, bf16[512,1536]{1,0:T(8,128)(2,1)S(1)}, f32[512,1536]{1,0:T(8,128)S(1)}, f32[512,1536]{1,0:T(8,128)}, bf...) custom-call(s32[1]{0:T(128)} %bitcast.ids, ...), custom_call_target="tpu_custom_call" | custom-call | flops 4831838208 | bytes 26738688 | tf_op jit(solution)/shard_map/pallas_call | solution.py:284
  52.1 19.6 %shard_map.275 = (bf16[16,120,768]{2,1,0:T(8,128)(2,1)}, bf16[16,120,768]{2,1,0:T(8,128)(2,1)}, f32[1,1536]{1,0:T(1,128)S(1)}, f32[1,1536]{1,0:T(1,128)S(1)}, f3...) custom-call(s32[2,16]{1,0:T(2,128)S(1)} %get-tuple-element.95.pos, ...), custom_call_target="tpu_custom_call" | custom-call | flops 7851737088 | bytes 28311552 | tf_op jit(solution)/shard_map/pallas_call | solution.py:414
  75.1 4.3 %shard_map.280 = (bf16[16,96,768]{2,1,0:T(8,128)(2,1)S(1)}, bf16[16,96,768]{2,1,0:T(8,128)(2,1)S(1)}) custom-call(s32[2,16]{1,0:T(2,128)S(1)} %get-tuple-element.92.pos, bf16[512,1536]{1,0:T(8,128)(2,1)S(1)} %get-tuple-element.82.gb_own, bf16[512,1536]{1,0:T(8,128)(2,1)S(1)} %copy-done.15, bf16[512,768]{1,0:T(8,128)(2,1)S(1)} %copy-done.21), custom_call_target="tpu_custom_call" | custom-call | flops 2415919104 | bytes 8650752 | tf_op jit(solution)/shard_map/pallas_call | solution.py:319
  79.8 11.8 %shard_map.276 = (bf16[16,144,384]{2,1,0:T(8,128)(2,1)S(1)}, f32[2,384]{1,0:T(2,128)S(1)}, f32[512,768]{1,0:T(8,128)S(1)}) custom-call(s32[1]{0:T(128)} %bitcast.ids, s32[1]{0:T(128)S(6)} %copy.31.bucket, s32[1,8]{1,0:T(1,128)S(1)} %copy-done.12, s32[1,8]{1,0:T(1,128)S(1)} %copy-done.10, s32[2,16]{1,0:T(2,128)S(1)} %get-tuple-element.97.pos, ...), custom_call_target="tpu_custom_call" | custom-call | flops 4127195136 | bytes 10420224 | tf_op jit(solution)/shard_map/pallas_call | solution.py:510
  91.8 3.5 %add_convert_fusion = bf16[16,120,768]{2,1,0:T(8,128)(2,1)S(1)} fusion(bf16[16,120,768]{2,1,0:T(8,128)(2,1)} %collective-permute-done.17, bf16[16,120,768]{2,1,0:T(8,128)(2,1)} %get-tuple-element.78), kind=kLoop, calls=%fused_computation | loop fusion | flops 5898240 | bytes 8847360 | tf_op jit(solution)/shard_map/convert_element_type | solution.py:574
  95.4 3.0 collective-permute-start.18
  98.4 2.5 add_convert_fusion.1
  103.6 11.3 %shard_map.277 = (bf16[16,144,384]{2,1,0:T(8,128)(2,1)S(1)}, f32[2,384]{1,0:T(2,128)S(1)}, f32[512,768]{1,0:T(8,128)}) custom-call(s32[1]{0:T(128)} %bitcast.ids, s32[1]{0:T(128)S(6)} %copy.31.bucket, s32[1,8]{1,0:T(1,128)S(1)} %copy-done.12, s32[1,8]{1,0:T(1,128)S(1)} %copy-done.10, s32[2,16]{1,0:T(2,128)S(1)} %get-tuple-element.97.pos, ...), custom_call_target="tpu_custom_call" | custom-call | flops 4127195136 | bytes 10420224 | tf_op jit(solution)/shard_map/pallas_call | solution.py:510
  120.0 7.8 %collective-permute-done.27 = bf16[8,96,768]{2,1,0:T(8,128)(2,1)S(1)} collective-permute-done((bf16[8,96,768]{2,1,0:T(8,128)(2,1)}, bf16[8,96,768]{2,1,0:T(8,128)(2,1)S(1)}, u32[]{:S(2)}, u32[]{:S(2)}) %collective-permute-start.27) | collective-permute-done | bytes 1179680 | tf_op jit(solution)/shard_map/ppermute | solution.py:571
  130.0 2.3 collective-permute-done.9
  132.7 8.8 %collective-permute-done.19 = bf16[4,120,768]{2,1,0:T(8,128)(2,1)S(1)} collective-permute-done((bf16[4,120,768]{2,1,0:T(8,128)(2,1)S(1)}, bf16[4,120,768]{2,1,0:T(8,128)(2,1)S(1)}, u32[]{:S(2)}, u32[]{:S(2)}) %collective-permute-start.19) | collective-permute-done | bytes 737312 | tf_op jit(solution)/shard_map/ppermute | solution.py:571
  141.7 2.4 collective-permute-start.20
  148.8 4.3 %collective-permute-done.20 = bf16[2,120,768]{2,1,0:T(8,128)(2,1)S(1)} collective-permute-done((bf16[2,120,768]{2,1,0:T(8,128)(2,1)S(1)}, bf16[2,120,768]{2,1,0:T(8,128)(2,1)S(1)}, u32[]{:S(2)}, u32[]{:S(2)}) %collective-permute-start.20) | collective-permute-done | bytes 368672 | tf_op jit(solution)/shard_map/ppermute | solution.py:571
  153.2 2.6 collective-permute-start.21
  157.7 3.5 %collective-permute-done.21 = bf16[1,120,768]{2,1,0:T(8,128)(2,1)S(1)} collective-permute-done((bf16[1,120,768]{2,1,0:T(8,128)(2,1)S(1)}, bf16[1,120,768]{2,1,0:T(8,128)(2,1)S(1)}, u32[]{:S(2)}, u32[]{:S(2)}) %collective-permute-start.21) | collective-permute-done | bytes 184352 | tf_op jit(solution)/shard_map/ppermute | solution.py:571
  161.3 3.5 %collective-permute-start.22 = (bf16[1,120,768]{2,1,0:T(8,128)(2,1)S(1)}, bf16[1,120,768]{2,1,0:T(8,128)(2,1)S(1)}, u32[]{:S(2)}, u32[]{:S(2)}) collective-permute-start(bf16[1,120,768]{2,1,0:T(8,128)(2,1)S(1)} %add_convert_fusion.12), channel_id=1, source_target_pairs={{0,16},{1,17},{2,18},{3,19},{4,20},{5,21},{6,22},{7,23},{8,24},{9,... | collective-permute-start | bytes 552968 | tf_op jit(solution)/shard_map/ppermute | solution.py:571
  165.0 12.3 %collective-permute-done.22 = bf16[1,120,768]{2,1,0:T(8,128)(2,1)S(1)} collective-permute-done((bf16[1,120,768]{2,1,0:T(8,128)(2,1)S(1)}, bf16[1,120,768]{2,1,0:T(8,128)(2,1)S(1)}, u32[]{:S(2)}, u32[]{:S(2)}) %collective-permute-start.22) | collective-permute-done | bytes 184352 | tf_op jit(solution)/shard_map/ppermute | solution.py:571
  177.3 5.3 %collective-permute-start.23 = (bf16[2,120,768]{2,1,0:T(8,128)(2,1)S(1)}, bf16[2,120,768]{2,1,0:T(8,128)(2,1)S(1)}, u32[]{:S(2)}, u32[]{:S(2)}) collective-permute-start(bf16[2,120,768]{2,1,0:T(8,128)(2,1)S(1)} %pad_maximum_fusion.6), channel_id=1, source_target_pairs={{0,4},{1,9},{2,6},{3,11},{4,0},{5,13},{6,2},{7,15},{8,12},{9,1},{1... | collective-permute-start | bytes 1105928 | tf_op jit(solution)/shard_map/ppermute | solution.py:571
  182.8 3.0 collective-permute-start.13
  185.8 8.6 %collective-permute-done.31 = bf16[1,96,768]{2,1,0:T(8,128)(2,1)S(1)} collective-permute-done((bf16[1,96,768]{2,1,0:T(8,128)(2,1)S(1)}, bf16[1,96,768]{2,1,0:T(8,128)(2,1)S(1)}, u32[]{:S(2)}, u32[]{:S(2)}) %collective-permute-start.31) | collective-permute-done | bytes 147488 | tf_op jit(solution)/shard_map/ppermute | solution.py:571
  198.6 3.0 collective-permute-done.32
  202.5 3.9 %collective-permute-start.33 = (bf16[4,96,768]{2,1,0:T(8,128)(2,1)}, bf16[4,96,768]{2,1,0:T(8,128)(2,1)}, u32[]{:S(2)}, u32[]{:S(2)}) collective-permute-start(bf16[4,96,768]{2,1,0:T(8,128)(2,1)} %pad_maximum_fusion.4), channel_id=1, source_target_pairs={{0,4},{1,3},{2,6},{3,1},{4,0},{5,7},{6,2},{7,5},{8,12},{9,11},{10,... | collective-permute-start | bytes 1769480 | tf_op jit(solution)/shard_map/ppermute | solution.py:571
  207.3 6.0 %collective-permute-done.24 = bf16[4,120,768]{2,1,0:T(8,128)(2,1)} collective-permute-done((bf16[4,120,768]{2,1,0:T(8,128)(2,1)S(1)}, bf16[4,120,768]{2,1,0:T(8,128)(2,1)}, u32[]{:S(2)}, u32[]{:S(2)}) %collective-permute-start.24) | collective-permute-done | bytes 737312 | tf_op jit(solution)/shard_map/ppermute | solution.py:571
  214.6 2.4 collective-permute-start.25
  229.3 51.5 %psum.7 = f32[12,768]{1,0:T(8,128)} all-reduce(f32[12,768]{1,0:T(8,128)} %reshape.221), channel_id=1, replica_groups=mesh['dp'=16,'tensor'=2] {'dp','tensor'}, use_global_device_ids=true, to_apply=%region_0.1 | all-reduce | flops 9216 | bytes 73728 | tf_op jit(solution)/shard_map/psum | solution.py:680
  289.1 3.4 %maximum_select_fusion.1 = bf16[1024,768]{1,0:T(8,128)(2,1)} fusion(bf16[512,768]{1,0:T(8,128)(2,1)} %collective-permute-done.6, bf16[512,768]{1,0:T(8,128)(2,1)} %get-tuple-element.53, pred[]{:T(512)S(6)} %eq.8), kind=kLoop, calls=%fused_computation.7 | loop fusion | flops 7077888 | bytes 3145729 | tf_op jit(solution)/shard_map/jit(_where)/select_n | solution.py:689
  292.5 5.1 %maximum_select_fusion = f32[1024,768]{1,0:T(8,128)} fusion(f32[512,768]{1,0:T(8,128)} %collective-permute-done.7, f32[512,768]{1,0:T(8,128)} %get-tuple-element.69, pred[]{:T(512)S(6)} %eq.8), kind=kLoop, calls=%fused_computation.3 | loop fusion | flops 2359296 | bytes 6291457 | tf_op jit(solution)/shard_map/jit(_where)/select_n | solution.py:689
  297.6 10.2 %shard_map.278 = f32[3,768,384]{2,1,0:T(8,128)} custom-call(s32[16]{0:T(128)S(1)} %slice_bitcast_fusion.2.pos, bf16[8,144,384]{2,1,0:T(8,128)(2,1)S(1)} %pad_maximum_fusion.2.low_ref, bf16[8,144,384]{2,1,0:T(8,128)(2,1)} %collective-permute-done.16.high_ref), custom_call_target="tpu_custom_call" | custom-call | bytes 5308416 | tf_op jit(solution)/shard_map/pallas_call | solution.py:540
  307.8 10.6 %shard_map.281 = f32[1536,768]{1,0:T(8,128)} custom-call(s32[16]{0:T(128)S(1)} %slice_bitcast_fusion.pos, bf16[8,96,768]{2,1,0:T(8,128)(2,1)S(1)} %pad_maximum_fusion.1.low_ref, bf16[8,96,768]{2,1,0:T(8,128)(2,1)} %collective-permute-done.34.high_ref), custom_call_target="tpu_custom_call" | custom-call | bytes 7077888 | tf_op jit(solution)/shard_map/pallas_call | solution.py:540
  318.3 10.2 %shard_map.279 = (f32[768,1536]{1,0:T(8,128)}, f32[384,768]{1,0:T(8,128)}) custom-call(s32[16]{0:T(128)S(1)} %slice_bitcast_fusion.1.pos, bf16[8,120,768]{2,1,0:T(8,128)(2,1)S(1)} %pad_maximum_fusion.low_ref, bf16[8,120,768]{2,1,0:T(8,128)(2,1)} %collective-permute-done.25.high_ref), custom_call_target="tpu_custom_call" | custom-call | bytes 8847360 | tf_op jit(solution)/shard_map/pallas_call | solution.py:540
  (235 shorter events, 66.3 us)
Async XLA Ops:
  0.6 28.5 %collective-permute-start.3 = (bf16[768,1536]{1,0:T(8,128)(2,1)}, bf16[768,1536]{1,0:T(8,128)(2,1)S(1)}, u32[]{:S(2)}, u32[]{:S(2)}) collective-permute-start(bf16[768,1536]{1,0:T(8,128)(2,1)} %up_own.3), channel_id=1, source_target_pairs={{0,1},{1,0},{2,3},{3,2},{4,5},{5,4},{6,7},{7,6},{8,9},{9,8},{10,11... | collective-permute-start | bytes 7077896 | tf_op jit(solution)/shard_map/ppermute | solution.py:558
  1.2 28.0 %collective-permute-start.5 = (bf16[1536,768]{1,0:T(8,128)(2,1)}, bf16[1536,768]{1,0:T(8,128)(2,1)}, u32[]{:S(2)}, u32[]{:S(2)}) collective-permute-start(bf16[1536,768]{1,0:T(8,128)(2,1)} %down_own.3), channel_id=1, source_target_pairs={{0,1},{1,0},{2,3},{3,2},{4,5},{5,4},{6,7},{7,6},{8,9},{9,8},{10,11... | collective-permute-start | bytes 7077896 | tf_op jit(solution)/shard_map/ppermute | solution.py:558
  1.2 16.0 %collective-permute-start = (bf16[3,768,384]{2,1,0:T(8,128)(2,1)}, bf16[3,768,384]{2,1,0:T(8,128)(2,1)}, u32[]{:S(2)}, u32[]{:S(2)}) collective-permute-start(bf16[3,768,384]{2,1,0:T(8,128)(2,1)} %w_ref.3), channel_id=1, source_target_pairs={{0,1},{1,0},{2,3},{3,2},{4,5},{5,4},{6,7},{7,6},{8,9},{9,8},{10,11... | collective-permute-start | bytes 5308424 | tf_op jit(solution)/shard_map/ppermute | solution.py:558
  1.7 15.6 %collective-permute-start.2 = (bf16[384,768]{1,0:T(8,128)(2,1)}, bf16[384,768]{1,0:T(8,128)(2,1)}, u32[]{:S(2)}, u32[]{:S(2)}) collective-permute-start(bf16[384,768]{1,0:T(8,128)(2,1)} %wo_ref.1), channel_id=1, source_target_pairs={{0,1},{1,0},{2,3},{3,2},{4,5},{5,4},{6,7},{7,6},{8,9},{9,8},{10,11... | collective-permute-start | bytes 1769480 | tf_op jit(solution)/shard_map/ppermute | solution.py:558
  1.8 14.3 %collective-permute-start.4 = (f32[1536]{0:T(1024)}, f32[1536]{0:T(1024)S(1)}, u32[]{:S(2)}, u32[]{:S(2)}) collective-permute-start(f32[1536]{0:T(1024)} %param.25), channel_id=1, source_target_pairs={{0,1},{1,0},{2,3},{3,2},{4,5},{5,4},{6,7},{7,6},{8,9},{9,8},{10,11... | collective-permute-start | bytes 18440 | tf_op jit(solution)/shard_map/ppermute | solution.py:558
  73.7 18.2 %collective-permute-start.17 = (bf16[16,120,768]{2,1,0:T(8,128)(2,1)}, bf16[16,120,768]{2,1,0:T(8,128)(2,1)}, u32[]{:S(2)}, u32[]{:S(2)}) collective-permute-start(bf16[16,120,768]{2,1,0:T(8,128)(2,1)} %get-tuple-element.79), channel_id=1, source_target_pairs={{0,1},{1,0},{2,3},{3,2},{4,5},{5,4},{6,7},{7,6},{8,9},{9,8},{10,11... | collective-permute-start | bytes 8847368 | tf_op jit(solution)/shard_map/ppermute | solution.py:558
  79.3 19.1 %collective-permute-start.26 = (bf16[16,96,768]{2,1,0:T(8,128)(2,1)S(1)}, bf16[16,96,768]{2,1,0:T(8,128)(2,1)}, u32[]{:S(2)}, u32[]{:S(2)}) collective-permute-start(bf16[16,96,768]{2,1,0:T(8,128)(2,1)S(1)} %get-tuple-element.85), channel_id=1, source_target_pairs={{0,1},{1,0},{2,3},{3,2},{4,5},{5,4},{6,7},{7,6},{8,9},{9,8},{10,11... | collective-permute-start | bytes 7077896 | tf_op jit(solution)/shard_map/ppermute | solution.py:558
  91.6 23.3 %collective-permute-start.8 = (bf16[16,144,384]{2,1,0:T(8,128)(2,1)S(1)}, bf16[16,144,384]{2,1,0:T(8,128)(2,1)}, u32[]{:S(2)}, u32[]{:S(2)}) collective-permute-start(bf16[16,144,384]{2,1,0:T(8,128)(2,1)S(1)} %get-tuple-element.71), channel_id=1, source_target_pairs={{0,1},{1,0},{2,3},{3,2},{4,5},{5,4},{6,7},{7,6},{8,9},{9,8},{10,11... | collective-permute-start | bytes 5308424 | tf_op jit(solution)/shard_map/ppermute | solution.py:558
  95.4 23.2 %collective-permute-start.18 = (bf16[8,120,768]{2,1,0:T(8,128)(2,1)S(1)}, bf16[8,120,768]{2,1,0:T(8,128)(2,1)S(1)}, u32[]{:S(2)}, u32[]{:S(2)}) collective-permute-start(bf16[8,120,768]{2,1,0:T(8,128)(2,1)S(1)} %slice.157), channel_id=1, source_target_pairs={{0,8},{1,3},{2,10},{3,1},{4,12},{5,7},{6,14},{7,5},{8,0},{9,11},{1... | collective-permute-start | bytes 4423688 | tf_op jit(solution)/shard_map/ppermute | solution.py:571
  102.0 25.8 %collective-permute-start.27 = (bf16[8,96,768]{2,1,0:T(8,128)(2,1)}, bf16[8,96,768]{2,1,0:T(8,128)(2,1)S(1)}, u32[]{:S(2)}, u32[]{:S(2)}) collective-permute-start(bf16[8,96,768]{2,1,0:T(8,128)(2,1)} %slice.169), channel_id=1, source_target_pairs={{0,2},{1,5},{2,0},{3,7},{4,6},{5,1},{6,4},{7,3},{8,10},{9,13},{10,... | collective-permute-start | bytes 3538952 | tf_op jit(solution)/shard_map/ppermute | solution.py:571
  117.0 15.3 %collective-permute-start.9 = (bf16[8,144,384]{2,1,0:T(8,128)(2,1)S(1)}, bf16[8,144,384]{2,1,0:T(8,128)(2,1)S(1)}, u32[]{:S(2)}, u32[]{:S(2)}) collective-permute-start(bf16[8,144,384]{2,1,0:T(8,128)(2,1)S(1)} %slice.148), channel_id=1, source_target_pairs={{0,4},{1,9},{2,6},{3,11},{4,0},{5,13},{6,2},{7,15},{8,12},{9,1},{1... | collective-permute-start | bytes 2654216 | tf_op jit(solution)/shard_map/ppermute | solution.py:571
  119.1 22.4 %collective-permute-start.19 = (bf16[4,120,768]{2,1,0:T(8,128)(2,1)S(1)}, bf16[4,120,768]{2,1,0:T(8,128)(2,1)S(1)}, u32[]{:S(2)}, u32[]{:S(2)}) collective-permute-start(bf16[4,120,768]{2,1,0:T(8,128)(2,1)S(1)} %slice.159), channel_id=1, source_target_pairs={{0,2},{1,5},{2,0},{3,7},{4,6},{5,1},{6,4},{7,3},{8,10},{9,13},{10,... | collective-permute-start | bytes 2211848 | tf_op jit(solution)/shard_map/ppermute | solution.py:571
  128.2 16.8 %collective-permute-start.28 = (bf16[4,96,768]{2,1,0:T(8,128)(2,1)S(1)}, bf16[4,96,768]{2,1,0:T(8,128)(2,1)S(1)}, u32[]{:S(2)}, u32[]{:S(2)}) collective-permute-start(bf16[4,96,768]{2,1,0:T(8,128)(2,1)S(1)} %slice.171), channel_id=1, source_target_pairs={{0,4},{1,3},{2,6},{3,1},{4,0},{5,7},{6,2},{7,5},{8,12},{9,11},{10,... | collective-permute-start | bytes 1769480 | tf_op jit(solution)/shard_map/ppermute | solution.py:571
  132.6 14.1 %collective-permute-start.10 = (bf16[4,144,384]{2,1,0:T(8,128)(2,1)S(1)}, bf16[4,144,384]{2,1,0:T(8,128)(2,1)S(1)}, u32[]{:S(2)}, u32[]{:S(2)}) collective-permute-start(bf16[4,144,384]{2,1,0:T(8,128)(2,1)S(1)} %slice.150), channel_id=1, source_target_pairs={{0,2},{1,5},{2,0},{3,7},{4,6},{5,1},{6,4},{7,3},{8,10},{9,13},{10,... | collective-permute-start | bytes 1327112 | tf_op jit(solution)/shard_map/ppermute | solution.py:571
  141.7 11.4 %collective-permute-start.20 = (bf16[2,120,768]{2,1,0:T(8,128)(2,1)S(1)}, bf16[2,120,768]{2,1,0:T(8,128)(2,1)S(1)}, u32[]{:S(2)}, u32[]{:S(2)}) collective-permute-start(bf16[2,120,768]{2,1,0:T(8,128)(2,1)S(1)} %slice.161), channel_id=1, source_target_pairs={{0,4},{1,9},{2,6},{3,11},{4,0},{5,13},{6,2},{7,15},{8,12},{9,1},{1... | collective-permute-start | bytes 1105928 | tf_op jit(solution)/shard_map/ppermute | solution.py:571
  145.1 10.7 %collective-permute-start.29 = (bf16[2,96,768]{2,1,0:T(8,128)(2,1)S(1)}, bf16[2,96,768]{2,1,0:T(8,128)(2,1)S(1)}, u32[]{:S(2)}, u32[]{:S(2)}) collective-permute-start(bf16[2,96,768]{2,1,0:T(8,128)(2,1)S(1)} %slice.173), channel_id=1, source_target_pairs={{0,8},{1,9},{2,10},{3,11},{4,12},{5,13},{6,14},{7,15},{8,0},{9,1},... | collective-permute-start | bytes 884744 | tf_op jit(solution)/shard_map/ppermute | solution.py:571
  146.9 17.9 %collective-permute-start.11 = (bf16[2,144,384]{2,1,0:T(8,128)(2,1)S(1)}, bf16[2,144,384]{2,1,0:T(8,128)(2,1)S(1)}, u32[]{:S(2)}, u32[]{:S(2)}) collective-permute-start(bf16[2,144,384]{2,1,0:T(8,128)(2,1)S(1)} %slice.152), channel_id=1, source_target_pairs={{0,8},{1,3},{2,10},{3,1},{4,12},{5,7},{6,14},{7,5},{8,0},{9,11},{1... | collective-permute-start | bytes 663560 | tf_op jit(solution)/shard_map/ppermute | solution.py:571
  155.9 26.8 %collective-permute-start.30 = (bf16[1,96,768]{2,1,0:T(8,128)(2,1)S(1)}, bf16[1,96,768]{2,1,0:T(8,128)(2,1)S(1)}, u32[]{:S(2)}, u32[]{:S(2)}) collective-permute-start(bf16[1,96,768]{2,1,0:T(8,128)(2,1)S(1)} %slice.175), channel_id=1, source_target_pairs={{0,16},{1,17},{2,18},{3,19},{4,20},{5,21},{6,22},{7,23},{8,24},{9,... | collective-permute-start | bytes 442376 | tf_op jit(solution)/shard_map/ppermute | solution.py:571
  161.3 16.0 %collective-permute-start.22 = (bf16[1,120,768]{2,1,0:T(8,128)(2,1)S(1)}, bf16[1,120,768]{2,1,0:T(8,128)(2,1)S(1)}, u32[]{:S(2)}, u32[]{:S(2)}) collective-permute-start(bf16[1,120,768]{2,1,0:T(8,128)(2,1)S(1)} %add_convert_fusion.12), channel_id=1, source_target_pairs={{0,16},{1,17},{2,18},{3,19},{4,20},{5,21},{6,22},{7,23},{8,24},{9,... | collective-permute-start | bytes 552968 | tf_op jit(solution)/shard_map/ppermute | solution.py:571
  164.9 17.9 %collective-permute-start.12 = (bf16[1,144,384]{2,1,0:T(8,128)(2,1)S(1)}, bf16[1,144,384]{2,1,0:T(8,128)(2,1)S(1)}, u32[]{:S(2)}, u32[]{:S(2)}) collective-permute-start(bf16[1,144,384]{2,1,0:T(8,128)(2,1)S(1)} %slice.154), channel_id=1, source_target_pairs={{0,16},{1,17},{2,18},{3,19},{4,20},{5,21},{6,22},{7,23},{8,24},{9,... | collective-permute-start | bytes 331784 | tf_op jit(solution)/shard_map/ppermute | solution.py:571
  177.3 17.2 %collective-permute-start.23 = (bf16[2,120,768]{2,1,0:T(8,128)(2,1)S(1)}, bf16[2,120,768]{2,1,0:T(8,128)(2,1)S(1)}, u32[]{:S(2)}, u32[]{:S(2)}) collective-permute-start(bf16[2,120,768]{2,1,0:T(8,128)(2,1)S(1)} %pad_maximum_fusion.6), channel_id=1, source_target_pairs={{0,4},{1,9},{2,6},{3,11},{4,0},{5,13},{6,2},{7,15},{8,12},{9,1},{1... | collective-permute-start | bytes 1105928 | tf_op jit(solution)/shard_map/ppermute | solution.py:571
  182.7 11.7 %collective-permute-start.31 = (bf16[1,96,768]{2,1,0:T(8,128)(2,1)S(1)}, bf16[1,96,768]{2,1,0:T(8,128)(2,1)S(1)}, u32[]{:S(2)}, u32[]{:S(2)}) collective-permute-start(bf16[1,96,768]{2,1,0:T(8,128)(2,1)S(1)} %add_convert_fusion.13), channel_id=1, source_target_pairs={{0,16},{1,17},{2,18},{3,19},{4,20},{5,21},{6,22},{7,23},{8,24},{9,... | collective-permute-start | bytes 442376 | tf_op jit(solution)/shard_map/ppermute | solution.py:571
  182.8 13.7 %collective-permute-start.13 = (bf16[1,144,384]{2,1,0:T(8,128)(2,1)S(1)}, bf16[1,144,384]{2,1,0:T(8,128)(2,1)S(1)}, u32[]{:S(2)}, u32[]{:S(2)}) collective-permute-start(bf16[1,144,384]{2,1,0:T(8,128)(2,1)S(1)} %add_convert_fusion.14), channel_id=1, source_target_pairs={{0,16},{1,17},{2,18},{3,19},{4,20},{5,21},{6,22},{7,23},{8,24},{9,... | collective-permute-start | bytes 331784 | tf_op jit(solution)/shard_map/ppermute | solution.py:571
  194.6 18.6 %collective-permute-start.24 = (bf16[4,120,768]{2,1,0:T(8,128)(2,1)S(1)}, bf16[4,120,768]{2,1,0:T(8,128)(2,1)}, u32[]{:S(2)}, u32[]{:S(2)}) collective-permute-start(bf16[4,120,768]{2,1,0:T(8,128)(2,1)S(1)} %pad_maximum_fusion.3), channel_id=1, source_target_pairs={{0,2},{1,5},{2,0},{3,7},{4,6},{5,1},{6,4},{7,3},{8,10},{9,13},{10,... | collective-permute-start | bytes 2211848 | tf_op jit(solution)/shard_map/ppermute | solution.py:571
  196.6 9.8 %collective-permute-start.14 = (bf16[2,144,384]{2,1,0:T(8,128)(2,1)S(1)}, bf16[2,144,384]{2,1,0:T(8,128)(2,1)S(1)}, u32[]{:S(2)}, u32[]{:S(2)}) collective-permute-start(bf16[2,144,384]{2,1,0:T(8,128)(2,1)S(1)} %pad_maximum_fusion.8), channel_id=1, source_target_pairs={{0,8},{1,3},{2,10},{3,1},{4,12},{5,7},{6,14},{7,5},{8,0},{9,11},{1... | collective-permute-start | bytes 663560 | tf_op jit(solution)/shard_map/ppermute | solution.py:571
  202.5 16.3 %collective-permute-start.33 = (bf16[4,96,768]{2,1,0:T(8,128)(2,1)}, bf16[4,96,768]{2,1,0:T(8,128)(2,1)}, u32[]{:S(2)}, u32[]{:S(2)}) collective-permute-start(bf16[4,96,768]{2,1,0:T(8,128)(2,1)} %pad_maximum_fusion.4), channel_id=1, source_target_pairs={{0,4},{1,3},{2,6},{3,1},{4,0},{5,7},{6,2},{7,5},{8,12},{9,11},{10,... | collective-permute-start | bytes 1769480 | tf_op jit(solution)/shard_map/ppermute | solution.py:571
  206.4 86.1 %collective-permute-start.7 = (f32[512,768]{1,0:T(8,128)}, f32[512,768]{1,0:T(8,128)}, u32[]{:S(2)}, u32[]{:S(2)}) collective-permute-start(f32[512,768]{1,0:T(8,128)} %get-tuple-element.69), channel_id=1, source_target_pairs={{0,1},{1,0},{2,3},{3,2},{4,5},{5,4},{6,7},{7,6},{8,9},{9,8},{10,11... | collective-permute-start | bytes 4718600 | tf_op jit(solution)/shard_map/ppermute | solution.py:558
  207.3 16.6 %collective-permute-start.15 = (bf16[4,144,384]{2,1,0:T(8,128)(2,1)}, bf16[4,144,384]{2,1,0:T(8,128)(2,1)}, u32[]{:S(2)}, u32[]{:S(2)}) collective-permute-start(bf16[4,144,384]{2,1,0:T(8,128)(2,1)} %pad_maximum_fusion.5), channel_id=1, source_target_pairs={{0,2},{1,5},{2,0},{3,7},{4,6},{5,1},{6,4},{7,3},{8,10},{9,13},{10,... | collective-permute-start | bytes 1327112 | tf_op jit(solution)/shard_map/ppermute | solution.py:571
  214.6 103.8 %collective-permute-start.25 = (bf16[8,120,768]{2,1,0:T(8,128)(2,1)S(1)}, bf16[8,120,768]{2,1,0:T(8,128)(2,1)}, u32[]{:S(2)}, u32[]{:S(2)}) collective-permute-start(bf16[8,120,768]{2,1,0:T(8,128)(2,1)S(1)} %pad_maximum_fusion.low_ref), channel_id=1, source_target_pairs={{0,8},{1,3},{2,10},{3,1},{4,12},{5,7},{6,14},{7,5},{8,0},{9,11},{1... | collective-permute-start | bytes 4423688 | tf_op jit(solution)/shard_map/ppermute | solution.py:571
  220.1 87.6 %collective-permute-start.34 = (bf16[8,96,768]{2,1,0:T(8,128)(2,1)S(1)}, bf16[8,96,768]{2,1,0:T(8,128)(2,1)}, u32[]{:S(2)}, u32[]{:S(2)}) collective-permute-start(bf16[8,96,768]{2,1,0:T(8,128)(2,1)S(1)} %pad_maximum_fusion.1.low_ref), channel_id=1, source_target_pairs={{0,2},{1,5},{2,0},{3,7},{4,6},{5,1},{6,4},{7,3},{8,10},{9,13},{10,... | collective-permute-start | bytes 3538952 | tf_op jit(solution)/shard_map/ppermute | solution.py:571
  220.7 68.4 %collective-permute-start.6 = (bf16[512,768]{1,0:T(8,128)(2,1)}, bf16[512,768]{1,0:T(8,128)(2,1)}, u32[]{:S(2)}, u32[]{:S(2)}) collective-permute-start(bf16[512,768]{1,0:T(8,128)(2,1)} %get-tuple-element.53), channel_id=1, source_target_pairs={{0,1},{1,0},{2,3},{3,2},{4,5},{5,4},{6,7},{7,6},{8,9},{9,8},{10,11... | collective-permute-start | bytes 2359304 | tf_op jit(solution)/shard_map/ppermute | solution.py:558
  225.2 72.3 %collective-permute-start.16 = (bf16[8,144,384]{2,1,0:T(8,128)(2,1)S(1)}, bf16[8,144,384]{2,1,0:T(8,128)(2,1)}, u32[]{:S(2)}, u32[]{:S(2)}) collective-permute-start(bf16[8,144,384]{2,1,0:T(8,128)(2,1)S(1)} %pad_maximum_fusion.2.low_ref), channel_id=1, source_target_pairs={{0,4},{1,9},{2,6},{3,11},{4,0},{5,13},{6,2},{7,15},{8,12},{9,1},{1... | collective-permute-start | bytes 2654216 | tf_op jit(solution)/shard_map/ppermute | solution.py:571
  (61 other events, 462.3 us)

commit v2 on v0

v2 whole, which is shorter than its diff:
```python
import functools

import jax
import jax.numpy as jnp
from jax import lax
from jax.experimental import pallas as pl
from jax.experimental.pallas import tpu as pltpu
from jax.sharding import PartitionSpec as P

HD = 64
BUCKET_LONG = 512
LANES = 128
EPS = 1e-05
F32 = jnp.float32
BF16 = jnp.bfloat16
NEG = -1e30
MIB = 1 << 20
VMEM_MIB = 16
COVER = 20

STEP_BITS = (
    ((0, 1, 2), (1, 0, 2)),
    ((2, 0, 1), (0, 1, 2)),
    ((1, 0, 2), (2, 1, 0)),
)


def dot_nn(left, right):
    return lax.dot_general(left, right, (((1,), (0,)), ((), ())), preferred_element_type=F32)


def dot_nt(left, right):
    return lax.dot_general(left, right, (((1,), (1,)), ((), ())), preferred_element_type=F32)


def dot_tn(left, right):
    return lax.dot_general(left, right, (((0,), (0,)), ((), ())), preferred_element_type=F32)


def resident():
    return pl.BlockSpec(memory_space=pltpu.VMEM)


def anywhere():
    return pl.BlockSpec(memory_space=pl.ANY)


def shaped(shape, dtype):
    return jax.ShapeDtypeStruct(shape, dtype)


def call(body, outs, scalars, operands, scratch=(), vmem=VMEM_MIB, flops=0, moved=0, trans=0, **kwargs):
    specs = kwargs.pop("in_specs", None) or [resident()] * len(operands)
    return pl.pallas_call(
        body,
        out_shape=outs,
        grid_spec=pltpu.PrefetchScalarGridSpec(
            num_scalar_prefetch=len(scalars),
            grid=(1,),
            in_specs=specs,
            out_specs=kwargs.pop("out_specs", None) or [resident()] * len(outs),
            scratch_shapes=list(scratch),
        ),
        compiler_params=pltpu.CompilerParams(dimension_semantics=("arbitrary",), vmem_limit_bytes=vmem * MIB),
        cost_estimate=pl.CostEstimate(flops=COVER * flops, bytes_accessed=moved, transcendentals=trans),
        **kwargs,
    )(*scalars, *operands)


def chunk_of(index, size):
    return pl.ds(pl.multiple_of(index * size, size), size)


def after(value, *earlier):
    return lax.optimization_barrier((value,) + earlier)[0]


def move_bits(number, pairs):
    out = 0
    for take, put in pairs:
        out = out | lax.shift_left(lax.shift_right_logical(number, take) & 1, put)
    return out


def spot_of(ids, batch, kind, number, count):
    steps = count.bit_length() - 1
    me = ids[1] & (count - 1)
    down = range(steps - 1, -1, -1)
    number = jnp.int32(number) if isinstance(number, int) else number
    spots = []
    for core in range(2):
        bits = STEP_BITS[batch][1 - core if kind == 1 else core][:steps]
        if kind == 2:
            spots.append(move_bits(number, zip(down, bits, strict=True)) ^ me)
        else:
            spots.append(move_bits(number ^ me, zip(bits, down, strict=True)))
    return jnp.where((ids[0] & 1) == 0, spots[0], spots[1])


def bucket_shift(bucket_ref):
    return jnp.where(bucket_ref[0] >= BUCKET_LONG, 9, 7)


def mask_columns(ids_ref, bucket_ref, lens_ref, rows):
    shift = bucket_shift(bucket_ref)
    first = ids_ref[0] * lax.shift_right_logical(BUCKET_LONG, shift)
    place = lax.broadcasted_iota(jnp.int32, (rows, LANES), 0)
    lane = lax.broadcasted_iota(jnp.int32, (rows, LANES), 1) & (HD - 1)
    seq = lax.shift_right_logical(place, jnp.full((rows, LANES), shift, jnp.int32))
    pos = place - lax.shift_left(seq, jnp.full((rows, LANES), shift, jnp.int32))
    length = jnp.full((rows, LANES), lens_ref[0, first], jnp.int32)
    for slot in range(1, 4):
        length = jnp.where(seq == slot, lens_ref[0, first + slot], length)
    hit = seq == lane
    query_cols = jnp.where(hit, 1.0, 0.0)
    key_cols = jnp.where(hit & (pos < length), 0.0, NEG)
    key_cols = jnp.where(lane < 4, key_cols, jnp.where(lane < 7, 1.0, 0.0))
    return query_cols.astype(BF16), key_cols.astype(BF16)


def low_half(rows):
    return lax.broadcasted_iota(jnp.int32, (rows, LANES), 1) < HD


def row_of(vec_ref):
    return vec_ref[...].reshape(1, -1)


def attn_fwd_body(last, ids, bucket, lens, x_ref, w_ref, b_ref, *rest):
    if last:
        (other_o, wo_own, wo_other, bias_out, gain, shift_vec) = rest[:6]
        qa_ref, k_ref, v_ref, o_ref, n_ref, rstd_ref, hb_ref = rest[6:13]
    else:
        qa_ref, k_ref, v_ref, o_ref = rest[:4]
    am_s, bm_s = rest[-2:]
    pairs, rows, _ = k_ref.shape
    am_s[...], bm_s[...] = mask_columns(ids, bucket, lens, rows)
    tile = rows // 2

    def pair(p, carry):
        cols = chunk_of(p, LANES)
        weights = jnp.concatenate([w_ref[n, :, cols] for n in range(3)], axis=1)
        qkv = dot_nn(x_ref[chunk_of(ids[0], rows), :], weights)
        qp = ((qkv[:, :LANES] + b_ref[0:1, cols]).astype(BF16).astype(F32) * 0.125).astype(BF16)
        kp = qkv[:, LANES : 2 * LANES].astype(BF16)
        vp = (qkv[:, 2 * LANES :] + b_ref[1:2, cols]).astype(BF16)
        k_ref[p] = kp
        v_ref[p] = vp
        bm = bm_s[...]
        low_r, low_t = low_half(rows), low_half(tile)
        lane = lax.broadcasted_iota(jnp.int32, (tile, LANES), 1) & (HD - 1)
        for rb in range(2):
            r = slice(rb * tile, (rb + 1) * tile)
            am = am_s[r, :]
            qpr = qp[r, :]
            sums = []
            for par in range(2):
                own_t = low_t if par == 0 else jnp.logical_not(low_t)
                own_r = low_r if par == 0 else jnp.logical_not(low_r)
                scores = dot_nt(jnp.where(own_t, qpr, am), jnp.where(own_r, kp, bm))
                top = jnp.max(scores, axis=1, keepdims=True)
                expo = jnp.exp(scores - top).astype(BF16)
                total = dot_nn(expo, jnp.where(own_r, vp, jnp.ones_like(vp)))
                sums.append(total)
                neg_log = -(top + jnp.log(jnp.where(own_t, 1.0, total)))
                hi = neg_log.astype(BF16)
                mid = (neg_log - hi.astype(F32)).astype(BF16)
                lo = (neg_log - hi.astype(F32) - mid.astype(F32)).astype(BF16)
                parts = jnp.where(lane == 4, hi, jnp.where(lane == 5, mid, jnp.where(lane == 6, lo, am)))
                qa_ref[2 * p + par, r, :] = jnp.where(own_t, qpr, parts)
            total = pltpu.roll(jnp.where(low_t, sums[1], sums[0]), HD, 1)
            o_ref[p, r, :] = (jnp.where(low_t, sums[0], sums[1]) / total).astype(BF16)
        return carry

    lax.fori_loop(0, pairs, pair, 0)
    if last:
        block = rows // 4
        gain_row, shift_row, bias_row = row_of(gain), row_of(shift_vec), row_of(bias_out)

        def norm(i, carry):
            r = chunk_of(i, block)
            heads = [o_ref[n, r, :] for n in range(pairs)] + [other_o[n, r, :] for n in range(pairs)]
            weights = jnp.concatenate([wo_own[...], wo_other[...]], axis=0)
            acc = dot_nn(jnp.concatenate(heads, axis=1), weights)
            acc += x_ref[pl.ds(pl.multiple_of(ids[0] * rows + i * block, block), block), :].astype(F32) + bias_row
            centre = acc - jnp.mean(acc, axis=1, keepdims=True)
            rstd = lax.rsqrt(jnp.mean(centre * centre, axis=1, keepdims=True) + EPS)
            normed = centre * rstd
            n_ref[r, :] = normed
            rstd_ref[r, :] = jnp.broadcast_to(rstd, (block, LANES))
            hb_ref[r, :] = (normed * gain_row + shift_row).astype(BF16)
            return carry

        lax.fori_loop(0, 4, norm, 0)


def attn_fwd(last, scal, tokens, w, b, rows, extra=()):
    width = tokens.shape[1]
    local = w.shape[2]
    pairs = local // LANES
    outs = [shaped((2 * pairs, rows, LANES), BF16)] + [shaped((pairs, rows, LANES), BF16)] * 3
    if last:
        outs += [shaped((rows, width), F32), shaped((rows, LANES), F32), shaped((rows, width), BF16)]
    return call(
        functools.partial(attn_fwd_body, last),
        outs,
        scal,
        (tokens, w, b, *extra),
        [pltpu.VMEM((rows, LANES), BF16)] * 2,
        flops=2 * rows * local * (3 * width + 4 * rows + (2 * width if last else 0)),
        moved=2 * (rows * width + 3 * width * local + 5 * rows * local),
        trans=2 * pairs * rows * rows,
    )


def keep_of(ids, bucket, keep, block):
    shift = bucket_shift(bucket)
    first = ids[0] * lax.shift_right_logical(BUCKET_LONG, shift)
    return keep[0, first + lax.shift_right_logical(block * LANES, shift)] > 0


def fold_rows(array_in):
    rows, cols = array_in.shape
    return jnp.sum(array_in.reshape(rows // 8, 8, cols), axis=0)


def ffn_fwd_body(
    ids, bucket, keep, hb_ref, n_ref, up_own, up_other, bu_own, bu_other, down_own, down_other,
    gain_a, shift_a, bias_down, gain_f, shift_f, x_ref, g_ref,
    gb_own, gb_other, gp_own, gp_other, mixed_ref, dr2_ref, df_ref, vec_ref, acc, fold_s,
):
    rows, width = hb_ref.shape
    acc[...] = n_ref[...] * row_of(gain_a) + (row_of(shift_a) + row_of(bias_down))
    half = rows // 2
    chunk = 256

    def hidden(i, carry):
        cols = chunk_of(i, chunk)
        for r in range(2):
            rs = slice(r * half, (r + 1) * half)
            hb = hb_ref[rs, :]
            total = None
            for up, bu, down, gb, gp in (
                (up_own, bu_own, down_own, gb_own, gp_own),
                (up_other, bu_other, down_other, gb_other, gp_other),
            ):
                u = dot_nn(hb, up[:, cols]) + bu[cols].reshape(1, -1)
                cdf = 0.5 * (1.0 + lax.erf(u * 0.7071067811865476))
                pdf = jnp.exp(-0.5 * u * u) * 0.3989422804014327
                gp[rs, cols] = cdf + u * pdf
                act = (u * cdf).astype(BF16)
                gb[rs, cols] = act
                part = dot_nn(act, down[cols, :])
                total = part if total is None else total + part
            acc[rs, :] += total
        return carry

    lax.fori_loop(0, up_own.shape[1] // chunk, hidden, 0)
    fold_s[...] = jnp.zeros_like(fold_s)
    gain_row, shift_row = row_of(gain_f), row_of(shift_f)

    def norm(blk, carry):
        r = chunk_of(blk, LANES)
        far = pl.ds(pl.multiple_of(ids[0] * rows + blk * LANES, LANES), LANES)
        kept = keep_of(ids, bucket, keep, blk)
        res = acc[r, :]
        centre = res - jnp.mean(res, axis=1, keepdims=True)
        rstd = lax.rsqrt(jnp.mean(centre * centre, axis=1, keepdims=True) + EPS)
        normed = centre * rstd
        final = normed * gain_row + shift_row
        mixed_ref[r, :] = jnp.where(kept, final, x_ref[far, :].astype(F32)).astype(BF16)
        grad = jnp.where(kept, g_ref[far, :].astype(F32), 0.0)
        fold_s[0] += fold_rows(grad * normed)
        fold_s[1] += fold_rows(grad)
        scaled = grad * gain_row
        mean_a = jnp.mean(scaled, axis=1, keepdims=True)
        mean_b = jnp.mean(scaled * normed, axis=1, keepdims=True)
        dr2 = (scaled - mean_a - normed * mean_b) * rstd
        dr2_ref[r, :] = dr2
        df = dr2.astype(BF16)
        df_ref[r, :] = df
        fold_s[2] += fold_rows(df.astype(F32))
        return carry

    lax.fori_loop(0, rows // LANES, norm, 0)
    vec_ref[...] = jnp.sum(fold_s[...], axis=1)


def ffn_fwd(scal, hb, n1, up_own, up_other, bu_own, bu_other, down_own, down_other, vecs, tokens, out_grad):
    rows, width = hb.shape
    hidden = up_own.shape[1]
    outs = [
        shaped((rows, hidden), BF16), shaped((rows, hidden), BF16),
        shaped((rows, hidden), F32), shaped((rows, hidden), F32),
        shaped((rows, width), BF16), shaped((rows, width), F32), shaped((rows, width), BF16),
        shaped((3, width), F32),
    ]
    return call(
        ffn_fwd_body,
        outs,
        scal,
        (hb, n1, up_own, up_other, bu_own, bu_other, down_own, down_other, *vecs, tokens, out_grad),
        [pltpu.VMEM((rows, width), F32), pltpu.VMEM((3, 8, width), F32)],
        flops=8 * rows * width * hidden,
        moved=12 * rows * hidden + 8 * width * hidden + 20 * rows * width,
        trans=4 * rows * hidden,
    )


def down_grad_body(kind, ids, gb_ref, df_ref, out_ref):
    count, size, _ = out_ref.shape
    per = 2 if count % 2 == 0 else 1

    def step(i, carry):
        value = dot_tn(gb_ref[:, chunk_of(i, per * size)], df_ref[...]).astype(BF16)
        for c in range(per):
            out_ref[spot_of(ids, 0, kind, i * per + c, count)] = value[c * size : (c + 1) * size, :]
        return carry

    lax.fori_loop(0, count // per, step, 0)


def down_grad(kind, ids, gb, df, count):
    rows, width = df.shape
    hidden = gb.shape[1]
    return call(
        functools.partial(down_grad_body, kind),
        [shaped((count, hidden // count, width), BF16)],
        (ids,),
        (gb, df),
        flops=2 * rows * width * hidden,
        moved=2 * rows * hidden + 2 * width * hidden + 2 * rows * width,
    )[0]


def ffn_bwd_body(kind, ids, df_ref, hb_ref, gp_ref, down_ref, up_ref, *rest):
    if kind == 1:
        dr2_ref, out_ref, bu_ref, acc = rest
        acc[...] = dr2_ref[...]
    else:
        acc_in, n_ref, rstd_ref, gain_a, out_ref, bu_ref, dr1_ref, da_ref, vec_ref, acc, fold_s = rest
        acc[...] = acc_in[...]
    rows, width = df_ref.shape
    count, lines, _ = out_ref.shape
    hidden = up_ref.shape[1]
    up_rows = width // count
    chunk = 384
    per_line = width // chunk

    def step(i, carry):
        cols = chunk_of(i, chunk)
        du = (dot_nt(df_ref[...], down_ref[cols, :]) * gp_ref[:, cols]).astype(BF16)
        bu_ref[:, cols] = jnp.sum(fold_rows(du.astype(F32)), axis=0, keepdims=True)
        value = dot_tn(hb_ref[...], du).astype(BF16)
        line, col = chunk_of(i // per_line, up_rows), chunk_of(i % per_line, chunk)
        for a in range(count):
            out_ref[spot_of(ids, 1, kind, a, count), line, col] = value[a * up_rows : (a + 1) * up_rows, :]
        acc[...] += dot_nt(du, up_ref[:, cols])
        return carry

    lax.fori_loop(0, hidden // chunk, step, 0)
    if kind == 0:
        fold_s[...] = jnp.zeros_like(fold_s)
        gain_row = row_of(gain_a)

        def norm(blk, carry):
            r = chunk_of(blk, LANES)
            grad = acc[r, :]
            normed = n_ref[r, :]
            fold_s[0] += fold_rows(grad * normed)
            fold_s[1] += fold_rows(grad)
            scaled = grad * gain_row
            mean_a = jnp.mean(scaled, axis=1, keepdims=True)
            mean_b = jnp.mean(scaled * normed, axis=1, keepdims=True)
            dr1 = (scaled - mean_a - normed * mean_b) * rstd_ref[r, 0:1]
            dr1_ref[r, :] = dr1
            da = dr1.astype(BF16)
            da_ref[r, :] = da
            fold_s[2] += fold_rows(da.astype(F32))
            return carry

        lax.fori_loop(0, rows // LANES, norm, 0)
        vec_ref[...] = jnp.sum(fold_s[...], axis=1)


def ffn_bwd(kind, ids, df, hb, gp, down, up, extra, count):
    rows, width = df.shape
    hidden = up.shape[1]
    outs = [shaped((count, width * hidden // (count * width), width), BF16), shaped((1, hidden), F32)]
    scratch = []
    if kind == 1:
        outs += [shaped((rows, width), F32)]
    else:
        outs += [shaped((rows, width), F32), shaped((rows, width), BF16), shaped((3, width), F32)]
        scratch = [pltpu.VMEM((rows, width), F32), pltpu.VMEM((3, 8, width), F32)]
    return call(
        functools.partial(ffn_bwd_body, kind),
        outs,
        (ids,),
        (df, hb, gp, down, up, *extra),
        scratch,
        flops=6 * rows * width * hidden,
        moved=4 * rows * hidden + 6 * width * hidden + 10 * rows * width,
    )


def attn_bwd_body(
    kind, ids, bucket, lens, keep, qa_ref, k_ref, v_ref, o_ref, da_ref, wo_ref, w_ref, x_ref, bu_ref, va_ref, vf_ref, *rest
):
    if kind == 1:
        dr1_ref, g_ref, dw_ref, ig_ref, bm_s = rest
    else:
        ig_in, dw_ref, ig_ref, bm_s = rest
    rows, width = da_ref.shape
    pairs = k_ref.shape[0]
    local = pairs * LANES
    count = dw_ref.shape[0]
    size, out_size, wide = width // count, local // count, width // local
    _, bm_s[...] = mask_columns(ids, bucket, lens, rows)
    if kind == 1:
        for blk in range(rows // LANES):
            r = slice(blk * LANES, (blk + 1) * LANES)
            far = pl.ds(pl.multiple_of(ids[0] * rows + blk * LANES, LANES), LANES)
            kept = keep_of(ids, bucket, keep, blk)
            ig_ref[r, :] = dr1_ref[r, :] + jnp.where(kept, 0.0, g_ref[far, :].astype(F32))
    else:
        ig_ref[...] = ig_in[...]
    tile = rows // 2

    def pair(p, carry):
        cols = chunk_of(p, LANES)
        kp = k_ref[p]
        vp = v_ref[p]
        bm = bm_s[...]
        low_t, low_r = low_half(tile), low_half(rows)
        zero_t, zero_r = jnp.zeros((tile, LANES), BF16), jnp.zeros((rows, LANES), BF16)
        wo = wo_ref[cols, :]
        dk_sum = dv_sum = None
        dqs = []
        for rb in range(2):
            r = slice(rb * tile, (rb + 1) * tile)
            dop = dot_nt(da_ref[r, :], wo).astype(BF16)
            dq = None
            for par in range(2):
                own_t = low_t if par == 0 else jnp.logical_not(low_t)
                own_r = low_r if par == 0 else jnp.logical_not(low_r)
                qa = qa_ref[2 * p + par, r, :]
                doa = jnp.where(own_t, dop, zero_t)
                prob = jnp.exp(dot_nt(jnp.where(own_r, kp, bm), qa))
                dprob = dot_nt(vp, doa)
                inner = jnp.sum(prob * dprob, axis=0, keepdims=True)
                dscore = (prob * (dprob - inner)).astype(BF16)
                dv = dot_nn(prob.astype(BF16), doa)
                dk = dot_nn(dscore, jnp.where(own_t, qa, zero_t))
                dqp = dot_tn(dscore, jnp.where(own_r, kp, zero_r))
                dv_sum = dv if dv_sum is None else dv_sum + dv
                dk_sum = dk if dk_sum is None else dk_sum + dk
                dq = dqp if dq is None else dq + dqp
            dqs.append((dq * 0.125).astype(BF16))
        dqp = jnp.concatenate(dqs, axis=0)
        dvp = dv_sum.astype(BF16)
        grads = jnp.concatenate([dqp, dk_sum.astype(BF16), dvp], axis=1)
        weights = jnp.concatenate([w_ref[n, :, cols] for n in range(3)], axis=1)
        ig_ref[...] += dot_nt(grads, weights)
        value = dot_tn(x_ref[chunk_of(ids[0], rows), :], grads).astype(BF16)
        heads = jnp.concatenate([o_ref[n] for n in range(pairs)], axis=1)
        da = [da_ref[:, pl.ds(pl.multiple_of(n * local + p * LANES, LANES), LANES)] for n in range(wide)]
        out_value = dot_tn(heads, jnp.concatenate(da, axis=1)).astype(BF16)
        small = [jnp.sum(fold_rows(g.astype(F32)), axis=0, keepdims=True) for g in (dqp, dvp)]
        for ref in (bu_ref, va_ref, vf_ref):
            for n in range(ref.shape[0]):
                for c in range(0, ref.shape[1], local):
                    small.append(ref[n : n + 1, pl.ds(pl.multiple_of(c + p * LANES, LANES), LANES)])
        line = lax.broadcasted_iota(jnp.int32, (8, LANES), 0)
        for a in range(count):
            spot = spot_of(ids, 2, kind, a, count)
            for n in range(3):
                part = value[a * size : (a + 1) * size, n * LANES : (n + 1) * LANES]
                dw_ref[spot, n * size : (n + 1) * size, cols] = part
            for n in range(wide):
                part = out_value[a * out_size : (a + 1) * out_size, n * LANES : (n + 1) * LANES]
                at = 3 * size + n * out_size
                dw_ref[spot, at : at + out_size, cols] = part
            tile_s = jnp.zeros((8, LANES), F32)
            for n, row in enumerate(small[a::count]):
                tile_s = jnp.where(line == n, row, tile_s)
            at = 3 * size + wide * out_size
            dw_ref[spot, at : at + 8, cols] = tile_s.astype(BF16)
        return carry

    lax.fori_loop(0, pairs, pair, 0)


def attn_bwd(kind, scal, qa, k, v, o, da, wo, w, tokens, smalls, extra, count):
    rows, width = da.shape
    pairs = k.shape[0]
    local = pairs * LANES
    lines = 4 * width // count + 8
    return call(
        functools.partial(attn_bwd_body, kind),
        [shaped((count, lines, local), BF16), shaped((rows, width), F32)],
        scal,
        (qa, k, v, o, da, wo, w, tokens, *smalls, *extra),
        [pltpu.VMEM((rows, LANES), BF16)],
        flops=2 * rows * local * (8 * width + 10 * rows),
        moved=2 * (rows * local * 4 + width * local * 7 + rows * width * 2) + 8 * rows * width,
        trans=2 * pairs * rows * rows,
    )


def place_body(batch, first, count, plan, small_plan, ids, *refs):
    pieces = refs[: 1 if small_plan is None else 2]
    refs = refs[len(pieces) + (len(plan) if first else 0) :]
    outs, refs = refs[: len(plan)], refs[len(plan) :]
    n_small = 0 if small_plan is None else len(small_plan)
    small_outs, refs = refs[:n_small], refs[n_small:]
    stages, sems = refs[:-1], refs[-1]
    half = pieces[0].shape[0]
    copies = []
    for q in range(half):
        a = spot_of(ids, batch, 2, first + q, count)
        for n, (parts, target) in enumerate(plan):
            for at, start, size in parts:
                stages[n][(q,) + at] = pieces[0][q, start : start + size, :].astype(F32)
            copy = pltpu.make_async_copy(stages[n].at[q], target(outs[n], a), sems.at[n, q])
            copy.start()
            copies.append(copy)
    for n in range(n_small):
        for line, c0, row in small_plan[n]:
            p = spot_of(ids, batch, 0, row % count, count)
            spot = pieces[0].shape[1] - 8 + row // count
            high = pieces[0][p & (half - 1), pieces[0].shape[1] - 8 :, :].astype(F32)
            low = pieces[1][p & (half - 1), pieces[0].shape[1] - 8 :, :].astype(F32)
            tile = jnp.where(p < half, low, high)
            width = tile.shape[1]
            value = tile[row // count : row // count + 1, :]
            if line is None:
                small_outs[n][c0 : c0 + width] = value.reshape(width)
            else:
                small_outs[n][line : line + 1, c0 : c0 + width] = value
    for copy in copies:
        copy.wait()


def place(batch, first, ids, pieces, outs, plan, stages, held=(), small_outs=(), small_plan=None):
    half = pieces[0].shape[0]
    return call(
        functools.partial(place_body, batch, first, 2 * half, plan, small_plan),
        list(outs) + list(small_outs),
        (ids,),
        (*pieces, *held),
        [pltpu.VMEM((half,) + st, F32) for st in stages] + [pltpu.SemaphoreType.DMA((len(outs), half))],
        moved=6 * half * pieces[0].shape[1] * pieces[0].shape[2],
        in_specs=[resident()] * len(pieces) + [anywhere()] * len(held),
        out_specs=[anywhere()] * len(outs) + [resident()] * len(small_outs),
        input_output_aliases={1 + len(pieces) + n: n for n in range(len(held))},
    )


def join_body(cores, ids, *refs):
    n = (len(refs) - 1) // 3
    owns, others, outs, sems = refs[:n], refs[n : 2 * n], refs[2 * n : 3 * n], refs[-1]
    copies = []
    for k in range(n):
        rows = owns[k].shape[0]
        for part, where in ((owns[k], ids[0]), (others[k], cores - 1 - ids[0])):
            target = outs[k].at[pl.ds(pl.multiple_of(where * rows, rows), rows), :]
            copies.append(pltpu.make_async_copy(part, target, sems.at[len(copies)]))
            copies[-1].start()
    for copy in copies:
        copy.wait()


def join(ids, cores, owns, others):
    return call(
        functools.partial(join_body, cores),
        [shaped((cores * o.shape[0], o.shape[1]), o.dtype) for o in owns],
        (ids,),
        (*owns, *others),
        [pltpu.SemaphoreType.DMA((2 * len(owns),))],
        moved=sum(4 * o.size * o.dtype.itemsize for o in owns),
        out_specs=[anywhere()] * len(owns),
    )


def swap_cores(array_in, cores):
    return lax.ppermute(array_in, "tensor", [(c, cores - 1 - c) for c in range(cores)])


class GroupSum:
    def __init__(self, mesh, batch, own, other_received):
        self.mesh, self.batch = mesh, batch
        self.halvings = own.shape[0].bit_length() - 1
        self.doublings = (mesh.shape["dp"] >> self.halvings).bit_length() - 1
        self.terms = [own, other_received]
        self.at = 0
        self.sent = None

    def exchange(self, array_in, bit_of):
        groups, cores = self.mesh.shape["dp"], self.mesh.shape["tensor"]
        pairs = [(i * cores + c, (i ^ (1 << bit_of(c))) * cores + c) for i in range(groups) for c in range(cores)]
        return lax.ppermute(array_in, ("dp", "tensor"), pairs)

    def total(self, terms):
        acc = terms[0].astype(F32)
        for term in terms[1:]:
            acc = acc + term.astype(F32)
        return acc.astype(BF16)

    def step(self, *earlier):
        bits = STEP_BITS[self.batch]
        terms = self.terms
        if earlier:
            terms = terms[:-1] + [after(terms[-1], *earlier)]
        if self.at < self.halvings:
            order = self.at
            half = terms[0].shape[0] // 2
            self.sent = self.total([term[half:] for term in terms])
            received = self.exchange(self.sent, lambda c: bits[c % 2][order])
            self.terms = [term[:half] for term in terms] + [received]
        elif self.at < self.halvings + self.doublings:
            bit = self.at
            self.sent = self.total(terms)
            self.terms = [self.sent, self.exchange(self.sent, lambda c: bit)]
        else:
            order = 2 * self.halvings + self.doublings - 1 - self.at
            first = order == self.halvings - 1
            self.sent = self.total(terms) if first else jnp.concatenate(terms, axis=0)
            self.terms = [self.sent, self.exchange(self.sent, lambda c: bits[c % 2][order])]
        self.at += 1
        return self.sent


def per_device(
    mesh,
    tokens,
    w_qkv,
    bias_qv,
    w_out,
    bias_out,
    gain_attn,
    shift_attn,
    w_up,
    bias_up,
    w_down,
    bias_down,
    gain_ffn,
    shift_ffn,
    out_grad,
    bucket_len,
    seq_lengths,
    keep_mask,
):
    cores = mesh.shape["tensor"]
    count = min(8, mesh.shape["dp"])
    width = tokens.shape[1]
    rows = tokens.shape[0] // cores
    hidden = w_up.shape[1]
    local = w_qkv.shape[2]
    ids = jnp.where(jnp.arange(2) == 0, lax.axis_index("tensor"), lax.axis_index("dp")).astype(jnp.int32)

    w_qkv_o = swap_cores(w_qkv, cores)
    bias_qv_o = swap_cores(bias_qv, cores)
    w_out_o = swap_cores(w_out, cores)
    bias_up_o = swap_cores(bias_up, cores)
    w_up_o = swap_cores(w_up, cores)
    w_down_o = swap_cores(w_down, cores)

    attn_scal = (ids, bucket_len, seq_lengths)
    qa, k, v, o = attn_fwd(False, attn_scal, tokens, w_qkv, bias_qv, rows)
    qa_o, k_o, v_o, o_o, n1, rstd, hb = attn_fwd(
        True,
        attn_scal,
        tokens,
        w_qkv_o,
        bias_qv_o,
        rows,
        (o, w_out_o, w_out, bias_out, gain_attn, shift_attn),
    )
    keep_scal = (ids, bucket_len, keep_mask)
    vecs = (gain_attn, shift_attn, bias_down, gain_ffn, shift_ffn)
    gb, gb_o, gp, gp_o, mixed, dr2, df, vec_f = ffn_fwd(
        keep_scal, hb, n1, w_up, w_up_o, bias_up, bias_up_o, w_down, w_down_o, vecs, tokens, out_grad
    )
    mixed_o = swap_cores(mixed, cores)
    down_other = down_grad(1, ids, gb_o, df, count)
    down_got = swap_cores(down_other, cores)
    down_own = down_grad(0, ids, gb, after(df, down_other), count)
    sum_down = GroupSum(mesh, 0, down_own, down_got)
    sent = sum_down.step()
    up_other, bu_o, dh = ffn_bwd(1, ids, after(df, sent), hb, gp_o, w_down_o, w_up_o, (dr2,), count)
    up_got = swap_cores(up_other, cores)
    up_own, bu, dr1, da, vec_a = ffn_bwd(0, ids, df, hb, gp, w_down, w_up, (dh, n1, rstd, gain_attn), count)
    sum_up = GroupSum(mesh, 1, up_own, up_got)
    sent = (sum_down.step(da), sum_up.step())
    bwd_scal = (ids, bucket_len, seq_lengths, keep_mask)
    qkv_other, ig_part = attn_bwd(
        1, bwd_scal, qa_o, k_o, v_o, o_o, after(da, *sent), w_out_o, w_qkv_o, tokens,
        (bu_o, vec_a, vec_f), (dr1, out_grad), count,
    )
    qkv_got = swap_cores(qkv_other, cores)
    sent = sum_down.step(ig_part)
    qkv_own, ig = attn_bwd(
        0, bwd_scal, qa, k, v, o, after(da, sent), w_out, w_qkv, tokens, (bu, vec_a, vec_f), (ig_part,), count
    )
    ig_o = swap_cores(ig, cores)
    sum_qkv = GroupSum(mesh, 2, qkv_own, qkv_got)
    steps = 2 * sum_down.halvings + sum_down.doublings
    size = hidden // count
    whole_cols = (slice(None), slice(None))

    def rows_at(size):
        return lambda out, a: out.at[pl.ds(pl.multiple_of(a * size, size), size), :]

    down_outs = [shaped((hidden, width), F32)]
    down_args = ([([(whole_cols, 0, size)], rows_at(size))], [(size, width)])
    size, out_size = width // count, local // count
    lines = hidden // width
    up_outs = [shaped((width, hidden), F32)]
    parts = [((slice(None), slice(n * width, (n + 1) * width)), n * size, size) for n in range(lines)]
    up_args = ([(parts, rows_at(size))], [(size, hidden)])
    qkv_outs = [shaped((3, width, local), F32), shaped((local, width), F32)]
    wide = width // local
    parts = [((slice(None), slice(n * local, (n + 1) * local)), 3 * size + n * out_size, out_size) for n in range(wide)]
    qkv_args = (
        [
            (
                [((n,) + whole_cols, n * size, size) for n in range(3)],
                lambda out, a: out.at[:, pl.ds(pl.multiple_of(a * size, size), size), :],
            ),
            (parts, rows_at(out_size)),
        ],
        [(3, size, local), (out_size, width)],
    )
    earlier = []
    for n in range(steps):
        sum_qkv.step(*earlier)
        earlier = [ig] if n == 0 else []
        for each in (sum_down, sum_up):
            if each.at < steps:
                each.step(*earlier[:1] if n == 0 else ())
                earlier.append(each.terms[-1])
                if each is sum_down and each.at == steps:
                    held = place(0, 0, ids, sum_down.terms[:1], down_outs, *down_args)
        if n == 1:
            out_mixed, out_ig = join(ids, cores, (mixed, ig), (mixed_o, ig_o))
            earlier.append(out_ig)
        if n == steps - 3:
            grad_w_down = place(0, count // 2, ids, sum_down.terms[1:], down_outs, *down_args, held)[0]
        if n == steps - 2:
            earlier.append(grad_w_down)
    held = place(1, 0, ids, sum_up.terms[:1], up_outs, *up_args)
    grad_w_up = place(1, count // 2, ids, sum_up.terms[1:], up_outs, *up_args, held)[0]
    held = place(2, 0, ids, sum_qkv.terms[:1], qkv_outs, *qkv_args)
    per_up, per_norm = hidden // local, width // local
    small_plan = [[(n, 0, n) for n in range(2)], [(None, c * local, 2 + c) for c in range(per_up)]]
    for n in range(6):
        small_plan.append([(None, c * local, 2 + per_up + n * per_norm + c) for c in range(per_norm)])
    small_outs = [shaped((2, local), F32), shaped((hidden,), F32)] + [shaped((width,), F32)] * 6
    grad_w_qkv, grad_w_out, grad_bias_qv, grad_bias_up, *norms = place(
        2, count // 2, ids, [sum_qkv.terms[1], sum_qkv.terms[0]], qkv_outs, *qkv_args, held, small_outs, small_plan
    )
    return (
        out_mixed,
        out_ig,
        grad_w_qkv,
        grad_bias_qv,
        grad_w_out,
        norms[2],
        norms[0],
        norms[1],
        grad_w_up,
        grad_bias_up,
        grad_w_down,
        norms[5],
        norms[3],
        norms[4],
    )


def solution(mesh):
    in_specs = (
        P("dp", None),
        P(None, None, "tensor"),
        P(None, "tensor"),
        P("tensor", None),
        P(),
        P(),
        P(),
        P(None, "tensor"),
        P("tensor"),
        P("tensor", None),
        P(),
        P(),
        P(),
        P("dp", None),
        P("dp"),
        P("dp", None),
        P("dp", None),
    )
    out_specs = (
        P("dp", None),
        P("dp", None),
        P(None, None, "tensor"),
        P(None, "tensor"),
        P("tensor", None),
        P(),
        P(),
        P(),
        P(None, "tensor"),
        P("tensor"),
        P("tensor", None),
        P(),
        P(),
        P(),
    )
    return jax.shard_map(
        functools.partial(per_device, mesh),
        mesh=mesh,
        in_specs=in_specs,
        out_specs=out_specs,
        check_vma=False,
    )
```

time: 705 us -> 235 us (0.33)
  waiting for transfers between devices: 397 us -> 99.7 us
  matrix products: 96.2 us -> 0 us
  Pallas kernels: 0 us -> 88.8 us
  blocking collectives: 81.3 us -> 0 us
  local copies, waits for them, and re-layouts: 62.2 us -> 6.73 us
  other arithmetic: 47.9 us -> 8.17 us
  starting transfers between devices: 0.2 us -> 29.3 us
  between operations: 15.2 us -> 2.22 us
    psum x5 -> x0, waiting for transfers between devices: 397 us -> none  [the longest x1 323 us: per_device(): lax.psum((grad_w_qkv, grad_bias_qv, grad_w_out, grad_bias_out, norm_local...]
    ppermute x0 -> x32, waiting for transfers between devices: none -> 99.7 us  [the longest x21 98.2 us: exchange(): return lax.ppermute(array_in, ('dp', 'tensor'), pairs)]
    dot_general x26 -> x0, matrix products: 96.2 us -> none  [the longest x1 17.9 us: per_device(): jnp.dot(normed_low, w_up, preferred_element_type=jnp.float32) + bias_up]
    pallas_call x0 -> x16, Pallas kernels: none -> 88.8 us  [call(): pl.pallas_call(body, out_shape=outs, grid_spec=pltpu.PrefetchScalarGridSp...]
    psum x1 -> x0, blocking collectives: 81.3 us -> none  [per_device(): lax.psum((grad_w_qkv, grad_bias_qv, grad_w_out, grad_bias_out, norm_local...]
    ppermute x0 -> x32, starting transfers between devices: none -> 29.3 us  [the longest x21 27 us: exchange(): return lax.ppermute(array_in, ('dp', 'tensor'), pairs)]
    reduce_sum x14 -> x0, other arithmetic: 28.1 us -> none  [the longest x4 12.7 us: layer_norm(): centre = residual - jnp.mean(residual, axis=-1, keepdims=True)]
    unnamed x122 -> x66, local copies, waits for them, and re-layouts: 23 us -> 6.73 us
  transfers between devices with their start and end apart: 5 -> 32, of which waited for: 4 -> 10; matrix products, arithmetic and copies ran while one was open for 3% -> 2% of each run, Pallas kernels for 0% -> 31%
where the time goes in v2:
time: 235 us
  waiting for transfers between devices  99.7 us (42%)
  Pallas kernels  88.8 us (38%)
  starting transfers between devices  29.3 us (12%)
  other arithmetic  8.17 us (3%)
  local copies, waits for them, and re-layouts  6.73 us (3%)
    ppermute x21, waiting for transfers between devices, exchange(): return lax.ppermute(array_in, ('dp', 'tensor'), pairs)  98.2 us
    pallas_call x16, Pallas kernels, call(): pl.pallas_call(body, out_shape=outs, grid_spec=pltpu.PrefetchScalarGridSp...  88.8 us
    ppermute x21, starting transfers between devices, exchange(): return lax.ppermute(array_in, ('dp', 'tensor'), pairs)  27 us
    convert_element_type x15, other arithmetic, total(): return acc.astype(BF16)  7.6 us
    unnamed x66, local copies, waits for them, and re-layouts  6.73 us
  transfers between devices with their start and end apart: 32, of which 10 were waited for; matrix products, arithmetic and copies ran while one was open for 2% of the time, Pallas kernels for 31%

profile of v2, /device:TPU:0, one launch (start us, length us, event | category | flops | bytes accessed | tf_op | source)
XLA Modules:
  0.0 234.9 jit_solution(10775054950031365007)
XLA Ops:
  7.1 6.7 %shard_map.272 = (bf16[6,512,128]{2,1,0:T(8,128)(2,1)S(1)}, bf16[3,512,128]{2,1,0:T(8,128)(2,1)S(1)}, bf16[3,512,128]{2,1,0:T(8,128)(2,1)S(1)}, bf16[3,512,128]{2,1,0:T(8,128)(2,1)S(1)}) custom-call(s32[2]{0:T(128)S(1)} %compare_select_fusion.ids, s32[1]{0:T(128)S(6)} %copy.39.bucket, s32[1,8]{1,0:T(1,128)S(1)} %copy-done.25, ...), custom_call_target="tpu_custom_call" | custom-call | flops 34225520640 | bytes 4521984 | tf_op jit(solution)/shard_map/pallas_call | solution.py:54
  14.1 10.7 %shard_map.273 = (bf16[6,512,128]{2,1,0:T(8,128)(2,1)S(1)}, bf16[3,512,128]{2,1,0:T(8,128)(2,1)S(1)}, bf16[3,512,128]{2,1,0:T(8,128)(2,1)S(1)}, bf16[3,512,128]{...) custom-call(s32[2]{0:T(128)S(1)} %compare_select_fusion.ids, ...), custom_call_target="tpu_custom_call" | custom-call | flops 46305116160 | bytes 4521984 | tf_op jit(solution)/shard_map/pallas_call | solution.py:54
  24.9 11.0 %shard_map.274 = (bf16[512,1536]{1,0:T(8,128)(2,1)S(1)}, bf16[512,1536]{1,0:T(8,128)(2,1)S(1)}, f32[512,1536]{1,0:T(8,128)S(1)}, f32[512,1536]{1,0:T(8,128)S(1)}...) custom-call(s32[2]{0:T(128)S(1)} %compare_select_fusion.ids, ...), custom_call_target="tpu_custom_call" | custom-call | flops 96636764160 | bytes 26738688 | tf_op jit(solution)/shard_map/pallas_call | solution.py:54
  35.9 2.6 %shard_map.275 = bf16[8,192,768]{2,1,0:T(8,128)(2,1)S(1)} custom-call(s32[2]{0:T(128)S(1)} %compare_select_fusion.ids, bf16[512,1536]{1,0:T(8,128)(2,1)S(1)} %get-tuple-element.83.gb_ref, bf16[512,768]{1,0:T(8,128)(2,1)S(1)} %get-tuple-element.85.df_ref), custom_call_target="tpu_custom_call" | custom-call | flops 24159191040 | bytes 4718592 | tf_op jit(solution)/shard_map/pallas_call | solution.py:54
  39.1 2.6 %shard_map.276 = bf16[8,192,768]{2,1,0:T(8,128)(2,1)S(1)} custom-call(s32[2]{0:T(128)S(1)} %compare_select_fusion.ids, bf16[512,1536]{1,0:T(8,128)(2,1)S(1)} %get-tuple-element.82.gb_ref, bf16[512,768]{1,0:T(8,128)(2,1)S(1)} %get-tuple-element.85.df_ref), custom_call_target="tpu_custom_call" | custom-call | flops 24159191040 | bytes 4718592 | tf_op jit(solution)/shard_map/pallas_call | solution.py:54
  44.8 2.9 %collective-permute-start.7 = (bf16[4,192,768]{2,1,0:T(8,128)(2,1)}, bf16[4,192,768]{2,1,0:T(8,128)(2,1)}, u32[]{:S(2)}, u32[]{:S(2)}) collective-permute-start(bf16[4,192,768]{2,1,0:T(8,128)(2,1)} %add_convert_fusion.2), channel_id=1, source_target_pairs={{0,2},{1,5},{2,0},{3,7},{4,6},{5,1},{6,4},{7,3},{8,10},{9,13},{10,... | collective-permute-start | bytes 3538952 | tf_op jit(solution)/shard_map/ppermute | solution.py:602
  47.6 6.7 %shard_map.277 = (bf16[8,192,768]{2,1,0:T(8,128)(2,1)S(1)}, f32[1,1536]{1,0:T(1,128)S(1)}, f32[512,768]{1,0:T(8,128)S(1)}) custom-call(s32[2]{0:T(128)S(1)} %compare_select_fusion.ids, bf16[512,768]{1,0:T(8,128)(2,1)S(1)} %get-tuple-element.85.df_ref, bf16[512,768]{1,0:T(8,128)(2,1)S(1)} %get-tuple-element.74.hb_ref, ...), custom_call_target="tpu_custom_call" | custom-call | flops 72477573120 | bytes 14155776 | tf_op jit(solution)/shard_map/pallas_call | solution.py:54
  54.5 7.8 %shard_map.278 = (bf16[8,192,768]{2,1,0:T(8,128)(2,1)S(1)}, f32[1,1536]{1,0:T(1,128)S(1)}, f32[512,768]{1,0:T(8,128)S(1)}, bf16[512,768]{1,0:T(8,128)(2,1)S(1)}, f32[3,768]{1,0:T(4,128)S(1)}) custom-call(s32[2]{0:T(128)S(1)} %compare_select_fusion.ids, bf16[512,768]{1,0:T(8,128)(2,1)S(1)} %get-tuple-element.85.df_ref, ...), custom_call_target="tpu_custom_call" | custom-call | flops 72477573120 | bytes 14155776 | tf_op jit(solution)/shard_map/pallas_call | solution.py:54
  64.1 1.9 collective-permute-start.8
  68.7 13.5 %shard_map.279 = (bf16[8,392,384]{2,1,0:T(8,128)(2,1)S(1)}, f32[512,768]{1,0:T(8,128)S(1)}) custom-call(s32[2]{0:T(128)S(1)} %compare_select_fusion.ids, s32[1]{0:T(128)S(6)} %copy.39.bucket, s32[1,8]{1,0:T(1,128)S(1)} %copy-done.26, s32[1,8]{1,0:T(1,128)S(1)} %copy-done.24, bf16[6,512,128]{2,1,0:T(8,128)(2,1)S(1)} %get-tuple-element.92.qa_ref, ...), custom_call_target="tpu_custom_call" | custom-call | flops 88583700480 | bytes 10420224 | tf_op jit(solution)/shard_map/pallas_call | solution.py:54
  85.5 11.6 %shard_map.280 = (bf16[8,392,384]{2,1,0:T(8,128)(2,1)S(1)}, f32[512,768]{1,0:T(8,128)S(1)}) custom-call(s32[2]{0:T(128)S(1)} %compare_select_fusion.ids, s32[1]{0:T(128)S(6)} %copy.39.bucket, s32[1,8]{1,0:T(1,128)S(1)} %copy-done.26, s32[1,8]{1,0:T(1,128)S(1)} %copy-done.24, bf16[6,512,128]{2,1,0:T(8,128)(2,1)S(1)} %get-tuple-element.77.qa_ref, ...), custom_call_target="tpu_custom_call" | custom-call | flops 88583700480 | bytes 10420224 | tf_op jit(solution)/shard_map/pallas_call | solution.py:54
  97.2 7.9 %collective-permute-done.16 = bf16[4,192,768]{2,1,0:T(8,128)(2,1)S(1)} collective-permute-done((bf16[4,192,768]{2,1,0:T(8,128)(2,1)S(1)}, bf16[4,192,768]{2,1,0:T(8,128)(2,1)S(1)}, u32[]{:S(2)}, u32[]{:S(2)}) %collective-permute-start.16) | collective-permute-done | bytes 1179680 | tf_op jit(solution)/shard_map/ppermute | solution.py:602
  106.5 5.5 %collective-permute-start.13 = (bf16[4,392,384]{2,1,0:T(8,128)(2,1)S(1)}, bf16[4,392,384]{2,1,0:T(8,128)(2,1)S(1)}, u32[]{:S(2)}, u32[]{:S(2)}) collective-permute-start(bf16[4,392,384]{2,1,0:T(8,128)(2,1)S(1)} %add_convert_fusion), channel_id=1, source_target_pairs={{0,4},{1,9},{2,6},{3,11},{4,0},{5,13},{6,2},{7,15},{8,12},{9,1},{1... | collective-permute-start | bytes 3612680 | tf_op jit(solution)/shard_map/ppermute | solution.py:602
  113.2 2.9 %collective-permute-start.15 = (bf16[1,192,768]{2,1,0:T(8,128)(2,1)S(1)}, bf16[1,192,768]{2,1,0:T(8,128)(2,1)S(1)}, u32[]{:S(2)}, u32[]{:S(2)}) collective-permute-start(bf16[1,192,768]{2,1,0:T(8,128)(2,1)S(1)} %add_convert_fusion.13), channel_id=1, source_target_pairs={{0,16},{1,17},{2,18},{3,19},{4,20},{5,21},{6,22},{7,23},{8,24},{9,... | collective-permute-start | bytes 884744 | tf_op jit(solution)/shard_map/ppermute | solution.py:602
  116.1 11.2 %collective-permute-done.15 = bf16[1,192,768]{2,1,0:T(8,128)(2,1)S(1)} collective-permute-done((bf16[1,192,768]{2,1,0:T(8,128)(2,1)S(1)}, bf16[1,192,768]{2,1,0:T(8,128)(2,1)S(1)}, u32[]{:S(2)}, u32[]{:S(2)}) %collective-permute-start.15) | collective-permute-done | bytes 294944 | tf_op jit(solution)/shard_map/ppermute | solution.py:602
  128.8 8.5 %collective-permute-done.19 = bf16[1,192,768]{2,1,0:T(8,128)(2,1)S(1)} collective-permute-done((bf16[1,192,768]{2,1,0:T(8,128)(2,1)S(1)}, bf16[1,192,768]{2,1,0:T(8,128)(2,1)S(1)}, u32[]{:S(2)}, u32[]{:S(2)}) %collective-permute-start.19) | collective-permute-done | bytes 294944 | tf_op jit(solution)/shard_map/ppermute | solution.py:602
  138.0 2.7 %collective-permute-start.23 = (bf16[1,192,768]{2,1,0:T(8,128)(2,1)S(1)}, bf16[1,192,768]{2,1,0:T(8,128)(2,1)S(1)}, u32[]{:S(2)}, u32[]{:S(2)}) collective-permute-start(bf16[1,192,768]{2,1,0:T(8,128)(2,1)S(1)} %add_convert_fusion.10), channel_id=1, source_target_pairs={{0,16},{1,17},{2,18},{3,19},{4,20},{5,21},{6,22},{7,23},{8,24},{9,... | collective-permute-start | bytes 884744 | tf_op jit(solution)/shard_map/ppermute | solution.py:602
  140.7 13.0 %collective-permute-done.22 = bf16[2,192,768]{2,1,0:T(8,128)(2,1)S(1)} collective-permute-done((bf16[2,192,768]{2,1,0:T(8,128)(2,1)S(1)}, bf16[2,192,768]{2,1,0:T(8,128)(2,1)S(1)}, u32[]{:S(2)}, u32[]{:S(2)}) %collective-permute-start.22) | collective-permute-done | bytes 589856 | tf_op jit(solution)/shard_map/ppermute | solution.py:602
  154.1 2.8 %shard_map.281 = (bf16[1024,768]{1,0:T(8,128)(2,1)}, f32[1024,768]{1,0:T(8,128)}) custom-call(s32[2]{0:T(128)S(1)} %compare_select_fusion.ids, bf16[512,768]{1,0:T(8,128)(2,1)S(1)} %get-tuple-element.76.refs_0_, f32[512,768]{1,0:T(8,128)S(1)} %get-tuple-element.107.refs_1_, bf16[512,768]{1,0:T(8,128)(2,1)S(1)} %collective-permute-done.10.refs_2_, ...), custom_call_target="tpu_custom_call" | custom-call | bytes 9437184 | tf_op jit(solution)/shard_map/pallas_call | solution.py:54
  158.4 5.5 %collective-permute-done.26 = bf16[1,192,768]{2,1,0:T(8,128)(2,1)S(1)} collective-permute-done((bf16[1,192,768]{2,1,0:T(8,128)(2,1)S(1)}, bf16[1,192,768]{2,1,0:T(8,128)(2,1)S(1)}, u32[]{:S(2)}, u32[]{:S(2)}) %collective-permute-start.26) | collective-permute-done | bytes 294944 | tf_op jit(solution)/shard_map/ppermute | solution.py:602
  164.0 2.1 collective-permute-start.28
  167.2 18.4 %collective-permute-done.28 = bf16[2,192,768]{2,1,0:T(8,128)(2,1)S(1)} collective-permute-done((bf16[2,192,768]{2,1,0:T(8,128)(2,1)S(1)}, bf16[2,192,768]{2,1,0:T(8,128)(2,1)S(1)}, u32[]{:S(2)}, u32[]{:S(2)}) %collective-permute-start.28) | collective-permute-done | bytes 589856 | tf_op jit(solution)/shard_map/ppermute | solution.py:602
  186.0 2.1 collective-permute-start.27
  188.0 17.2 %collective-permute-done.27 = bf16[1,392,384]{2,1,0:T(8,128)(2,1)S(1)} collective-permute-done((bf16[1,392,384]{2,1,0:T(8,128)(2,1)S(1)}, bf16[1,392,384]{2,1,0:T(8,128)(2,1)S(1)}, u32[]{:S(2)}, u32[]{:S(2)}) %collective-permute-start.27) | collective-permute-done | bytes 301088 | tf_op jit(solution)/shard_map/ppermute | solution.py:602
  205.4 2.0 shard_map.282.refs_1_
  207.4 2.0 shard_map.283
  209.5 6.0 %collective-permute-done.29 = bf16[2,392,384]{2,1,0:T(8,128)(2,1)S(1)} collective-permute-done((bf16[2,392,384]{2,1,0:T(8,128)(2,1)S(1)}, bf16[2,392,384]{2,1,0:T(8,128)(2,1)S(1)}, u32[]{:S(2)}, u32[]{:S(2)}) %collective-permute-start.29) | collective-permute-done | bytes 602144 | tf_op jit(solution)/shard_map/ppermute | solution.py:602
  215.7 2.0 shard_map.286.refs_1_
  217.7 2.0 shard_map.287
  219.7 2.0 shard_map.284
  221.7 10.4 %collective-permute-done.31.refs_0_ = bf16[4,392,384]{2,1,0:T(8,128)(2,1)S(1)} collective-permute-done((bf16[4,392,384]{2,1,0:T(8,128)(2,1)S(1)}, bf16[4,392,384]{2,1,0:T(8,128)(2,1)S(1)}, u32[]{:S(2)}, u32[]{:S(2)}) %collective-permute-start.31) | collective-permute-done | bytes 1204256 | tf_op jit(solution)/shard_map/ppermute | solution.py:602
  232.1 2.6 %shard_map.285 = (f32[3,768,384]{2,1,0:T(8,128)}, f32[384,768]{1,0:T(8,128)}, f32[2,384]{1,0:T(2,128)}, f32[1536]{0:T(1024)}, f32[768]{0:T(1024)}, /*index=5*/f3...) custom-call(s32[2]{0:T(128)S(1)} %compare_select_fusion.ids, ...), custom_call_target="tpu_custom_call", output_to_operand_aliasing={{0}: (3, {}), {1}: (4, {})} | custom-call | bytes 3612672 | tf_op jit(solution)/shard_map/pallas_call | solution.py:54
  (136 shorter events, 25.8 us)
Async XLA Ops:
  0.6 13.3 %collective-permute-start = (bf16[3,768,384]{2,1,0:T(8,128)(2,1)}, bf16[3,768,384]{2,1,0:T(8,128)(2,1)}, u32[]{:S(2)}, u32[]{:S(2)}) collective-permute-start(bf16[3,768,384]{2,1,0:T(8,128)(2,1)} %w_ref.3), channel_id=1, source_target_pairs={{0,1},{1,0},{2,3},{3,2},{4,5},{5,4},{6,7},{7,6},{8,9},{9,8},{10,11... | collective-permute-start | bytes 5308424 | tf_op jit(solution)/shard_map/ppermute | solution.py:587
  1.2 12.6 %collective-permute-start.1 = (f32[2,384]{1,0:T(2,128)}, f32[2,384]{1,0:T(2,128)S(1)}, u32[]{:S(2)}, u32[]{:S(2)}) collective-permute-start(f32[2,384]{1,0:T(2,128)} %b_ref.1), channel_id=1, source_target_pairs={{0,1},{1,0},{2,3},{3,2},{4,5},{5,4},{6,7},{7,6},{8,9},{9,8},{10,11... | collective-permute-start | bytes 9224 | tf_op jit(solution)/shard_map/ppermute | solution.py:587
  1.2 12.7 %collective-permute-start.2 = (bf16[384,768]{1,0:T(8,128)(2,1)}, bf16[384,768]{1,0:T(8,128)(2,1)S(1)}, u32[]{:S(2)}, u32[]{:S(2)}) collective-permute-start(bf16[384,768]{1,0:T(8,128)(2,1)} %wo_ref.1), channel_id=1, source_target_pairs={{0,1},{1,0},{2,3},{3,2},{4,5},{5,4},{6,7},{7,6},{8,9},{9,8},{10,11... | collective-permute-start | bytes 1769480 | tf_op jit(solution)/shard_map/ppermute | solution.py:587
  1.7 23.2 %collective-permute-start.3 = (bf16[768,1536]{1,0:T(8,128)(2,1)}, bf16[768,1536]{1,0:T(8,128)(2,1)S(1)}, u32[]{:S(2)}, u32[]{:S(2)}) collective-permute-start(bf16[768,1536]{1,0:T(8,128)(2,1)} %up_ref.1), channel_id=1, source_target_pairs={{0,1},{1,0},{2,3},{3,2},{4,5},{5,4},{6,7},{7,6},{8,9},{9,8},{10,11... | collective-permute-start | bytes 7077896 | tf_op jit(solution)/shard_map/ppermute | solution.py:587
  1.8 23.1 %collective-permute-start.4 = (f32[1536]{0:T(1024)}, f32[1536]{0:T(1024)S(1)}, u32[]{:S(2)}, u32[]{:S(2)}) collective-permute-start(f32[1536]{0:T(1024)} %bu_own.1), channel_id=1, source_target_pairs={{0,1},{1,0},{2,3},{3,2},{4,5},{5,4},{6,7},{7,6},{8,9},{9,8},{10,11... | collective-permute-start | bytes 18440 | tf_op jit(solution)/shard_map/ppermute | solution.py:587
  13.8 11.0 %collective-permute-start.5 = (bf16[1536,768]{1,0:T(8,128)(2,1)S(1)}, bf16[1536,768]{1,0:T(8,128)(2,1)S(1)}, u32[]{:S(2)}, u32[]{:S(2)}) collective-permute-start(bf16[1536,768]{1,0:T(8,128)(2,1)S(1)} %copy-done.5), channel_id=1, source_target_pairs={{0,1},{1,0},{2,3},{3,2},{4,5},{5,4},{6,7},{7,6},{8,9},{9,8},{10,11... | collective-permute-start | bytes 7077896 | tf_op jit(solution)/shard_map/ppermute | solution.py:587
  38.6 4.7 %collective-permute-start.6 = (bf16[8,192,768]{2,1,0:T(8,128)(2,1)S(1)}, bf16[8,192,768]{2,1,0:T(8,128)(2,1)S(1)}, u32[]{:S(2)}, u32[]{:S(2)}) collective-permute-start(bf16[8,192,768]{2,1,0:T(8,128)(2,1)S(1)} %shard_map.275), channel_id=1, source_target_pairs={{0,1},{1,0},{2,3},{3,2},{4,5},{5,4},{6,7},{7,6},{8,9},{9,8},{10,11... | collective-permute-start | bytes 7077896 | tf_op jit(solution)/shard_map/ppermute | solution.py:587
  44.8 17.6 %collective-permute-start.7 = (bf16[4,192,768]{2,1,0:T(8,128)(2,1)}, bf16[4,192,768]{2,1,0:T(8,128)(2,1)}, u32[]{:S(2)}, u32[]{:S(2)}) collective-permute-start(bf16[4,192,768]{2,1,0:T(8,128)(2,1)} %add_convert_fusion.2), channel_id=1, source_target_pairs={{0,2},{1,5},{2,0},{3,7},{4,6},{5,1},{6,4},{7,3},{8,10},{9,13},{10,... | collective-permute-start | bytes 3538952 | tf_op jit(solution)/shard_map/ppermute | solution.py:602
  54.4 11.6 %collective-permute-start.9 = (bf16[8,192,768]{2,1,0:T(8,128)(2,1)S(1)}, bf16[8,192,768]{2,1,0:T(8,128)(2,1)S(1)}, u32[]{:S(2)}, u32[]{:S(2)}) collective-permute-start(bf16[8,192,768]{2,1,0:T(8,128)(2,1)S(1)} %get-tuple-element.97), channel_id=1, source_target_pairs={{0,1},{1,0},{2,3},{3,2},{4,5},{5,4},{6,7},{7,6},{8,9},{9,8},{10,11... | collective-permute-start | bytes 7077896 | tf_op jit(solution)/shard_map/ppermute | solution.py:587
  64.1 18.2 %collective-permute-start.8 = (bf16[2,192,768]{2,1,0:T(8,128)(2,1)S(1)}, bf16[2,192,768]{2,1,0:T(8,128)(2,1)S(1)}, u32[]{:S(2)}, u32[]{:S(2)}) collective-permute-start(bf16[2,192,768]{2,1,0:T(8,128)(2,1)S(1)} %add_convert_fusion.5), channel_id=1, source_target_pairs={{0,4},{1,3},{2,6},{3,1},{4,0},{5,7},{6,2},{7,5},{8,12},{9,11},{10,... | collective-permute-start | bytes 1769480 | tf_op jit(solution)/shard_map/ppermute | solution.py:602
  83.4 13.8 %collective-permute-start.14 = (bf16[1,192,768]{2,1,0:T(8,128)(2,1)S(1)}, bf16[1,192,768]{2,1,0:T(8,128)(2,1)S(1)}, u32[]{:S(2)}, u32[]{:S(2)}) collective-permute-start(bf16[1,192,768]{2,1,0:T(8,128)(2,1)S(1)} %add_convert_fusion.14), channel_id=1, source_target_pairs={{0,8},{1,9},{2,10},{3,11},{4,12},{5,13},{6,14},{7,15},{8,0},{9,1},... | collective-permute-start | bytes 884744 | tf_op jit(solution)/shard_map/ppermute | solution.py:602
  85.0 20.0 %collective-permute-start.16 = (bf16[4,192,768]{2,1,0:T(8,128)(2,1)S(1)}, bf16[4,192,768]{2,1,0:T(8,128)(2,1)S(1)}, u32[]{:S(2)}, u32[]{:S(2)}) collective-permute-start(bf16[4,192,768]{2,1,0:T(8,128)(2,1)S(1)} %add_convert_fusion.1), channel_id=1, source_target_pairs={{0,8},{1,3},{2,10},{3,1},{4,12},{5,7},{6,14},{7,5},{8,0},{9,11},{1... | collective-permute-start | bytes 3538952 | tf_op jit(solution)/shard_map/ppermute | solution.py:602
  85.5 20.7 %collective-permute-start.12 = (bf16[8,392,384]{2,1,0:T(8,128)(2,1)S(1)}, bf16[8,392,384]{2,1,0:T(8,128)(2,1)S(1)}, u32[]{:S(2)}, u32[]{:S(2)}) collective-permute-start(bf16[8,392,384]{2,1,0:T(8,128)(2,1)S(1)} %get-tuple-element.111), channel_id=1, source_target_pairs={{0,1},{1,0},{2,3},{3,2},{4,5},{5,4},{6,7},{7,6},{8,9},{9,8},{10,11... | collective-permute-start | bytes 7225352 | tf_op jit(solution)/shard_map/ppermute | solution.py:587
  105.3 22.3 %collective-permute-start.17 = (bf16[2,192,768]{2,1,0:T(8,128)(2,1)S(1)}, bf16[2,192,768]{2,1,0:T(8,128)(2,1)S(1)}, u32[]{:S(2)}, u32[]{:S(2)}) collective-permute-start(bf16[2,192,768]{2,1,0:T(8,128)(2,1)S(1)} %add_convert_fusion.4), channel_id=1, source_target_pairs={{0,2},{1,5},{2,0},{3,7},{4,6},{5,1},{6,4},{7,3},{8,10},{9,13},{10,... | collective-permute-start | bytes 1769480 | tf_op jit(solution)/shard_map/ppermute | solution.py:602
  106.5 30.9 %collective-permute-start.13 = (bf16[4,392,384]{2,1,0:T(8,128)(2,1)S(1)}, bf16[4,392,384]{2,1,0:T(8,128)(2,1)S(1)}, u32[]{:S(2)}, u32[]{:S(2)}) collective-permute-start(bf16[4,392,384]{2,1,0:T(8,128)(2,1)S(1)} %add_convert_fusion), channel_id=1, source_target_pairs={{0,4},{1,9},{2,6},{3,11},{4,0},{5,13},{6,2},{7,15},{8,12},{9,1},{1... | collective-permute-start | bytes 3612680 | tf_op jit(solution)/shard_map/ppermute | solution.py:602
  113.2 14.1 %collective-permute-start.15 = (bf16[1,192,768]{2,1,0:T(8,128)(2,1)S(1)}, bf16[1,192,768]{2,1,0:T(8,128)(2,1)S(1)}, u32[]{:S(2)}, u32[]{:S(2)}) collective-permute-start(bf16[1,192,768]{2,1,0:T(8,128)(2,1)S(1)} %add_convert_fusion.13), channel_id=1, source_target_pairs={{0,16},{1,17},{2,18},{3,19},{4,20},{5,21},{6,22},{7,23},{8,24},{9,... | collective-permute-start | bytes 884744 | tf_op jit(solution)/shard_map/ppermute | solution.py:602
  116.1 38.0 %collective-permute-start.11 = (f32[512,768]{1,0:T(8,128)S(1)}, f32[512,768]{1,0:T(8,128)S(1)}, u32[]{:S(2)}, u32[]{:S(2)}) collective-permute-start(f32[512,768]{1,0:T(8,128)S(1)} %get-tuple-element.107.refs_1_), channel_id=1, source_target_pairs={{0,1},{1,0},{2,3},{3,2},{4,5},{5,4},{6,7},{7,6},{8,9},{9,8},{10,11... | collective-permute-start | bytes 4718600 | tf_op jit(solution)/shard_map/ppermute | solution.py:587
  127.4 9.9 %collective-permute-start.19 = (bf16[1,192,768]{2,1,0:T(8,128)(2,1)S(1)}, bf16[1,192,768]{2,1,0:T(8,128)(2,1)S(1)}, u32[]{:S(2)}, u32[]{:S(2)}) collective-permute-start(bf16[1,192,768]{2,1,0:T(8,128)(2,1)S(1)} %add_convert_fusion.12), channel_id=1, source_target_pairs={{0,8},{1,9},{2,10},{3,11},{4,12},{5,13},{6,14},{7,15},{8,0},{9,1},... | collective-permute-start | bytes 884744 | tf_op jit(solution)/shard_map/ppermute | solution.py:602
  127.5 26.6 %collective-permute-start.10 = (bf16[512,768]{1,0:T(8,128)(2,1)S(1)}, bf16[512,768]{1,0:T(8,128)(2,1)S(1)}, u32[]{:S(2)}, u32[]{:S(2)}) collective-permute-start(bf16[512,768]{1,0:T(8,128)(2,1)S(1)} %get-tuple-element.76.refs_0_), channel_id=1, source_target_pairs={{0,1},{1,0},{2,3},{3,2},{4,5},{5,4},{6,7},{7,6},{8,9},{9,8},{10,11... | collective-permute-start | bytes 2359304 | tf_op jit(solution)/shard_map/ppermute | solution.py:587
  127.7 10.0 %collective-permute-start.20 = (bf16[1,192,768]{2,1,0:T(8,128)(2,1)S(1)}, bf16[1,192,768]{2,1,0:T(8,128)(2,1)S(1)}, u32[]{:S(2)}, u32[]{:S(2)}) collective-permute-start(bf16[1,192,768]{2,1,0:T(8,128)(2,1)S(1)} %add_convert_fusion.11), channel_id=1, source_target_pairs={{0,4},{1,9},{2,6},{3,11},{4,0},{5,13},{6,2},{7,15},{8,12},{9,1},{1... | collective-permute-start | bytes 884744 | tf_op jit(solution)/shard_map/ppermute | solution.py:602
  137.3 16.3 %collective-permute-start.22 = (bf16[2,192,768]{2,1,0:T(8,128)(2,1)S(1)}, bf16[2,192,768]{2,1,0:T(8,128)(2,1)S(1)}, u32[]{:S(2)}, u32[]{:S(2)}) collective-permute-start(bf16[2,192,768]{2,1,0:T(8,128)(2,1)S(1)} %pad_maximum_fusion.4), channel_id=1, source_target_pairs={{0,4},{1,3},{2,6},{3,1},{4,0},{5,7},{6,2},{7,5},{8,12},{9,11},{10,... | collective-permute-start | bytes 1769480 | tf_op jit(solution)/shard_map/ppermute | solution.py:602
  137.7 19.2 %collective-permute-start.18 = (bf16[2,392,384]{2,1,0:T(8,128)(2,1)S(1)}, bf16[2,392,384]{2,1,0:T(8,128)(2,1)S(1)}, u32[]{:S(2)}, u32[]{:S(2)}) collective-permute-start(bf16[2,392,384]{2,1,0:T(8,128)(2,1)S(1)} %add_convert_fusion.3), channel_id=1, source_target_pairs={{0,2},{1,5},{2,0},{3,7},{4,6},{5,1},{6,4},{7,3},{8,10},{9,13},{10,... | collective-permute-start | bytes 1806344 | tf_op jit(solution)/shard_map/ppermute | solution.py:602
  138.0 15.9 %collective-permute-start.23 = (bf16[1,192,768]{2,1,0:T(8,128)(2,1)S(1)}, bf16[1,192,768]{2,1,0:T(8,128)(2,1)S(1)}, u32[]{:S(2)}, u32[]{:S(2)}) collective-permute-start(bf16[1,192,768]{2,1,0:T(8,128)(2,1)S(1)} %add_convert_fusion.10), channel_id=1, source_target_pairs={{0,16},{1,17},{2,18},{3,19},{4,20},{5,21},{6,22},{7,23},{8,24},{9,... | collective-permute-start | bytes 884744 | tf_op jit(solution)/shard_map/ppermute | solution.py:602
  153.8 32.1 %collective-permute-start.25 = (bf16[4,192,768]{2,1,0:T(8,128)(2,1)S(1)}, bf16[4,192,768]{2,1,0:T(8,128)(2,1)S(1)}, u32[]{:S(2)}, u32[]{:S(2)}) collective-permute-start(bf16[4,192,768]{2,1,0:T(8,128)(2,1)S(1)} %pad_maximum_fusion.1.refs_0_), channel_id=1, source_target_pairs={{0,2},{1,5},{2,0},{3,7},{4,6},{5,1},{6,4},{7,3},{8,10},{9,13},{10,... | collective-permute-start | bytes 3538952 | tf_op jit(solution)/shard_map/ppermute | solution.py:602
  154.0 10.0 %collective-permute-start.26 = (bf16[1,192,768]{2,1,0:T(8,128)(2,1)S(1)}, bf16[1,192,768]{2,1,0:T(8,128)(2,1)S(1)}, u32[]{:S(2)}, u32[]{:S(2)}) collective-permute-start(bf16[1,192,768]{2,1,0:T(8,128)(2,1)S(1)} %add_convert_fusion.9), channel_id=1, source_target_pairs={{0,4},{1,9},{2,6},{3,11},{4,0},{5,13},{6,2},{7,15},{8,12},{9,1},{1... | collective-permute-start | bytes 884744 | tf_op jit(solution)/shard_map/ppermute | solution.py:602
  157.0 9.1 %collective-permute-start.21 = (bf16[1,392,384]{2,1,0:T(8,128)(2,1)S(1)}, bf16[1,392,384]{2,1,0:T(8,128)(2,1)S(1)}, u32[]{:S(2)}, u32[]{:S(2)}) collective-permute-start(bf16[1,392,384]{2,1,0:T(8,128)(2,1)S(1)} %add_convert_fusion.8), channel_id=1, source_target_pairs={{0,8},{1,3},{2,10},{3,1},{4,12},{5,7},{6,14},{7,5},{8,0},{9,11},{1... | collective-permute-start | bytes 903176 | tf_op jit(solution)/shard_map/ppermute | solution.py:602
  164.0 21.6 %collective-permute-start.28 = (bf16[2,192,768]{2,1,0:T(8,128)(2,1)S(1)}, bf16[2,192,768]{2,1,0:T(8,128)(2,1)S(1)}, u32[]{:S(2)}, u32[]{:S(2)}) collective-permute-start(bf16[2,192,768]{2,1,0:T(8,128)(2,1)S(1)} %pad_maximum_fusion.5), channel_id=1, source_target_pairs={{0,2},{1,5},{2,0},{3,7},{4,6},{5,1},{6,4},{7,3},{8,10},{9,13},{10,... | collective-permute-start | bytes 1769480 | tf_op jit(solution)/shard_map/ppermute | solution.py:602
  166.3 19.6 %collective-permute-start.24 = (bf16[1,392,384]{2,1,0:T(8,128)(2,1)S(1)}, bf16[1,392,384]{2,1,0:T(8,128)(2,1)S(1)}, u32[]{:S(2)}, u32[]{:S(2)}) collective-permute-start(bf16[1,392,384]{2,1,0:T(8,128)(2,1)S(1)} %add_convert_fusion.7), channel_id=1, source_target_pairs={{0,16},{1,17},{2,18},{3,19},{4,20},{5,21},{6,22},{7,23},{8,24},{9,... | collective-permute-start | bytes 903176 | tf_op jit(solution)/shard_map/ppermute | solution.py:602
  185.8 23.7 %collective-permute-start.30 = (bf16[4,192,768]{2,1,0:T(8,128)(2,1)S(1)}, bf16[4,192,768]{2,1,0:T(8,128)(2,1)S(1)}, u32[]{:S(2)}, u32[]{:S(2)}) collective-permute-start(bf16[4,192,768]{2,1,0:T(8,128)(2,1)S(1)} %pad_maximum_fusion.2.refs_0_), channel_id=1, source_target_pairs={{0,8},{1,3},{2,10},{3,1},{4,12},{5,7},{6,14},{7,5},{8,0},{9,11},{1... | collective-permute-start | bytes 3538952 | tf_op jit(solution)/shard_map/ppermute | solution.py:602
  186.0 19.3 %collective-permute-start.27 = (bf16[1,392,384]{2,1,0:T(8,128)(2,1)S(1)}, bf16[1,392,384]{2,1,0:T(8,128)(2,1)S(1)}, u32[]{:S(2)}, u32[]{:S(2)}) collective-permute-start(bf16[1,392,384]{2,1,0:T(8,128)(2,1)S(1)} %add_convert_fusion.6), channel_id=1, source_target_pairs={{0,8},{1,3},{2,10},{3,1},{4,12},{5,7},{6,14},{7,5},{8,0},{9,11},{1... | collective-permute-start | bytes 903176 | tf_op jit(solution)/shard_map/ppermute | solution.py:602
  205.3 10.1 %collective-permute-start.29 = (bf16[2,392,384]{2,1,0:T(8,128)(2,1)S(1)}, bf16[2,392,384]{2,1,0:T(8,128)(2,1)S(1)}, u32[]{:S(2)}, u32[]{:S(2)}) collective-permute-start(bf16[2,392,384]{2,1,0:T(8,128)(2,1)S(1)} %pad_maximum_fusion.3), channel_id=1, source_target_pairs={{0,2},{1,5},{2,0},{3,7},{4,6},{5,1},{6,4},{7,3},{8,10},{9,13},{10,... | collective-permute-start | bytes 1806344 | tf_op jit(solution)/shard_map/ppermute | solution.py:602
  215.6 16.5 %collective-permute-start.31 = (bf16[4,392,384]{2,1,0:T(8,128)(2,1)S(1)}, bf16[4,392,384]{2,1,0:T(8,128)(2,1)S(1)}, u32[]{:S(2)}, u32[]{:S(2)}) collective-permute-start(bf16[4,392,384]{2,1,0:T(8,128)(2,1)S(1)} %pad_maximum_fusion.refs_0_.refs_1_), channel_id=1, source_target_pairs={{0,4},{1,9},{2,6},{3,11},{4,0},{5,13},{6,2},{7,15},{8,12},{9,1},{1... | collective-permute-start | bytes 3612680 | tf_op jit(solution)/shard_map/ppermute | solution.py:602
  (33 other events, 264.7 us)

commit v3 on v2

--- a/solution.py
+++ b/solution.py
@@ -18,11 +18,10 @@
 VMEM_MIB = 16
 COVER = 20
 
-STEP_BITS = (
-    ((0, 1, 2), (1, 0, 2)),
-    ((2, 0, 1), (0, 1, 2)),
-    ((1, 0, 2), (2, 1, 0)),
-)
+STEP_BITS = ((((0, 2, 1), (2, 1, 0)), ((1, 2, 0), (2, 0, 1))), (((1, 0, 2), (1, 2, 0)), ((0, 1, 2), (0, 1, 2))), (((0, 1, 2), (1, 2, 0)), ((1, 0, 2), (1, 0, 2))))
+EARLY = ((0,), (), (0, 1), (0, 1))
+ROUNDS = ((2, 1, 0), (2, 1, 0), (2, 1, 0), (2, 1, 0), (2, 1), (2,), (2,))
+JOIN_AT = 1
 
 
 def dot_nn(left, right):
@@ -82,18 +81,22 @@
     return out
 
 
+def step_bits(batch, core, gathering, steps):
+    return [bit for bit in STEP_BITS[batch][core % 2][gathering] if bit < steps]
+
+
 def spot_of(ids, batch, kind, number, count):
     steps = count.bit_length() - 1
     me = ids[1] & (count - 1)
-    down = range(steps - 1, -1, -1)
     number = jnp.int32(number) if isinstance(number, int) else number
     spots = []
     for core in range(2):
-        bits = STEP_BITS[batch][1 - core if kind == 1 else core][:steps]
+        bits = step_bits(batch, 1 - core if kind == 1 else core, kind > 1, steps)
+        places = range(steps) if kind > 1 else range(steps - 1, -1, -1)
         if kind == 2:
-            spots.append(move_bits(number, zip(down, bits, strict=True)) ^ me)
+            spots.append(move_bits(number, zip(places, bits, strict=True)) ^ me)
         else:
-            spots.append(move_bits(number ^ me, zip(bits, down, strict=True)))
+            spots.append(move_bits(number ^ me, zip(bits, places, strict=True)))
     return jnp.where((ids[0] & 1) == 0, spots[0], spots[1])
 
 
@@ -527,7 +530,7 @@
             copies.append(copy)
     for n in range(n_small):
         for line, c0, row in small_plan[n]:
-            p = spot_of(ids, batch, 0, row % count, count)
+            p = spot_of(ids, batch, 3, row % count, count)
             spot = pieces[0].shape[1] - 8 + row // count
             high = pieces[0][p & (half - 1), pieces[0].shape[1] - 8 :, :].astype(F32)
             low = pieces[1][p & (half - 1), pieces[0].shape[1] - 8 :, :].astype(F32)
@@ -591,7 +594,7 @@
     def __init__(self, mesh, batch, own, other_received):
         self.mesh, self.batch = mesh, batch
         self.halvings = own.shape[0].bit_length() - 1
-        self.doublings = (mesh.shape["dp"] >> self.halvings).bit_length() - 1
+        self.steps = 2 * self.halvings + 1
         self.terms = [own, other_received]
         self.at = 0
         self.sent = None
@@ -608,25 +611,26 @@
         return acc.astype(BF16)
 
     def step(self, *earlier):
-        bits = STEP_BITS[self.batch]
         terms = self.terms
         if earlier:
             terms = terms[:-1] + [after(terms[-1], *earlier)]
-        if self.at < self.halvings:
-            order = self.at
+        n = self.at
+        if n < self.halvings:
             half = terms[0].shape[0] // 2
             self.sent = self.total([term[half:] for term in terms])
-            received = self.exchange(self.sent, lambda c: bits[c % 2][order])
+            received = self.exchange(self.sent, lambda c: step_bits(self.batch, c, 0, self.halvings)[n])
             self.terms = [term[:half] for term in terms] + [received]
-        elif self.at < self.halvings + self.doublings:
-            bit = self.at
-            self.sent = self.total(terms)
-            self.terms = [self.sent, self.exchange(self.sent, lambda c: bit)]
+        elif n == self.halvings:
+            doublings = (self.mesh.shape["dp"] >> self.halvings).bit_length() - 1
+            for k in range(doublings):
+                self.sent = self.total(terms)
+                terms = [self.sent, self.exchange(self.sent, lambda c, k=k: self.halvings + k)]
+            self.terms = terms
         else:
-            order = 2 * self.halvings + self.doublings - 1 - self.at
-            first = order == self.halvings - 1
-            self.sent = self.total(terms) if first else jnp.concatenate(terms, axis=0)
-            self.terms = [self.sent, self.exchange(self.sent, lambda c: bits[c % 2][order])]
+            n -= self.halvings + 1
+            self.sent = self.total(terms) if n == 0 else jnp.concatenate(terms, axis=0)
+            received = self.exchange(self.sent, lambda c: step_bits(self.batch, c, 1, self.halvings)[n])
+            self.terms = [self.sent, received]
         self.at += 1
         return self.sent
 
@@ -686,26 +690,38 @@
     down_other = down_grad(1, ids, gb_o, df, count)
     down_got = swap_cores(down_other, cores)
     down_own = down_grad(0, ids, gb, after(df, down_other), count)
-    sum_down = GroupSum(mesh, 0, down_own, down_got)
-    sent = sum_down.step()
-    up_other, bu_o, dh = ffn_bwd(1, ids, after(df, sent), hb, gp_o, w_down_o, w_up_o, (dr2,), count)
+    sums = [GroupSum(mesh, 0, down_own, down_got)]
+
+    landed = []
+
+    def exchange_all(batches, *earlier):
+        earlier += tuple(landed)
+        landed.clear()
+        sents = [sums[batch].step(*earlier) for batch in batches]
+        landed.extend(sums[batch].terms[-1] for batch in batches)
+        return sents
+
+    sent = exchange_all(EARLY[0])
+    up_other, bu_o, dh = ffn_bwd(1, ids, after(df, *sent), hb, gp_o, w_down_o, w_up_o, (dr2,), count)
     up_got = swap_cores(up_other, cores)
-    up_own, bu, dr1, da, vec_a = ffn_bwd(0, ids, df, hb, gp, w_down, w_up, (dh, n1, rstd, gain_attn), count)
-    sum_up = GroupSum(mesh, 1, up_own, up_got)
-    sent = (sum_down.step(da), sum_up.step())
+    sent = exchange_all(EARLY[1], dh) if EARLY[1] else []
+    up_own, bu, dr1, da, vec_a = ffn_bwd(
+        0, ids, after(df, *sent), hb, gp, w_down, w_up, (dh, n1, rstd, gain_attn), count
+    )
+    sums.append(GroupSum(mesh, 1, up_own, up_got))
+    sent = exchange_all(EARLY[2], da)
     bwd_scal = (ids, bucket_len, seq_lengths, keep_mask)
     qkv_other, ig_part = attn_bwd(
         1, bwd_scal, qa_o, k_o, v_o, o_o, after(da, *sent), w_out_o, w_qkv_o, tokens,
         (bu_o, vec_a, vec_f), (dr1, out_grad), count,
     )
     qkv_got = swap_cores(qkv_other, cores)
-    sent = sum_down.step(ig_part)
+    sent = exchange_all(EARLY[3], ig_part, mixed_o)
     qkv_own, ig = attn_bwd(
-        0, bwd_scal, qa, k, v, o, after(da, sent), w_out, w_qkv, tokens, (bu, vec_a, vec_f), (ig_part,), count
+        0, bwd_scal, qa, k, v, o, after(da, *sent), w_out, w_qkv, tokens, (bu, vec_a, vec_f), (ig_part,), count
     )
     ig_o = swap_cores(ig, cores)
-    sum_qkv = GroupSum(mesh, 2, qkv_own, qkv_got)
-    steps = 2 * sum_down.halvings + sum_down.doublings
+    sums.append(GroupSum(mesh, 2, qkv_own, qkv_got))
     size = hidden // count
     whole_cols = (slice(None), slice(None))
 
@@ -732,34 +748,41 @@
         ],
         [(3, size, local), (out_size, width)],
     )
-    earlier = []
-    for n in range(steps):
-        sum_qkv.step(*earlier)
-        earlier = [ig] if n == 0 else []
-        for each in (sum_down, sum_up):
-            if each.at < steps:
-                each.step(*earlier[:1] if n == 0 else ())
-                earlier.append(each.terms[-1])
-                if each is sum_down and each.at == steps:
-                    held = place(0, 0, ids, sum_down.terms[:1], down_outs, *down_args)
-        if n == 1:
-            out_mixed, out_ig = join(ids, cores, (mixed, ig), (mixed_o, ig_o))
-            earlier.append(out_ig)
-        if n == steps - 3:
-            grad_w_down = place(0, count // 2, ids, sum_down.terms[1:], down_outs, *down_args, held)[0]
-        if n == steps - 2:
-            earlier.append(grad_w_down)
-    held = place(1, 0, ids, sum_up.terms[:1], up_outs, *up_args)
-    grad_w_up = place(1, count // 2, ids, sum_up.terms[1:], up_outs, *up_args, held)[0]
-    held = place(2, 0, ids, sum_qkv.terms[:1], qkv_outs, *qkv_args)
     per_up, per_norm = hidden // local, width // local
     small_plan = [[(n, 0, n) for n in range(2)], [(None, c * local, 2 + c) for c in range(per_up)]]
     for n in range(6):
         small_plan.append([(None, c * local, 2 + per_up + n * per_norm + c) for c in range(per_norm)])
     small_outs = [shaped((2, local), F32), shaped((hidden,), F32)] + [shaped((width,), F32)] * 6
-    grad_w_qkv, grad_w_out, grad_bias_qv, grad_bias_up, *norms = place(
-        2, count // 2, ids, [sum_qkv.terms[1], sum_qkv.terms[0]], qkv_outs, *qkv_args, held, small_outs, small_plan
-    )
+    plans = ((down_outs, *down_args), (up_outs, *up_args), (qkv_outs, *qkv_args))
+    held, placed = {}, {}
+    fillers = [ig]
+    for number, batches in enumerate(ROUNDS):
+        ready = tuple(landed) + tuple(fillers)
+        later = []
+        if number == JOIN_AT:
+            out_mixed, out_ig = join(ids, cores, (mixed, after(ig, *ready)), (mixed_o, ig_o))
+            later.append(out_ig)
+        for batch in (0, 1):
+            each = sums[batch]
+            if each.at == each.steps and batch not in placed:
+                pieces = [after(each.terms[1], *ready)]
+                placed[batch] = place(batch, count // 2, ids, pieces, *plans[batch], held[batch])
+                later.append(placed[batch][0])
+        exchange_all([batch for batch in batches if sums[batch].at < sums[batch].steps], *fillers)
+        fillers = later
+        for batch, each in enumerate(sums):
+            if each.at == each.steps and batch not in held:
+                held[batch] = place(batch, 0, ids, each.terms[:1], *plans[batch])
+    for batch in range(3):
+        if batch not in placed:
+            pieces = [sums[batch].terms[1]]
+            if batch < 2:
+                placed[batch] = place(batch, count // 2, ids, pieces, *plans[batch], held[batch])
+            else:
+                pieces += sums[2].terms[:1]
+                placed[2] = place(2, count // 2, ids, pieces, *plans[2], held[2], small_outs, small_plan)
+    grad_w_down, grad_w_up = placed[0][0], placed[1][0]
+    grad_w_qkv, grad_w_out, grad_bias_qv, grad_bias_up, *norms = placed[2]
     return (
         out_mixed,
         out_ig,

time: 235 us -> 212 us (0.902)
  waiting for transfers between devices: 99.7 us -> 74.8 us
  starting transfers between devices: 29.3 us -> 32.4 us
  local copies, waits for them, and re-layouts: 6.73 us -> 4.35 us
    ppermute x21, waiting for transfers between devices: 98.2 us -> 72.3 us  [exchange(): return lax.ppermute(array_in, ('dp', 'tensor'), pairs)]
    ppermute x21, starting transfers between devices: 27 us -> 30 us  [exchange(): return lax.ppermute(array_in, ('dp', 'tensor'), pairs)]
    unnamed x66 -> x58, local copies, waits for them, and re-layouts: 6.73 us -> 4.35 us
  transfers between devices with their start and end apart: 32 -> 32, of which waited for: 10 -> 13; matrix products, arithmetic and copies ran while one was open for 2% -> 3% of each run, Pallas kernels for 31% -> 35%
where the time goes in v3:
time: 212 us
  Pallas kernels  90.5 us (43%)
  waiting for transfers between devices  74.8 us (35%)
  starting transfers between devices  32.4 us (15%)
  other arithmetic  7.86 us (4%)
  local copies, waits for them, and re-layouts  4.35 us (2%)
    pallas_call x16, Pallas kernels, call(): pl.pallas_call(body, out_shape=outs, grid_spec=pltpu.PrefetchScalarGridSp...  90.5 us
    ppermute x21, waiting for transfers between devices, exchange(): return lax.ppermute(array_in, ('dp', 'tensor'), pairs)  72.3 us
    ppermute x21, starting transfers between devices, exchange(): return lax.ppermute(array_in, ('dp', 'tensor'), pairs)  30 us
    convert_element_type x15, other arithmetic, total(): return acc.astype(BF16)  7.29 us
    unnamed x58, local copies, waits for them, and re-layouts  4.35 us
  transfers between devices with their start and end apart: 32, of which 13 were waited for; matrix products, arithmetic and copies ran while one was open for 3% of the time, Pallas kernels for 35%

profile of v3, /device:TPU:0, one launch (start us, length us, event | category | flops | bytes accessed | tf_op | source)
XLA Modules:
  0.0 212.0 jit_solution(12318396845312942205)
XLA Ops:
  7.1 6.7 %shard_map.272 = (bf16[6,512,128]{2,1,0:T(8,128)(2,1)S(1)}, bf16[3,512,128]{2,1,0:T(8,128)(2,1)S(1)}, bf16[3,512,128]{2,1,0:T(8,128)(2,1)S(1)}, bf16[3,512,128]{2,1,0:T(8,128)(2,1)S(1)}) custom-call(s32[2]{0:T(128)S(1)} %compare_select_fusion.ids, s32[1]{0:T(128)S(6)} %copy.39.bucket, s32[1,8]{1,0:T(1,128)S(1)} %copy-done.23, ...), custom_call_target="tpu_custom_call" | custom-call | flops 34225520640 | bytes 4521984 | tf_op jit(solution)/shard_map/pallas_call | solution.py:53
  14.1 10.7 %shard_map.273 = (bf16[6,512,128]{2,1,0:T(8,128)(2,1)S(1)}, bf16[3,512,128]{2,1,0:T(8,128)(2,1)S(1)}, bf16[3,512,128]{2,1,0:T(8,128)(2,1)S(1)}, bf16[3,512,128]{...) custom-call(s32[2]{0:T(128)S(1)} %compare_select_fusion.ids, ...), custom_call_target="tpu_custom_call" | custom-call | flops 46305116160 | bytes 4521984 | tf_op jit(solution)/shard_map/pallas_call | solution.py:53
  24.9 11.7 %shard_map.274 = (bf16[512,1536]{1,0:T(8,128)(2,1)S(1)}, bf16[512,1536]{1,0:T(8,128)(2,1)S(1)}, f32[512,1536]{1,0:T(8,128)S(1)}, f32[512,1536]{1,0:T(8,128)S(1)}...) custom-call(s32[2]{0:T(128)S(1)} %compare_select_fusion.ids, ...), custom_call_target="tpu_custom_call" | custom-call | flops 96636764160 | bytes 26738688 | tf_op jit(solution)/shard_map/pallas_call | solution.py:53
  36.7 2.6 %shard_map.275 = bf16[8,192,768]{2,1,0:T(8,128)(2,1)S(1)} custom-call(s32[2]{0:T(128)S(1)} %compare_select_fusion.ids, bf16[512,1536]{1,0:T(8,128)(2,1)S(1)} %get-tuple-element.96.gb_ref, bf16[512,768]{1,0:T(8,128)(2,1)S(1)} %get-tuple-element.98.df_ref), custom_call_target="tpu_custom_call" | custom-call | flops 24159191040 | bytes 4718592 | tf_op jit(solution)/shard_map/pallas_call | solution.py:53
  39.9 2.6 %shard_map.276 = bf16[8,192,768]{2,1,0:T(8,128)(2,1)S(1)} custom-call(s32[2]{0:T(128)S(1)} %compare_select_fusion.ids, bf16[512,1536]{1,0:T(8,128)(2,1)S(1)} %get-tuple-element.95.gb_ref, bf16[512,768]{1,0:T(8,128)(2,1)S(1)} %get-tuple-element.98.df_ref), custom_call_target="tpu_custom_call" | custom-call | flops 24159191040 | bytes 4718592 | tf_op jit(solution)/shard_map/pallas_call | solution.py:53
  42.6 2.5 %collective-permute-done.6 = bf16[8,192,768]{2,1,0:T(8,128)(2,1)S(1)} collective-permute-done((bf16[8,192,768]{2,1,0:T(8,128)(2,1)S(1)}, bf16[8,192,768]{2,1,0:T(8,128)(2,1)S(1)}, u32[]{:S(2)}, u32[]{:S(2)}) %collective-permute-start.6) | collective-permute-done | bytes 2359328 | tf_op jit(solution)/shard_map/ppermute | solution.py:590
  46.6 2.9 %collective-permute-start.7 = (bf16[4,192,768]{2,1,0:T(8,128)(2,1)}, bf16[4,192,768]{2,1,0:T(8,128)(2,1)}, u32[]{:S(2)}, u32[]{:S(2)}) collective-permute-start(bf16[4,192,768]{2,1,0:T(8,128)(2,1)} %add_convert_fusion.2), channel_id=1, source_target_pairs={{0,2},{1,5},{2,0},{3,7},{4,6},{5,1},{6,4},{7,3},{8,10},{9,13},{10,... | collective-permute-start | bytes 3538952 | tf_op jit(solution)/shard_map/ppermute | solution.py:605
  49.5 6.7 %shard_map.277 = (bf16[8,192,768]{2,1,0:T(8,128)(2,1)S(1)}, f32[1,1536]{1,0:T(1,128)S(1)}, f32[512,768]{1,0:T(8,128)S(1)}) custom-call(s32[2]{0:T(128)S(1)} %compare_select_fusion.ids, bf16[512,768]{1,0:T(8,128)(2,1)S(1)} %get-tuple-element.98.df_ref, bf16[512,768]{1,0:T(8,128)(2,1)S(1)} %get-tuple-element.87.hb_ref, ...), custom_call_target="tpu_custom_call" | custom-call | flops 72477573120 | bytes 14155776 | tf_op jit(solution)/shard_map/pallas_call | solution.py:53
  56.4 7.9 %shard_map.278 = (bf16[8,192,768]{2,1,0:T(8,128)(2,1)S(1)}, f32[1,1536]{1,0:T(1,128)S(1)}, f32[512,768]{1,0:T(8,128)S(1)}, bf16[512,768]{1,0:T(8,128)(2,1)S(1)}, f32[3,768]{1,0:T(4,128)S(1)}) custom-call(s32[2]{0:T(128)S(1)} %compare_select_fusion.ids, bf16[512,768]{1,0:T(8,128)(2,1)S(1)} %get-tuple-element.98.df_ref, ...), custom_call_target="tpu_custom_call" | custom-call | flops 72477573120 | bytes 14155776 | tf_op jit(solution)/shard_map/pallas_call | solution.py:53
  65.6 1.9 collective-permute-start.8
  67.8 1.6 collective-permute-start.11
  69.4 13.2 %shard_map.279 = (bf16[8,392,384]{2,1,0:T(8,128)(2,1)S(1)}, f32[512,768]{1,0:T(8,128)S(1)}) custom-call(s32[2]{0:T(128)S(1)} %compare_select_fusion.ids, s32[1]{0:T(128)S(6)} %copy.39.bucket, s32[1,8]{1,0:T(1,128)S(1)} %copy-done.24, s32[1,8]{1,0:T(1,128)S(1)} %copy-done.22, bf16[6,512,128]{2,1,0:T(8,128)(2,1)S(1)} %get-tuple-element.105.qa_ref, ...), custom_call_target="tpu_custom_call" | custom-call | flops 88583700480 | bytes 10420224 | tf_op jit(solution)/shard_map/pallas_call | solution.py:53
  88.7 11.4 %shard_map.280 = (bf16[8,392,384]{2,1,0:T(8,128)(2,1)S(1)}, f32[512,768]{1,0:T(8,128)S(1)}) custom-call(s32[2]{0:T(128)S(1)} %compare_select_fusion.ids, s32[1]{0:T(128)S(6)} %copy.39.bucket, s32[1,8]{1,0:T(1,128)S(1)} %copy-done.24, s32[1,8]{1,0:T(1,128)S(1)} %copy-done.22, bf16[6,512,128]{2,1,0:T(8,128)(2,1)S(1)} %get-tuple-element.90.qa_ref, ...), custom_call_target="tpu_custom_call" | custom-call | flops 88583700480 | bytes 10420224 | tf_op jit(solution)/shard_map/pallas_call | solution.py:53
  102.9 2.7 %collective-permute-start.17 = (bf16[1,192,768]{2,1,0:T(8,128)(2,1)S(1)}, bf16[1,192,768]{2,1,0:T(8,128)(2,1)S(1)}, u32[]{:S(2)}, u32[]{:S(2)}) collective-permute-start(bf16[1,192,768]{2,1,0:T(8,128)(2,1)S(1)} %add_convert_fusion.12), channel_id=1, source_target_pairs={{0,16},{1,17},{2,18},{3,19},{4,20},{5,21},{6,22},{7,23},{8,24},{9,... | collective-permute-start | bytes 884744 | tf_op jit(solution)/shard_map/ppermute | solution.py:605
  105.6 11.3 %collective-permute-done.16 = bf16[1,192,768]{2,1,0:T(8,128)(2,1)S(1)} collective-permute-done((bf16[1,192,768]{2,1,0:T(8,128)(2,1)S(1)}, bf16[1,192,768]{2,1,0:T(8,128)(2,1)S(1)}, u32[]{:S(2)}, u32[]{:S(2)}) %collective-permute-start.16) | collective-permute-done | bytes 294944 | tf_op jit(solution)/shard_map/ppermute | solution.py:605
  116.8 2.5 %collective-permute-done.17 = bf16[1,192,768]{2,1,0:T(8,128)(2,1)S(1)} collective-permute-done((bf16[1,192,768]{2,1,0:T(8,128)(2,1)S(1)}, bf16[1,192,768]{2,1,0:T(8,128)(2,1)S(1)}, u32[]{:S(2)}, u32[]{:S(2)}) %collective-permute-start.17) | collective-permute-done | bytes 294944 | tf_op jit(solution)/shard_map/ppermute | solution.py:605
  120.8 4.0 %collective-permute-start.21 = (bf16[1,192,768]{2,1,0:T(8,128)(2,1)S(1)}, bf16[1,192,768]{2,1,0:T(8,128)(2,1)S(1)}, u32[]{:S(2)}, u32[]{:S(2)}) collective-permute-start(bf16[1,192,768]{2,1,0:T(8,128)(2,1)S(1)} %add_convert_fusion.10), channel_id=1, source_target_pairs={{0,8},{1,9},{2,10},{3,11},{4,12},{5,13},{6,14},{7,15},{8,0},{9,1},... | collective-permute-start | bytes 884744 | tf_op jit(solution)/shard_map/ppermute | solution.py:605
  124.8 4.1 %shard_map.281 = (bf16[1024,768]{1,0:T(8,128)(2,1)}, f32[1024,768]{1,0:T(8,128)}) custom-call(s32[2]{0:T(128)S(1)} %compare_select_fusion.ids, bf16[512,768]{1,0:T(8,128)(2,1)} %get-tuple-element.89.refs_0_, f32[512,768]{1,0:T(8,128)S(1)} %get-tuple-element.128.refs_1_, bf16[512,768]{1,0:T(8,128)(2,1)} %collective-permute-done.10.refs_2_, ...), custom_call_target="tpu_custom_call" | custom-call | bytes 9437184 | tf_op jit(solution)/shard_map/pallas_call | solution.py:53
  128.9 5.7 %collective-permute-done.20 = bf16[1,192,768]{2,1,0:T(8,128)(2,1)S(1)} collective-permute-done((bf16[1,192,768]{2,1,0:T(8,128)(2,1)S(1)}, bf16[1,192,768]{2,1,0:T(8,128)(2,1)S(1)}, u32[]{:S(2)}, u32[]{:S(2)}) %collective-permute-start.20) | collective-permute-done | bytes 294944 | tf_op jit(solution)/shard_map/ppermute | solution.py:605
  137.7 11.9 %collective-permute-done.23 = bf16[1,192,768]{2,1,0:T(8,128)(2,1)S(1)} collective-permute-done((bf16[1,192,768]{2,1,0:T(8,128)(2,1)S(1)}, bf16[1,192,768]{2,1,0:T(8,128)(2,1)S(1)}, u32[]{:S(2)}, u32[]{:S(2)}) %collective-permute-start.23) | collective-permute-done | bytes 294944 | tf_op jit(solution)/shard_map/ppermute | solution.py:605
  150.9 3.5 %collective-permute-start.25 = (bf16[1,392,384]{2,1,0:T(8,128)(2,1)S(1)}, bf16[1,392,384]{2,1,0:T(8,128)(2,1)S(1)}, u32[]{:S(2)}, u32[]{:S(2)}) collective-permute-start(bf16[1,392,384]{2,1,0:T(8,128)(2,1)S(1)} %add_convert_fusion.7), channel_id=1, source_target_pairs={{0,16},{1,17},{2,18},{3,19},{4,20},{5,21},{6,22},{7,23},{8,24},{9,... | collective-permute-start | bytes 903176 | tf_op jit(solution)/shard_map/ppermute | solution.py:605
  154.5 10.2 %collective-permute-done.25 = bf16[1,392,384]{2,1,0:T(8,128)(2,1)S(1)} collective-permute-done((bf16[1,392,384]{2,1,0:T(8,128)(2,1)S(1)}, bf16[1,392,384]{2,1,0:T(8,128)(2,1)S(1)}, u32[]{:S(2)}, u32[]{:S(2)}) %collective-permute-start.25) | collective-permute-done | bytes 301088 | tf_op jit(solution)/shard_map/ppermute | solution.py:605
  168.3 2.0 shard_map.282.refs_1_
  170.3 2.0 shard_map.283
  172.3 4.9 %collective-permute-done.28 = bf16[1,392,384]{2,1,0:T(8,128)(2,1)S(1)} collective-permute-done((bf16[1,392,384]{2,1,0:T(8,128)(2,1)S(1)}, bf16[1,392,384]{2,1,0:T(8,128)(2,1)S(1)}, u32[]{:S(2)}, u32[]{:S(2)}) %collective-permute-start.28) | collective-permute-done | bytes 301088 | tf_op jit(solution)/shard_map/ppermute | solution.py:605
  177.3 5.1 %collective-permute-done.29.refs_0_ = bf16[4,192,768]{2,1,0:T(8,128)(2,1)S(1)} collective-permute-done((bf16[4,192,768]{2,1,0:T(8,128)(2,1)S(1)}, bf16[4,192,768]{2,1,0:T(8,128)(2,1)S(1)}, u32[]{:S(2)}, u32[]{:S(2)}) %collective-permute-start.29) | collective-permute-done | bytes 1179680 | tf_op jit(solution)/shard_map/ppermute | solution.py:605
  184.0 2.0 shard_map.284.refs_1_
  186.0 2.0 shard_map.285
  188.0 4.5 %collective-permute-done.30 = bf16[2,392,384]{2,1,0:T(8,128)(2,1)S(1)} collective-permute-done((bf16[2,392,384]{2,1,0:T(8,128)(2,1)S(1)}, bf16[2,392,384]{2,1,0:T(8,128)(2,1)S(1)}, u32[]{:S(2)}, u32[]{:S(2)}) %collective-permute-start.30) | collective-permute-done | bytes 602144 | tf_op jit(solution)/shard_map/ppermute | solution.py:605
  194.0 2.0 shard_map.286
  196.0 13.2 %collective-permute-done.31.refs_0_ = bf16[4,392,384]{2,1,0:T(8,128)(2,1)S(1)} collective-permute-done((bf16[4,392,384]{2,1,0:T(8,128)(2,1)S(1)}, bf16[4,392,384]{2,1,0:T(8,128)(2,1)S(1)}, u32[]{:S(2)}, u32[]{:S(2)}) %collective-permute-start.31) | collective-permute-done | bytes 1204256 | tf_op jit(solution)/shard_map/ppermute | solution.py:605
  209.2 2.6 %shard_map.287 = (f32[3,768,384]{2,1,0:T(8,128)}, f32[384,768]{1,0:T(8,128)}, f32[2,384]{1,0:T(2,128)}, f32[1536]{0:T(1024)}, f32[768]{0:T(1024)}, /*index=5*/f3...) custom-call(s32[2]{0:T(128)S(1)} %compare_select_fusion.ids, ...), custom_call_target="tpu_custom_call", output_to_operand_aliasing={{0}: (3, {}), {1}: (4, {})} | custom-call | bytes 3612672 | tf_op jit(solution)/shard_map/pallas_call | solution.py:53
  (128 shorter events, 31.1 us)
Async XLA Ops:
  0.6 13.3 %collective-permute-start = (bf16[3,768,384]{2,1,0:T(8,128)(2,1)}, bf16[3,768,384]{2,1,0:T(8,128)(2,1)}, u32[]{:S(2)}, u32[]{:S(2)}) collective-permute-start(bf16[3,768,384]{2,1,0:T(8,128)(2,1)} %w_ref.3), channel_id=1, source_target_pairs={{0,1},{1,0},{2,3},{3,2},{4,5},{5,4},{6,7},{7,6},{8,9},{9,8},{10,11... | collective-permute-start | bytes 5308424 | tf_op jit(solution)/shard_map/ppermute | solution.py:590
  1.2 12.6 %collective-permute-start.1 = (f32[2,384]{1,0:T(2,128)}, f32[2,384]{1,0:T(2,128)S(1)}, u32[]{:S(2)}, u32[]{:S(2)}) collective-permute-start(f32[2,384]{1,0:T(2,128)} %b_ref.1), channel_id=1, source_target_pairs={{0,1},{1,0},{2,3},{3,2},{4,5},{5,4},{6,7},{7,6},{8,9},{9,8},{10,11... | collective-permute-start | bytes 9224 | tf_op jit(solution)/shard_map/ppermute | solution.py:590
  1.2 12.7 %collective-permute-start.2 = (bf16[384,768]{1,0:T(8,128)(2,1)}, bf16[384,768]{1,0:T(8,128)(2,1)S(1)}, u32[]{:S(2)}, u32[]{:S(2)}) collective-permute-start(bf16[384,768]{1,0:T(8,128)(2,1)} %wo_ref.1), channel_id=1, source_target_pairs={{0,1},{1,0},{2,3},{3,2},{4,5},{5,4},{6,7},{7,6},{8,9},{9,8},{10,11... | collective-permute-start | bytes 1769480 | tf_op jit(solution)/shard_map/ppermute | solution.py:590
  1.7 23.2 %collective-permute-start.3 = (bf16[768,1536]{1,0:T(8,128)(2,1)}, bf16[768,1536]{1,0:T(8,128)(2,1)S(1)}, u32[]{:S(2)}, u32[]{:S(2)}) collective-permute-start(bf16[768,1536]{1,0:T(8,128)(2,1)} %up_ref.1), channel_id=1, source_target_pairs={{0,1},{1,0},{2,3},{3,2},{4,5},{5,4},{6,7},{7,6},{8,9},{9,8},{10,11... | collective-permute-start | bytes 7077896 | tf_op jit(solution)/shard_map/ppermute | solution.py:590
  1.8 23.1 %collective-permute-start.4 = (f32[1536]{0:T(1024)}, f32[1536]{0:T(1024)S(1)}, u32[]{:S(2)}, u32[]{:S(2)}) collective-permute-start(f32[1536]{0:T(1024)} %bu_own.1), channel_id=1, source_target_pairs={{0,1},{1,0},{2,3},{3,2},{4,5},{5,4},{6,7},{7,6},{8,9},{9,8},{10,11... | collective-permute-start | bytes 18440 | tf_op jit(solution)/shard_map/ppermute | solution.py:590
  13.8 11.0 %collective-permute-start.5 = (bf16[1536,768]{1,0:T(8,128)(2,1)S(1)}, bf16[1536,768]{1,0:T(8,128)(2,1)S(1)}, u32[]{:S(2)}, u32[]{:S(2)}) collective-permute-start(bf16[1536,768]{1,0:T(8,128)(2,1)S(1)} %copy-done.3), channel_id=1, source_target_pairs={{0,1},{1,0},{2,3},{3,2},{4,5},{5,4},{6,7},{7,6},{8,9},{9,8},{10,11... | collective-permute-start | bytes 7077896 | tf_op jit(solution)/shard_map/ppermute | solution.py:590
  39.3 5.8 %collective-permute-start.6 = (bf16[8,192,768]{2,1,0:T(8,128)(2,1)S(1)}, bf16[8,192,768]{2,1,0:T(8,128)(2,1)S(1)}, u32[]{:S(2)}, u32[]{:S(2)}) collective-permute-start(bf16[8,192,768]{2,1,0:T(8,128)(2,1)S(1)} %shard_map.275), channel_id=1, source_target_pairs={{0,1},{1,0},{2,3},{3,2},{4,5},{5,4},{6,7},{7,6},{8,9},{9,8},{10,11... | collective-permute-start | bytes 7077896 | tf_op jit(solution)/shard_map/ppermute | solution.py:590
  39.8 42.9 %collective-permute-start.10 = (bf16[512,768]{1,0:T(8,128)(2,1)}, bf16[512,768]{1,0:T(8,128)(2,1)}, u32[]{:S(2)}, u32[]{:S(2)}) collective-permute-start(bf16[512,768]{1,0:T(8,128)(2,1)} %get-tuple-element.89.refs_0_), channel_id=1, source_target_pairs={{0,1},{1,0},{2,3},{3,2},{4,5},{5,4},{6,7},{7,6},{8,9},{9,8},{10,11... | collective-permute-start | bytes 2359304 | tf_op jit(solution)/shard_map/ppermute | solution.py:590
  46.6 17.6 %collective-permute-start.7 = (bf16[4,192,768]{2,1,0:T(8,128)(2,1)}, bf16[4,192,768]{2,1,0:T(8,128)(2,1)}, u32[]{:S(2)}, u32[]{:S(2)}) collective-permute-start(bf16[4,192,768]{2,1,0:T(8,128)(2,1)} %add_convert_fusion.2), channel_id=1, source_target_pairs={{0,2},{1,5},{2,0},{3,7},{4,6},{5,1},{6,4},{7,3},{8,10},{9,13},{10,... | collective-permute-start | bytes 3538952 | tf_op jit(solution)/shard_map/ppermute | solution.py:605
  56.3 11.2 %collective-permute-start.9 = (bf16[8,192,768]{2,1,0:T(8,128)(2,1)S(1)}, bf16[8,192,768]{2,1,0:T(8,128)(2,1)S(1)}, u32[]{:S(2)}, u32[]{:S(2)}) collective-permute-start(bf16[8,192,768]{2,1,0:T(8,128)(2,1)S(1)} %get-tuple-element.110), channel_id=1, source_target_pairs={{0,1},{1,0},{2,3},{3,2},{4,5},{5,4},{6,7},{7,6},{8,9},{9,8},{10,11... | collective-permute-start | bytes 7077896 | tf_op jit(solution)/shard_map/ppermute | solution.py:590
  65.6 17.1 %collective-permute-start.8 = (bf16[2,192,768]{2,1,0:T(8,128)(2,1)S(1)}, bf16[2,192,768]{2,1,0:T(8,128)(2,1)S(1)}, u32[]{:S(2)}, u32[]{:S(2)}) collective-permute-start(bf16[2,192,768]{2,1,0:T(8,128)(2,1)S(1)} %add_convert_fusion.5), channel_id=1, source_target_pairs={{0,8},{1,9},{2,10},{3,11},{4,12},{5,13},{6,14},{7,15},{8,0},{9,1},... | collective-permute-start | bytes 1769480 | tf_op jit(solution)/shard_map/ppermute | solution.py:605
  67.8 16.3 %collective-permute-start.11 = (bf16[4,192,768]{2,1,0:T(8,128)(2,1)S(1)}, bf16[4,192,768]{2,1,0:T(8,128)(2,1)S(1)}, u32[]{:S(2)}, u32[]{:S(2)}) collective-permute-start(bf16[4,192,768]{2,1,0:T(8,128)(2,1)S(1)} %add_convert_fusion.1), channel_id=1, source_target_pairs={{0,4},{1,3},{2,6},{3,1},{4,0},{5,7},{6,2},{7,5},{8,12},{9,11},{10,... | collective-permute-start | bytes 3538952 | tf_op jit(solution)/shard_map/ppermute | solution.py:605
  82.6 17.5 %collective-permute-start.12 = (bf16[8,392,384]{2,1,0:T(8,128)(2,1)S(1)}, bf16[8,392,384]{2,1,0:T(8,128)(2,1)S(1)}, u32[]{:S(2)}, u32[]{:S(2)}) collective-permute-start(bf16[8,392,384]{2,1,0:T(8,128)(2,1)S(1)} %get-tuple-element.124), channel_id=1, source_target_pairs={{0,1},{1,0},{2,3},{3,2},{4,5},{5,4},{6,7},{7,6},{8,9},{9,8},{10,11... | collective-permute-start | bytes 7225352 | tf_op jit(solution)/shard_map/ppermute | solution.py:590
  85.6 14.5 %collective-permute-start.13 = (bf16[1,192,768]{2,1,0:T(8,128)(2,1)S(1)}, bf16[1,192,768]{2,1,0:T(8,128)(2,1)S(1)}, u32[]{:S(2)}, u32[]{:S(2)}) collective-permute-start(bf16[1,192,768]{2,1,0:T(8,128)(2,1)S(1)} %add_convert_fusion.14), channel_id=1, source_target_pairs={{0,4},{1,3},{2,6},{3,1},{4,0},{5,7},{6,2},{7,5},{8,12},{9,11},{10,... | collective-permute-start | bytes 884744 | tf_op jit(solution)/shard_map/ppermute | solution.py:605
  87.2 13.0 %collective-permute-start.14 = (bf16[2,192,768]{2,1,0:T(8,128)(2,1)S(1)}, bf16[2,192,768]{2,1,0:T(8,128)(2,1)S(1)}, u32[]{:S(2)}, u32[]{:S(2)}) collective-permute-start(bf16[2,192,768]{2,1,0:T(8,128)(2,1)S(1)} %add_convert_fusion.4), channel_id=1, source_target_pairs={{0,2},{1,5},{2,0},{3,7},{4,6},{5,1},{6,4},{7,3},{8,10},{9,13},{10,... | collective-permute-start | bytes 1769480 | tf_op jit(solution)/shard_map/ppermute | solution.py:605
  100.5 18.9 %collective-permute-start.15 = (bf16[4,392,384]{2,1,0:T(8,128)(2,1)S(1)}, bf16[4,392,384]{2,1,0:T(8,128)(2,1)S(1)}, u32[]{:S(2)}, u32[]{:S(2)}) collective-permute-start(bf16[4,392,384]{2,1,0:T(8,128)(2,1)S(1)} %add_convert_fusion), channel_id=1, source_target_pairs={{0,2},{1,5},{2,0},{3,7},{4,6},{5,1},{6,4},{7,3},{8,10},{9,13},{10,... | collective-permute-start | bytes 3612680 | tf_op jit(solution)/shard_map/ppermute | solution.py:605
  101.1 23.7 %collective-permute-start.18 = (f32[512,768]{1,0:T(8,128)S(1)}, f32[512,768]{1,0:T(8,128)S(1)}, u32[]{:S(2)}, u32[]{:S(2)}) collective-permute-start(f32[512,768]{1,0:T(8,128)S(1)} %get-tuple-element.128.refs_1_), channel_id=1, source_target_pairs={{0,1},{1,0},{2,3},{3,2},{4,5},{5,4},{6,7},{7,6},{8,9},{9,8},{10,11... | collective-permute-start | bytes 4718600 | tf_op jit(solution)/shard_map/ppermute | solution.py:590
  101.3 15.6 %collective-permute-start.16 = (bf16[1,192,768]{2,1,0:T(8,128)(2,1)S(1)}, bf16[1,192,768]{2,1,0:T(8,128)(2,1)S(1)}, u32[]{:S(2)}, u32[]{:S(2)}) collective-permute-start(bf16[1,192,768]{2,1,0:T(8,128)(2,1)S(1)} %add_convert_fusion.13), channel_id=1, source_target_pairs={{0,8},{1,9},{2,10},{3,11},{4,12},{5,13},{6,14},{7,15},{8,0},{9,1},... | collective-permute-start | bytes 884744 | tf_op jit(solution)/shard_map/ppermute | solution.py:605
  102.9 16.5 %collective-permute-start.17 = (bf16[1,192,768]{2,1,0:T(8,128)(2,1)S(1)}, bf16[1,192,768]{2,1,0:T(8,128)(2,1)S(1)}, u32[]{:S(2)}, u32[]{:S(2)}) collective-permute-start(bf16[1,192,768]{2,1,0:T(8,128)(2,1)S(1)} %add_convert_fusion.12), channel_id=1, source_target_pairs={{0,16},{1,17},{2,18},{3,19},{4,20},{5,21},{6,22},{7,23},{8,24},{9,... | collective-permute-start | bytes 884744 | tf_op jit(solution)/shard_map/ppermute | solution.py:605
  119.6 15.2 %collective-permute-start.19 = (bf16[2,392,384]{2,1,0:T(8,128)(2,1)S(1)}, bf16[2,392,384]{2,1,0:T(8,128)(2,1)S(1)}, u32[]{:S(2)}, u32[]{:S(2)}) collective-permute-start(bf16[2,392,384]{2,1,0:T(8,128)(2,1)S(1)} %add_convert_fusion.3), channel_id=1, source_target_pairs={{0,4},{1,3},{2,6},{3,1},{4,0},{5,7},{6,2},{7,5},{8,12},{9,11},{10,... | collective-permute-start | bytes 1806344 | tf_op jit(solution)/shard_map/ppermute | solution.py:605
  120.4 14.2 %collective-permute-start.20 = (bf16[1,192,768]{2,1,0:T(8,128)(2,1)S(1)}, bf16[1,192,768]{2,1,0:T(8,128)(2,1)S(1)}, u32[]{:S(2)}, u32[]{:S(2)}) collective-permute-start(bf16[1,192,768]{2,1,0:T(8,128)(2,1)S(1)} %add_convert_fusion.11), channel_id=1, source_target_pairs={{0,16},{1,17},{2,18},{3,19},{4,20},{5,21},{6,22},{7,23},{8,24},{9,... | collective-permute-start | bytes 884744 | tf_op jit(solution)/shard_map/ppermute | solution.py:605
  120.8 14.1 %collective-permute-start.21 = (bf16[1,192,768]{2,1,0:T(8,128)(2,1)S(1)}, bf16[1,192,768]{2,1,0:T(8,128)(2,1)S(1)}, u32[]{:S(2)}, u32[]{:S(2)}) collective-permute-start(bf16[1,192,768]{2,1,0:T(8,128)(2,1)S(1)} %add_convert_fusion.10), channel_id=1, source_target_pairs={{0,8},{1,9},{2,10},{3,11},{4,12},{5,13},{6,14},{7,15},{8,0},{9,1},... | collective-permute-start | bytes 884744 | tf_op jit(solution)/shard_map/ppermute | solution.py:605
  134.9 14.7 %collective-permute-start.24 = (bf16[2,192,768]{2,1,0:T(8,128)(2,1)S(1)}, bf16[2,192,768]{2,1,0:T(8,128)(2,1)S(1)}, u32[]{:S(2)}, u32[]{:S(2)}) collective-permute-start(bf16[2,192,768]{2,1,0:T(8,128)(2,1)S(1)} %pad_maximum_fusion.4), channel_id=1, source_target_pairs={{0,4},{1,3},{2,6},{3,1},{4,0},{5,7},{6,2},{7,5},{8,12},{9,11},{10,... | collective-permute-start | bytes 1769480 | tf_op jit(solution)/shard_map/ppermute | solution.py:605
  135.8 13.8 %collective-permute-start.22 = (bf16[1,392,384]{2,1,0:T(8,128)(2,1)S(1)}, bf16[1,392,384]{2,1,0:T(8,128)(2,1)S(1)}, u32[]{:S(2)}, u32[]{:S(2)}) collective-permute-start(bf16[1,392,384]{2,1,0:T(8,128)(2,1)S(1)} %add_convert_fusion.8), channel_id=1, source_target_pairs={{0,8},{1,9},{2,10},{3,11},{4,12},{5,13},{6,14},{7,15},{8,0},{9,1},... | collective-permute-start | bytes 903176 | tf_op jit(solution)/shard_map/ppermute | solution.py:605
  136.1 13.5 %collective-permute-start.23 = (bf16[1,192,768]{2,1,0:T(8,128)(2,1)S(1)}, bf16[1,192,768]{2,1,0:T(8,128)(2,1)S(1)}, u32[]{:S(2)}, u32[]{:S(2)}) collective-permute-start(bf16[1,192,768]{2,1,0:T(8,128)(2,1)S(1)} %add_convert_fusion.9), channel_id=1, source_target_pairs={{0,4},{1,3},{2,6},{3,1},{4,0},{5,7},{6,2},{7,5},{8,12},{9,11},{10,... | collective-permute-start | bytes 884744 | tf_op jit(solution)/shard_map/ppermute | solution.py:605
  149.7 16.3 %collective-permute-start.27 = (bf16[4,192,768]{2,1,0:T(8,128)(2,1)S(1)}, bf16[4,192,768]{2,1,0:T(8,128)(2,1)S(1)}, u32[]{:S(2)}, u32[]{:S(2)}) collective-permute-start(bf16[4,192,768]{2,1,0:T(8,128)(2,1)S(1)} %pad_maximum_fusion.1.refs_0_), channel_id=1, source_target_pairs={{0,2},{1,5},{2,0},{3,7},{4,6},{5,1},{6,4},{7,3},{8,10},{9,13},{10,... | collective-permute-start | bytes 3538952 | tf_op jit(solution)/shard_map/ppermute | solution.py:605
  150.7 15.3 %collective-permute-start.26 = (bf16[2,192,768]{2,1,0:T(8,128)(2,1)S(1)}, bf16[2,192,768]{2,1,0:T(8,128)(2,1)S(1)}, u32[]{:S(2)}, u32[]{:S(2)}) collective-permute-start(bf16[2,192,768]{2,1,0:T(8,128)(2,1)S(1)} %pad_maximum_fusion.5), channel_id=1, source_target_pairs={{0,8},{1,5},{2,10},{3,7},{4,12},{5,1},{6,14},{7,3},{8,0},{9,13},{1... | collective-permute-start | bytes 1769480 | tf_op jit(solution)/shard_map/ppermute | solution.py:605
  150.9 13.7 %collective-permute-start.25 = (bf16[1,392,384]{2,1,0:T(8,128)(2,1)S(1)}, bf16[1,392,384]{2,1,0:T(8,128)(2,1)S(1)}, u32[]{:S(2)}, u32[]{:S(2)}) collective-permute-start(bf16[1,392,384]{2,1,0:T(8,128)(2,1)S(1)} %add_convert_fusion.7), channel_id=1, source_target_pairs={{0,16},{1,17},{2,18},{3,19},{4,20},{5,21},{6,22},{7,23},{8,24},{9,... | collective-permute-start | bytes 903176 | tf_op jit(solution)/shard_map/ppermute | solution.py:605
  166.1 16.3 %collective-permute-start.29 = (bf16[4,192,768]{2,1,0:T(8,128)(2,1)S(1)}, bf16[4,192,768]{2,1,0:T(8,128)(2,1)S(1)}, u32[]{:S(2)}, u32[]{:S(2)}) collective-permute-start(bf16[4,192,768]{2,1,0:T(8,128)(2,1)S(1)} %pad_maximum_fusion.2.refs_0_), channel_id=1, source_target_pairs={{0,2},{1,9},{2,0},{3,11},{4,6},{5,13},{6,4},{7,15},{8,10},{9,1},{1... | collective-permute-start | bytes 3538952 | tf_op jit(solution)/shard_map/ppermute | solution.py:605
  167.5 9.8 %collective-permute-start.28 = (bf16[1,392,384]{2,1,0:T(8,128)(2,1)S(1)}, bf16[1,392,384]{2,1,0:T(8,128)(2,1)S(1)}, u32[]{:S(2)}, u32[]{:S(2)}) collective-permute-start(bf16[1,392,384]{2,1,0:T(8,128)(2,1)S(1)} %add_convert_fusion.6), channel_id=1, source_target_pairs={{0,4},{1,5},{2,6},{3,7},{4,0},{5,1},{6,2},{7,3},{8,12},{9,13},{10,... | collective-permute-start | bytes 903176 | tf_op jit(solution)/shard_map/ppermute | solution.py:605
  182.5 10.1 %collective-permute-start.30 = (bf16[2,392,384]{2,1,0:T(8,128)(2,1)S(1)}, bf16[2,392,384]{2,1,0:T(8,128)(2,1)S(1)}, u32[]{:S(2)}, u32[]{:S(2)}) collective-permute-start(bf16[2,392,384]{2,1,0:T(8,128)(2,1)S(1)} %pad_maximum_fusion.3), channel_id=1, source_target_pairs={{0,8},{1,3},{2,10},{3,1},{4,12},{5,7},{6,14},{7,5},{8,0},{9,11},{1... | collective-permute-start | bytes 1806344 | tf_op jit(solution)/shard_map/ppermute | solution.py:605
  192.7 16.5 %collective-permute-start.31 = (bf16[4,392,384]{2,1,0:T(8,128)(2,1)S(1)}, bf16[4,392,384]{2,1,0:T(8,128)(2,1)S(1)}, u32[]{:S(2)}, u32[]{:S(2)}) collective-permute-start(bf16[4,392,384]{2,1,0:T(8,128)(2,1)S(1)} %pad_maximum_fusion.refs_0_.refs_1_), channel_id=1, source_target_pairs={{0,2},{1,9},{2,0},{3,11},{4,6},{5,13},{6,4},{7,15},{8,10},{9,1},{1... | collective-permute-start | bytes 3612680 | tf_op jit(solution)/shard_map/ppermute | solution.py:605
  (29 other events, 182.1 us)

commit v4 on v3

--- a/solution.py
+++ b/solution.py
@@ -18,10 +18,11 @@
 VMEM_MIB = 16
 COVER = 20
 
-STEP_BITS = ((((0, 2, 1), (2, 1, 0)), ((1, 2, 0), (2, 0, 1))), (((1, 0, 2), (1, 2, 0)), ((0, 1, 2), (0, 1, 2))), (((0, 1, 2), (1, 2, 0)), ((1, 0, 2), (1, 0, 2))))
-EARLY = ((0,), (), (0, 1), (0, 1))
-ROUNDS = ((2, 1, 0), (2, 1, 0), (2, 1, 0), (2, 1, 0), (2, 1), (2,), (2,))
-JOIN_AT = 1
+STEP_BITS = ((((1, 0, 2), (2, 1, 0)), ((0, 1, 2), (2, 0, 1))), (((1, 2, 0), (2, 1, 0)), ((0, 2, 1), (2, 0, 1))), (((0, 1, 2), (2, 0, 1)), ((1, 0, 2), (1, 0, 2))), (((0, 1, 2), (0, 2, 1)), ((1, 0, 2), (2, 1, 0))), (((0, 1, 2), (2, 0, 1)), ((1, 0, 2), (0, 1, 2))), (((0, 1, 2), (0, 1, 2)), ((1, 0, 2), (2, 0, 1))))
+PARTS = 2
+EARLY = (((0,), (1,)), ((0,),), ((0, 2), (1, 3)), ((0, 2), (1, 3)))
+TURNS = ((4, 2, 0), (5, 3, 1)) * 7
+JOIN_AT = 3
 
 
 def dot_nn(left, right):
@@ -311,13 +312,15 @@
 
 
 def down_grad_body(kind, ids, gb_ref, df_ref, out_ref):
-    count, size, _ = out_ref.shape
+    _, count, size, _ = out_ref.shape
     per = 2 if count % 2 == 0 else 1
 
     def step(i, carry):
-        value = dot_tn(gb_ref[:, chunk_of(i, per * size)], df_ref[...]).astype(BF16)
+        value = dot_tn(gb_ref[:, chunk_of(i, per * PARTS * size)], df_ref[...]).astype(BF16)
         for c in range(per):
-            out_ref[spot_of(ids, 0, kind, i * per + c, count)] = value[c * size : (c + 1) * size, :]
+            for part in range(PARTS):
+                first = (c * PARTS + part) * size
+                out_ref[part, spot_of(ids, part, kind, i * per + c, count)] = value[first : first + size, :]
         return carry
 
     lax.fori_loop(0, count // per, step, 0)
@@ -328,7 +331,7 @@
     hidden = gb.shape[1]
     return call(
         functools.partial(down_grad_body, kind),
-        [shaped((count, hidden // count, width), BF16)],
+        [shaped((PARTS, count, hidden // (count * PARTS), width), BF16)],
         (ids,),
         (gb, df),
         flops=2 * rows * width * hidden,
@@ -344,7 +347,7 @@
         acc_in, n_ref, rstd_ref, gain_a, out_ref, bu_ref, dr1_ref, da_ref, vec_ref, acc, fold_s = rest
         acc[...] = acc_in[...]
     rows, width = df_ref.shape
-    count, lines, _ = out_ref.shape
+    _, count, _, _ = out_ref.shape
     hidden = up_ref.shape[1]
     up_rows = width // count
     chunk = 384
@@ -355,9 +358,11 @@
         du = (dot_nt(df_ref[...], down_ref[cols, :]) * gp_ref[:, cols]).astype(BF16)
         bu_ref[:, cols] = jnp.sum(fold_rows(du.astype(F32)), axis=0, keepdims=True)
         value = dot_tn(hb_ref[...], du).astype(BF16)
-        line, col = chunk_of(i // per_line, up_rows), chunk_of(i % per_line, chunk)
+        part, col = i // per_line, chunk_of(i % per_line, chunk)
         for a in range(count):
-            out_ref[spot_of(ids, 1, kind, a, count), line, col] = value[a * up_rows : (a + 1) * up_rows, :]
+            spots = [spot_of(ids, 2 + n, kind, a, count) for n in range(PARTS)]
+            spot = jnp.where(part == 0, spots[0], spots[1])
+            out_ref[part, spot, :, col] = value[a * up_rows : (a + 1) * up_rows, :]
         acc[...] += dot_nt(du, up_ref[:, cols])
         return carry
 
@@ -389,7 +394,7 @@
 def ffn_bwd(kind, ids, df, hb, gp, down, up, extra, count):
     rows, width = df.shape
     hidden = up.shape[1]
-    outs = [shaped((count, width * hidden // (count * width), width), BF16), shaped((1, hidden), F32)]
+    outs = [shaped((hidden // width, count, width // count, width), BF16), shaped((1, hidden), F32)]
     scratch = []
     if kind == 1:
         outs += [shaped((rows, width), F32)]
@@ -417,7 +422,7 @@
     rows, width = da_ref.shape
     pairs = k_ref.shape[0]
     local = pairs * LANES
-    count = dw_ref.shape[0]
+    count = dw_ref.shape[1]
     size, out_size, wide = width // count, local // count, width // local
     _, bm_s[...] = mask_columns(ids, bucket, lens, rows)
     if kind == 1:
@@ -476,19 +481,20 @@
                     small.append(ref[n : n + 1, pl.ds(pl.multiple_of(c + p * LANES, LANES), LANES)])
         line = lax.broadcasted_iota(jnp.int32, (8, LANES), 0)
         for a in range(count):
-            spot = spot_of(ids, 2, kind, a, count)
-            for n in range(3):
-                part = value[a * size : (a + 1) * size, n * LANES : (n + 1) * LANES]
-                dw_ref[spot, n * size : (n + 1) * size, cols] = part
+            spots = [spot_of(ids, 4 + n, kind, a, count) for n in range(PARTS)]
+            rows_a = slice(a * size, (a + 1) * size)
+            dw_ref[0, spots[0], 0:size, cols] = value[rows_a, 0:LANES]
+            dw_ref[0, spots[0], size : 2 * size, cols] = value[rows_a, LANES : 2 * LANES]
+            dw_ref[1, spots[1], 0:size, cols] = value[rows_a, 2 * LANES :]
             for n in range(wide):
                 part = out_value[a * out_size : (a + 1) * out_size, n * LANES : (n + 1) * LANES]
-                at = 3 * size + n * out_size
-                dw_ref[spot, at : at + out_size, cols] = part
+                at = size + n * out_size
+                dw_ref[1, spots[1], at : at + out_size, cols] = part
             tile_s = jnp.zeros((8, LANES), F32)
+            dw_ref[0, spots[0], 2 * size : 2 * size + 8, cols] = tile_s.astype(BF16)
             for n, row in enumerate(small[a::count]):
                 tile_s = jnp.where(line == n, row, tile_s)
-            at = 3 * size + wide * out_size
-            dw_ref[spot, at : at + 8, cols] = tile_s.astype(BF16)
+            dw_ref[1, spots[1], 2 * size : 2 * size + 8, cols] = tile_s.astype(BF16)
         return carry
 
     lax.fori_loop(0, pairs, pair, 0)
@@ -498,10 +504,10 @@
     rows, width = da.shape
     pairs = k.shape[0]
     local = pairs * LANES
-    lines = 4 * width // count + 8
+    lines = 2 * width // count + 8
     return call(
         functools.partial(attn_bwd_body, kind),
-        [shaped((count, lines, local), BF16), shaped((rows, width), F32)],
+        [shaped((PARTS, count, lines, local), BF16), shaped((rows, width), F32)],
         scal,
         (qa, k, v, o, da, wo, w, tokens, *smalls, *extra),
         [pltpu.VMEM((rows, LANES), BF16)],
@@ -511,17 +517,17 @@
     )
 
 
-def place_body(batch, first, count, plan, small_plan, ids, *refs):
+def place_body(part, first, count, plan, n_held, small_plan, ids, *refs):
     pieces = refs[: 1 if small_plan is None else 2]
-    refs = refs[len(pieces) + (len(plan) if first else 0) :]
+    refs = refs[len(pieces) + n_held :]
     outs, refs = refs[: len(plan)], refs[len(plan) :]
     n_small = 0 if small_plan is None else len(small_plan)
     small_outs, refs = refs[:n_small], refs[n_small:]
     stages, sems = refs[:-1], refs[-1]
-    half = pieces[0].shape[0]
+    half, lines, _ = pieces[0].shape
     copies = []
     for q in range(half):
-        a = spot_of(ids, batch, 2, first + q, count)
+        a = spot_of(ids, part, 2, first + q, count)
         for n, (parts, target) in enumerate(plan):
             for at, start, size in parts:
                 stages[n][(q,) + at] = pieces[0][q, start : start + size, :].astype(F32)
@@ -530,10 +536,9 @@
             copies.append(copy)
     for n in range(n_small):
         for line, c0, row in small_plan[n]:
-            p = spot_of(ids, batch, 3, row % count, count)
-            spot = pieces[0].shape[1] - 8 + row // count
-            high = pieces[0][p & (half - 1), pieces[0].shape[1] - 8 :, :].astype(F32)
-            low = pieces[1][p & (half - 1), pieces[0].shape[1] - 8 :, :].astype(F32)
+            p = spot_of(ids, part, 3, row % count, count)
+            high = pieces[0][p & (half - 1), lines - 8 :, :].astype(F32)
+            low = pieces[1][p & (half - 1), lines - 8 :, :].astype(F32)
             tile = jnp.where(p < half, low, high)
             width = tile.shape[1]
             value = tile[row // count : row // count + 1, :]
@@ -545,14 +550,15 @@
         copy.wait()
 
 
-def place(batch, first, ids, pieces, outs, plan, stages, held=(), small_outs=(), small_plan=None):
+def place(part, first, ids, pieces, plan, held=(), small_outs=(), small_plan=None):
     half = pieces[0].shape[0]
+    outs = [shaped(entry[0], F32) for entry in plan]
     return call(
-        functools.partial(place_body, batch, first, 2 * half, plan, small_plan),
-        list(outs) + list(small_outs),
+        functools.partial(place_body, part, first, 2 * half, [entry[2:] for entry in plan], len(held), small_plan),
+        outs + list(small_outs),
         (ids,),
         (*pieces, *held),
-        [pltpu.VMEM((half,) + st, F32) for st in stages] + [pltpu.SemaphoreType.DMA((len(outs), half))],
+        [pltpu.VMEM((half,) + entry[1], F32) for entry in plan] + [pltpu.SemaphoreType.DMA((len(outs), half))],
         moved=6 * half * pieces[0].shape[1] * pieces[0].shape[2],
         in_specs=[resident()] * len(pieces) + [anywhere()] * len(held),
         out_specs=[anywhere()] * len(outs) + [resident()] * len(small_outs),
@@ -690,99 +696,126 @@
     down_other = down_grad(1, ids, gb_o, df, count)
     down_got = swap_cores(down_other, cores)
     down_own = down_grad(0, ids, gb, after(df, down_other), count)
-    sums = [GroupSum(mesh, 0, down_own, down_got)]
-
-    landed = []
-
-    def exchange_all(batches, *earlier):
-        earlier += tuple(landed)
-        landed.clear()
-        sents = [sums[batch].step(*earlier) for batch in batches]
-        landed.extend(sums[batch].terms[-1] for batch in batches)
-        return sents
-
-    sent = exchange_all(EARLY[0])
+    sums = []
+
+    def add_sums(own, received):
+        for part in range(PARTS):
+            sums.append(GroupSum(mesh, len(sums), own[part], received[part]))
+
+    add_sums(down_own, down_got)
+    landed, sents = [[], []], [[], []]
+
+    def exchange(parts, *earlier):
+        which = parts[0] % 2
+        earlier += tuple(landed[which]) + tuple(sents[1 - which])
+        sents[which] = [sums[part].step(*earlier) for part in parts]
+        landed[which] = [sums[part].terms[-1] for part in parts]
+
+    def exchange_all(stage, *earlier):
+        for parts in EARLY[stage]:
+            exchange(parts, *earlier)
+        return sents[0] + sents[1]
+
+    sent = exchange_all(0, df)
     up_other, bu_o, dh = ffn_bwd(1, ids, after(df, *sent), hb, gp_o, w_down_o, w_up_o, (dr2,), count)
     up_got = swap_cores(up_other, cores)
-    sent = exchange_all(EARLY[1], dh) if EARLY[1] else []
+    sent = exchange_all(1, dh)
     up_own, bu, dr1, da, vec_a = ffn_bwd(
         0, ids, after(df, *sent), hb, gp, w_down, w_up, (dh, n1, rstd, gain_attn), count
     )
-    sums.append(GroupSum(mesh, 1, up_own, up_got))
-    sent = exchange_all(EARLY[2], da)
+    add_sums(up_own, up_got)
+    sent = exchange_all(2, da)
     bwd_scal = (ids, bucket_len, seq_lengths, keep_mask)
     qkv_other, ig_part = attn_bwd(
         1, bwd_scal, qa_o, k_o, v_o, o_o, after(da, *sent), w_out_o, w_qkv_o, tokens,
         (bu_o, vec_a, vec_f), (dr1, out_grad), count,
     )
     qkv_got = swap_cores(qkv_other, cores)
-    sent = exchange_all(EARLY[3], ig_part, mixed_o)
+    sent = exchange_all(3, ig_part, mixed_o)
     qkv_own, ig = attn_bwd(
         0, bwd_scal, qa, k, v, o, after(da, *sent), w_out, w_qkv, tokens, (bu, vec_a, vec_f), (ig_part,), count
     )
     ig_o = swap_cores(ig, cores)
-    sums.append(GroupSum(mesh, 2, qkv_own, qkv_got))
-    size = hidden // count
-    whole_cols = (slice(None), slice(None))
-
-    def rows_at(size):
-        return lambda out, a: out.at[pl.ds(pl.multiple_of(a * size, size), size), :]
-
-    down_outs = [shaped((hidden, width), F32)]
-    down_args = ([([(whole_cols, 0, size)], rows_at(size))], [(size, width)])
-    size, out_size = width // count, local // count
-    lines = hidden // width
-    up_outs = [shaped((width, hidden), F32)]
-    parts = [((slice(None), slice(n * width, (n + 1) * width)), n * size, size) for n in range(lines)]
-    up_args = ([(parts, rows_at(size))], [(size, hidden)])
-    qkv_outs = [shaped((3, width, local), F32), shaped((local, width), F32)]
-    wide = width // local
-    parts = [((slice(None), slice(n * local, (n + 1) * local)), 3 * size + n * out_size, out_size) for n in range(wide)]
-    qkv_args = (
+    add_sums(qkv_own, qkv_got)
+
+    def rows_at(each, size, shift=0, cols=slice(None)):
+        def target(out, a):
+            start = pl.multiple_of(a * each, each)
+            return out.at[pl.ds(start + shift, size), cols]
+
+        return target
+
+    every = (slice(None), slice(None))
+    size, out_size, wide = width // count, local // count, width // local
+    half_rows = hidden // (count * PARTS)
+    plans = []
+    for part in range(PARTS):
+        target = rows_at(PARTS * half_rows, half_rows, part * half_rows)
+        plans.append([((hidden, width), (half_rows, width), [(every, 0, half_rows)], target)])
+    for part in range(hidden // width):
+        target = rows_at(size, size, 0, slice(part * width, (part + 1) * width))
+        plans.append([((width, hidden), (size, width), [(every, 0, size)], target)])
+
+    def planes_at(first, planes):
+        return lambda out, a: out.at[first : first + planes, pl.ds(pl.multiple_of(a * size, size), size), :]
+
+    shape = (3, width, local)
+    plans.append([(shape, (2, size, local), [((n,) + every, n * size, size) for n in range(2)], planes_at(0, 2))])
+    pieces = [((slice(None), slice(n * local, (n + 1) * local)), size + n * out_size, out_size) for n in range(wide)]
+    plans.append(
         [
-            (
-                [((n,) + whole_cols, n * size, size) for n in range(3)],
-                lambda out, a: out.at[:, pl.ds(pl.multiple_of(a * size, size), size), :],
-            ),
-            (parts, rows_at(out_size)),
-        ],
-        [(3, size, local), (out_size, width)],
+            (shape, (1, size, local), [((0,) + every, 0, size)], planes_at(2, 1)),
+            ((local, width), (out_size, width), pieces, rows_at(out_size, out_size)),
+        ]
     )
     per_up, per_norm = hidden // local, width // local
     small_plan = [[(n, 0, n) for n in range(2)], [(None, c * local, 2 + c) for c in range(per_up)]]
     for n in range(6):
         small_plan.append([(None, c * local, 2 + per_up + n * per_norm + c) for c in range(per_norm)])
     small_outs = [shaped((2, local), F32), shaped((hidden,), F32)] + [shaped((width,), F32)] * 6
-    plans = ((down_outs, *down_args), (up_outs, *up_args), (qkv_outs, *qkv_args))
-    held, placed = {}, {}
+    held = {0: [], 1: [], 2: []}
+    small = []
+
+    def put(part, late, *earlier):
+        each = sums[part]
+        pieces = [after(each.terms[1] if late else each.terms[0], *earlier)] if earlier else [each.terms[1 if late else 0]]
+        first = count // 2 if late else 0
+        batch = part // PARTS
+        extra = held[batch][: len(plans[part])]
+        if late and part == len(plans) - 1:
+            placed = place(part, first, ids, pieces + [each.terms[0]], plans[part], extra, small_outs, small_plan)
+            small.extend(placed[len(plans[part]) :])
+            placed = placed[: len(plans[part])]
+        else:
+            placed = place(part, first, ids, pieces, plans[part], extra)
+        held[batch] = list(placed) + held[batch][len(placed) :]
+        return placed[0]
+
+    put_early, put_late = set(), set()
     fillers = [ig]
-    for number, batches in enumerate(ROUNDS):
-        ready = tuple(landed) + tuple(fillers)
-        later = []
-        if number == JOIN_AT:
-            out_mixed, out_ig = join(ids, cores, (mixed, after(ig, *ready)), (mixed_o, ig_o))
+    for turn, parts in enumerate(TURNS):
+        active = [part for part in parts if sums[part].at < sums[part].steps]
+        earlier, later = fillers, []
+        if turn == JOIN_AT:
+            out_mixed, out_ig = join(ids, cores, (mixed, after(ig, *sents[0])), (mixed_o, ig_o))
             later.append(out_ig)
-        for batch in (0, 1):
-            each = sums[batch]
-            if each.at == each.steps and batch not in placed:
-                pieces = [after(each.terms[1], *ready)]
-                placed[batch] = place(batch, count // 2, ids, pieces, *plans[batch], held[batch])
-                later.append(placed[batch][0])
-        exchange_all([batch for batch in batches if sums[batch].at < sums[batch].steps], *fillers)
+        for part in parts:
+            if sums[part].at == sums[part].steps and part not in put_late and part < 4:
+                later.append(put(part, True, *landed[part % 2]))
+                put_late.add(part)
+        if active:
+            exchange(active, *earlier)
+        for part in parts:
+            if sums[part].at == sums[part].steps and part not in put_early:
+                put(part, False)
+                put_early.add(part)
         fillers = later
-        for batch, each in enumerate(sums):
-            if each.at == each.steps and batch not in held:
-                held[batch] = place(batch, 0, ids, each.terms[:1], *plans[batch])
-    for batch in range(3):
-        if batch not in placed:
-            pieces = [sums[batch].terms[1]]
-            if batch < 2:
-                placed[batch] = place(batch, count // 2, ids, pieces, *plans[batch], held[batch])
-            else:
-                pieces += sums[2].terms[:1]
-                placed[2] = place(2, count // 2, ids, pieces, *plans[2], held[2], small_outs, small_plan)
-    grad_w_down, grad_w_up = placed[0][0], placed[1][0]
-    grad_w_qkv, grad_w_out, grad_bias_qv, grad_bias_up, *norms = placed[2]
+    for part in range(len(plans)):
+        if part not in put_late:
+            put(part, True)
+    grad_w_down, grad_w_up = held[0][0], held[1][0]
+    grad_w_qkv, grad_w_out = held[2]
+    grad_bias_qv, grad_bias_up, *norms = small
     return (
         out_mixed,
         out_ig,

time: 212 us -> 205 us (0.967)
  waiting for transfers between devices: 74.8 us -> 37.3 us
  starting transfers between devices: 32.4 us -> 54.8 us
  Pallas kernels: 90.5 us -> 97.9 us
    ppermute x21 -> x42, waiting for transfers between devices: 72.3 us -> 34.7 us  [exchange(): return lax.ppermute(array_in, ('dp', 'tensor'), pairs)]
    ppermute x21 -> x42, starting transfers between devices: 30 us -> 52.3 us  [exchange(): return lax.ppermute(array_in, ('dp', 'tensor'), pairs)]
    pallas_call x16 -> x22, Pallas kernels: 90.5 us -> 97.9 us  [call(): pl.pallas_call(body, out_shape=outs, grid_spec=pltpu.PrefetchScalarGridSp...]
    convert_element_type x15 -> x30, other arithmetic: 7.29 us -> 6.58 us  [total(): return acc.astype(BF16)]
    unnamed x58 -> x54, local copies, waits for them, and re-layouts: 4.35 us -> 4.79 us
  transfers between devices with their start and end apart: 32 -> 53, of which waited for: 13 -> 14; matrix products, arithmetic and copies ran while one was open for 3% -> 4% of each run, Pallas kernels for 35% -> 40%
where the time goes in v4:
time: 205 us
  Pallas kernels  97.9 us (48%)
  starting transfers between devices  54.8 us (27%)
  waiting for transfers between devices  37.3 us (18%)
  other arithmetic  7.18 us (4%)
  local copies, waits for them, and re-layouts  5.35 us (3%)
  between operations  2.36 us (1%)
    pallas_call x22, Pallas kernels, call(): pl.pallas_call(body, out_shape=outs, grid_spec=pltpu.PrefetchScalarGridSp...  97.9 us
    ppermute x42, starting transfers between devices, exchange(): return lax.ppermute(array_in, ('dp', 'tensor'), pairs)  52.3 us
    ppermute x42, waiting for transfers between devices, exchange(): return lax.ppermute(array_in, ('dp', 'tensor'), pairs)  34.7 us
    convert_element_type x30, other arithmetic, total(): return acc.astype(BF16)  6.58 us
    unnamed x54, local copies, waits for them, and re-layouts  4.79 us
  transfers between devices with their start and end apart: 53, of which 14 were waited for; matrix products, arithmetic and copies ran while one was open for 4% of the time, Pallas kernels for 40%

profile of v4, /device:TPU:0, one launch (start us, length us, event | category | flops | bytes accessed | tf_op | source)
XLA Modules:
  0.0 204.8 jit_solution(16212691747977356958)
XLA Ops:
  7.1 6.7 %shard_map.272 = (bf16[6,512,128]{2,1,0:T(8,128)(2,1)S(1)}, bf16[3,512,128]{2,1,0:T(8,128)(2,1)S(1)}, bf16[3,512,128]{2,1,0:T(8,128)(2,1)S(1)}, bf16[3,512,128]{2,1,0:T(8,128)(2,1)S(1)}) custom-call(s32[2]{0:T(128)S(1)} %compare_select_fusion.ids, s32[1]{0:T(128)S(6)} %copy.51.bucket, s32[1,8]{1,0:T(1,128)S(1)} %copy-done.21, ...), custom_call_target="tpu_custom_call" | custom-call | flops 34225520640 | bytes 4521984 | tf_op jit(solution)/shard_map/pallas_call | solution.py:54
  14.1 10.7 %shard_map.273 = (bf16[6,512,128]{2,1,0:T(8,128)(2,1)S(1)}, bf16[3,512,128]{2,1,0:T(8,128)(2,1)S(1)}, bf16[3,512,128]{2,1,0:T(8,128)(2,1)S(1)}, bf16[3,512,128]{...) custom-call(s32[2]{0:T(128)S(1)} %compare_select_fusion.ids, ...), custom_call_target="tpu_custom_call" | custom-call | flops 46305116160 | bytes 4521984 | tf_op jit(solution)/shard_map/pallas_call | solution.py:54
  24.9 11.7 %shard_map.274 = (bf16[512,1536]{1,0:T(8,128)(2,1)S(1)}, bf16[512,1536]{1,0:T(8,128)(2,1)S(1)}, f32[512,1536]{1,0:T(8,128)S(1)}, f32[512,1536]{1,0:T(8,128)S(1)}...) custom-call(s32[2]{0:T(128)S(1)} %compare_select_fusion.ids, ...), custom_call_target="tpu_custom_call" | custom-call | flops 96636764160 | bytes 26738688 | tf_op jit(solution)/shard_map/pallas_call | solution.py:54
  36.7 2.6 %shard_map.275 = bf16[2,8,96,768]{3,2,1,0:T(8,128)(2,1)S(1)} custom-call(s32[2]{0:T(128)S(1)} %compare_select_fusion.ids, bf16[512,1536]{1,0:T(8,128)(2,1)S(1)} %get-tuple-element.120.gb_ref, bf16[512,768]{1,0:T(8,128)(2,1)S(1)} %get-tuple-element.129.df_ref), custom_call_target="tpu_custom_call" | custom-call | flops 24159191040 | bytes 4718592 | tf_op jit(solution)/shard_map/pallas_call | solution.py:54
  39.9 2.6 %shard_map.276 = bf16[2,8,96,768]{3,2,1,0:T(8,128)(2,1)S(1)} custom-call(s32[2]{0:T(128)S(1)} %compare_select_fusion.ids, bf16[512,1536]{1,0:T(8,128)(2,1)S(1)} %get-tuple-element.119.gb_ref, bf16[512,768]{1,0:T(8,128)(2,1)S(1)} %get-tuple-element.129.df_ref), custom_call_target="tpu_custom_call" | custom-call | flops 24159191040 | bytes 4718592 | tf_op jit(solution)/shard_map/pallas_call | solution.py:54
  42.5 2.6 %collective-permute-done.6 = bf16[2,8,96,768]{3,2,1,0:T(8,128)(2,1)S(1)} collective-permute-done((bf16[2,8,96,768]{3,2,1,0:T(8,128)(2,1)S(1)}, bf16[2,8,96,768]{3,2,1,0:T(8,128)(2,1)S(1)}, u32[]{:S(2)}, u32[]{:S(2)}) %collective-permute-start.6) | collective-permute-done | bytes 2359328 | tf_op jit(solution)/shard_map/ppermute | solution.py:596
  45.4 3.0 %collective-permute-start.7 = (bf16[4,96,768]{2,1,0:T(8,128)(2,1)S(1)}, bf16[4,96,768]{2,1,0:T(8,128)(2,1)S(1)}, u32[]{:S(2)}, u32[]{:S(2)}) collective-permute-start(bf16[4,96,768]{2,1,0:T(8,128)(2,1)S(1)} %fusion.5), channel_id=1, source_target_pairs={{0,4},{1,3},{2,6},{3,1},{4,0},{5,7},{6,2},{7,5},{8,12},{9,11},{10,... | collective-permute-start | bytes 1769480 | tf_op jit(solution)/shard_map/ppermute | solution.py:611
  49.4 6.7 %shard_map.277 = (bf16[2,8,96,768]{3,2,1,0:T(8,128)(2,1)S(1)}, f32[1,1536]{1,0:T(1,128)S(1)}, f32[512,768]{1,0:T(8,128)S(1)}) custom-call(s32[2]{0:T(128)S(1)} %compare_select_fusion.ids, bf16[512,768]{1,0:T(8,128)(2,1)S(1)} %get-tuple-element.129.df_ref, bf16[512,768]{1,0:T(8,128)(2,1)S(1)} %get-tuple-element.112.hb_ref, ...), custom_call_target="tpu_custom_call" | custom-call | flops 72477573120 | bytes 14155776 | tf_op jit(solution)/shard_map/pallas_call | solution.py:54
  56.3 2.1 %collective-permute-start.8 = (bf16[2,96,768]{2,1,0:T(8,128)(2,1)S(1)}, bf16[2,96,768]{2,1,0:T(8,128)(2,1)S(1)}, u32[]{:S(2)}, u32[]{:S(2)}) collective-permute-start(bf16[2,96,768]{2,1,0:T(8,128)(2,1)S(1)} %fusion.17), channel_id=1, source_target_pairs={{0,2},{1,5},{2,0},{3,7},{4,6},{5,1},{6,4},{7,3},{8,10},{9,13},{10,... | collective-permute-start | bytes 884744 | tf_op jit(solution)/shard_map/ppermute | solution.py:611
  58.4 7.9 %shard_map.278 = (bf16[2,8,96,768]{3,2,1,0:T(8,128)(2,1)S(1)}, f32[1,1536]{1,0:T(1,128)S(1)}, f32[512,768]{1,0:T(8,128)S(1)}, bf16[512,768]{1,0:T(8,128)(2,1)S(1)}, f32[3,768]{1,0:T(4,128)S(1)}) custom-call(s32[2]{0:T(128)S(1)} %compare_select_fusion.ids, bf16[512,768]{1,0:T(8,128)(2,1)S(1)} %get-tuple-element.129.df_ref, ...), custom_call_target="tpu_custom_call" | custom-call | flops 72477573120 | bytes 14155776 | tf_op jit(solution)/shard_map/pallas_call | solution.py:54
  66.4 1.6 collective-permute-start.9
  72.3 13.2 %shard_map.279 = (bf16[2,8,200,384]{3,2,1,0:T(8,128)(2,1)S(1)}, f32[512,768]{1,0:T(8,128)S(1)}) custom-call(s32[2]{0:T(128)S(1)} %compare_select_fusion.ids, s32[1]{0:T(128)S(6)} %copy.51.bucket, s32[1,8]{1,0:T(1,128)S(1)} %copy-done.22, s32[1,8]{1,0:T(1,128)S(1)} %copy-done.20, bf16[6,512,128]{2,1,0:T(8,128)(2,1)S(1)} %get-tuple-element.134.qa_ref, ...), custom_call_target="tpu_custom_call" | custom-call | flops 88583700480 | bytes 10420224 | tf_op jit(solution)/shard_map/pallas_call | solution.py:54
  85.8 2.7 %collective-permute-start.17 = (bf16[1,96,768]{2,1,0:T(8,128)(2,1)S(1)}, bf16[1,96,768]{2,1,0:T(8,128)(2,1)S(1)}, u32[]{:S(2)}, u32[]{:S(2)}) collective-permute-start(bf16[1,96,768]{2,1,0:T(8,128)(2,1)S(1)} %fusion.59), channel_id=1, source_target_pairs={{0,16},{1,17},{2,18},{3,19},{4,20},{5,21},{6,22},{7,23},{8,24},{9,... | collective-permute-start | bytes 442376 | tf_op jit(solution)/shard_map/ppermute | solution.py:611
  93.0 11.7 %shard_map.280 = (bf16[2,8,200,384]{3,2,1,0:T(8,128)(2,1)S(1)}, f32[512,768]{1,0:T(8,128)S(1)}) custom-call(s32[2]{0:T(128)S(1)} %compare_select_fusion.ids, s32[1]{0:T(128)S(6)} %copy.51.bucket, s32[1,8]{1,0:T(1,128)S(1)} %copy-done.22, s32[1,8]{1,0:T(1,128)S(1)} %copy-done.20, bf16[6,512,128]{2,1,0:T(8,128)(2,1)S(1)} %get-tuple-element.115.qa_ref, ...), custom_call_target="tpu_custom_call" | custom-call | flops 88583700480 | bytes 10420224 | tf_op jit(solution)/shard_map/pallas_call | solution.py:54
  104.9 1.6 collective-permute-start.20
  115.1 2.6 %collective-permute-done.19 = bf16[4,200,384]{2,1,0:T(8,128)(2,1)S(1)} collective-permute-done((bf16[4,200,384]{2,1,0:T(8,128)(2,1)S(1)}, bf16[4,200,384]{2,1,0:T(8,128)(2,1)S(1)}, u32[]{:S(2)}, u32[]{:S(2)}) %collective-permute-start.19) | collective-permute-done | bytes 614432 | tf_op jit(solution)/shard_map/ppermute | solution.py:611
  119.8 8.3 %collective-permute-done.27 = bf16[1,96,768]{2,1,0:T(8,128)(2,1)S(1)} collective-permute-done((bf16[1,96,768]{2,1,0:T(8,128)(2,1)S(1)}, bf16[1,96,768]{2,1,0:T(8,128)(2,1)S(1)}, u32[]{:S(2)}, u32[]{:S(2)}) %collective-permute-start.27) | collective-permute-done | bytes 147488 | tf_op jit(solution)/shard_map/ppermute | solution.py:611
  130.9 4.1 %shard_map.281 = (bf16[1024,768]{1,0:T(8,128)(2,1)}, f32[1024,768]{1,0:T(8,128)}) custom-call(s32[2]{0:T(128)S(1)} %compare_select_fusion.ids, bf16[512,768]{1,0:T(8,128)(2,1)} %get-tuple-element.114.refs_0_, f32[512,768]{1,0:T(8,128)S(1)} %get-tuple-element.167.refs_1_, bf16[512,768]{1,0:T(8,128)(2,1)} %collective-permute-done.12.refs_2_, ...), custom_call_target="tpu_custom_call" | custom-call | bytes 9437184 | tf_op jit(solution)/shard_map/pallas_call | solution.py:54
  135.1 1.6 collective-permute-start.30
  140.1 1.6 collective-permute-start.37
  144.7 2.6 %collective-permute-done.37 = bf16[1,96,768]{2,1,0:T(8,128)(2,1)S(1)} collective-permute-done((bf16[1,96,768]{2,1,0:T(8,128)(2,1)S(1)}, bf16[1,96,768]{2,1,0:T(8,128)(2,1)S(1)}, u32[]{:S(2)}, u32[]{:S(2)}) %collective-permute-start.37) | collective-permute-done | bytes 147488 | tf_op jit(solution)/shard_map/ppermute | solution.py:611
  149.0 1.9 collective-permute-start.43
  155.3 2.7 %collective-permute-start.40 = (bf16[1,200,384]{2,1,0:T(8,128)(2,1)S(1)}, bf16[1,200,384]{2,1,0:T(8,128)(2,1)S(1)}, u32[]{:S(2)}, u32[]{:S(2)}) collective-permute-start(bf16[1,200,384]{2,1,0:T(8,128)(2,1)S(1)} %fusion.31), channel_id=1, source_target_pairs={{0,16},{1,17},{2,18},{3,19},{4,20},{5,21},{6,22},{7,23},{8,24},{9,... | collective-permute-start | bytes 460808 | tf_op jit(solution)/shard_map/ppermute | solution.py:611
  158.0 2.5 %collective-permute-start.41 = (bf16[2,96,768]{2,1,0:T(8,128)(2,1)S(1)}, bf16[2,96,768]{2,1,0:T(8,128)(2,1)S(1)}, u32[]{:S(2)}, u32[]{:S(2)}) collective-permute-start(bf16[2,96,768]{2,1,0:T(8,128)(2,1)S(1)} %pad_maximum_fusion.11), channel_id=1, source_target_pairs={{0,8},{1,5},{2,10},{3,7},{4,12},{5,1},{6,14},{7,3},{8,0},{9,13},{1... | collective-permute-start | bytes 884744 | tf_op jit(solution)/shard_map/ppermute | solution.py:611
  160.7 1.7 collective-permute-done.40
  162.4 6.1 %collective-permute-done.41 = bf16[2,96,768]{2,1,0:T(8,128)(2,1)S(1)} collective-permute-done((bf16[2,96,768]{2,1,0:T(8,128)(2,1)S(1)}, bf16[2,96,768]{2,1,0:T(8,128)(2,1)S(1)}, u32[]{:S(2)}, u32[]{:S(2)}) %collective-permute-start.41) | collective-permute-done | bytes 294944 | tf_op jit(solution)/shard_map/ppermute | solution.py:611
  169.9 2.0 collective-permute-start.47
  186.1 3.1 %collective-permute-done.49 = bf16[2,200,384]{2,1,0:T(8,128)(2,1)S(1)} collective-permute-done((bf16[2,200,384]{2,1,0:T(8,128)(2,1)S(1)}, bf16[2,200,384]{2,1,0:T(8,128)(2,1)S(1)}, u32[]{:S(2)}, u32[]{:S(2)}) %collective-permute-start.49) | collective-permute-done | bytes 307232 | tf_op jit(solution)/shard_map/ppermute | solution.py:611
  191.8 1.6 shard_map.291
  193.4 5.1 %collective-permute-done.52.refs_0_ = bf16[4,200,384]{2,1,0:T(8,128)(2,1)S(1)} collective-permute-done((bf16[4,200,384]{2,1,0:T(8,128)(2,1)S(1)}, bf16[4,200,384]{2,1,0:T(8,128)(2,1)S(1)}, u32[]{:S(2)}, u32[]{:S(2)}) %collective-permute-start.52) | collective-permute-done | bytes 614432 | tf_op jit(solution)/shard_map/ppermute | solution.py:611
  200.1 2.3 %collective-permute-done.51.refs_0_ = bf16[4,200,384]{2,1,0:T(8,128)(2,1)S(1)} collective-permute-done((bf16[4,200,384]{2,1,0:T(8,128)(2,1)S(1)}, bf16[4,200,384]{2,1,0:T(8,128)(2,1)S(1)}, u32[]{:S(2)}, u32[]{:S(2)}) %collective-permute-start.51) | collective-permute-done | bytes 614432 | tf_op jit(solution)/shard_map/ppermute | solution.py:611
  202.4 2.2 %shard_map.293 = (f32[3,768,384]{2,1,0:T(8,128)}, f32[384,768]{1,0:T(8,128)}, f32[2,384]{1,0:T(2,128)}, f32[1536]{0:T(1024)}, f32[768]{0:T(1024)}, /*index=5*/f3...) custom-call(s32[2]{0:T(128)S(1)} %compare_select_fusion.ids, ...), custom_call_target="tpu_custom_call", output_to_operand_aliasing={{0}: (3, {}), {1}: (4, {})} | custom-call | bytes 1843200 | tf_op jit(solution)/shard_map/pallas_call | solution.py:54
  (196 shorter events, 62.9 us)
Async XLA Ops:
  0.6 13.3 %collective-permute-start = (bf16[3,768,384]{2,1,0:T(8,128)(2,1)}, bf16[3,768,384]{2,1,0:T(8,128)(2,1)}, u32[]{:S(2)}, u32[]{:S(2)}) collective-permute-start(bf16[3,768,384]{2,1,0:T(8,128)(2,1)} %w_ref.3), channel_id=1, source_target_pairs={{0,1},{1,0},{2,3},{3,2},{4,5},{5,4},{6,7},{7,6},{8,9},{9,8},{10,11... | collective-permute-start | bytes 5308424 | tf_op jit(solution)/shard_map/ppermute | solution.py:596
  1.2 12.6 %collective-permute-start.1 = (f32[2,384]{1,0:T(2,128)}, f32[2,384]{1,0:T(2,128)S(1)}, u32[]{:S(2)}, u32[]{:S(2)}) collective-permute-start(f32[2,384]{1,0:T(2,128)} %b_ref.1), channel_id=1, source_target_pairs={{0,1},{1,0},{2,3},{3,2},{4,5},{5,4},{6,7},{7,6},{8,9},{9,8},{10,11... | collective-permute-start | bytes 9224 | tf_op jit(solution)/shard_map/ppermute | solution.py:596
  1.2 12.7 %collective-permute-start.2 = (bf16[384,768]{1,0:T(8,128)(2,1)}, bf16[384,768]{1,0:T(8,128)(2,1)S(1)}, u32[]{:S(2)}, u32[]{:S(2)}) collective-permute-start(bf16[384,768]{1,0:T(8,128)(2,1)} %wo_ref.1), channel_id=1, source_target_pairs={{0,1},{1,0},{2,3},{3,2},{4,5},{5,4},{6,7},{7,6},{8,9},{9,8},{10,11... | collective-permute-start | bytes 1769480 | tf_op jit(solution)/shard_map/ppermute | solution.py:596
  1.7 23.2 %collective-permute-start.3 = (bf16[768,1536]{1,0:T(8,128)(2,1)}, bf16[768,1536]{1,0:T(8,128)(2,1)S(1)}, u32[]{:S(2)}, u32[]{:S(2)}) collective-permute-start(bf16[768,1536]{1,0:T(8,128)(2,1)} %up_ref.1), channel_id=1, source_target_pairs={{0,1},{1,0},{2,3},{3,2},{4,5},{5,4},{6,7},{7,6},{8,9},{9,8},{10,11... | collective-permute-start | bytes 7077896 | tf_op jit(solution)/shard_map/ppermute | solution.py:596
  1.8 23.1 %collective-permute-start.4 = (f32[1536]{0:T(1024)}, f32[1536]{0:T(1024)S(1)}, u32[]{:S(2)}, u32[]{:S(2)}) collective-permute-start(f32[1536]{0:T(1024)} %bu_own.1), channel_id=1, source_target_pairs={{0,1},{1,0},{2,3},{3,2},{4,5},{5,4},{6,7},{7,6},{8,9},{9,8},{10,11... | collective-permute-start | bytes 18440 | tf_op jit(solution)/shard_map/ppermute | solution.py:596
  13.8 11.0 %collective-permute-start.5 = (bf16[1536,768]{1,0:T(8,128)(2,1)S(1)}, bf16[1536,768]{1,0:T(8,128)(2,1)S(1)}, u32[]{:S(2)}, u32[]{:S(2)}) collective-permute-start(bf16[1536,768]{1,0:T(8,128)(2,1)S(1)} %copy-done.1), channel_id=1, source_target_pairs={{0,1},{1,0},{2,3},{3,2},{4,5},{5,4},{6,7},{7,6},{8,9},{9,8},{10,11... | collective-permute-start | bytes 7077896 | tf_op jit(solution)/shard_map/ppermute | solution.py:596
  39.8 45.7 %collective-permute-start.12 = (bf16[512,768]{1,0:T(8,128)(2,1)}, bf16[512,768]{1,0:T(8,128)(2,1)}, u32[]{:S(2)}, u32[]{:S(2)}) collective-permute-start(bf16[512,768]{1,0:T(8,128)(2,1)} %get-tuple-element.114.refs_0_), channel_id=1, source_target_pairs={{0,1},{1,0},{2,3},{3,2},{4,5},{5,4},{6,7},{7,6},{8,9},{9,8},{10,11... | collective-permute-start | bytes 2359304 | tf_op jit(solution)/shard_map/ppermute | solution.py:596
  49.3 19.7 %collective-permute-start.11 = (bf16[4,96,768]{2,1,0:T(8,128)(2,1)}, bf16[4,96,768]{2,1,0:T(8,128)(2,1)}, u32[]{:S(2)}, u32[]{:S(2)}) collective-permute-start(bf16[4,96,768]{2,1,0:T(8,128)(2,1)} %fusion.4), channel_id=1, source_target_pairs={{0,4},{1,3},{2,6},{3,1},{4,0},{5,7},{6,2},{7,5},{8,12},{9,11},{10,... | collective-permute-start | bytes 1769480 | tf_op jit(solution)/shard_map/ppermute | solution.py:611
  56.1 12.0 %collective-permute-start.10 = (bf16[2,8,96,768]{3,2,1,0:T(8,128)(2,1)S(1)}, bf16[2,8,96,768]{3,2,1,0:T(8,128)(2,1)S(1)}, u32[]{:S(2)}, u32[]{:S(2)}) collective-permute-start(bf16[2,8,96,768]{3,2,1,0:T(8,128)(2,1)S(1)} %get-tuple-element.139), channel_id=1, source_target_pairs={{0,1},{1,0},{2,3},{3,2},{4,5},{5,4},{6,7},{7,6},{8,9},{9,8},{10,11... | collective-permute-start | bytes 7077896 | tf_op jit(solution)/shard_map/ppermute | solution.py:596
  66.4 19.2 %collective-permute-start.9 = (bf16[1,96,768]{2,1,0:T(8,128)(2,1)S(1)}, bf16[1,96,768]{2,1,0:T(8,128)(2,1)S(1)}, u32[]{:S(2)}, u32[]{:S(2)}) collective-permute-start(bf16[1,96,768]{2,1,0:T(8,128)(2,1)S(1)} %fusion.55), channel_id=1, source_target_pairs={{0,8},{1,9},{2,10},{3,11},{4,12},{5,13},{6,14},{7,15},{8,0},{9,1},... | collective-permute-start | bytes 442376 | tf_op jit(solution)/shard_map/ppermute | solution.py:611
  68.4 17.2 %collective-permute-start.13 = (bf16[4,96,768]{2,1,0:T(8,128)(2,1)S(1)}, bf16[4,96,768]{2,1,0:T(8,128)(2,1)S(1)}, u32[]{:S(2)}, u32[]{:S(2)}) collective-permute-start(bf16[4,96,768]{2,1,0:T(8,128)(2,1)S(1)} %fusion.3), channel_id=1, source_target_pairs={{0,2},{1,5},{2,0},{3,7},{4,6},{5,1},{6,4},{7,3},{8,10},{9,13},{10,... | collective-permute-start | bytes 1769480 | tf_op jit(solution)/shard_map/ppermute | solution.py:611
  70.8 19.3 %collective-permute-start.14 = (bf16[2,96,768]{2,1,0:T(8,128)(2,1)S(1)}, bf16[2,96,768]{2,1,0:T(8,128)(2,1)S(1)}, u32[]{:S(2)}, u32[]{:S(2)}) collective-permute-start(bf16[2,96,768]{2,1,0:T(8,128)(2,1)S(1)} %fusion.15), channel_id=1, source_target_pairs={{0,8},{1,9},{2,10},{3,11},{4,12},{5,13},{6,14},{7,15},{8,0},{9,1},... | collective-permute-start | bytes 884744 | tf_op jit(solution)/shard_map/ppermute | solution.py:611
  71.3 18.8 %collective-permute-start.15 = (bf16[4,96,768]{2,1,0:T(8,128)(2,1)S(1)}, bf16[4,96,768]{2,1,0:T(8,128)(2,1)S(1)}, u32[]{:S(2)}, u32[]{:S(2)}) collective-permute-start(bf16[4,96,768]{2,1,0:T(8,128)(2,1)S(1)} %fusion.2), channel_id=1, source_target_pairs={{0,2},{1,5},{2,0},{3,7},{4,6},{5,1},{6,4},{7,3},{8,10},{9,13},{10,... | collective-permute-start | bytes 1769480 | tf_op jit(solution)/shard_map/ppermute | solution.py:611
  85.5 21.0 %collective-permute-start.16 = (bf16[2,8,200,384]{3,2,1,0:T(8,128)(2,1)S(1)}, bf16[2,8,200,384]{3,2,1,0:T(8,128)(2,1)S(1)}, u32[]{:S(2)}, u32[]{:S(2)}) collective-permute-start(bf16[2,8,200,384]{3,2,1,0:T(8,128)(2,1)S(1)} %get-tuple-element.157), channel_id=1, source_target_pairs={{0,1},{1,0},{2,3},{3,2},{4,5},{5,4},{6,7},{7,6},{8,9},{9,8},{10,11... | collective-permute-start | bytes 7372808 | tf_op jit(solution)/shard_map/ppermute | solution.py:596
  85.8 18.9 %collective-permute-start.17 = (bf16[1,96,768]{2,1,0:T(8,128)(2,1)S(1)}, bf16[1,96,768]{2,1,0:T(8,128)(2,1)S(1)}, u32[]{:S(2)}, u32[]{:S(2)}) collective-permute-start(bf16[1,96,768]{2,1,0:T(8,128)(2,1)S(1)} %fusion.59), channel_id=1, source_target_pairs={{0,16},{1,17},{2,18},{3,19},{4,20},{5,21},{6,22},{7,23},{8,24},{9,... | collective-permute-start | bytes 442376 | tf_op jit(solution)/shard_map/ppermute | solution.py:611
  88.5 16.2 %collective-permute-start.18 = (bf16[2,96,768]{2,1,0:T(8,128)(2,1)S(1)}, bf16[2,96,768]{2,1,0:T(8,128)(2,1)S(1)}, u32[]{:S(2)}, u32[]{:S(2)}) collective-permute-start(bf16[2,96,768]{2,1,0:T(8,128)(2,1)S(1)} %fusion.13), channel_id=1, source_target_pairs={{0,4},{1,3},{2,6},{3,1},{4,0},{5,7},{6,2},{7,5},{8,12},{9,11},{10,... | collective-permute-start | bytes 884744 | tf_op jit(solution)/shard_map/ppermute | solution.py:611
  91.2 16.3 %collective-permute-start.22 = (bf16[1,96,768]{2,1,0:T(8,128)(2,1)S(1)}, bf16[1,96,768]{2,1,0:T(8,128)(2,1)S(1)}, u32[]{:S(2)}, u32[]{:S(2)}) collective-permute-start(bf16[1,96,768]{2,1,0:T(8,128)(2,1)S(1)} %fusion.52), channel_id=1, source_target_pairs={{0,2},{1,5},{2,0},{3,7},{4,6},{5,1},{6,4},{7,3},{8,10},{9,13},{10,... | collective-permute-start | bytes 442376 | tf_op jit(solution)/shard_map/ppermute | solution.py:611
  92.3 16.1 %collective-permute-start.23 = (bf16[2,96,768]{2,1,0:T(8,128)(2,1)S(1)}, bf16[2,96,768]{2,1,0:T(8,128)(2,1)S(1)}, u32[]{:S(2)}, u32[]{:S(2)}) collective-permute-start(bf16[2,96,768]{2,1,0:T(8,128)(2,1)S(1)} %fusion.11), channel_id=1, source_target_pairs={{0,4},{1,3},{2,6},{3,1},{4,0},{5,7},{6,2},{7,5},{8,12},{9,11},{10,... | collective-permute-start | bytes 884744 | tf_op jit(solution)/shard_map/ppermute | solution.py:611
  104.7 25.8 %collective-permute-start.24 = (f32[512,768]{1,0:T(8,128)S(1)}, f32[512,768]{1,0:T(8,128)S(1)}, u32[]{:S(2)}, u32[]{:S(2)}) collective-permute-start(f32[512,768]{1,0:T(8,128)S(1)} %get-tuple-element.167.refs_1_), channel_id=1, source_target_pairs={{0,1},{1,0},{2,3},{3,2},{4,5},{5,4},{6,7},{7,6},{8,9},{9,8},{10,11... | collective-permute-start | bytes 4718600 | tf_op jit(solution)/shard_map/ppermute | solution.py:596
  108.6 21.0 %collective-permute-start.25 = (bf16[4,200,384]{2,1,0:T(8,128)(2,1)S(1)}, bf16[4,200,384]{2,1,0:T(8,128)(2,1)S(1)}, u32[]{:S(2)}, u32[]{:S(2)}) collective-permute-start(bf16[4,200,384]{2,1,0:T(8,128)(2,1)S(1)} %fusion), channel_id=1, source_target_pairs={{0,2},{1,5},{2,0},{3,7},{4,6},{5,1},{6,4},{7,3},{8,10},{9,13},{10,... | collective-permute-start | bytes 1843208 | tf_op jit(solution)/shard_map/ppermute | solution.py:611
  114.7 13.4 %collective-permute-start.27 = (bf16[1,96,768]{2,1,0:T(8,128)(2,1)S(1)}, bf16[1,96,768]{2,1,0:T(8,128)(2,1)S(1)}, u32[]{:S(2)}, u32[]{:S(2)}) collective-permute-start(bf16[1,96,768]{2,1,0:T(8,128)(2,1)S(1)} %fusion.43), channel_id=1, source_target_pairs={{0,16},{1,17},{2,18},{3,19},{4,20},{5,21},{6,22},{7,23},{8,24},{9,... | collective-permute-start | bytes 442376 | tf_op jit(solution)/shard_map/ppermute | solution.py:611
  117.9 18.8 %collective-permute-start.31 = (bf16[2,200,384]{2,1,0:T(8,128)(2,1)S(1)}, bf16[2,200,384]{2,1,0:T(8,128)(2,1)S(1)}, u32[]{:S(2)}, u32[]{:S(2)}) collective-permute-start(bf16[2,200,384]{2,1,0:T(8,128)(2,1)S(1)} %fusion.9), channel_id=1, source_target_pairs={{0,4},{1,3},{2,6},{3,1},{4,0},{5,7},{6,2},{7,5},{8,12},{9,11},{10,... | collective-permute-start | bytes 921608 | tf_op jit(solution)/shard_map/ppermute | solution.py:611
  119.4 15.7 %collective-permute-start.32 = (bf16[1,96,768]{2,1,0:T(8,128)(2,1)S(1)}, bf16[1,96,768]{2,1,0:T(8,128)(2,1)S(1)}, u32[]{:S(2)}, u32[]{:S(2)}) collective-permute-start(bf16[1,96,768]{2,1,0:T(8,128)(2,1)S(1)} %fusion.39), channel_id=1, source_target_pairs={{0,16},{1,17},{2,18},{3,19},{4,20},{5,21},{6,22},{7,23},{8,24},{9,... | collective-permute-start | bytes 442376 | tf_op jit(solution)/shard_map/ppermute | solution.py:611
  129.7 12.2 %collective-permute-start.28 = (bf16[2,200,384]{2,1,0:T(8,128)(2,1)S(1)}, bf16[2,200,384]{2,1,0:T(8,128)(2,1)S(1)}, u32[]{:S(2)}, u32[]{:S(2)}) collective-permute-start(bf16[2,200,384]{2,1,0:T(8,128)(2,1)S(1)} %fusion.7), channel_id=1, source_target_pairs={{0,4},{1,3},{2,6},{3,1},{4,0},{5,7},{6,2},{7,5},{8,12},{9,11},{10,... | collective-permute-start | bytes 921608 | tf_op jit(solution)/shard_map/ppermute | solution.py:611
  136.9 11.9 %collective-permute-start.35 = (bf16[4,96,768]{2,1,0:T(8,128)(2,1)S(1)}, bf16[4,96,768]{2,1,0:T(8,128)(2,1)S(1)}, u32[]{:S(2)}, u32[]{:S(2)}) collective-permute-start(bf16[4,96,768]{2,1,0:T(8,128)(2,1)S(1)} %pad_maximum_fusion.2.refs_0_), channel_id=1, source_target_pairs={{0,2},{1,5},{2,0},{3,7},{4,6},{5,1},{6,4},{7,3},{8,10},{9,13},{10,... | collective-permute-start | bytes 1769480 | tf_op jit(solution)/shard_map/ppermute | solution.py:611
  142.0 11.6 %collective-permute-start.34 = (bf16[1,200,384]{2,1,0:T(8,128)(2,1)S(1)}, bf16[1,200,384]{2,1,0:T(8,128)(2,1)S(1)}, u32[]{:S(2)}, u32[]{:S(2)}) collective-permute-start(bf16[1,200,384]{2,1,0:T(8,128)(2,1)S(1)} %fusion.24), channel_id=1, source_target_pairs={{0,8},{1,9},{2,10},{3,11},{4,12},{5,13},{6,14},{7,15},{8,0},{9,1},... | collective-permute-start | bytes 460808 | tf_op jit(solution)/shard_map/ppermute | solution.py:611
  149.0 11.6 %collective-permute-start.43 = (bf16[1,200,384]{2,1,0:T(8,128)(2,1)S(1)}, bf16[1,200,384]{2,1,0:T(8,128)(2,1)S(1)}, u32[]{:S(2)}, u32[]{:S(2)}) collective-permute-start(bf16[1,200,384]{2,1,0:T(8,128)(2,1)S(1)} %fusion.21), channel_id=1, source_target_pairs={{0,16},{1,17},{2,18},{3,19},{4,20},{5,21},{6,22},{7,23},{8,24},{9,... | collective-permute-start | bytes 460808 | tf_op jit(solution)/shard_map/ppermute | solution.py:611
  154.1 14.3 %collective-permute-start.42 = (bf16[4,96,768]{2,1,0:T(8,128)(2,1)S(1)}, bf16[4,96,768]{2,1,0:T(8,128)(2,1)S(1)}, u32[]{:S(2)}, u32[]{:S(2)}) collective-permute-start(bf16[4,96,768]{2,1,0:T(8,128)(2,1)S(1)} %pad_maximum_fusion.3.refs_0_), channel_id=1, source_target_pairs={{0,2},{1,5},{2,0},{3,7},{4,6},{5,1},{6,4},{7,3},{8,10},{9,13},{10,... | collective-permute-start | bytes 1769480 | tf_op jit(solution)/shard_map/ppermute | solution.py:611
  160.6 15.7 %collective-permute-start.46 = (bf16[4,96,768]{2,1,0:T(8,128)(2,1)S(1)}, bf16[4,96,768]{2,1,0:T(8,128)(2,1)S(1)}, u32[]{:S(2)}, u32[]{:S(2)}) collective-permute-start(bf16[4,96,768]{2,1,0:T(8,128)(2,1)S(1)} %pad_maximum_fusion.4.refs_0_), channel_id=1, source_target_pairs={{0,4},{1,9},{2,6},{3,11},{4,0},{5,13},{6,2},{7,15},{8,12},{9,1},{1... | collective-permute-start | bytes 1769480 | tf_op jit(solution)/shard_map/ppermute | solution.py:611
  168.5 13.7 %collective-permute-start.48 = (bf16[4,96,768]{2,1,0:T(8,128)(2,1)S(1)}, bf16[4,96,768]{2,1,0:T(8,128)(2,1)S(1)}, u32[]{:S(2)}, u32[]{:S(2)}) collective-permute-start(bf16[4,96,768]{2,1,0:T(8,128)(2,1)S(1)} %pad_maximum_fusion.5.refs_0_), channel_id=1, source_target_pairs={{0,4},{1,3},{2,6},{3,1},{4,0},{5,7},{6,2},{7,5},{8,12},{9,11},{10,... | collective-permute-start | bytes 1769480 | tf_op jit(solution)/shard_map/ppermute | solution.py:611
  184.7 13.8 %collective-permute-start.52 = (bf16[4,200,384]{2,1,0:T(8,128)(2,1)S(1)}, bf16[4,200,384]{2,1,0:T(8,128)(2,1)S(1)}, u32[]{:S(2)}, u32[]{:S(2)}) collective-permute-start(bf16[4,200,384]{2,1,0:T(8,128)(2,1)S(1)} %pad_maximum_fusion.refs_0_), channel_id=1, source_target_pairs={{0,4},{1,9},{2,6},{3,11},{4,0},{5,13},{6,2},{7,15},{8,12},{9,1},{1... | collective-permute-start | bytes 1843208 | tf_op jit(solution)/shard_map/ppermute | solution.py:611
  189.3 13.2 %collective-permute-start.51 = (bf16[4,200,384]{2,1,0:T(8,128)(2,1)S(1)}, bf16[4,200,384]{2,1,0:T(8,128)(2,1)S(1)}, u32[]{:S(2)}, u32[]{:S(2)}) collective-permute-start(bf16[4,200,384]{2,1,0:T(8,128)(2,1)S(1)} %pad_maximum_fusion.1.refs_0_.refs_1_), channel_id=1, source_target_pairs={{0,8},{1,5},{2,10},{3,7},{4,12},{5,1},{6,14},{7,3},{8,0},{9,13},{1... | collective-permute-start | bytes 1843208 | tf_op jit(solution)/shard_map/ppermute | solution.py:611
  (48 other events, 355.7 us)

commit v5 on v4

--- a/solution.py
+++ b/solution.py
@@ -22,7 +22,7 @@
 PARTS = 2
 EARLY = (((0,), (1,)), ((0,),), ((0, 2), (1, 3)), ((0, 2), (1, 3)))
 TURNS = ((4, 2, 0), (5, 3, 1)) * 7
-JOIN_AT = 3
+JOIN_AT = 2
 
 
 def dot_nn(left, right):
@@ -134,17 +134,33 @@
     if last:
         (other_o, wo_own, wo_other, bias_out, gain, shift_vec) = rest[:6]
         qa_ref, k_ref, v_ref, o_ref, n_ref, rstd_ref, hb_ref = rest[6:13]
+        am_s, bm_s = rest[13:]
     else:
-        qa_ref, k_ref, v_ref, o_ref = rest[:4]
-    am_s, bm_s = rest[-2:]
+        qa_ref, k_ref, v_ref, o_ref, am_s, bm_s, x_s, w_s, b_s, sems = rest
     pairs, rows, _ = k_ref.shape
+    if not last:
+        copies = [pltpu.make_async_copy(x_ref.at[chunk_of(ids[0], rows), :], x_s, sems.at[0])]
+        copies.append(pltpu.make_async_copy(b_ref, b_s, sems.at[1]))
+        for p in range(pairs):
+            cols = slice(p * LANES, (p + 1) * LANES)
+            copies.append(pltpu.make_async_copy(w_ref.at[:, :, cols], w_s.at[p], sems.at[2 + p]))
+        for copy in copies:
+            copy.start()
+        b_ref = b_s
     am_s[...], bm_s[...] = mask_columns(ids, bucket, lens, rows)
     tile = rows // 2
+    if not last:
+        copies[0].wait()
+        copies[1].wait()
 
     def pair(p, carry):
         cols = chunk_of(p, LANES)
-        weights = jnp.concatenate([w_ref[n, :, cols] for n in range(3)], axis=1)
-        qkv = dot_nn(x_ref[chunk_of(ids[0], rows), :], weights)
+        if last:
+            weights = jnp.concatenate([w_ref[n, :, cols] for n in range(3)], axis=1)
+            qkv = dot_nn(x_ref[chunk_of(ids[0], rows), :], weights)
+        else:
+            pltpu.make_async_copy(w_ref.at[:, :, slice(0, LANES)], w_s.at[p], sems.at[2 + p]).wait()
+            qkv = dot_nn(x_s[...], jnp.concatenate([w_s[p, n] for n in range(3)], axis=1))
         qp = ((qkv[:, :LANES] + b_ref[0:1, cols]).astype(BF16).astype(F32) * 0.125).astype(BF16)
         kp = qkv[:, LANES : 2 * LANES].astype(BF16)
         vp = (qkv[:, 2 * LANES :] + b_ref[1:2, cols]).astype(BF16)
@@ -195,7 +211,7 @@
             hb_ref[r, :] = (normed * gain_row + shift_row).astype(BF16)
             return carry
 
-        lax.fori_loop(0, 4, norm, 0)
+        lax.fori_loop(0, 4, norm, 0, unroll=True)
 
 
 def attn_fwd(last, scal, tokens, w, b, rows, extra=()):
@@ -205,12 +221,20 @@
     outs = [shaped((2 * pairs, rows, LANES), BF16)] + [shaped((pairs, rows, LANES), BF16)] * 3
     if last:
         outs += [shaped((rows, width), F32), shaped((rows, LANES), F32), shaped((rows, width), BF16)]
+    scratch = [pltpu.VMEM((rows, LANES), BF16)] * 2
+    specs = None
+    if not last:
+        scratch += [pltpu.VMEM((rows, width), BF16), pltpu.VMEM((pairs, 3, width, LANES), BF16)]
+        scratch += [pltpu.VMEM(b.shape, F32), pltpu.SemaphoreType.DMA((2 + pairs,))]
+        specs = [anywhere()] * 3
+        tokens, w, b = (pltpu.with_memory_space_constraint(each, pltpu.HBM) for each in (tokens, w, b))
     return call(
         functools.partial(attn_fwd_body, last),
         outs,
         scal,
         (tokens, w, b, *extra),
-        [pltpu.VMEM((rows, LANES), BF16)] * 2,
+        scratch,
+        in_specs=specs,
         flops=2 * rows * local * (3 * width + 4 * rows + (2 * width if last else 0)),
         moved=2 * (rows * width + 3 * width * local + 5 * rows * local),
         trans=2 * pairs * rows * rows,
@@ -259,7 +283,7 @@
             acc[rs, :] += total
         return carry
 
-    lax.fori_loop(0, up_own.shape[1] // chunk, hidden, 0)
+    lax.fori_loop(0, up_own.shape[1] // chunk, hidden, 0, unroll=2)
     fold_s[...] = jnp.zeros_like(fold_s)
     gain_row, shift_row = row_of(gain_f), row_of(shift_f)
 
@@ -286,7 +310,7 @@
         fold_s[2] += fold_rows(df.astype(F32))
         return carry
 
-    lax.fori_loop(0, rows // LANES, norm, 0)
+    lax.fori_loop(0, rows // LANES, norm, 0, unroll=True)
     vec_ref[...] = jnp.sum(fold_s[...], axis=1)
 
 
@@ -323,7 +347,7 @@
                 out_ref[part, spot_of(ids, part, kind, i * per + c, count)] = value[first : first + size, :]
         return carry
 
-    lax.fori_loop(0, count // per, step, 0)
+    lax.fori_loop(0, count // per, step, 0, unroll=4)
 
 
 def down_grad(kind, ids, gb, df, count):
@@ -366,7 +390,7 @@
         acc[...] += dot_nt(du, up_ref[:, cols])
         return carry
 
-    lax.fori_loop(0, hidden // chunk, step, 0)
+    lax.fori_loop(0, hidden // chunk, step, 0, unroll=2)
     if kind == 0:
         fold_s[...] = jnp.zeros_like(fold_s)
         gain_row = row_of(gain_a)
@@ -387,7 +411,7 @@
             fold_s[2] += fold_rows(da.astype(F32))
             return carry
 
-        lax.fori_loop(0, rows // LANES, norm, 0)
+        lax.fori_loop(0, rows // LANES, norm, 0, unroll=True)
         vec_ref[...] = jnp.sum(fold_s[...], axis=1)
 
 
@@ -703,13 +727,14 @@
             sums.append(GroupSum(mesh, len(sums), own[part], received[part]))
 
     add_sums(down_own, down_got)
-    landed, sents = [[], []], [[], []]
+    landed, sents, final = [[], []], [[], []], [[], []]
 
     def exchange(parts, *earlier):
         which = parts[0] % 2
         earlier += tuple(landed[which]) + tuple(sents[1 - which])
         sents[which] = [sums[part].step(*earlier) for part in parts]
-        landed[which] = [sums[part].terms[-1] for part in parts]
+        landed[which] = final[which] + [sums[part].terms[-1] for part in parts if sums[part].at < sums[part].steps]
+        final[which] = [sums[part].terms[-1] for part in parts if sums[part].at == sums[part].steps]
 
     def exchange_all(stage, *earlier):
         for parts in EARLY[stage]:

time: 205 us -> 198 us (0.966)
  starting transfers between devices: 54.8 us -> 49.8 us
  waiting for transfers between devices: 37.3 us -> 42.2 us
  local copies, waits for them, and re-layouts: 5.35 us -> 1.34 us
  Pallas kernels: 97.9 us -> 95.4 us
    ppermute x42, starting transfers between devices: 52.3 us -> 47.1 us  [exchange(): return lax.ppermute(array_in, ('dp', 'tensor'), pairs)]
    ppermute x42, waiting for transfers between devices: 34.7 us -> 38.9 us  [exchange(): return lax.ppermute(array_in, ('dp', 'tensor'), pairs)]
    unnamed x54 -> x48, local copies, waits for them, and re-layouts: 4.79 us -> 0.79 us
    pallas_call x22, Pallas kernels: 97.9 us -> 95.4 us  [call(): pl.pallas_call(body, out_shape=outs, grid_spec=pltpu.PrefetchScalarGridSp...]
  transfers between devices with their start and end apart: 53 -> 53, of which waited for: 14 -> 14; matrix products, arithmetic and copies ran while one was open for 4% -> 4% of each run, Pallas kernels for 40% -> 41%
where the time goes in v5:
time: 198 us
  Pallas kernels  95.4 us (48%)
  starting transfers between devices  49.8 us (25%)
  waiting for transfers between devices  42.2 us (21%)
  other arithmetic  7.17 us (4%)
  between operations  2.34 us (1%)
    pallas_call x22, Pallas kernels, call(): pl.pallas_call(body, out_shape=outs, grid_spec=pltpu.PrefetchScalarGridSp...  95.4 us
    ppermute x42, starting transfers between devices, exchange(): return lax.ppermute(array_in, ('dp', 'tensor'), pairs)  47.1 us
    ppermute x42, waiting for transfers between devices, exchange(): return lax.ppermute(array_in, ('dp', 'tensor'), pairs)  38.9 us
    convert_element_type x30, other arithmetic, total(): return acc.astype(BF16)  6.58 us
  transfers between devices with their start and end apart: 53, of which 14 were waited for; matrix products, arithmetic and copies ran while one was open for 4% of the time, Pallas kernels for 41%

profile of v5, /device:TPU:0, one launch (start us, length us, event | category | flops | bytes accessed | tf_op | source)
XLA Modules:
  0.0 198.2 jit_solution(1270544453789696672)
XLA Ops:
  3.5 8.2 %shard_map.272 = (bf16[6,512,128]{2,1,0:T(8,128)(2,1)S(1)}, bf16[3,512,128]{2,1,0:T(8,128)(2,1)S(1)}, bf16[3,512,128]{2,1,0:T(8,128)(2,1)S(1)}, bf16[3,512,128]{2,1,0:T(8,128)(2,1)S(1)}) custom-call(s32[2]{0:T(128)S(1)} %compare_select_fusion.ids, s32[1]{0:T(128)S(6)} %copy.51.bucket, s32[1,8]{1,0:T(1,128)S(1)} %copy-done.18, bf16[1024,768]{1,0:T(8,128)(2,1)} %x_ref.9, ...), custom_call_target="tpu_custom_call" | custom-call | flops 34225520640 | bytes 4521984 | tf_op jit(solution)/shard_map/pallas_call | solution.py:54
  12.0 9.6 %shard_map.273 = (bf16[6,512,128]{2,1,0:T(8,128)(2,1)S(1)}, bf16[3,512,128]{2,1,0:T(8,128)(2,1)S(1)}, bf16[3,512,128]{2,1,0:T(8,128)(2,1)S(1)}, bf16[3,512,128]{...) custom-call(s32[2]{0:T(128)S(1)} %compare_select_fusion.ids, ...), custom_call_target="tpu_custom_call" | custom-call | flops 46305116160 | bytes 4521984 | tf_op jit(solution)/shard_map/pallas_call | solution.py:54
  21.8 10.8 %shard_map.274 = (bf16[512,1536]{1,0:T(8,128)(2,1)S(1)}, bf16[512,1536]{1,0:T(8,128)(2,1)S(1)}, f32[512,1536]{1,0:T(8,128)S(1)}, f32[512,1536]{1,0:T(8,128)S(1)}...) custom-call(s32[2]{0:T(128)S(1)} %compare_select_fusion.ids, ...), custom_call_target="tpu_custom_call" | custom-call | flops 96636764160 | bytes 26738688 | tf_op jit(solution)/shard_map/pallas_call | solution.py:54
  32.6 2.0 %shard_map.275 = bf16[2,8,96,768]{3,2,1,0:T(8,128)(2,1)S(1)} custom-call(s32[2]{0:T(128)S(1)} %compare_select_fusion.ids, bf16[512,1536]{1,0:T(8,128)(2,1)S(1)} %get-tuple-element.120.gb_ref, bf16[512,768]{1,0:T(8,128)(2,1)S(1)} %get-tuple-element.129.df_ref), custom_call_target="tpu_custom_call" | custom-call | flops 24159191040 | bytes 4718592 | tf_op jit(solution)/shard_map/pallas_call | solution.py:54
  35.2 2.0 %shard_map.276 = bf16[2,8,96,768]{3,2,1,0:T(8,128)(2,1)S(1)} custom-call(s32[2]{0:T(128)S(1)} %compare_select_fusion.ids, bf16[512,1536]{1,0:T(8,128)(2,1)S(1)} %get-tuple-element.119.gb_ref, bf16[512,768]{1,0:T(8,128)(2,1)S(1)} %get-tuple-element.129.df_ref), custom_call_target="tpu_custom_call" | custom-call | flops 24159191040 | bytes 4718592 | tf_op jit(solution)/shard_map/pallas_call | solution.py:54
  37.1 3.2 %collective-permute-done.6 = bf16[2,8,96,768]{3,2,1,0:T(8,128)(2,1)S(1)} collective-permute-done((bf16[2,8,96,768]{3,2,1,0:T(8,128)(2,1)S(1)}, bf16[2,8,96,768]{3,2,1,0:T(8,128)(2,1)S(1)}, u32[]{:S(2)}, u32[]{:S(2)}) %collective-permute-start.6) | collective-permute-done | bytes 2359328 | tf_op jit(solution)/shard_map/ppermute | solution.py:620
  40.7 3.0 %collective-permute-start.7 = (bf16[4,96,768]{2,1,0:T(8,128)(2,1)S(1)}, bf16[4,96,768]{2,1,0:T(8,128)(2,1)S(1)}, u32[]{:S(2)}, u32[]{:S(2)}) collective-permute-start(bf16[4,96,768]{2,1,0:T(8,128)(2,1)S(1)} %fusion.5), channel_id=1, source_target_pairs={{0,4},{1,3},{2,6},{3,1},{4,0},{5,7},{6,2},{7,5},{8,12},{9,11},{10,... | collective-permute-start | bytes 1769480 | tf_op jit(solution)/shard_map/ppermute | solution.py:635
  44.6 6.6 %shard_map.277 = (bf16[2,8,96,768]{3,2,1,0:T(8,128)(2,1)S(1)}, f32[1,1536]{1,0:T(1,128)S(1)}, f32[512,768]{1,0:T(8,128)S(1)}) custom-call(s32[2]{0:T(128)S(1)} %compare_select_fusion.ids, bf16[512,768]{1,0:T(8,128)(2,1)S(1)} %get-tuple-element.129.df_ref, bf16[512,768]{1,0:T(8,128)(2,1)S(1)} %get-tuple-element.112.hb_ref, ...), custom_call_target="tpu_custom_call" | custom-call | flops 72477573120 | bytes 14155776 | tf_op jit(solution)/shard_map/pallas_call | solution.py:54
  51.6 2.1 %collective-permute-start.8 = (bf16[2,96,768]{2,1,0:T(8,128)(2,1)S(1)}, bf16[2,96,768]{2,1,0:T(8,128)(2,1)S(1)}, u32[]{:S(2)}, u32[]{:S(2)}) collective-permute-start(bf16[2,96,768]{2,1,0:T(8,128)(2,1)S(1)} %fusion.17), channel_id=1, source_target_pairs={{0,2},{1,5},{2,0},{3,7},{4,6},{5,1},{6,4},{7,3},{8,10},{9,13},{10,... | collective-permute-start | bytes 884744 | tf_op jit(solution)/shard_map/ppermute | solution.py:635
  53.7 7.5 %shard_map.278 = (bf16[2,8,96,768]{3,2,1,0:T(8,128)(2,1)S(1)}, f32[1,1536]{1,0:T(1,128)S(1)}, f32[512,768]{1,0:T(8,128)S(1)}, bf16[512,768]{1,0:T(8,128)(2,1)S(1)}, f32[3,768]{1,0:T(4,128)S(1)}) custom-call(s32[2]{0:T(128)S(1)} %compare_select_fusion.ids, bf16[512,768]{1,0:T(8,128)(2,1)S(1)} %get-tuple-element.129.df_ref, ...), custom_call_target="tpu_custom_call" | custom-call | flops 72477573120 | bytes 14155776 | tf_op jit(solution)/shard_map/pallas_call | solution.py:54
  61.2 1.6 collective-permute-start.9
  67.1 13.1 %shard_map.279 = (bf16[2,8,200,384]{3,2,1,0:T(8,128)(2,1)S(1)}, f32[512,768]{1,0:T(8,128)S(1)}) custom-call(s32[2]{0:T(128)S(1)} %compare_select_fusion.ids, s32[1]{0:T(128)S(6)} %copy.51.bucket, s32[1,8]{1,0:T(1,128)S(1)} %copy-done.19, s32[1,8]{1,0:T(1,128)S(1)} %copy-done.17, bf16[6,512,128]{2,1,0:T(8,128)(2,1)S(1)} %get-tuple-element.134.qa_ref, ...), custom_call_target="tpu_custom_call" | custom-call | flops 88583700480 | bytes 10420224 | tf_op jit(solution)/shard_map/pallas_call | solution.py:54
  80.7 2.6 %collective-permute-start.17 = (bf16[1,96,768]{2,1,0:T(8,128)(2,1)S(1)}, bf16[1,96,768]{2,1,0:T(8,128)(2,1)S(1)}, u32[]{:S(2)}, u32[]{:S(2)}) collective-permute-start(bf16[1,96,768]{2,1,0:T(8,128)(2,1)S(1)} %fusion.59), channel_id=1, source_target_pairs={{0,16},{1,17},{2,18},{3,19},{4,20},{5,21},{6,22},{7,23},{8,24},{9,... | collective-permute-start | bytes 442376 | tf_op jit(solution)/shard_map/ppermute | solution.py:635
  88.3 11.7 %shard_map.280 = (bf16[2,8,200,384]{3,2,1,0:T(8,128)(2,1)S(1)}, f32[512,768]{1,0:T(8,128)S(1)}) custom-call(s32[2]{0:T(128)S(1)} %compare_select_fusion.ids, s32[1]{0:T(128)S(6)} %copy.51.bucket, s32[1,8]{1,0:T(1,128)S(1)} %copy-done.19, s32[1,8]{1,0:T(1,128)S(1)} %copy-done.17, bf16[6,512,128]{2,1,0:T(8,128)(2,1)S(1)} %get-tuple-element.115.qa_ref, ...), custom_call_target="tpu_custom_call" | custom-call | flops 88583700480 | bytes 10420224 | tf_op jit(solution)/shard_map/pallas_call | solution.py:54
  100.1 1.6 collective-permute-start.26
  105.2 1.6 collective-permute-start.23
  106.8 4.1 %shard_map.281 = (bf16[1024,768]{1,0:T(8,128)(2,1)}, f32[1024,768]{1,0:T(8,128)}) custom-call(s32[2]{0:T(128)S(1)} %compare_select_fusion.ids, bf16[512,768]{1,0:T(8,128)(2,1)} %get-tuple-element.114.refs_0_, f32[512,768]{1,0:T(8,128)S(1)} %get-tuple-element.161.refs_1_, bf16[512,768]{1,0:T(8,128)(2,1)} %collective-permute-done.12.refs_2_, ...), custom_call_target="tpu_custom_call" | custom-call | bytes 9437184 | tf_op jit(solution)/shard_map/pallas_call | solution.py:54
  114.1 2.0 %collective-permute-start.32 = (bf16[1,96,768]{2,1,0:T(8,128)(2,1)S(1)}, bf16[1,96,768]{2,1,0:T(8,128)(2,1)S(1)}, u32[]{:S(2)}, u32[]{:S(2)}) collective-permute-start(bf16[1,96,768]{2,1,0:T(8,128)(2,1)S(1)} %fusion.39), channel_id=1, source_target_pairs={{0,16},{1,17},{2,18},{3,19},{4,20},{5,21},{6,22},{7,23},{8,24},{9,... | collective-permute-start | bytes 442376 | tf_op jit(solution)/shard_map/ppermute | solution.py:635
  117.4 6.9 %collective-permute-done.24 = bf16[1,96,768]{2,1,0:T(8,128)(2,1)S(1)} collective-permute-done((bf16[1,96,768]{2,1,0:T(8,128)(2,1)S(1)}, bf16[1,96,768]{2,1,0:T(8,128)(2,1)S(1)}, u32[]{:S(2)}, u32[]{:S(2)}) %collective-permute-start.24) | collective-permute-done | bytes 147488 | tf_op jit(solution)/shard_map/ppermute | solution.py:635
  125.5 3.5 %collective-permute-done.32 = bf16[1,96,768]{2,1,0:T(8,128)(2,1)S(1)} collective-permute-done((bf16[1,96,768]{2,1,0:T(8,128)(2,1)S(1)}, bf16[1,96,768]{2,1,0:T(8,128)(2,1)S(1)}, u32[]{:S(2)}, u32[]{:S(2)}) %collective-permute-start.32) | collective-permute-done | bytes 147488 | tf_op jit(solution)/shard_map/ppermute | solution.py:635
  131.1 2.1 %collective-permute-start.36 = (bf16[1,200,384]{2,1,0:T(8,128)(2,1)S(1)}, bf16[1,200,384]{2,1,0:T(8,128)(2,1)S(1)}, u32[]{:S(2)}, u32[]{:S(2)}) collective-permute-start(bf16[1,200,384]{2,1,0:T(8,128)(2,1)S(1)} %fusion.27), channel_id=1, source_target_pairs={{0,8},{1,9},{2,10},{3,11},{4,12},{5,13},{6,14},{7,15},{8,0},{9,1},... | collective-permute-start | bytes 460808 | tf_op jit(solution)/shard_map/ppermute | solution.py:635
  137.4 5.0 %collective-permute-done.37 = bf16[1,96,768]{2,1,0:T(8,128)(2,1)S(1)} collective-permute-done((bf16[1,96,768]{2,1,0:T(8,128)(2,1)S(1)}, bf16[1,96,768]{2,1,0:T(8,128)(2,1)S(1)}, u32[]{:S(2)}, u32[]{:S(2)}) %collective-permute-start.37) | collective-permute-done | bytes 147488 | tf_op jit(solution)/shard_map/ppermute | solution.py:635
  147.3 2.4 %collective-permute-done.39 = bf16[2,96,768]{2,1,0:T(8,128)(2,1)S(1)} collective-permute-done((bf16[2,96,768]{2,1,0:T(8,128)(2,1)S(1)}, bf16[2,96,768]{2,1,0:T(8,128)(2,1)S(1)}, u32[]{:S(2)}, u32[]{:S(2)}) %collective-permute-start.39) | collective-permute-done | bytes 294944 | tf_op jit(solution)/shard_map/ppermute | solution.py:635
  150.9 2.0 collective-permute-start.47
  153.4 2.3 %collective-permute-start.45 = (bf16[4,96,768]{2,1,0:T(8,128)(2,1)S(1)}, bf16[4,96,768]{2,1,0:T(8,128)(2,1)S(1)}, u32[]{:S(2)}, u32[]{:S(2)}) collective-permute-start(bf16[4,96,768]{2,1,0:T(8,128)(2,1)S(1)} %pad_maximum_fusion.4.refs_0_), channel_id=1, source_target_pairs={{0,4},{1,9},{2,6},{3,11},{4,0},{5,13},{6,2},{7,15},{8,12},{9,1},{1... | collective-permute-start | bytes 1769480 | tf_op jit(solution)/shard_map/ppermute | solution.py:635
  155.8 2.0 collective-permute-done.40
  157.8 4.8 %collective-permute-done.41 = bf16[2,96,768]{2,1,0:T(8,128)(2,1)S(1)} collective-permute-done((bf16[2,96,768]{2,1,0:T(8,128)(2,1)S(1)}, bf16[2,96,768]{2,1,0:T(8,128)(2,1)S(1)}, u32[]{:S(2)}, u32[]{:S(2)}) %collective-permute-start.41) | collective-permute-done | bytes 294944 | tf_op jit(solution)/shard_map/ppermute | solution.py:635
  166.3 1.6 shard_map.288
  172.4 1.6 shard_map.286.refs_1_
  183.9 1.6 shard_map.291
  185.5 8.7 %collective-permute-done.52.refs_0_ = bf16[4,200,384]{2,1,0:T(8,128)(2,1)S(1)} collective-permute-done((bf16[4,200,384]{2,1,0:T(8,128)(2,1)S(1)}, bf16[4,200,384]{2,1,0:T(8,128)(2,1)S(1)}, u32[]{:S(2)}, u32[]{:S(2)}) %collective-permute-start.52) | collective-permute-done | bytes 614432 | tf_op jit(solution)/shard_map/ppermute | solution.py:635
  195.8 2.2 %shard_map.293 = (f32[3,768,384]{2,1,0:T(8,128)}, f32[384,768]{1,0:T(8,128)}, f32[2,384]{1,0:T(2,128)}, f32[1536]{0:T(1024)}, f32[768]{0:T(1024)}, /*index=5*/f3...) custom-call(s32[2]{0:T(128)S(1)} %compare_select_fusion.ids, ...), custom_call_target="tpu_custom_call", output_to_operand_aliasing={{0}: (3, {}), {1}: (4, {})} | custom-call | bytes 1843200 | tf_op jit(solution)/shard_map/pallas_call | solution.py:54
  (190 shorter events, 55.8 us)
Async XLA Ops:
  0.6 11.3 %collective-permute-start = (bf16[3,768,384]{2,1,0:T(8,128)(2,1)}, bf16[3,768,384]{2,1,0:T(8,128)(2,1)}, u32[]{:S(2)}, u32[]{:S(2)}) collective-permute-start(bf16[3,768,384]{2,1,0:T(8,128)(2,1)} %w_ref.3), channel_id=1, source_target_pairs={{0,1},{1,0},{2,3},{3,2},{4,5},{5,4},{6,7},{7,6},{8,9},{9,8},{10,11... | collective-permute-start | bytes 5308424 | tf_op jit(solution)/shard_map/ppermute | solution.py:620
  1.7 20.0 %collective-permute-start.3 = (bf16[768,1536]{1,0:T(8,128)(2,1)}, bf16[768,1536]{1,0:T(8,128)(2,1)S(1)}, u32[]{:S(2)}, u32[]{:S(2)}) collective-permute-start(bf16[768,1536]{1,0:T(8,128)(2,1)} %up_ref.1), channel_id=1, source_target_pairs={{0,1},{1,0},{2,3},{3,2},{4,5},{5,4},{6,7},{7,6},{8,9},{9,8},{10,11... | collective-permute-start | bytes 7077896 | tf_op jit(solution)/shard_map/ppermute | solution.py:620
  1.8 19.9 %collective-permute-start.4 = (f32[1536]{0:T(1024)}, f32[1536]{0:T(1024)S(1)}, u32[]{:S(2)}, u32[]{:S(2)}) collective-permute-start(f32[1536]{0:T(1024)} %bu_own.1), channel_id=1, source_target_pairs={{0,1},{1,0},{2,3},{3,2},{4,5},{5,4},{6,7},{7,6},{8,9},{9,8},{10,11... | collective-permute-start | bytes 18440 | tf_op jit(solution)/shard_map/ppermute | solution.py:620
  35.1 45.2 %collective-permute-start.12 = (bf16[512,768]{1,0:T(8,128)(2,1)}, bf16[512,768]{1,0:T(8,128)(2,1)}, u32[]{:S(2)}, u32[]{:S(2)}) collective-permute-start(bf16[512,768]{1,0:T(8,128)(2,1)} %get-tuple-element.114.refs_0_), channel_id=1, source_target_pairs={{0,1},{1,0},{2,3},{3,2},{4,5},{5,4},{6,7},{7,6},{8,9},{9,8},{10,11... | collective-permute-start | bytes 2359304 | tf_op jit(solution)/shard_map/ppermute | solution.py:620
  44.6 19.7 %collective-permute-start.11 = (bf16[4,96,768]{2,1,0:T(8,128)(2,1)}, bf16[4,96,768]{2,1,0:T(8,128)(2,1)}, u32[]{:S(2)}, u32[]{:S(2)}) collective-permute-start(bf16[4,96,768]{2,1,0:T(8,128)(2,1)} %fusion.4), channel_id=1, source_target_pairs={{0,4},{1,3},{2,6},{3,1},{4,0},{5,7},{6,2},{7,5},{8,12},{9,11},{10,... | collective-permute-start | bytes 1769480 | tf_op jit(solution)/shard_map/ppermute | solution.py:635
  51.3 11.6 %collective-permute-start.10 = (bf16[2,8,96,768]{3,2,1,0:T(8,128)(2,1)S(1)}, bf16[2,8,96,768]{3,2,1,0:T(8,128)(2,1)S(1)}, u32[]{:S(2)}, u32[]{:S(2)}) collective-permute-start(bf16[2,8,96,768]{3,2,1,0:T(8,128)(2,1)S(1)} %get-tuple-element.139), channel_id=1, source_target_pairs={{0,1},{1,0},{2,3},{3,2},{4,5},{5,4},{6,7},{7,6},{8,9},{9,8},{10,11... | collective-permute-start | bytes 7077896 | tf_op jit(solution)/shard_map/ppermute | solution.py:620
  61.2 19.3 %collective-permute-start.9 = (bf16[1,96,768]{2,1,0:T(8,128)(2,1)S(1)}, bf16[1,96,768]{2,1,0:T(8,128)(2,1)S(1)}, u32[]{:S(2)}, u32[]{:S(2)}) collective-permute-start(bf16[1,96,768]{2,1,0:T(8,128)(2,1)S(1)} %fusion.55), channel_id=1, source_target_pairs={{0,8},{1,9},{2,10},{3,11},{4,12},{5,13},{6,14},{7,15},{8,0},{9,1},... | collective-permute-start | bytes 442376 | tf_op jit(solution)/shard_map/ppermute | solution.py:635
  63.2 17.3 %collective-permute-start.13 = (bf16[4,96,768]{2,1,0:T(8,128)(2,1)S(1)}, bf16[4,96,768]{2,1,0:T(8,128)(2,1)S(1)}, u32[]{:S(2)}, u32[]{:S(2)}) collective-permute-start(bf16[4,96,768]{2,1,0:T(8,128)(2,1)S(1)} %fusion.3), channel_id=1, source_target_pairs={{0,2},{1,5},{2,0},{3,7},{4,6},{5,1},{6,4},{7,3},{8,10},{9,13},{10,... | collective-permute-start | bytes 1769480 | tf_op jit(solution)/shard_map/ppermute | solution.py:635
  65.6 19.3 %collective-permute-start.14 = (bf16[2,96,768]{2,1,0:T(8,128)(2,1)S(1)}, bf16[2,96,768]{2,1,0:T(8,128)(2,1)S(1)}, u32[]{:S(2)}, u32[]{:S(2)}) collective-permute-start(bf16[2,96,768]{2,1,0:T(8,128)(2,1)S(1)} %fusion.15), channel_id=1, source_target_pairs={{0,8},{1,9},{2,10},{3,11},{4,12},{5,13},{6,14},{7,15},{8,0},{9,1},... | collective-permute-start | bytes 884744 | tf_op jit(solution)/shard_map/ppermute | solution.py:635
  66.1 18.8 %collective-permute-start.15 = (bf16[4,96,768]{2,1,0:T(8,128)(2,1)S(1)}, bf16[4,96,768]{2,1,0:T(8,128)(2,1)S(1)}, u32[]{:S(2)}, u32[]{:S(2)}) collective-permute-start(bf16[4,96,768]{2,1,0:T(8,128)(2,1)S(1)} %fusion.2), channel_id=1, source_target_pairs={{0,2},{1,5},{2,0},{3,7},{4,6},{5,1},{6,4},{7,3},{8,10},{9,13},{10,... | collective-permute-start | bytes 1769480 | tf_op jit(solution)/shard_map/ppermute | solution.py:635
  80.3 21.5 %collective-permute-start.16 = (bf16[2,8,200,384]{3,2,1,0:T(8,128)(2,1)S(1)}, bf16[2,8,200,384]{3,2,1,0:T(8,128)(2,1)S(1)}, u32[]{:S(2)}, u32[]{:S(2)}) collective-permute-start(bf16[2,8,200,384]{3,2,1,0:T(8,128)(2,1)S(1)} %get-tuple-element.157), channel_id=1, source_target_pairs={{0,1},{1,0},{2,3},{3,2},{4,5},{5,4},{6,7},{7,6},{8,9},{9,8},{10,11... | collective-permute-start | bytes 7372808 | tf_op jit(solution)/shard_map/ppermute | solution.py:620
  80.7 19.2 %collective-permute-start.17 = (bf16[1,96,768]{2,1,0:T(8,128)(2,1)S(1)}, bf16[1,96,768]{2,1,0:T(8,128)(2,1)S(1)}, u32[]{:S(2)}, u32[]{:S(2)}) collective-permute-start(bf16[1,96,768]{2,1,0:T(8,128)(2,1)S(1)} %fusion.59), channel_id=1, source_target_pairs={{0,16},{1,17},{2,18},{3,19},{4,20},{5,21},{6,22},{7,23},{8,24},{9,... | collective-permute-start | bytes 442376 | tf_op jit(solution)/shard_map/ppermute | solution.py:635
  83.5 16.5 %collective-permute-start.18 = (bf16[2,96,768]{2,1,0:T(8,128)(2,1)S(1)}, bf16[2,96,768]{2,1,0:T(8,128)(2,1)S(1)}, u32[]{:S(2)}, u32[]{:S(2)}) collective-permute-start(bf16[2,96,768]{2,1,0:T(8,128)(2,1)S(1)} %fusion.13), channel_id=1, source_target_pairs={{0,4},{1,3},{2,6},{3,1},{4,0},{5,7},{6,2},{7,5},{8,12},{9,11},{10,... | collective-permute-start | bytes 884744 | tf_op jit(solution)/shard_map/ppermute | solution.py:635
  86.0 16.8 %collective-permute-start.20 = (bf16[1,96,768]{2,1,0:T(8,128)(2,1)S(1)}, bf16[1,96,768]{2,1,0:T(8,128)(2,1)S(1)}, u32[]{:S(2)}, u32[]{:S(2)}) collective-permute-start(bf16[1,96,768]{2,1,0:T(8,128)(2,1)S(1)} %fusion.52), channel_id=1, source_target_pairs={{0,2},{1,5},{2,0},{3,7},{4,6},{5,1},{6,4},{7,3},{8,10},{9,13},{10,... | collective-permute-start | bytes 442376 | tf_op jit(solution)/shard_map/ppermute | solution.py:635
  87.1 16.3 %collective-permute-start.21 = (bf16[2,96,768]{2,1,0:T(8,128)(2,1)S(1)}, bf16[2,96,768]{2,1,0:T(8,128)(2,1)S(1)}, u32[]{:S(2)}, u32[]{:S(2)}) collective-permute-start(bf16[2,96,768]{2,1,0:T(8,128)(2,1)S(1)} %fusion.11), channel_id=1, source_target_pairs={{0,4},{1,3},{2,6},{3,1},{4,0},{5,7},{6,2},{7,5},{8,12},{9,11},{10,... | collective-permute-start | bytes 884744 | tf_op jit(solution)/shard_map/ppermute | solution.py:635
  100.1 11.8 %collective-permute-start.26 = (bf16[1,96,768]{2,1,0:T(8,128)(2,1)S(1)}, bf16[1,96,768]{2,1,0:T(8,128)(2,1)S(1)}, u32[]{:S(2)}, u32[]{:S(2)}) collective-permute-start(bf16[1,96,768]{2,1,0:T(8,128)(2,1)S(1)} %fusion.49), channel_id=1, source_target_pairs={{0,8},{1,9},{2,10},{3,11},{4,12},{5,13},{6,14},{7,15},{8,0},{9,1},... | collective-permute-start | bytes 442376 | tf_op jit(solution)/shard_map/ppermute | solution.py:635
  103.5 20.8 %collective-permute-start.22 = (bf16[4,200,384]{2,1,0:T(8,128)(2,1)S(1)}, bf16[4,200,384]{2,1,0:T(8,128)(2,1)S(1)}, u32[]{:S(2)}, u32[]{:S(2)}) collective-permute-start(bf16[4,200,384]{2,1,0:T(8,128)(2,1)S(1)} %fusion), channel_id=1, source_target_pairs={{0,2},{1,5},{2,0},{3,7},{4,6},{5,1},{6,4},{7,3},{8,10},{9,13},{10,... | collective-permute-start | bytes 1843208 | tf_op jit(solution)/shard_map/ppermute | solution.py:635
  112.0 12.3 %collective-permute-start.24 = (bf16[1,96,768]{2,1,0:T(8,128)(2,1)S(1)}, bf16[1,96,768]{2,1,0:T(8,128)(2,1)S(1)}, u32[]{:S(2)}, u32[]{:S(2)}) collective-permute-start(bf16[1,96,768]{2,1,0:T(8,128)(2,1)S(1)} %fusion.43), channel_id=1, source_target_pairs={{0,16},{1,17},{2,18},{3,19},{4,20},{5,21},{6,22},{7,23},{8,24},{9,... | collective-permute-start | bytes 442376 | tf_op jit(solution)/shard_map/ppermute | solution.py:635
  113.2 15.8 %collective-permute-start.31 = (bf16[2,200,384]{2,1,0:T(8,128)(2,1)S(1)}, bf16[2,200,384]{2,1,0:T(8,128)(2,1)S(1)}, u32[]{:S(2)}, u32[]{:S(2)}) collective-permute-start(bf16[2,200,384]{2,1,0:T(8,128)(2,1)S(1)} %fusion.9), channel_id=1, source_target_pairs={{0,4},{1,3},{2,6},{3,1},{4,0},{5,7},{6,2},{7,5},{8,12},{9,11},{10,... | collective-permute-start | bytes 921608 | tf_op jit(solution)/shard_map/ppermute | solution.py:635
  114.1 14.9 %collective-permute-start.32 = (bf16[1,96,768]{2,1,0:T(8,128)(2,1)S(1)}, bf16[1,96,768]{2,1,0:T(8,128)(2,1)S(1)}, u32[]{:S(2)}, u32[]{:S(2)}) collective-permute-start(bf16[1,96,768]{2,1,0:T(8,128)(2,1)S(1)} %fusion.39), channel_id=1, source_target_pairs={{0,16},{1,17},{2,18},{3,19},{4,20},{5,21},{6,22},{7,23},{8,24},{9,... | collective-permute-start | bytes 442376 | tf_op jit(solution)/shard_map/ppermute | solution.py:635
  116.1 12.9 %collective-permute-start.33 = (bf16[2,96,768]{2,1,0:T(8,128)(2,1)S(1)}, bf16[2,96,768]{2,1,0:T(8,128)(2,1)S(1)}, u32[]{:S(2)}, u32[]{:S(2)}) collective-permute-start(bf16[2,96,768]{2,1,0:T(8,128)(2,1)S(1)} %pad_maximum_fusion.8), channel_id=1, source_target_pairs={{0,4},{1,3},{2,6},{3,1},{4,0},{5,7},{6,2},{7,5},{8,12},{9,11},{10,... | collective-permute-start | bytes 884744 | tf_op jit(solution)/shard_map/ppermute | solution.py:635
  124.4 11.6 %collective-permute-start.28 = (bf16[2,200,384]{2,1,0:T(8,128)(2,1)S(1)}, bf16[2,200,384]{2,1,0:T(8,128)(2,1)S(1)}, u32[]{:S(2)}, u32[]{:S(2)}) collective-permute-start(bf16[2,200,384]{2,1,0:T(8,128)(2,1)S(1)} %fusion.7), channel_id=1, source_target_pairs={{0,4},{1,3},{2,6},{3,1},{4,0},{5,7},{6,2},{7,5},{8,12},{9,11},{10,... | collective-permute-start | bytes 921608 | tf_op jit(solution)/shard_map/ppermute | solution.py:635
  129.2 15.4 %collective-permute-start.35 = (bf16[4,96,768]{2,1,0:T(8,128)(2,1)S(1)}, bf16[4,96,768]{2,1,0:T(8,128)(2,1)S(1)}, u32[]{:S(2)}, u32[]{:S(2)}) collective-permute-start(bf16[4,96,768]{2,1,0:T(8,128)(2,1)S(1)} %pad_maximum_fusion.2.refs_0_), channel_id=1, source_target_pairs={{0,2},{1,5},{2,0},{3,7},{4,6},{5,1},{6,4},{7,3},{8,10},{9,13},{10,... | collective-permute-start | bytes 1769480 | tf_op jit(solution)/shard_map/ppermute | solution.py:635
  131.1 12.1 %collective-permute-start.36 = (bf16[1,200,384]{2,1,0:T(8,128)(2,1)S(1)}, bf16[1,200,384]{2,1,0:T(8,128)(2,1)S(1)}, u32[]{:S(2)}, u32[]{:S(2)}) collective-permute-start(bf16[1,200,384]{2,1,0:T(8,128)(2,1)S(1)} %fusion.27), channel_id=1, source_target_pairs={{0,8},{1,9},{2,10},{3,11},{4,12},{5,13},{6,14},{7,15},{8,0},{9,1},... | collective-permute-start | bytes 460808 | tf_op jit(solution)/shard_map/ppermute | solution.py:635
  136.1 11.2 %collective-permute-start.34 = (bf16[1,200,384]{2,1,0:T(8,128)(2,1)S(1)}, bf16[1,200,384]{2,1,0:T(8,128)(2,1)S(1)}, u32[]{:S(2)}, u32[]{:S(2)}) collective-permute-start(bf16[1,200,384]{2,1,0:T(8,128)(2,1)S(1)} %fusion.24), channel_id=1, source_target_pairs={{0,8},{1,9},{2,10},{3,11},{4,12},{5,13},{6,14},{7,15},{8,0},{9,1},... | collective-permute-start | bytes 460808 | tf_op jit(solution)/shard_map/ppermute | solution.py:635
  150.4 12.2 %collective-permute-start.41 = (bf16[2,96,768]{2,1,0:T(8,128)(2,1)S(1)}, bf16[2,96,768]{2,1,0:T(8,128)(2,1)S(1)}, u32[]{:S(2)}, u32[]{:S(2)}) collective-permute-start(bf16[2,96,768]{2,1,0:T(8,128)(2,1)S(1)} %pad_maximum_fusion.11), channel_id=1, source_target_pairs={{0,8},{1,5},{2,10},{3,7},{4,12},{5,1},{6,14},{7,3},{8,0},{9,13},{1... | collective-permute-start | bytes 884744 | tf_op jit(solution)/shard_map/ppermute | solution.py:635
  150.9 15.3 %collective-permute-start.47 = (bf16[4,96,768]{2,1,0:T(8,128)(2,1)S(1)}, bf16[4,96,768]{2,1,0:T(8,128)(2,1)S(1)}, u32[]{:S(2)}, u32[]{:S(2)}) collective-permute-start(bf16[4,96,768]{2,1,0:T(8,128)(2,1)S(1)} %pad_maximum_fusion.3.refs_0_), channel_id=1, source_target_pairs={{0,2},{1,5},{2,0},{3,7},{4,6},{5,1},{6,4},{7,3},{8,10},{9,13},{10,... | collective-permute-start | bytes 1769480 | tf_op jit(solution)/shard_map/ppermute | solution.py:635
  153.4 19.1 %collective-permute-start.45 = (bf16[4,96,768]{2,1,0:T(8,128)(2,1)S(1)}, bf16[4,96,768]{2,1,0:T(8,128)(2,1)S(1)}, u32[]{:S(2)}, u32[]{:S(2)}) collective-permute-start(bf16[4,96,768]{2,1,0:T(8,128)(2,1)S(1)} %pad_maximum_fusion.4.refs_0_), channel_id=1, source_target_pairs={{0,4},{1,9},{2,6},{3,11},{4,0},{5,13},{6,2},{7,15},{8,12},{9,1},{1... | collective-permute-start | bytes 1769480 | tf_op jit(solution)/shard_map/ppermute | solution.py:635
  155.8 12.1 %collective-permute-start.46 = (bf16[1,200,384]{2,1,0:T(8,128)(2,1)S(1)}, bf16[1,200,384]{2,1,0:T(8,128)(2,1)S(1)}, u32[]{:S(2)}, u32[]{:S(2)}) collective-permute-start(bf16[1,200,384]{2,1,0:T(8,128)(2,1)S(1)} %add_convert_fusion.1), channel_id=1, source_target_pairs={{0,8},{1,3},{2,10},{3,1},{4,12},{5,7},{6,14},{7,5},{8,0},{9,11},{1... | collective-permute-start | bytes 460808 | tf_op jit(solution)/shard_map/ppermute | solution.py:635
  162.7 12.5 %collective-permute-start.49 = (bf16[4,96,768]{2,1,0:T(8,128)(2,1)S(1)}, bf16[4,96,768]{2,1,0:T(8,128)(2,1)S(1)}, u32[]{:S(2)}, u32[]{:S(2)}) collective-permute-start(bf16[4,96,768]{2,1,0:T(8,128)(2,1)S(1)} %pad_maximum_fusion.5.refs_0_), channel_id=1, source_target_pairs={{0,4},{1,3},{2,6},{3,1},{4,0},{5,7},{6,2},{7,5},{8,12},{9,11},{10,... | collective-permute-start | bytes 1769480 | tf_op jit(solution)/shard_map/ppermute | solution.py:635
  178.2 16.0 %collective-permute-start.52 = (bf16[4,200,384]{2,1,0:T(8,128)(2,1)S(1)}, bf16[4,200,384]{2,1,0:T(8,128)(2,1)S(1)}, u32[]{:S(2)}, u32[]{:S(2)}) collective-permute-start(bf16[4,200,384]{2,1,0:T(8,128)(2,1)S(1)} %pad_maximum_fusion.refs_0_), channel_id=1, source_target_pairs={{0,4},{1,9},{2,6},{3,11},{4,0},{5,13},{6,2},{7,15},{8,12},{9,1},{1... | collective-permute-start | bytes 1843208 | tf_op jit(solution)/shard_map/ppermute | solution.py:635
  181.1 14.7 %collective-permute-start.51 = (bf16[4,200,384]{2,1,0:T(8,128)(2,1)S(1)}, bf16[4,200,384]{2,1,0:T(8,128)(2,1)S(1)}, u32[]{:S(2)}, u32[]{:S(2)}) collective-permute-start(bf16[4,200,384]{2,1,0:T(8,128)(2,1)S(1)} %pad_maximum_fusion.1.refs_0_.refs_1_), channel_id=1, source_target_pairs={{0,8},{1,5},{2,10},{3,7},{4,12},{5,1},{6,14},{7,3},{8,0},{9,13},{1... | collective-permute-start | bytes 1843208 | tf_op jit(solution)/shard_map/ppermute | solution.py:635
  (45 other events, 363.8 us)

commit v6 on v5

--- a/solution.py
+++ b/solution.py
@@ -18,7 +18,7 @@
 VMEM_MIB = 16
 COVER = 20
 
-STEP_BITS = ((((1, 0, 2), (2, 1, 0)), ((0, 1, 2), (2, 0, 1))), (((1, 2, 0), (2, 1, 0)), ((0, 2, 1), (2, 0, 1))), (((0, 1, 2), (2, 0, 1)), ((1, 0, 2), (1, 0, 2))), (((0, 1, 2), (0, 2, 1)), ((1, 0, 2), (2, 1, 0))), (((0, 1, 2), (2, 0, 1)), ((1, 0, 2), (0, 1, 2))), (((0, 1, 2), (0, 1, 2)), ((1, 0, 2), (2, 0, 1))))
+STEP_BITS = ((((1, 0, 2), (2, 1, 0)), ((0, 1, 2), (2, 0, 1))), (((1, 2, 0), (2, 1, 0)), ((0, 2, 1), (2, 0, 1))), (((0, 1, 2), (2, 0, 1)), ((1, 0, 2), (1, 0, 2))), (((0, 1, 2), (0, 2, 1)), ((1, 0, 2), (2, 1, 0))), (((0, 1, 2), (2, 0, 1)), ((1, 0, 2), (0, 1, 2))), (((0, 1, 2), (0, 1, 2)), ((1, 0, 2), (1, 2, 0))))
 PARTS = 2
 EARLY = (((0,), (1,)), ((0,),), ((0, 2), (1, 3)), ((0, 2), (1, 3)))
 TURNS = ((4, 2, 0), (5, 3, 1)) * 7

time: 198 us -> 194 us (0.980)
  waiting for transfers between devices: 42.2 us -> 38.2 us
    ppermute x42, waiting for transfers between devices: 38.9 us -> 35 us  [exchange(): return lax.ppermute(array_in, ('dp', 'tensor'), pairs)]
  transfers between devices with their start and end apart: 53 -> 53, of which waited for: 14 -> 15; matrix products, arithmetic and copies ran while one was open for 4% -> 4% of each run, Pallas kernels for 41% -> 42%
where the time goes in v6:
time: 194 us
  Pallas kernels  95.4 us (49%)
  starting transfers between devices  49.3 us (25%)
  waiting for transfers between devices  38.2 us (20%)
  other arithmetic  7.17 us (4%)
  between operations  2.35 us (1%)
    pallas_call x22, Pallas kernels, call(): pl.pallas_call(body, out_shape=outs, grid_spec=pltpu.PrefetchScalarGridSp...  95.4 us
    ppermute x42, starting transfers between devices, exchange(): return lax.ppermute(array_in, ('dp', 'tensor'), pairs)  46.6 us
    ppermute x42, waiting for transfers between devices, exchange(): return lax.ppermute(array_in, ('dp', 'tensor'), pairs)  35 us
    convert_element_type x30, other arithmetic, total(): return acc.astype(BF16)  6.58 us
  transfers between devices with their start and end apart: 53, of which 15 were waited for; matrix products, arithmetic and copies ran while one was open for 4% of the time, Pallas kernels for 42%

profile of v6, /device:TPU:0, one launch (start us, length us, event | category | flops | bytes accessed | tf_op | source)
XLA Modules:
  0.0 193.7 jit_solution(10196539706326308625)
XLA Ops:
  3.5 8.2 %shard_map.272 = (bf16[6,512,128]{2,1,0:T(8,128)(2,1)S(1)}, bf16[3,512,128]{2,1,0:T(8,128)(2,1)S(1)}, bf16[3,512,128]{2,1,0:T(8,128)(2,1)S(1)}, bf16[3,512,128]{2,1,0:T(8,128)(2,1)S(1)}) custom-call(s32[2]{0:T(128)S(1)} %compare_select_fusion.ids, s32[1]{0:T(128)S(6)} %copy.51.bucket, s32[1,8]{1,0:T(1,128)S(1)} %copy-done.18, bf16[1024,768]{1,0:T(8,128)(2,1)} %x_ref.9, ...), custom_call_target="tpu_custom_call" | custom-call | flops 34225520640 | bytes 4521984 | tf_op jit(solution)/shard_map/pallas_call | solution.py:54
  12.0 9.6 %shard_map.273 = (bf16[6,512,128]{2,1,0:T(8,128)(2,1)S(1)}, bf16[3,512,128]{2,1,0:T(8,128)(2,1)S(1)}, bf16[3,512,128]{2,1,0:T(8,128)(2,1)S(1)}, bf16[3,512,128]{...) custom-call(s32[2]{0:T(128)S(1)} %compare_select_fusion.ids, ...), custom_call_target="tpu_custom_call" | custom-call | flops 46305116160 | bytes 4521984 | tf_op jit(solution)/shard_map/pallas_call | solution.py:54
  21.8 10.8 %shard_map.274 = (bf16[512,1536]{1,0:T(8,128)(2,1)S(1)}, bf16[512,1536]{1,0:T(8,128)(2,1)S(1)}, f32[512,1536]{1,0:T(8,128)S(1)}, f32[512,1536]{1,0:T(8,128)S(1)}...) custom-call(s32[2]{0:T(128)S(1)} %compare_select_fusion.ids, ...), custom_call_target="tpu_custom_call" | custom-call | flops 96636764160 | bytes 26738688 | tf_op jit(solution)/shard_map/pallas_call | solution.py:54
  32.6 2.0 %shard_map.275 = bf16[2,8,96,768]{3,2,1,0:T(8,128)(2,1)S(1)} custom-call(s32[2]{0:T(128)S(1)} %compare_select_fusion.ids, bf16[512,1536]{1,0:T(8,128)(2,1)S(1)} %get-tuple-element.120.gb_ref, bf16[512,768]{1,0:T(8,128)(2,1)S(1)} %get-tuple-element.129.df_ref), custom_call_target="tpu_custom_call" | custom-call | flops 24159191040 | bytes 4718592 | tf_op jit(solution)/shard_map/pallas_call | solution.py:54
  35.2 2.0 %shard_map.276 = bf16[2,8,96,768]{3,2,1,0:T(8,128)(2,1)S(1)} custom-call(s32[2]{0:T(128)S(1)} %compare_select_fusion.ids, bf16[512,1536]{1,0:T(8,128)(2,1)S(1)} %get-tuple-element.119.gb_ref, bf16[512,768]{1,0:T(8,128)(2,1)S(1)} %get-tuple-element.129.df_ref), custom_call_target="tpu_custom_call" | custom-call | flops 24159191040 | bytes 4718592 | tf_op jit(solution)/shard_map/pallas_call | solution.py:54
  37.1 3.2 %collective-permute-done.6 = bf16[2,8,96,768]{3,2,1,0:T(8,128)(2,1)S(1)} collective-permute-done((bf16[2,8,96,768]{3,2,1,0:T(8,128)(2,1)S(1)}, bf16[2,8,96,768]{3,2,1,0:T(8,128)(2,1)S(1)}, u32[]{:S(2)}, u32[]{:S(2)}) %collective-permute-start.6) | collective-permute-done | bytes 2359328 | tf_op jit(solution)/shard_map/ppermute | solution.py:620
  40.7 3.0 %collective-permute-start.7 = (bf16[4,96,768]{2,1,0:T(8,128)(2,1)S(1)}, bf16[4,96,768]{2,1,0:T(8,128)(2,1)S(1)}, u32[]{:S(2)}, u32[]{:S(2)}) collective-permute-start(bf16[4,96,768]{2,1,0:T(8,128)(2,1)S(1)} %fusion.5), channel_id=1, source_target_pairs={{0,4},{1,3},{2,6},{3,1},{4,0},{5,7},{6,2},{7,5},{8,12},{9,11},{10,... | collective-permute-start | bytes 1769480 | tf_op jit(solution)/shard_map/ppermute | solution.py:635
  44.6 6.6 %shard_map.277 = (bf16[2,8,96,768]{3,2,1,0:T(8,128)(2,1)S(1)}, f32[1,1536]{1,0:T(1,128)S(1)}, f32[512,768]{1,0:T(8,128)S(1)}) custom-call(s32[2]{0:T(128)S(1)} %compare_select_fusion.ids, bf16[512,768]{1,0:T(8,128)(2,1)S(1)} %get-tuple-element.129.df_ref, bf16[512,768]{1,0:T(8,128)(2,1)S(1)} %get-tuple-element.112.hb_ref, ...), custom_call_target="tpu_custom_call" | custom-call | flops 72477573120 | bytes 14155776 | tf_op jit(solution)/shard_map/pallas_call | solution.py:54
  51.6 2.1 %collective-permute-start.8 = (bf16[2,96,768]{2,1,0:T(8,128)(2,1)S(1)}, bf16[2,96,768]{2,1,0:T(8,128)(2,1)S(1)}, u32[]{:S(2)}, u32[]{:S(2)}) collective-permute-start(bf16[2,96,768]{2,1,0:T(8,128)(2,1)S(1)} %fusion.17), channel_id=1, source_target_pairs={{0,2},{1,5},{2,0},{3,7},{4,6},{5,1},{6,4},{7,3},{8,10},{9,13},{10,... | collective-permute-start | bytes 884744 | tf_op jit(solution)/shard_map/ppermute | solution.py:635
  53.7 7.5 %shard_map.278 = (bf16[2,8,96,768]{3,2,1,0:T(8,128)(2,1)S(1)}, f32[1,1536]{1,0:T(1,128)S(1)}, f32[512,768]{1,0:T(8,128)S(1)}, bf16[512,768]{1,0:T(8,128)(2,1)S(1)}, f32[3,768]{1,0:T(4,128)S(1)}) custom-call(s32[2]{0:T(128)S(1)} %compare_select_fusion.ids, bf16[512,768]{1,0:T(8,128)(2,1)S(1)} %get-tuple-element.129.df_ref, ...), custom_call_target="tpu_custom_call" | custom-call | flops 72477573120 | bytes 14155776 | tf_op jit(solution)/shard_map/pallas_call | solution.py:54
  61.2 1.6 collective-permute-start.9
  67.1 13.1 %shard_map.279 = (bf16[2,8,200,384]{3,2,1,0:T(8,128)(2,1)S(1)}, f32[512,768]{1,0:T(8,128)S(1)}) custom-call(s32[2]{0:T(128)S(1)} %compare_select_fusion.ids, s32[1]{0:T(128)S(6)} %copy.51.bucket, s32[1,8]{1,0:T(1,128)S(1)} %copy-done.19, s32[1,8]{1,0:T(1,128)S(1)} %copy-done.17, bf16[6,512,128]{2,1,0:T(8,128)(2,1)S(1)} %get-tuple-element.134.qa_ref, ...), custom_call_target="tpu_custom_call" | custom-call | flops 88583700480 | bytes 10420224 | tf_op jit(solution)/shard_map/pallas_call | solution.py:54
  80.7 2.6 %collective-permute-start.17 = (bf16[1,96,768]{2,1,0:T(8,128)(2,1)S(1)}, bf16[1,96,768]{2,1,0:T(8,128)(2,1)S(1)}, u32[]{:S(2)}, u32[]{:S(2)}) collective-permute-start(bf16[1,96,768]{2,1,0:T(8,128)(2,1)S(1)} %fusion.59), channel_id=1, source_target_pairs={{0,16},{1,17},{2,18},{3,19},{4,20},{5,21},{6,22},{7,23},{8,24},{9,... | collective-permute-start | bytes 442376 | tf_op jit(solution)/shard_map/ppermute | solution.py:635
  88.3 11.7 %shard_map.280 = (bf16[2,8,200,384]{3,2,1,0:T(8,128)(2,1)S(1)}, f32[512,768]{1,0:T(8,128)S(1)}) custom-call(s32[2]{0:T(128)S(1)} %compare_select_fusion.ids, s32[1]{0:T(128)S(6)} %copy.51.bucket, s32[1,8]{1,0:T(1,128)S(1)} %copy-done.19, s32[1,8]{1,0:T(1,128)S(1)} %copy-done.17, bf16[6,512,128]{2,1,0:T(8,128)(2,1)S(1)} %get-tuple-element.115.qa_ref, ...), custom_call_target="tpu_custom_call" | custom-call | flops 88583700480 | bytes 10420224 | tf_op jit(solution)/shard_map/pallas_call | solution.py:54
  100.1 1.6 collective-permute-start.26
  105.2 1.6 collective-permute-start.23
  106.8 4.1 %shard_map.281 = (bf16[1024,768]{1,0:T(8,128)(2,1)}, f32[1024,768]{1,0:T(8,128)}) custom-call(s32[2]{0:T(128)S(1)} %compare_select_fusion.ids, bf16[512,768]{1,0:T(8,128)(2,1)} %get-tuple-element.114.refs_0_, f32[512,768]{1,0:T(8,128)S(1)} %get-tuple-element.161.refs_1_, bf16[512,768]{1,0:T(8,128)(2,1)} %collective-permute-done.12.refs_2_, ...), custom_call_target="tpu_custom_call" | custom-call | bytes 9437184 | tf_op jit(solution)/shard_map/pallas_call | solution.py:54
  114.1 2.0 %collective-permute-start.32 = (bf16[1,96,768]{2,1,0:T(8,128)(2,1)S(1)}, bf16[1,96,768]{2,1,0:T(8,128)(2,1)S(1)}, u32[]{:S(2)}, u32[]{:S(2)}) collective-permute-start(bf16[1,96,768]{2,1,0:T(8,128)(2,1)S(1)} %fusion.39), channel_id=1, source_target_pairs={{0,16},{1,17},{2,18},{3,19},{4,20},{5,21},{6,22},{7,23},{8,24},{9,... | collective-permute-start | bytes 442376 | tf_op jit(solution)/shard_map/ppermute | solution.py:635
  117.4 6.9 %collective-permute-done.24 = bf16[1,96,768]{2,1,0:T(8,128)(2,1)S(1)} collective-permute-done((bf16[1,96,768]{2,1,0:T(8,128)(2,1)S(1)}, bf16[1,96,768]{2,1,0:T(8,128)(2,1)S(1)}, u32[]{:S(2)}, u32[]{:S(2)}) %collective-permute-start.24) | collective-permute-done | bytes 147488 | tf_op jit(solution)/shard_map/ppermute | solution.py:635
  125.5 3.5 %collective-permute-done.32 = bf16[1,96,768]{2,1,0:T(8,128)(2,1)S(1)} collective-permute-done((bf16[1,96,768]{2,1,0:T(8,128)(2,1)S(1)}, bf16[1,96,768]{2,1,0:T(8,128)(2,1)S(1)}, u32[]{:S(2)}, u32[]{:S(2)}) %collective-permute-start.32) | collective-permute-done | bytes 147488 | tf_op jit(solution)/shard_map/ppermute | solution.py:635
  131.1 2.1 %collective-permute-start.36 = (bf16[1,200,384]{2,1,0:T(8,128)(2,1)S(1)}, bf16[1,200,384]{2,1,0:T(8,128)(2,1)S(1)}, u32[]{:S(2)}, u32[]{:S(2)}) collective-permute-start(bf16[1,200,384]{2,1,0:T(8,128)(2,1)S(1)} %fusion.27), channel_id=1, source_target_pairs={{0,8},{1,9},{2,10},{3,11},{4,12},{5,13},{6,14},{7,15},{8,0},{9,1},... | collective-permute-start | bytes 460808 | tf_op jit(solution)/shard_map/ppermute | solution.py:635
  137.4 5.0 %collective-permute-done.37 = bf16[1,96,768]{2,1,0:T(8,128)(2,1)S(1)} collective-permute-done((bf16[1,96,768]{2,1,0:T(8,128)(2,1)S(1)}, bf16[1,96,768]{2,1,0:T(8,128)(2,1)S(1)}, u32[]{:S(2)}, u32[]{:S(2)}) %collective-permute-start.37) | collective-permute-done | bytes 147488 | tf_op jit(solution)/shard_map/ppermute | solution.py:635
  147.3 2.4 %collective-permute-done.39 = bf16[2,96,768]{2,1,0:T(8,128)(2,1)S(1)} collective-permute-done((bf16[2,96,768]{2,1,0:T(8,128)(2,1)S(1)}, bf16[2,96,768]{2,1,0:T(8,128)(2,1)S(1)}, u32[]{:S(2)}, u32[]{:S(2)}) %collective-permute-start.39) | collective-permute-done | bytes 294944 | tf_op jit(solution)/shard_map/ppermute | solution.py:635
  150.9 2.0 %collective-permute-start.47 = (bf16[4,96,768]{2,1,0:T(8,128)(2,1)S(1)}, bf16[4,96,768]{2,1,0:T(8,128)(2,1)S(1)}, u32[]{:S(2)}, u32[]{:S(2)}) collective-permute-start(bf16[4,96,768]{2,1,0:T(8,128)(2,1)S(1)} %pad_maximum_fusion.3.refs_0_), channel_id=1, source_target_pairs={{0,2},{1,5},{2,0},{3,7},{4,6},{5,1},{6,4},{7,3},{8,10},{9,13},{10,... | collective-permute-start | bytes 1769480 | tf_op jit(solution)/shard_map/ppermute | solution.py:635
  153.4 2.3 %collective-permute-start.45 = (bf16[4,96,768]{2,1,0:T(8,128)(2,1)S(1)}, bf16[4,96,768]{2,1,0:T(8,128)(2,1)S(1)}, u32[]{:S(2)}, u32[]{:S(2)}) collective-permute-start(bf16[4,96,768]{2,1,0:T(8,128)(2,1)S(1)} %pad_maximum_fusion.4.refs_0_), channel_id=1, source_target_pairs={{0,4},{1,9},{2,6},{3,11},{4,0},{5,13},{6,2},{7,15},{8,12},{9,1},{1... | collective-permute-start | bytes 1769480 | tf_op jit(solution)/shard_map/ppermute | solution.py:635
  155.8 2.0 %collective-permute-done.40 = bf16[1,200,384]{2,1,0:T(8,128)(2,1)S(1)} collective-permute-done((bf16[1,200,384]{2,1,0:T(8,128)(2,1)S(1)}, bf16[1,200,384]{2,1,0:T(8,128)(2,1)S(1)}, u32[]{:S(2)}, u32[]{:S(2)}) %collective-permute-start.40) | collective-permute-done | bytes 153632 | tf_op jit(solution)/shard_map/ppermute | solution.py:635
  157.8 4.8 %collective-permute-done.41 = bf16[2,96,768]{2,1,0:T(8,128)(2,1)S(1)} collective-permute-done((bf16[2,96,768]{2,1,0:T(8,128)(2,1)S(1)}, bf16[2,96,768]{2,1,0:T(8,128)(2,1)S(1)}, u32[]{:S(2)}, u32[]{:S(2)}) %collective-permute-start.41) | collective-permute-done | bytes 294944 | tf_op jit(solution)/shard_map/ppermute | solution.py:635
  166.3 1.6 shard_map.288
  178.7 2.3 %collective-permute-done.48 = bf16[2,200,384]{2,1,0:T(8,128)(2,1)S(1)} collective-permute-done((bf16[2,200,384]{2,1,0:T(8,128)(2,1)S(1)}, bf16[2,200,384]{2,1,0:T(8,128)(2,1)S(1)}, u32[]{:S(2)}, u32[]{:S(2)}) %collective-permute-start.48) | collective-permute-done | bytes 307232 | tf_op jit(solution)/shard_map/ppermute | solution.py:635
  183.9 1.6 shard_map.291
  185.5 2.6 %collective-permute-done.52.refs_0_ = bf16[4,200,384]{2,1,0:T(8,128)(2,1)S(1)} collective-permute-done((bf16[4,200,384]{2,1,0:T(8,128)(2,1)S(1)}, bf16[4,200,384]{2,1,0:T(8,128)(2,1)S(1)}, u32[]{:S(2)}, u32[]{:S(2)}) %collective-permute-start.52) | collective-permute-done | bytes 614432 | tf_op jit(solution)/shard_map/ppermute | solution.py:635
  191.3 2.2 %shard_map.293 = (f32[3,768,384]{2,1,0:T(8,128)}, f32[384,768]{1,0:T(8,128)}, f32[2,384]{1,0:T(2,128)}, f32[1536]{0:T(1024)}, f32[768]{0:T(1024)}, /*index=5*/f3...) custom-call(s32[2]{0:T(128)S(1)} %compare_select_fusion.ids, ...), custom_call_target="tpu_custom_call", output_to_operand_aliasing={{0}: (3, {}), {1}: (4, {})} | custom-call | bytes 1843200 | tf_op jit(solution)/shard_map/pallas_call | solution.py:54
  (190 shorter events, 56.6 us)
Async XLA Ops:
  0.6 11.3 %collective-permute-start = (bf16[3,768,384]{2,1,0:T(8,128)(2,1)}, bf16[3,768,384]{2,1,0:T(8,128)(2,1)}, u32[]{:S(2)}, u32[]{:S(2)}) collective-permute-start(bf16[3,768,384]{2,1,0:T(8,128)(2,1)} %w_ref.3), channel_id=1, source_target_pairs={{0,1},{1,0},{2,3},{3,2},{4,5},{5,4},{6,7},{7,6},{8,9},{9,8},{10,11... | collective-permute-start | bytes 5308424 | tf_op jit(solution)/shard_map/ppermute | solution.py:620
  1.7 20.0 %collective-permute-start.3 = (bf16[768,1536]{1,0:T(8,128)(2,1)}, bf16[768,1536]{1,0:T(8,128)(2,1)S(1)}, u32[]{:S(2)}, u32[]{:S(2)}) collective-permute-start(bf16[768,1536]{1,0:T(8,128)(2,1)} %up_ref.1), channel_id=1, source_target_pairs={{0,1},{1,0},{2,3},{3,2},{4,5},{5,4},{6,7},{7,6},{8,9},{9,8},{10,11... | collective-permute-start | bytes 7077896 | tf_op jit(solution)/shard_map/ppermute | solution.py:620
  1.8 19.9 %collective-permute-start.4 = (f32[1536]{0:T(1024)}, f32[1536]{0:T(1024)S(1)}, u32[]{:S(2)}, u32[]{:S(2)}) collective-permute-start(f32[1536]{0:T(1024)} %bu_own.1), channel_id=1, source_target_pairs={{0,1},{1,0},{2,3},{3,2},{4,5},{5,4},{6,7},{7,6},{8,9},{9,8},{10,11... | collective-permute-start | bytes 18440 | tf_op jit(solution)/shard_map/ppermute | solution.py:620
  35.1 45.2 %collective-permute-start.12 = (bf16[512,768]{1,0:T(8,128)(2,1)}, bf16[512,768]{1,0:T(8,128)(2,1)}, u32[]{:S(2)}, u32[]{:S(2)}) collective-permute-start(bf16[512,768]{1,0:T(8,128)(2,1)} %get-tuple-element.114.refs_0_), channel_id=1, source_target_pairs={{0,1},{1,0},{2,3},{3,2},{4,5},{5,4},{6,7},{7,6},{8,9},{9,8},{10,11... | collective-permute-start | bytes 2359304 | tf_op jit(solution)/shard_map/ppermute | solution.py:620
  44.6 19.7 %collective-permute-start.11 = (bf16[4,96,768]{2,1,0:T(8,128)(2,1)}, bf16[4,96,768]{2,1,0:T(8,128)(2,1)}, u32[]{:S(2)}, u32[]{:S(2)}) collective-permute-start(bf16[4,96,768]{2,1,0:T(8,128)(2,1)} %fusion.4), channel_id=1, source_target_pairs={{0,4},{1,3},{2,6},{3,1},{4,0},{5,7},{6,2},{7,5},{8,12},{9,11},{10,... | collective-permute-start | bytes 1769480 | tf_op jit(solution)/shard_map/ppermute | solution.py:635
  51.3 11.6 %collective-permute-start.10 = (bf16[2,8,96,768]{3,2,1,0:T(8,128)(2,1)S(1)}, bf16[2,8,96,768]{3,2,1,0:T(8,128)(2,1)S(1)}, u32[]{:S(2)}, u32[]{:S(2)}) collective-permute-start(bf16[2,8,96,768]{3,2,1,0:T(8,128)(2,1)S(1)} %get-tuple-element.139), channel_id=1, source_target_pairs={{0,1},{1,0},{2,3},{3,2},{4,5},{5,4},{6,7},{7,6},{8,9},{9,8},{10,11... | collective-permute-start | bytes 7077896 | tf_op jit(solution)/shard_map/ppermute | solution.py:620
  61.2 19.3 %collective-permute-start.9 = (bf16[1,96,768]{2,1,0:T(8,128)(2,1)S(1)}, bf16[1,96,768]{2,1,0:T(8,128)(2,1)S(1)}, u32[]{:S(2)}, u32[]{:S(2)}) collective-permute-start(bf16[1,96,768]{2,1,0:T(8,128)(2,1)S(1)} %fusion.55), channel_id=1, source_target_pairs={{0,8},{1,9},{2,10},{3,11},{4,12},{5,13},{6,14},{7,15},{8,0},{9,1},... | collective-permute-start | bytes 442376 | tf_op jit(solution)/shard_map/ppermute | solution.py:635
  63.2 17.3 %collective-permute-start.13 = (bf16[4,96,768]{2,1,0:T(8,128)(2,1)S(1)}, bf16[4,96,768]{2,1,0:T(8,128)(2,1)S(1)}, u32[]{:S(2)}, u32[]{:S(2)}) collective-permute-start(bf16[4,96,768]{2,1,0:T(8,128)(2,1)S(1)} %fusion.3), channel_id=1, source_target_pairs={{0,2},{1,5},{2,0},{3,7},{4,6},{5,1},{6,4},{7,3},{8,10},{9,13},{10,... | collective-permute-start | bytes 1769480 | tf_op jit(solution)/shard_map/ppermute | solution.py:635
  65.6 19.3 %collective-permute-start.14 = (bf16[2,96,768]{2,1,0:T(8,128)(2,1)S(1)}, bf16[2,96,768]{2,1,0:T(8,128)(2,1)S(1)}, u32[]{:S(2)}, u32[]{:S(2)}) collective-permute-start(bf16[2,96,768]{2,1,0:T(8,128)(2,1)S(1)} %fusion.15), channel_id=1, source_target_pairs={{0,8},{1,9},{2,10},{3,11},{4,12},{5,13},{6,14},{7,15},{8,0},{9,1},... | collective-permute-start | bytes 884744 | tf_op jit(solution)/shard_map/ppermute | solution.py:635
  66.1 18.8 %collective-permute-start.15 = (bf16[4,96,768]{2,1,0:T(8,128)(2,1)S(1)}, bf16[4,96,768]{2,1,0:T(8,128)(2,1)S(1)}, u32[]{:S(2)}, u32[]{:S(2)}) collective-permute-start(bf16[4,96,768]{2,1,0:T(8,128)(2,1)S(1)} %fusion.2), channel_id=1, source_target_pairs={{0,2},{1,5},{2,0},{3,7},{4,6},{5,1},{6,4},{7,3},{8,10},{9,13},{10,... | collective-permute-start | bytes 1769480 | tf_op jit(solution)/shard_map/ppermute | solution.py:635
  80.3 21.5 %collective-permute-start.16 = (bf16[2,8,200,384]{3,2,1,0:T(8,128)(2,1)S(1)}, bf16[2,8,200,384]{3,2,1,0:T(8,128)(2,1)S(1)}, u32[]{:S(2)}, u32[]{:S(2)}) collective-permute-start(bf16[2,8,200,384]{3,2,1,0:T(8,128)(2,1)S(1)} %get-tuple-element.157), channel_id=1, source_target_pairs={{0,1},{1,0},{2,3},{3,2},{4,5},{5,4},{6,7},{7,6},{8,9},{9,8},{10,11... | collective-permute-start | bytes 7372808 | tf_op jit(solution)/shard_map/ppermute | solution.py:620
  80.7 19.2 %collective-permute-start.17 = (bf16[1,96,768]{2,1,0:T(8,128)(2,1)S(1)}, bf16[1,96,768]{2,1,0:T(8,128)(2,1)S(1)}, u32[]{:S(2)}, u32[]{:S(2)}) collective-permute-start(bf16[1,96,768]{2,1,0:T(8,128)(2,1)S(1)} %fusion.59), channel_id=1, source_target_pairs={{0,16},{1,17},{2,18},{3,19},{4,20},{5,21},{6,22},{7,23},{8,24},{9,... | collective-permute-start | bytes 442376 | tf_op jit(solution)/shard_map/ppermute | solution.py:635
  83.5 16.5 %collective-permute-start.18 = (bf16[2,96,768]{2,1,0:T(8,128)(2,1)S(1)}, bf16[2,96,768]{2,1,0:T(8,128)(2,1)S(1)}, u32[]{:S(2)}, u32[]{:S(2)}) collective-permute-start(bf16[2,96,768]{2,1,0:T(8,128)(2,1)S(1)} %fusion.13), channel_id=1, source_target_pairs={{0,4},{1,3},{2,6},{3,1},{4,0},{5,7},{6,2},{7,5},{8,12},{9,11},{10,... | collective-permute-start | bytes 884744 | tf_op jit(solution)/shard_map/ppermute | solution.py:635
  86.0 16.8 %collective-permute-start.20 = (bf16[1,96,768]{2,1,0:T(8,128)(2,1)S(1)}, bf16[1,96,768]{2,1,0:T(8,128)(2,1)S(1)}, u32[]{:S(2)}, u32[]{:S(2)}) collective-permute-start(bf16[1,96,768]{2,1,0:T(8,128)(2,1)S(1)} %fusion.52), channel_id=1, source_target_pairs={{0,2},{1,5},{2,0},{3,7},{4,6},{5,1},{6,4},{7,3},{8,10},{9,13},{10,... | collective-permute-start | bytes 442376 | tf_op jit(solution)/shard_map/ppermute | solution.py:635
  87.1 16.3 %collective-permute-start.21 = (bf16[2,96,768]{2,1,0:T(8,128)(2,1)S(1)}, bf16[2,96,768]{2,1,0:T(8,128)(2,1)S(1)}, u32[]{:S(2)}, u32[]{:S(2)}) collective-permute-start(bf16[2,96,768]{2,1,0:T(8,128)(2,1)S(1)} %fusion.11), channel_id=1, source_target_pairs={{0,4},{1,3},{2,6},{3,1},{4,0},{5,7},{6,2},{7,5},{8,12},{9,11},{10,... | collective-permute-start | bytes 884744 | tf_op jit(solution)/shard_map/ppermute | solution.py:635
  100.1 11.8 %collective-permute-start.26 = (bf16[1,96,768]{2,1,0:T(8,128)(2,1)S(1)}, bf16[1,96,768]{2,1,0:T(8,128)(2,1)S(1)}, u32[]{:S(2)}, u32[]{:S(2)}) collective-permute-start(bf16[1,96,768]{2,1,0:T(8,128)(2,1)S(1)} %fusion.49), channel_id=1, source_target_pairs={{0,8},{1,9},{2,10},{3,11},{4,12},{5,13},{6,14},{7,15},{8,0},{9,1},... | collective-permute-start | bytes 442376 | tf_op jit(solution)/shard_map/ppermute | solution.py:635
  103.5 20.8 %collective-permute-start.22 = (bf16[4,200,384]{2,1,0:T(8,128)(2,1)S(1)}, bf16[4,200,384]{2,1,0:T(8,128)(2,1)S(1)}, u32[]{:S(2)}, u32[]{:S(2)}) collective-permute-start(bf16[4,200,384]{2,1,0:T(8,128)(2,1)S(1)} %fusion), channel_id=1, source_target_pairs={{0,2},{1,5},{2,0},{3,7},{4,6},{5,1},{6,4},{7,3},{8,10},{9,13},{10,... | collective-permute-start | bytes 1843208 | tf_op jit(solution)/shard_map/ppermute | solution.py:635
  105.2 11.0 %collective-permute-start.23 = (bf16[1,96,768]{2,1,0:T(8,128)(2,1)S(1)}, bf16[1,96,768]{2,1,0:T(8,128)(2,1)S(1)}, u32[]{:S(2)}, u32[]{:S(2)}) collective-permute-start(bf16[1,96,768]{2,1,0:T(8,128)(2,1)S(1)} %fusion.46), channel_id=1, source_target_pairs={{0,8},{1,9},{2,10},{3,11},{4,12},{5,13},{6,14},{7,15},{8,0},{9,1},... | collective-permute-start | bytes 442376 | tf_op jit(solution)/shard_map/ppermute | solution.py:635
  112.0 12.3 %collective-permute-start.24 = (bf16[1,96,768]{2,1,0:T(8,128)(2,1)S(1)}, bf16[1,96,768]{2,1,0:T(8,128)(2,1)S(1)}, u32[]{:S(2)}, u32[]{:S(2)}) collective-permute-start(bf16[1,96,768]{2,1,0:T(8,128)(2,1)S(1)} %fusion.43), channel_id=1, source_target_pairs={{0,16},{1,17},{2,18},{3,19},{4,20},{5,21},{6,22},{7,23},{8,24},{9,... | collective-permute-start | bytes 442376 | tf_op jit(solution)/shard_map/ppermute | solution.py:635
  113.2 15.8 %collective-permute-start.31 = (bf16[2,200,384]{2,1,0:T(8,128)(2,1)S(1)}, bf16[2,200,384]{2,1,0:T(8,128)(2,1)S(1)}, u32[]{:S(2)}, u32[]{:S(2)}) collective-permute-start(bf16[2,200,384]{2,1,0:T(8,128)(2,1)S(1)} %fusion.9), channel_id=1, source_target_pairs={{0,4},{1,3},{2,6},{3,1},{4,0},{5,7},{6,2},{7,5},{8,12},{9,11},{10,... | collective-permute-start | bytes 921608 | tf_op jit(solution)/shard_map/ppermute | solution.py:635
  114.1 14.9 %collective-permute-start.32 = (bf16[1,96,768]{2,1,0:T(8,128)(2,1)S(1)}, bf16[1,96,768]{2,1,0:T(8,128)(2,1)S(1)}, u32[]{:S(2)}, u32[]{:S(2)}) collective-permute-start(bf16[1,96,768]{2,1,0:T(8,128)(2,1)S(1)} %fusion.39), channel_id=1, source_target_pairs={{0,16},{1,17},{2,18},{3,19},{4,20},{5,21},{6,22},{7,23},{8,24},{9,... | collective-permute-start | bytes 442376 | tf_op jit(solution)/shard_map/ppermute | solution.py:635
  116.1 12.9 %collective-permute-start.33 = (bf16[2,96,768]{2,1,0:T(8,128)(2,1)S(1)}, bf16[2,96,768]{2,1,0:T(8,128)(2,1)S(1)}, u32[]{:S(2)}, u32[]{:S(2)}) collective-permute-start(bf16[2,96,768]{2,1,0:T(8,128)(2,1)S(1)} %pad_maximum_fusion.8), channel_id=1, source_target_pairs={{0,4},{1,3},{2,6},{3,1},{4,0},{5,7},{6,2},{7,5},{8,12},{9,11},{10,... | collective-permute-start | bytes 884744 | tf_op jit(solution)/shard_map/ppermute | solution.py:635
  124.4 11.6 %collective-permute-start.28 = (bf16[2,200,384]{2,1,0:T(8,128)(2,1)S(1)}, bf16[2,200,384]{2,1,0:T(8,128)(2,1)S(1)}, u32[]{:S(2)}, u32[]{:S(2)}) collective-permute-start(bf16[2,200,384]{2,1,0:T(8,128)(2,1)S(1)} %fusion.7), channel_id=1, source_target_pairs={{0,4},{1,3},{2,6},{3,1},{4,0},{5,7},{6,2},{7,5},{8,12},{9,11},{10,... | collective-permute-start | bytes 921608 | tf_op jit(solution)/shard_map/ppermute | solution.py:635
  129.2 15.4 %collective-permute-start.35 = (bf16[4,96,768]{2,1,0:T(8,128)(2,1)S(1)}, bf16[4,96,768]{2,1,0:T(8,128)(2,1)S(1)}, u32[]{:S(2)}, u32[]{:S(2)}) collective-permute-start(bf16[4,96,768]{2,1,0:T(8,128)(2,1)S(1)} %pad_maximum_fusion.2.refs_0_), channel_id=1, source_target_pairs={{0,2},{1,5},{2,0},{3,7},{4,6},{5,1},{6,4},{7,3},{8,10},{9,13},{10,... | collective-permute-start | bytes 1769480 | tf_op jit(solution)/shard_map/ppermute | solution.py:635
  131.1 12.1 %collective-permute-start.36 = (bf16[1,200,384]{2,1,0:T(8,128)(2,1)S(1)}, bf16[1,200,384]{2,1,0:T(8,128)(2,1)S(1)}, u32[]{:S(2)}, u32[]{:S(2)}) collective-permute-start(bf16[1,200,384]{2,1,0:T(8,128)(2,1)S(1)} %fusion.27), channel_id=1, source_target_pairs={{0,8},{1,9},{2,10},{3,11},{4,12},{5,13},{6,14},{7,15},{8,0},{9,1},... | collective-permute-start | bytes 460808 | tf_op jit(solution)/shard_map/ppermute | solution.py:635
  136.1 11.2 %collective-permute-start.34 = (bf16[1,200,384]{2,1,0:T(8,128)(2,1)S(1)}, bf16[1,200,384]{2,1,0:T(8,128)(2,1)S(1)}, u32[]{:S(2)}, u32[]{:S(2)}) collective-permute-start(bf16[1,200,384]{2,1,0:T(8,128)(2,1)S(1)} %fusion.24), channel_id=1, source_target_pairs={{0,8},{1,9},{2,10},{3,11},{4,12},{5,13},{6,14},{7,15},{8,0},{9,1},... | collective-permute-start | bytes 460808 | tf_op jit(solution)/shard_map/ppermute | solution.py:635
  136.2 11.0 %collective-permute-start.38 = (bf16[1,96,768]{2,1,0:T(8,128)(2,1)S(1)}, bf16[1,96,768]{2,1,0:T(8,128)(2,1)S(1)}, u32[]{:S(2)}, u32[]{:S(2)}) collective-permute-start(bf16[1,96,768]{2,1,0:T(8,128)(2,1)S(1)} %add_convert_fusion.2), channel_id=1, source_target_pairs={{0,2},{1,9},{2,0},{3,11},{4,6},{5,13},{6,4},{7,15},{8,10},{9,1},{1... | collective-permute-start | bytes 442376 | tf_op jit(solution)/shard_map/ppermute | solution.py:635
  150.4 12.2 %collective-permute-start.41 = (bf16[2,96,768]{2,1,0:T(8,128)(2,1)S(1)}, bf16[2,96,768]{2,1,0:T(8,128)(2,1)S(1)}, u32[]{:S(2)}, u32[]{:S(2)}) collective-permute-start(bf16[2,96,768]{2,1,0:T(8,128)(2,1)S(1)} %pad_maximum_fusion.11), channel_id=1, source_target_pairs={{0,8},{1,5},{2,10},{3,7},{4,12},{5,1},{6,14},{7,3},{8,0},{9,13},{1... | collective-permute-start | bytes 884744 | tf_op jit(solution)/shard_map/ppermute | solution.py:635
  150.9 15.3 %collective-permute-start.47 = (bf16[4,96,768]{2,1,0:T(8,128)(2,1)S(1)}, bf16[4,96,768]{2,1,0:T(8,128)(2,1)S(1)}, u32[]{:S(2)}, u32[]{:S(2)}) collective-permute-start(bf16[4,96,768]{2,1,0:T(8,128)(2,1)S(1)} %pad_maximum_fusion.3.refs_0_), channel_id=1, source_target_pairs={{0,2},{1,5},{2,0},{3,7},{4,6},{5,1},{6,4},{7,3},{8,10},{9,13},{10,... | collective-permute-start | bytes 1769480 | tf_op jit(solution)/shard_map/ppermute | solution.py:635
  153.4 19.1 %collective-permute-start.45 = (bf16[4,96,768]{2,1,0:T(8,128)(2,1)S(1)}, bf16[4,96,768]{2,1,0:T(8,128)(2,1)S(1)}, u32[]{:S(2)}, u32[]{:S(2)}) collective-permute-start(bf16[4,96,768]{2,1,0:T(8,128)(2,1)S(1)} %pad_maximum_fusion.4.refs_0_), channel_id=1, source_target_pairs={{0,4},{1,9},{2,6},{3,11},{4,0},{5,13},{6,2},{7,15},{8,12},{9,1},{1... | collective-permute-start | bytes 1769480 | tf_op jit(solution)/shard_map/ppermute | solution.py:635
  155.8 12.1 %collective-permute-start.46 = (bf16[1,200,384]{2,1,0:T(8,128)(2,1)S(1)}, bf16[1,200,384]{2,1,0:T(8,128)(2,1)S(1)}, u32[]{:S(2)}, u32[]{:S(2)}) collective-permute-start(bf16[1,200,384]{2,1,0:T(8,128)(2,1)S(1)} %add_convert_fusion.1), channel_id=1, source_target_pairs={{0,8},{1,3},{2,10},{3,1},{4,12},{5,7},{6,14},{7,5},{8,0},{9,11},{1... | collective-permute-start | bytes 460808 | tf_op jit(solution)/shard_map/ppermute | solution.py:635
  162.7 13.6 %collective-permute-start.49 = (bf16[4,96,768]{2,1,0:T(8,128)(2,1)S(1)}, bf16[4,96,768]{2,1,0:T(8,128)(2,1)S(1)}, u32[]{:S(2)}, u32[]{:S(2)}) collective-permute-start(bf16[4,96,768]{2,1,0:T(8,128)(2,1)S(1)} %pad_maximum_fusion.5.refs_0_), channel_id=1, source_target_pairs={{0,4},{1,3},{2,6},{3,1},{4,0},{5,7},{6,2},{7,5},{8,12},{9,11},{10,... | collective-permute-start | bytes 1769480 | tf_op jit(solution)/shard_map/ppermute | solution.py:635
  (45 other events, 361.9 us)

commit v7 on v6

--- a/solution.py
+++ b/solution.py
@@ -347,7 +347,7 @@
                 out_ref[part, spot_of(ids, part, kind, i * per + c, count)] = value[first : first + size, :]
         return carry
 
-    lax.fori_loop(0, count // per, step, 0, unroll=4)
+    lax.fori_loop(0, count // per, step, 0, unroll=2)
 
 
 def down_grad(kind, ids, gb, df, count):
@@ -390,7 +390,7 @@
         acc[...] += dot_nt(du, up_ref[:, cols])
         return carry
 
-    lax.fori_loop(0, hidden // chunk, step, 0, unroll=2)
+    lax.fori_loop(0, hidden // chunk, step, 0, unroll=4 if kind == 0 else 2)
     if kind == 0:
         fold_s[...] = jnp.zeros_like(fold_s)
         gain_row = row_of(gain_a)

time: 194 us -> 194 us (level)
  transfers between devices with their start and end apart: 53 -> 53, of which waited for: 15 -> 16; matrix products, arithmetic and copies ran while one was open for 4% -> 4% of each run, Pallas kernels for 42% -> 41%
where the time goes in v7:
time: 194 us
  Pallas kernels  95.2 us (49%)
  starting transfers between devices  49.8 us (26%)
  waiting for transfers between devices  38.4 us (20%)
  other arithmetic  7.11 us (4%)
  between operations  2.37 us (1%)
    pallas_call x22, Pallas kernels, call(): pl.pallas_call(body, out_shape=outs, grid_spec=pltpu.PrefetchScalarGridSp...  95.2 us
    ppermute x42, starting transfers between devices, exchange(): return lax.ppermute(array_in, ('dp', 'tensor'), pairs)  47.1 us
    ppermute x42, waiting for transfers between devices, exchange(): return lax.ppermute(array_in, ('dp', 'tensor'), pairs)  35.3 us
    convert_element_type x30, other arithmetic, total(): return acc.astype(BF16)  6.52 us
  transfers between devices with their start and end apart: 53, of which 16 were waited for; matrix products, arithmetic and copies ran while one was open for 4% of the time, Pallas kernels for 41%

profile of v7, /device:TPU:0, one launch (start us, length us, event | category | flops | bytes accessed | tf_op | source)
XLA Modules:
  0.0 194.2 jit_solution(14942094285684118019)
XLA Ops:
  3.5 8.2 %shard_map.272 = (bf16[6,512,128]{2,1,0:T(8,128)(2,1)S(1)}, bf16[3,512,128]{2,1,0:T(8,128)(2,1)S(1)}, bf16[3,512,128]{2,1,0:T(8,128)(2,1)S(1)}, bf16[3,512,128]{2,1,0:T(8,128)(2,1)S(1)}) custom-call(s32[2]{0:T(128)S(1)} %compare_select_fusion.ids, s32[1]{0:T(128)S(6)} %copy.51.bucket, s32[1,8]{1,0:T(1,128)S(1)} %copy-done.18, bf16[1024,768]{1,0:T(8,128)(2,1)} %x_ref.9, ...), custom_call_target="tpu_custom_call" | custom-call | flops 34225520640 | bytes 4521984 | tf_op jit(solution)/shard_map/pallas_call | solution.py:54
  12.0 9.6 %shard_map.273 = (bf16[6,512,128]{2,1,0:T(8,128)(2,1)S(1)}, bf16[3,512,128]{2,1,0:T(8,128)(2,1)S(1)}, bf16[3,512,128]{2,1,0:T(8,128)(2,1)S(1)}, bf16[3,512,128]{...) custom-call(s32[2]{0:T(128)S(1)} %compare_select_fusion.ids, ...), custom_call_target="tpu_custom_call" | custom-call | flops 46305116160 | bytes 4521984 | tf_op jit(solution)/shard_map/pallas_call | solution.py:54
  21.8 10.8 %shard_map.274 = (bf16[512,1536]{1,0:T(8,128)(2,1)S(1)}, bf16[512,1536]{1,0:T(8,128)(2,1)S(1)}, f32[512,1536]{1,0:T(8,128)S(1)}, f32[512,1536]{1,0:T(8,128)S(1)}...) custom-call(s32[2]{0:T(128)S(1)} %compare_select_fusion.ids, ...), custom_call_target="tpu_custom_call" | custom-call | flops 96636764160 | bytes 26738688 | tf_op jit(solution)/shard_map/pallas_call | solution.py:54
  32.6 2.2 %shard_map.275 = bf16[2,8,96,768]{3,2,1,0:T(8,128)(2,1)S(1)} custom-call(s32[2]{0:T(128)S(1)} %compare_select_fusion.ids, bf16[512,1536]{1,0:T(8,128)(2,1)S(1)} %get-tuple-element.120.gb_ref, bf16[512,768]{1,0:T(8,128)(2,1)S(1)} %get-tuple-element.129.df_ref), custom_call_target="tpu_custom_call" | custom-call | flops 24159191040 | bytes 4718592 | tf_op jit(solution)/shard_map/pallas_call | solution.py:54
  35.3 2.2 %shard_map.276 = bf16[2,8,96,768]{3,2,1,0:T(8,128)(2,1)S(1)} custom-call(s32[2]{0:T(128)S(1)} %compare_select_fusion.ids, bf16[512,1536]{1,0:T(8,128)(2,1)S(1)} %get-tuple-element.119.gb_ref, bf16[512,768]{1,0:T(8,128)(2,1)S(1)} %get-tuple-element.129.df_ref), custom_call_target="tpu_custom_call" | custom-call | flops 24159191040 | bytes 4718592 | tf_op jit(solution)/shard_map/pallas_call | solution.py:54
  37.5 3.0 %collective-permute-done.6 = bf16[2,8,96,768]{3,2,1,0:T(8,128)(2,1)S(1)} collective-permute-done((bf16[2,8,96,768]{3,2,1,0:T(8,128)(2,1)S(1)}, bf16[2,8,96,768]{3,2,1,0:T(8,128)(2,1)S(1)}, u32[]{:S(2)}, u32[]{:S(2)}) %collective-permute-start.6) | collective-permute-done | bytes 2359328 | tf_op jit(solution)/shard_map/ppermute | solution.py:620
  40.9 3.0 %collective-permute-start.7 = (bf16[4,96,768]{2,1,0:T(8,128)(2,1)S(1)}, bf16[4,96,768]{2,1,0:T(8,128)(2,1)S(1)}, u32[]{:S(2)}, u32[]{:S(2)}) collective-permute-start(bf16[4,96,768]{2,1,0:T(8,128)(2,1)S(1)} %fusion.5), channel_id=1, source_target_pairs={{0,4},{1,3},{2,6},{3,1},{4,0},{5,7},{6,2},{7,5},{8,12},{9,11},{10,... | collective-permute-start | bytes 1769480 | tf_op jit(solution)/shard_map/ppermute | solution.py:635
  44.8 6.6 %shard_map.277 = (bf16[2,8,96,768]{3,2,1,0:T(8,128)(2,1)S(1)}, f32[1,1536]{1,0:T(1,128)S(1)}, f32[512,768]{1,0:T(8,128)S(1)}) custom-call(s32[2]{0:T(128)S(1)} %compare_select_fusion.ids, bf16[512,768]{1,0:T(8,128)(2,1)S(1)} %get-tuple-element.129.df_ref, bf16[512,768]{1,0:T(8,128)(2,1)S(1)} %get-tuple-element.112.hb_ref, ...), custom_call_target="tpu_custom_call" | custom-call | flops 72477573120 | bytes 14155776 | tf_op jit(solution)/shard_map/pallas_call | solution.py:54
  51.8 2.1 %collective-permute-start.8 = (bf16[2,96,768]{2,1,0:T(8,128)(2,1)S(1)}, bf16[2,96,768]{2,1,0:T(8,128)(2,1)S(1)}, u32[]{:S(2)}, u32[]{:S(2)}) collective-permute-start(bf16[2,96,768]{2,1,0:T(8,128)(2,1)S(1)} %fusion.17), channel_id=1, source_target_pairs={{0,2},{1,5},{2,0},{3,7},{4,6},{5,1},{6,4},{7,3},{8,10},{9,13},{10,... | collective-permute-start | bytes 884744 | tf_op jit(solution)/shard_map/ppermute | solution.py:635
  53.9 6.6 %shard_map.278 = (bf16[2,8,96,768]{3,2,1,0:T(8,128)(2,1)S(1)}, f32[1,1536]{1,0:T(1,128)S(1)}, f32[512,768]{1,0:T(8,128)S(1)}, bf16[512,768]{1,0:T(8,128)(2,1)S(1)}, f32[3,768]{1,0:T(4,128)S(1)}) custom-call(s32[2]{0:T(128)S(1)} %compare_select_fusion.ids, bf16[512,768]{1,0:T(8,128)(2,1)S(1)} %get-tuple-element.129.df_ref, ...), custom_call_target="tpu_custom_call" | custom-call | flops 72477573120 | bytes 14155776 | tf_op jit(solution)/shard_map/pallas_call | solution.py:54
  60.7 1.9 collective-permute-start.9
  67.3 13.3 %shard_map.279 = (bf16[2,8,200,384]{3,2,1,0:T(8,128)(2,1)S(1)}, f32[512,768]{1,0:T(8,128)S(1)}) custom-call(s32[2]{0:T(128)S(1)} %compare_select_fusion.ids, s32[1]{0:T(128)S(6)} %copy.51.bucket, s32[1,8]{1,0:T(1,128)S(1)} %copy-done.19, s32[1,8]{1,0:T(1,128)S(1)} %copy-done.17, bf16[6,512,128]{2,1,0:T(8,128)(2,1)S(1)} %get-tuple-element.134.qa_ref, ...), custom_call_target="tpu_custom_call" | custom-call | flops 88583700480 | bytes 10420224 | tf_op jit(solution)/shard_map/pallas_call | solution.py:54
  81.1 2.6 %collective-permute-start.17 = (bf16[1,96,768]{2,1,0:T(8,128)(2,1)S(1)}, bf16[1,96,768]{2,1,0:T(8,128)(2,1)S(1)}, u32[]{:S(2)}, u32[]{:S(2)}) collective-permute-start(bf16[1,96,768]{2,1,0:T(8,128)(2,1)S(1)} %fusion.59), channel_id=1, source_target_pairs={{0,16},{1,17},{2,18},{3,19},{4,20},{5,21},{6,22},{7,23},{8,24},{9,... | collective-permute-start | bytes 442376 | tf_op jit(solution)/shard_map/ppermute | solution.py:635
  88.7 11.7 %shard_map.280 = (bf16[2,8,200,384]{3,2,1,0:T(8,128)(2,1)S(1)}, f32[512,768]{1,0:T(8,128)S(1)}) custom-call(s32[2]{0:T(128)S(1)} %compare_select_fusion.ids, s32[1]{0:T(128)S(6)} %copy.51.bucket, s32[1,8]{1,0:T(1,128)S(1)} %copy-done.19, s32[1,8]{1,0:T(1,128)S(1)} %copy-done.17, bf16[6,512,128]{2,1,0:T(8,128)(2,1)S(1)} %get-tuple-element.115.qa_ref, ...), custom_call_target="tpu_custom_call" | custom-call | flops 88583700480 | bytes 10420224 | tf_op jit(solution)/shard_map/pallas_call | solution.py:54
  100.6 1.6 collective-permute-start.26
  105.6 1.6 collective-permute-start.23
  107.3 4.1 %shard_map.281 = (bf16[1024,768]{1,0:T(8,128)(2,1)}, f32[1024,768]{1,0:T(8,128)}) custom-call(s32[2]{0:T(128)S(1)} %compare_select_fusion.ids, bf16[512,768]{1,0:T(8,128)(2,1)} %get-tuple-element.114.refs_0_, f32[512,768]{1,0:T(8,128)S(1)} %get-tuple-element.161.refs_1_, bf16[512,768]{1,0:T(8,128)(2,1)} %collective-permute-done.12.refs_2_, ...), custom_call_target="tpu_custom_call" | custom-call | bytes 9437184 | tf_op jit(solution)/shard_map/pallas_call | solution.py:54
  114.5 2.0 %collective-permute-start.32 = (bf16[1,96,768]{2,1,0:T(8,128)(2,1)S(1)}, bf16[1,96,768]{2,1,0:T(8,128)(2,1)S(1)}, u32[]{:S(2)}, u32[]{:S(2)}) collective-permute-start(bf16[1,96,768]{2,1,0:T(8,128)(2,1)S(1)} %fusion.39), channel_id=1, source_target_pairs={{0,16},{1,17},{2,18},{3,19},{4,20},{5,21},{6,22},{7,23},{8,24},{9,... | collective-permute-start | bytes 442376 | tf_op jit(solution)/shard_map/ppermute | solution.py:635
  117.8 6.9 %collective-permute-done.24 = bf16[1,96,768]{2,1,0:T(8,128)(2,1)S(1)} collective-permute-done((bf16[1,96,768]{2,1,0:T(8,128)(2,1)S(1)}, bf16[1,96,768]{2,1,0:T(8,128)(2,1)S(1)}, u32[]{:S(2)}, u32[]{:S(2)}) %collective-permute-start.24) | collective-permute-done | bytes 147488 | tf_op jit(solution)/shard_map/ppermute | solution.py:635
  125.9 3.5 %collective-permute-done.32 = bf16[1,96,768]{2,1,0:T(8,128)(2,1)S(1)} collective-permute-done((bf16[1,96,768]{2,1,0:T(8,128)(2,1)S(1)}, bf16[1,96,768]{2,1,0:T(8,128)(2,1)S(1)}, u32[]{:S(2)}, u32[]{:S(2)}) %collective-permute-start.32) | collective-permute-done | bytes 147488 | tf_op jit(solution)/shard_map/ppermute | solution.py:635
  131.5 2.1 %collective-permute-start.36 = (bf16[1,200,384]{2,1,0:T(8,128)(2,1)S(1)}, bf16[1,200,384]{2,1,0:T(8,128)(2,1)S(1)}, u32[]{:S(2)}, u32[]{:S(2)}) collective-permute-start(bf16[1,200,384]{2,1,0:T(8,128)(2,1)S(1)} %fusion.27), channel_id=1, source_target_pairs={{0,8},{1,9},{2,10},{3,11},{4,12},{5,13},{6,14},{7,15},{8,0},{9,1},... | collective-permute-start | bytes 460808 | tf_op jit(solution)/shard_map/ppermute | solution.py:635
  134.8 1.7 collective-permute-done.30
  137.9 5.1 %collective-permute-done.37 = bf16[1,96,768]{2,1,0:T(8,128)(2,1)S(1)} collective-permute-done((bf16[1,96,768]{2,1,0:T(8,128)(2,1)S(1)}, bf16[1,96,768]{2,1,0:T(8,128)(2,1)S(1)}, u32[]{:S(2)}, u32[]{:S(2)}) %collective-permute-start.37) | collective-permute-done | bytes 147488 | tf_op jit(solution)/shard_map/ppermute | solution.py:635
  147.7 2.5 %collective-permute-done.39 = bf16[2,96,768]{2,1,0:T(8,128)(2,1)S(1)} collective-permute-done((bf16[2,96,768]{2,1,0:T(8,128)(2,1)S(1)}, bf16[2,96,768]{2,1,0:T(8,128)(2,1)S(1)}, u32[]{:S(2)}, u32[]{:S(2)}) %collective-permute-start.39) | collective-permute-done | bytes 294944 | tf_op jit(solution)/shard_map/ppermute | solution.py:635
  151.3 2.0 %collective-permute-start.47 = (bf16[4,96,768]{2,1,0:T(8,128)(2,1)S(1)}, bf16[4,96,768]{2,1,0:T(8,128)(2,1)S(1)}, u32[]{:S(2)}, u32[]{:S(2)}) collective-permute-start(bf16[4,96,768]{2,1,0:T(8,128)(2,1)S(1)} %pad_maximum_fusion.3.refs_0_), channel_id=1, source_target_pairs={{0,2},{1,5},{2,0},{3,7},{4,6},{5,1},{6,4},{7,3},{8,10},{9,13},{10,... | collective-permute-start | bytes 1769480 | tf_op jit(solution)/shard_map/ppermute | solution.py:635
  153.7 2.5 %collective-permute-start.45 = (bf16[4,96,768]{2,1,0:T(8,128)(2,1)S(1)}, bf16[4,96,768]{2,1,0:T(8,128)(2,1)S(1)}, u32[]{:S(2)}, u32[]{:S(2)}) collective-permute-start(bf16[4,96,768]{2,1,0:T(8,128)(2,1)S(1)} %pad_maximum_fusion.4.refs_0_), channel_id=1, source_target_pairs={{0,4},{1,9},{2,6},{3,11},{4,0},{5,13},{6,2},{7,15},{8,12},{9,1},{1... | collective-permute-start | bytes 1769480 | tf_op jit(solution)/shard_map/ppermute | solution.py:635
  156.3 1.9 collective-permute-done.40
  158.2 4.9 %collective-permute-done.41 = bf16[2,96,768]{2,1,0:T(8,128)(2,1)S(1)} collective-permute-done((bf16[2,96,768]{2,1,0:T(8,128)(2,1)S(1)}, bf16[2,96,768]{2,1,0:T(8,128)(2,1)S(1)}, u32[]{:S(2)}, u32[]{:S(2)}) %collective-permute-start.41) | collective-permute-done | bytes 294944 | tf_op jit(solution)/shard_map/ppermute | solution.py:635
  179.2 2.3 %collective-permute-done.48 = bf16[2,200,384]{2,1,0:T(8,128)(2,1)S(1)} collective-permute-done((bf16[2,200,384]{2,1,0:T(8,128)(2,1)S(1)}, bf16[2,200,384]{2,1,0:T(8,128)(2,1)S(1)}, u32[]{:S(2)}, u32[]{:S(2)}) %collective-permute-start.48) | collective-permute-done | bytes 307232 | tf_op jit(solution)/shard_map/ppermute | solution.py:635
  184.3 1.6 shard_map.291
  185.9 2.7 %collective-permute-done.52.refs_0_ = bf16[4,200,384]{2,1,0:T(8,128)(2,1)S(1)} collective-permute-done((bf16[4,200,384]{2,1,0:T(8,128)(2,1)S(1)}, bf16[4,200,384]{2,1,0:T(8,128)(2,1)S(1)}, u32[]{:S(2)}, u32[]{:S(2)}) %collective-permute-start.52) | collective-permute-done | bytes 614432 | tf_op jit(solution)/shard_map/ppermute | solution.py:635
  191.8 2.2 %shard_map.293 = (f32[3,768,384]{2,1,0:T(8,128)}, f32[384,768]{1,0:T(8,128)}, f32[2,384]{1,0:T(2,128)}, f32[1536]{0:T(1024)}, f32[768]{0:T(1024)}, /*index=5*/f3...) custom-call(s32[2]{0:T(128)S(1)} %compare_select_fusion.ids, ...), custom_call_target="tpu_custom_call", output_to_operand_aliasing={{0}: (3, {}), {1}: (4, {})} | custom-call | bytes 1843200 | tf_op jit(solution)/shard_map/pallas_call | solution.py:54
  (190 shorter events, 56.7 us)
Async XLA Ops:
  0.6 11.3 %collective-permute-start = (bf16[3,768,384]{2,1,0:T(8,128)(2,1)}, bf16[3,768,384]{2,1,0:T(8,128)(2,1)}, u32[]{:S(2)}, u32[]{:S(2)}) collective-permute-start(bf16[3,768,384]{2,1,0:T(8,128)(2,1)} %w_ref.3), channel_id=1, source_target_pairs={{0,1},{1,0},{2,3},{3,2},{4,5},{5,4},{6,7},{7,6},{8,9},{9,8},{10,11... | collective-permute-start | bytes 5308424 | tf_op jit(solution)/shard_map/ppermute | solution.py:620
  1.7 20.0 %collective-permute-start.3 = (bf16[768,1536]{1,0:T(8,128)(2,1)}, bf16[768,1536]{1,0:T(8,128)(2,1)S(1)}, u32[]{:S(2)}, u32[]{:S(2)}) collective-permute-start(bf16[768,1536]{1,0:T(8,128)(2,1)} %up_ref.1), channel_id=1, source_target_pairs={{0,1},{1,0},{2,3},{3,2},{4,5},{5,4},{6,7},{7,6},{8,9},{9,8},{10,11... | collective-permute-start | bytes 7077896 | tf_op jit(solution)/shard_map/ppermute | solution.py:620
  1.8 19.9 %collective-permute-start.4 = (f32[1536]{0:T(1024)}, f32[1536]{0:T(1024)S(1)}, u32[]{:S(2)}, u32[]{:S(2)}) collective-permute-start(f32[1536]{0:T(1024)} %bu_own.1), channel_id=1, source_target_pairs={{0,1},{1,0},{2,3},{3,2},{4,5},{5,4},{6,7},{7,6},{8,9},{9,8},{10,11... | collective-permute-start | bytes 18440 | tf_op jit(solution)/shard_map/ppermute | solution.py:620
  35.3 45.4 %collective-permute-start.12 = (bf16[512,768]{1,0:T(8,128)(2,1)}, bf16[512,768]{1,0:T(8,128)(2,1)}, u32[]{:S(2)}, u32[]{:S(2)}) collective-permute-start(bf16[512,768]{1,0:T(8,128)(2,1)} %get-tuple-element.114.refs_0_), channel_id=1, source_target_pairs={{0,1},{1,0},{2,3},{3,2},{4,5},{5,4},{6,7},{7,6},{8,9},{9,8},{10,11... | collective-permute-start | bytes 2359304 | tf_op jit(solution)/shard_map/ppermute | solution.py:620
  44.8 19.7 %collective-permute-start.11 = (bf16[4,96,768]{2,1,0:T(8,128)(2,1)}, bf16[4,96,768]{2,1,0:T(8,128)(2,1)}, u32[]{:S(2)}, u32[]{:S(2)}) collective-permute-start(bf16[4,96,768]{2,1,0:T(8,128)(2,1)} %fusion.4), channel_id=1, source_target_pairs={{0,4},{1,3},{2,6},{3,1},{4,0},{5,7},{6,2},{7,5},{8,12},{9,11},{10,... | collective-permute-start | bytes 1769480 | tf_op jit(solution)/shard_map/ppermute | solution.py:635
  51.5 11.1 %collective-permute-start.10 = (bf16[2,8,96,768]{3,2,1,0:T(8,128)(2,1)S(1)}, bf16[2,8,96,768]{3,2,1,0:T(8,128)(2,1)S(1)}, u32[]{:S(2)}, u32[]{:S(2)}) collective-permute-start(bf16[2,8,96,768]{3,2,1,0:T(8,128)(2,1)S(1)} %get-tuple-element.139), channel_id=1, source_target_pairs={{0,1},{1,0},{2,3},{3,2},{4,5},{5,4},{6,7},{7,6},{8,9},{9,8},{10,11... | collective-permute-start | bytes 7077896 | tf_op jit(solution)/shard_map/ppermute | solution.py:620
  60.7 20.3 %collective-permute-start.9 = (bf16[1,96,768]{2,1,0:T(8,128)(2,1)S(1)}, bf16[1,96,768]{2,1,0:T(8,128)(2,1)S(1)}, u32[]{:S(2)}, u32[]{:S(2)}) collective-permute-start(bf16[1,96,768]{2,1,0:T(8,128)(2,1)S(1)} %fusion.55), channel_id=1, source_target_pairs={{0,8},{1,9},{2,10},{3,11},{4,12},{5,13},{6,14},{7,15},{8,0},{9,1},... | collective-permute-start | bytes 442376 | tf_op jit(solution)/shard_map/ppermute | solution.py:635
  62.9 18.0 %collective-permute-start.13 = (bf16[4,96,768]{2,1,0:T(8,128)(2,1)S(1)}, bf16[4,96,768]{2,1,0:T(8,128)(2,1)S(1)}, u32[]{:S(2)}, u32[]{:S(2)}) collective-permute-start(bf16[4,96,768]{2,1,0:T(8,128)(2,1)S(1)} %fusion.3), channel_id=1, source_target_pairs={{0,2},{1,5},{2,0},{3,7},{4,6},{5,1},{6,4},{7,3},{8,10},{9,13},{10,... | collective-permute-start | bytes 1769480 | tf_op jit(solution)/shard_map/ppermute | solution.py:635
  65.7 19.5 %collective-permute-start.14 = (bf16[2,96,768]{2,1,0:T(8,128)(2,1)S(1)}, bf16[2,96,768]{2,1,0:T(8,128)(2,1)S(1)}, u32[]{:S(2)}, u32[]{:S(2)}) collective-permute-start(bf16[2,96,768]{2,1,0:T(8,128)(2,1)S(1)} %fusion.15), channel_id=1, source_target_pairs={{0,8},{1,9},{2,10},{3,11},{4,12},{5,13},{6,14},{7,15},{8,0},{9,1},... | collective-permute-start | bytes 884744 | tf_op jit(solution)/shard_map/ppermute | solution.py:635
  66.2 19.0 %collective-permute-start.15 = (bf16[4,96,768]{2,1,0:T(8,128)(2,1)S(1)}, bf16[4,96,768]{2,1,0:T(8,128)(2,1)S(1)}, u32[]{:S(2)}, u32[]{:S(2)}) collective-permute-start(bf16[4,96,768]{2,1,0:T(8,128)(2,1)S(1)} %fusion.2), channel_id=1, source_target_pairs={{0,2},{1,5},{2,0},{3,7},{4,6},{5,1},{6,4},{7,3},{8,10},{9,13},{10,... | collective-permute-start | bytes 1769480 | tf_op jit(solution)/shard_map/ppermute | solution.py:635
  80.7 21.6 %collective-permute-start.16 = (bf16[2,8,200,384]{3,2,1,0:T(8,128)(2,1)S(1)}, bf16[2,8,200,384]{3,2,1,0:T(8,128)(2,1)S(1)}, u32[]{:S(2)}, u32[]{:S(2)}) collective-permute-start(bf16[2,8,200,384]{3,2,1,0:T(8,128)(2,1)S(1)} %get-tuple-element.157), channel_id=1, source_target_pairs={{0,1},{1,0},{2,3},{3,2},{4,5},{5,4},{6,7},{7,6},{8,9},{9,8},{10,11... | collective-permute-start | bytes 7372808 | tf_op jit(solution)/shard_map/ppermute | solution.py:620
  81.1 19.3 %collective-permute-start.17 = (bf16[1,96,768]{2,1,0:T(8,128)(2,1)S(1)}, bf16[1,96,768]{2,1,0:T(8,128)(2,1)S(1)}, u32[]{:S(2)}, u32[]{:S(2)}) collective-permute-start(bf16[1,96,768]{2,1,0:T(8,128)(2,1)S(1)} %fusion.59), channel_id=1, source_target_pairs={{0,16},{1,17},{2,18},{3,19},{4,20},{5,21},{6,22},{7,23},{8,24},{9,... | collective-permute-start | bytes 442376 | tf_op jit(solution)/shard_map/ppermute | solution.py:635
  83.9 16.6 %collective-permute-start.18 = (bf16[2,96,768]{2,1,0:T(8,128)(2,1)S(1)}, bf16[2,96,768]{2,1,0:T(8,128)(2,1)S(1)}, u32[]{:S(2)}, u32[]{:S(2)}) collective-permute-start(bf16[2,96,768]{2,1,0:T(8,128)(2,1)S(1)} %fusion.13), channel_id=1, source_target_pairs={{0,4},{1,3},{2,6},{3,1},{4,0},{5,7},{6,2},{7,5},{8,12},{9,11},{10,... | collective-permute-start | bytes 884744 | tf_op jit(solution)/shard_map/ppermute | solution.py:635
  86.4 16.8 %collective-permute-start.20 = (bf16[1,96,768]{2,1,0:T(8,128)(2,1)S(1)}, bf16[1,96,768]{2,1,0:T(8,128)(2,1)S(1)}, u32[]{:S(2)}, u32[]{:S(2)}) collective-permute-start(bf16[1,96,768]{2,1,0:T(8,128)(2,1)S(1)} %fusion.52), channel_id=1, source_target_pairs={{0,2},{1,5},{2,0},{3,7},{4,6},{5,1},{6,4},{7,3},{8,10},{9,13},{10,... | collective-permute-start | bytes 442376 | tf_op jit(solution)/shard_map/ppermute | solution.py:635
  87.4 16.4 %collective-permute-start.21 = (bf16[2,96,768]{2,1,0:T(8,128)(2,1)S(1)}, bf16[2,96,768]{2,1,0:T(8,128)(2,1)S(1)}, u32[]{:S(2)}, u32[]{:S(2)}) collective-permute-start(bf16[2,96,768]{2,1,0:T(8,128)(2,1)S(1)} %fusion.11), channel_id=1, source_target_pairs={{0,4},{1,3},{2,6},{3,1},{4,0},{5,7},{6,2},{7,5},{8,12},{9,11},{10,... | collective-permute-start | bytes 884744 | tf_op jit(solution)/shard_map/ppermute | solution.py:635
  100.6 11.8 %collective-permute-start.26 = (bf16[1,96,768]{2,1,0:T(8,128)(2,1)S(1)}, bf16[1,96,768]{2,1,0:T(8,128)(2,1)S(1)}, u32[]{:S(2)}, u32[]{:S(2)}) collective-permute-start(bf16[1,96,768]{2,1,0:T(8,128)(2,1)S(1)} %fusion.49), channel_id=1, source_target_pairs={{0,8},{1,9},{2,10},{3,11},{4,12},{5,13},{6,14},{7,15},{8,0},{9,1},... | collective-permute-start | bytes 442376 | tf_op jit(solution)/shard_map/ppermute | solution.py:635
  104.0 20.8 %collective-permute-start.22 = (bf16[4,200,384]{2,1,0:T(8,128)(2,1)S(1)}, bf16[4,200,384]{2,1,0:T(8,128)(2,1)S(1)}, u32[]{:S(2)}, u32[]{:S(2)}) collective-permute-start(bf16[4,200,384]{2,1,0:T(8,128)(2,1)S(1)} %fusion), channel_id=1, source_target_pairs={{0,2},{1,5},{2,0},{3,7},{4,6},{5,1},{6,4},{7,3},{8,10},{9,13},{10,... | collective-permute-start | bytes 1843208 | tf_op jit(solution)/shard_map/ppermute | solution.py:635
  105.6 10.9 %collective-permute-start.23 = (bf16[1,96,768]{2,1,0:T(8,128)(2,1)S(1)}, bf16[1,96,768]{2,1,0:T(8,128)(2,1)S(1)}, u32[]{:S(2)}, u32[]{:S(2)}) collective-permute-start(bf16[1,96,768]{2,1,0:T(8,128)(2,1)S(1)} %fusion.46), channel_id=1, source_target_pairs={{0,8},{1,9},{2,10},{3,11},{4,12},{5,13},{6,14},{7,15},{8,0},{9,1},... | collective-permute-start | bytes 442376 | tf_op jit(solution)/shard_map/ppermute | solution.py:635
  112.4 12.3 %collective-permute-start.24 = (bf16[1,96,768]{2,1,0:T(8,128)(2,1)S(1)}, bf16[1,96,768]{2,1,0:T(8,128)(2,1)S(1)}, u32[]{:S(2)}, u32[]{:S(2)}) collective-permute-start(bf16[1,96,768]{2,1,0:T(8,128)(2,1)S(1)} %fusion.43), channel_id=1, source_target_pairs={{0,16},{1,17},{2,18},{3,19},{4,20},{5,21},{6,22},{7,23},{8,24},{9,... | collective-permute-start | bytes 442376 | tf_op jit(solution)/shard_map/ppermute | solution.py:635
  113.6 15.8 %collective-permute-start.31 = (bf16[2,200,384]{2,1,0:T(8,128)(2,1)S(1)}, bf16[2,200,384]{2,1,0:T(8,128)(2,1)S(1)}, u32[]{:S(2)}, u32[]{:S(2)}) collective-permute-start(bf16[2,200,384]{2,1,0:T(8,128)(2,1)S(1)} %fusion.9), channel_id=1, source_target_pairs={{0,4},{1,3},{2,6},{3,1},{4,0},{5,7},{6,2},{7,5},{8,12},{9,11},{10,... | collective-permute-start | bytes 921608 | tf_op jit(solution)/shard_map/ppermute | solution.py:635
  114.5 15.0 %collective-permute-start.32 = (bf16[1,96,768]{2,1,0:T(8,128)(2,1)S(1)}, bf16[1,96,768]{2,1,0:T(8,128)(2,1)S(1)}, u32[]{:S(2)}, u32[]{:S(2)}) collective-permute-start(bf16[1,96,768]{2,1,0:T(8,128)(2,1)S(1)} %fusion.39), channel_id=1, source_target_pairs={{0,16},{1,17},{2,18},{3,19},{4,20},{5,21},{6,22},{7,23},{8,24},{9,... | collective-permute-start | bytes 442376 | tf_op jit(solution)/shard_map/ppermute | solution.py:635
  116.5 12.9 %collective-permute-start.33 = (bf16[2,96,768]{2,1,0:T(8,128)(2,1)S(1)}, bf16[2,96,768]{2,1,0:T(8,128)(2,1)S(1)}, u32[]{:S(2)}, u32[]{:S(2)}) collective-permute-start(bf16[2,96,768]{2,1,0:T(8,128)(2,1)S(1)} %pad_maximum_fusion.8), channel_id=1, source_target_pairs={{0,4},{1,3},{2,6},{3,1},{4,0},{5,7},{6,2},{7,5},{8,12},{9,11},{10,... | collective-permute-start | bytes 884744 | tf_op jit(solution)/shard_map/ppermute | solution.py:635
  124.8 11.6 %collective-permute-start.28 = (bf16[2,200,384]{2,1,0:T(8,128)(2,1)S(1)}, bf16[2,200,384]{2,1,0:T(8,128)(2,1)S(1)}, u32[]{:S(2)}, u32[]{:S(2)}) collective-permute-start(bf16[2,200,384]{2,1,0:T(8,128)(2,1)S(1)} %fusion.7), channel_id=1, source_target_pairs={{0,4},{1,3},{2,6},{3,1},{4,0},{5,7},{6,2},{7,5},{8,12},{9,11},{10,... | collective-permute-start | bytes 921608 | tf_op jit(solution)/shard_map/ppermute | solution.py:635
  129.6 15.3 %collective-permute-start.35 = (bf16[4,96,768]{2,1,0:T(8,128)(2,1)S(1)}, bf16[4,96,768]{2,1,0:T(8,128)(2,1)S(1)}, u32[]{:S(2)}, u32[]{:S(2)}) collective-permute-start(bf16[4,96,768]{2,1,0:T(8,128)(2,1)S(1)} %pad_maximum_fusion.2.refs_0_), channel_id=1, source_target_pairs={{0,2},{1,5},{2,0},{3,7},{4,6},{5,1},{6,4},{7,3},{8,10},{9,13},{10,... | collective-permute-start | bytes 1769480 | tf_op jit(solution)/shard_map/ppermute | solution.py:635
  131.5 12.1 %collective-permute-start.36 = (bf16[1,200,384]{2,1,0:T(8,128)(2,1)S(1)}, bf16[1,200,384]{2,1,0:T(8,128)(2,1)S(1)}, u32[]{:S(2)}, u32[]{:S(2)}) collective-permute-start(bf16[1,200,384]{2,1,0:T(8,128)(2,1)S(1)} %fusion.27), channel_id=1, source_target_pairs={{0,8},{1,9},{2,10},{3,11},{4,12},{5,13},{6,14},{7,15},{8,0},{9,1},... | collective-permute-start | bytes 460808 | tf_op jit(solution)/shard_map/ppermute | solution.py:635
  136.6 11.1 %collective-permute-start.34 = (bf16[1,200,384]{2,1,0:T(8,128)(2,1)S(1)}, bf16[1,200,384]{2,1,0:T(8,128)(2,1)S(1)}, u32[]{:S(2)}, u32[]{:S(2)}) collective-permute-start(bf16[1,200,384]{2,1,0:T(8,128)(2,1)S(1)} %fusion.24), channel_id=1, source_target_pairs={{0,8},{1,9},{2,10},{3,11},{4,12},{5,13},{6,14},{7,15},{8,0},{9,1},... | collective-permute-start | bytes 460808 | tf_op jit(solution)/shard_map/ppermute | solution.py:635
  136.7 11.0 %collective-permute-start.38 = (bf16[1,96,768]{2,1,0:T(8,128)(2,1)S(1)}, bf16[1,96,768]{2,1,0:T(8,128)(2,1)S(1)}, u32[]{:S(2)}, u32[]{:S(2)}) collective-permute-start(bf16[1,96,768]{2,1,0:T(8,128)(2,1)S(1)} %add_convert_fusion.2), channel_id=1, source_target_pairs={{0,2},{1,9},{2,0},{3,11},{4,6},{5,13},{6,4},{7,15},{8,10},{9,1},{1... | collective-permute-start | bytes 442376 | tf_op jit(solution)/shard_map/ppermute | solution.py:635
  150.9 12.2 %collective-permute-start.41 = (bf16[2,96,768]{2,1,0:T(8,128)(2,1)S(1)}, bf16[2,96,768]{2,1,0:T(8,128)(2,1)S(1)}, u32[]{:S(2)}, u32[]{:S(2)}) collective-permute-start(bf16[2,96,768]{2,1,0:T(8,128)(2,1)S(1)} %pad_maximum_fusion.11), channel_id=1, source_target_pairs={{0,8},{1,5},{2,10},{3,7},{4,12},{5,1},{6,14},{7,3},{8,0},{9,13},{1... | collective-permute-start | bytes 884744 | tf_op jit(solution)/shard_map/ppermute | solution.py:635
  151.3 15.4 %collective-permute-start.47 = (bf16[4,96,768]{2,1,0:T(8,128)(2,1)S(1)}, bf16[4,96,768]{2,1,0:T(8,128)(2,1)S(1)}, u32[]{:S(2)}, u32[]{:S(2)}) collective-permute-start(bf16[4,96,768]{2,1,0:T(8,128)(2,1)S(1)} %pad_maximum_fusion.3.refs_0_), channel_id=1, source_target_pairs={{0,2},{1,5},{2,0},{3,7},{4,6},{5,1},{6,4},{7,3},{8,10},{9,13},{10,... | collective-permute-start | bytes 1769480 | tf_op jit(solution)/shard_map/ppermute | solution.py:635
  153.7 19.2 %collective-permute-start.45 = (bf16[4,96,768]{2,1,0:T(8,128)(2,1)S(1)}, bf16[4,96,768]{2,1,0:T(8,128)(2,1)S(1)}, u32[]{:S(2)}, u32[]{:S(2)}) collective-permute-start(bf16[4,96,768]{2,1,0:T(8,128)(2,1)S(1)} %pad_maximum_fusion.4.refs_0_), channel_id=1, source_target_pairs={{0,4},{1,9},{2,6},{3,11},{4,0},{5,13},{6,2},{7,15},{8,12},{9,1},{1... | collective-permute-start | bytes 1769480 | tf_op jit(solution)/shard_map/ppermute | solution.py:635
  156.2 12.1 %collective-permute-start.46 = (bf16[1,200,384]{2,1,0:T(8,128)(2,1)S(1)}, bf16[1,200,384]{2,1,0:T(8,128)(2,1)S(1)}, u32[]{:S(2)}, u32[]{:S(2)}) collective-permute-start(bf16[1,200,384]{2,1,0:T(8,128)(2,1)S(1)} %add_convert_fusion.1), channel_id=1, source_target_pairs={{0,8},{1,3},{2,10},{3,1},{4,12},{5,7},{6,14},{7,5},{8,0},{9,11},{1... | collective-permute-start | bytes 460808 | tf_op jit(solution)/shard_map/ppermute | solution.py:635
  163.2 13.6 %collective-permute-start.49 = (bf16[4,96,768]{2,1,0:T(8,128)(2,1)S(1)}, bf16[4,96,768]{2,1,0:T(8,128)(2,1)S(1)}, u32[]{:S(2)}, u32[]{:S(2)}) collective-permute-start(bf16[4,96,768]{2,1,0:T(8,128)(2,1)S(1)} %pad_maximum_fusion.5.refs_0_), channel_id=1, source_target_pairs={{0,4},{1,3},{2,6},{3,1},{4,0},{5,7},{6,2},{7,5},{8,12},{9,11},{10,... | collective-permute-start | bytes 1769480 | tf_op jit(solution)/shard_map/ppermute | solution.py:635
  (45 other events, 363.6 us)
